TPU v7x, 32 devices: a whole 2x2x4 slice. The times are simulated.
32 devices in a mesh: dp: 8 (over z, y), col: 4 (over x, core).
Axes of the slice: x: 2, y: 2, z: 4, core: 2. Of those that a mesh axis runs over, the one named last changes fastest.
Arguments:
- tokens: bfloat16 [8192, 8192], P('dp', 'col'), may hold values from -6 to 6
- out_grad: bfloat16 [8192, 8192], P(('dp', 'col')), may hold values from -6 to 6
- weight: float32 [8192, 8192], P('dp', 'col'), may hold values from -6 to 6
- second: float32 [8192, 8192], P('dp', 'col'), may hold values from 0.0001 to 0.001
- momentum: float32 [8192, 512], P(('dp', 'col')), may hold values from -0.12 to 0.12
- sign_seed: int32 [1], replicated, may hold values from 0 to 999999
- step_number: int32 [1], replicated, may hold values from 1 to 999999
Outputs:
- new_weight: float32 [8192, 8192], P('dp', 'col')
- new_second: float32 [8192, 8192], P('dp', 'col')
- new_momentum: float32 [8192, 512], P(('dp', 'col'))
All inputs are finite; a program needn't handle non-finite values.
Results may differ from a plain program's by a relative error of at most 0.00097.
Values may be sent and summed in bfloat16 or wider, within the bound.
No kernel may reach another device: no remote copies, remote signals or barrier semaphores. Data moves between devices by JAX's collectives and lax.ppermute only.
A program may use at most 128 MiB of HBM per device.

v0:
```python
import functools
import math

import jax
import jax.numpy as jnp
from jax import lax
from jax.experimental import pallas as pl
from jax.experimental.pallas import tpu as pltpu
from jax.sharding import PartitionSpec as P


AXES = ("dp", "col")
LANES = 128


def low_bits(mixed):
    mixed = mixed ^ lax.shift_right_logical(mixed, 16)
    mixed = mixed * 2127912213
    mixed = mixed ^ lax.shift_right_logical(mixed, 13)
    mixed = mixed * 1103515245
    mixed = mixed ^ lax.shift_right_logical(mixed, 16)
    return mixed & (1 << 20)


def sign_table(sign_seed, step_number, first_row, row_count, low_rank):
    row_ids = first_row + lax.iota(jnp.int32, row_count)
    col_ids = lax.iota(jnp.int32, low_rank)
    flat_index = row_ids[:, None] * low_rank + col_ids[None, :]
    seeded = sign_seed[0] * 1664525 + step_number[0] * 1013904223
    return jnp.where(low_bits(flat_index * 747796405 + seeded) == 0, 1.0, -1.0)


def contract(left_rows, right_rows):
    return lax.dot_general(
        left_rows, right_rows, (((0,), (0,)), ((), ())), preferred_element_type=jnp.float32
    )


def general(tokens, out_grad, weight, second, momentum, sign_seed, step_number):
    local_tokens, din_local = tokens.shape
    low_rank = momentum.shape[1]
    owner_rows = momentum.shape[0]
    inv_root = 1.0 / jnp.sqrt(jnp.float32(low_rank))
    col_position = lax.axis_index("col")
    sign_block = sign_table(sign_seed, step_number, col_position * din_local, din_local, low_rank)
    partial_sketch = (
        jnp.dot(tokens, sign_block.astype(jnp.bfloat16), preferred_element_type=jnp.float32)
        * inv_root
    )
    quarter = lax.psum_scatter(partial_sketch, "col", scatter_dimension=0, tiled=True)
    sketch = quarter.astype(jnp.bfloat16)
    total_tokens = lax.axis_size("dp") * local_tokens
    data_count = lax.axis_size("dp")
    col_count = lax.axis_size("col")
    quarter_rows = out_grad.shape[0]
    grouped = out_grad.reshape(quarter_rows, data_count, col_count, owner_rows)
    grouped = jnp.transpose(grouped, (0, 2, 1, 3)).reshape(
        quarter_rows, col_count, data_count * owner_rows
    )
    regrouped = lax.all_to_all(grouped, "col", split_axis=1, concat_axis=0, tiled=True)
    regrouped = regrouped.reshape(quarter_rows * col_count, data_count * owner_rows)
    shard_sketch = lax.all_gather(sketch, "col", axis=0, tiled=True)
    projected = lax.psum_scatter(
        contract(regrouped, shard_sketch), "dp", scatter_dimension=0, tiled=True
    )
    projected = projected / jnp.float32(total_tokens)
    new_momentum = 0.8 * momentum + 0.2 * projected
    row_block = lax.all_gather(new_momentum, "col", axis=0, tiled=True)
    dense_grad = (
        lax.dot_general(
            row_block,
            sign_block,
            (((1,), (1,)), ((), ())),
            precision=lax.Precision.HIGHEST,
            preferred_element_type=jnp.float32,
        )
        * inv_root
    )
    new_second = 0.95 * second + 0.05 * dense_grad * dense_grad
    new_weight = weight - 0.5 * dense_grad / (jnp.sqrt(new_second) + 1e-08)
    return (new_weight, new_second, new_momentum)


def params(vmem=56 * 1024 * 1024, axes=1):
    return pltpu.CompilerParams(
        dimension_semantics=("arbitrary",) * axes, vmem_limit_bytes=vmem
    )


def pack_kernel(groups, width, part, seeded, og_ref, *refs):
    if seeded:
        seed_ref, step_ref, *refs = refs
        columns_ref, *refs = refs
        *refs, seed, step, seed_sem = refs
        copies = [
            pltpu.make_async_copy(seed_ref, seed, seed_sem.at[0]),
            pltpu.make_async_copy(step_ref, step, seed_sem.at[1]),
        ]
        for copy in copies:
            copy.start()
    n_out = len(groups)
    outs = refs[:n_out]
    stage, in_sem, out_sem = refs[n_out:]
    me = lax.axis_index("dp") * lax.axis_size("col") + lax.axis_index("col")
    loads = []
    slot = 0
    for group in groups:
        mine = []
        for rel, half in group:
            first = pl.multiple_of((me ^ rel) * width + half * part, part)
            copy = pltpu.make_async_copy(
                og_ref.at[:, pl.ds(first, part)], stage.at[slot], in_sem.at[slot]
            )
            copy.start()
            mine.append(copy)
            slot += 1
        loads.append(mine)
    if seeded:
        for copy in copies:
            copy.wait()
        constant = seed[...] * 1664525 + step[...] * 1013904223
        ids = lax.broadcasted_iota(jnp.int32, columns_ref.shape, 1)
        columns_ref[...] = ids * 747796405 + constant
    stores = []
    slot = 0
    for index, group in enumerate(groups):
        for copy in loads[index]:
            copy.wait()
        store = pltpu.make_async_copy(
            stage.at[pl.ds(slot, len(group))], outs[index], out_sem.at[index]
        )
        store.start()
        stores.append(store)
        slot += len(group)
    for store in stores:
        store.wait()


def pack(out_grad, groups, width, part, seeds=(), low_rank=None):
    rows = out_grad.shape[0]
    count = sum(len(group) for group in groups)
    hbm = pl.BlockSpec(memory_space=pl.ANY)
    out_specs = [hbm] * len(groups)
    out_shape = [
        jax.ShapeDtypeStruct((len(group), rows, part), out_grad.dtype) for group in groups
    ]
    scratch = [
        pltpu.VMEM((count, rows, part), out_grad.dtype),
        pltpu.SemaphoreType.DMA((count,)),
        pltpu.SemaphoreType.DMA((len(groups),)),
    ]
    if seeds:
        out_specs = [pl.BlockSpec(memory_space=pltpu.VMEM)] + out_specs
        out_shape = [jax.ShapeDtypeStruct((1, low_rank), jnp.int32)] + out_shape
        scratch += [pltpu.VMEM((1, 1), jnp.int32)] * 2 + [pltpu.SemaphoreType.DMA((2,))]
    return pl.pallas_call(
        functools.partial(pack_kernel, groups, width, part, bool(seeds)),
        in_specs=[hbm] * (1 + len(seeds)),
        out_specs=out_specs,
        out_shape=out_shape,
        scratch_shapes=scratch,
        compiler_params=pltpu.CompilerParams(vmem_limit_bytes=8 * 1024 * 1024),
        cost_estimate=pl.CostEstimate(
            flops=0, bytes_accessed=4 * count * rows * part, transcendentals=0
        ),
        name="pack",
    )(pltpu.with_memory_space_constraint(out_grad, pltpu.HBM), *seeds)


CHUNKS = 4
STRIP = 32


def sketch_kernel(first, din_local, *refs):
    if first:
        columns_ref, tok_ref, signs_ref, send_ref, keep_ref, tok, acc, sem = refs
    else:
        tok_ref, signs_ref, send_ref, keep_ref, tok, acc, sem = refs
    quarter, low_rank = keep_ref.shape
    chunk = din_local // CHUNKS
    col = lax.axis_index("col")
    group = col ^ (X if first else 0)
    loads = []
    for part in range(CHUNKS):
        at = pl.ds(part * chunk, chunk)
        mine = []
        for slot, rel in enumerate((CORE, 0)):
            rows = pl.ds(pl.multiple_of((group ^ rel) * quarter, quarter), quarter)
            copy = pltpu.make_async_copy(
                tok_ref.at[rows, at],
                tok.at[pl.ds(slot * quarter, quarter), at],
                sem.at[part, slot],
            )
            copy.start()
            mine.append(copy)
        loads.append(mine)
    if first:
        row_factor = low_rank * 747796405
        row_factor = (row_factor + (1 << 31)) % (1 << 32) - (1 << 31)
        local = lax.broadcasted_iota(jnp.int32, (STRIP, low_rank), 0) * row_factor
        local = local + columns_ref[...]
    for part in range(CHUNKS):
        at = slice(part * chunk, (part + 1) * chunk)
        if first:
            for row in range(part * chunk, (part + 1) * chunk, STRIP):
                mixed = local + (col * din_local + row) * row_factor
                strip = jnp.where(low_bits(mixed) == 0, 1.0, -1.0)
                signs_ref[row : row + STRIP, :] = strip.astype(jnp.bfloat16)
        for copy in loads[part]:
            copy.wait()
        product = jnp.dot(tok[:, at], signs_ref[at, :], preferred_element_type=jnp.float32)
        if part > 0:
            product += acc[...]
        if part < CHUNKS - 1:
            acc[...] = product
        else:
            send_ref[...] = product[:quarter]
            keep_ref[...] = product[quarter:]


def sketch_parts(tokens, low_rank, signs, columns):
    local_tokens, din_local = tokens.shape
    half = local_tokens // 2
    quarter = half // 2
    first = signs is None
    vmem = pl.BlockSpec(memory_space=pltpu.VMEM)
    hbm = pl.BlockSpec(memory_space=pl.ANY)
    parts = [jax.ShapeDtypeStruct((quarter, low_rank), jnp.float32)] * 2
    tokens = pltpu.with_memory_space_constraint(tokens, pltpu.HBM)
    if first:
        in_specs, args = [vmem, hbm], (columns, tokens)
        out_shape = [jax.ShapeDtypeStruct((din_local, low_rank), jnp.bfloat16)] + parts
    else:
        in_specs, args = [hbm, vmem], (tokens, signs)
        out_shape = parts
    return pl.pallas_call(
        functools.partial(sketch_kernel, first, din_local),
        in_specs=in_specs,
        out_specs=[vmem] * len(out_shape),
        out_shape=out_shape,
        scratch_shapes=[
            pltpu.VMEM((half, din_local), tokens.dtype),
            pltpu.VMEM((half, low_rank), jnp.float32),
            pltpu.SemaphoreType.DMA((CHUNKS, 2)),
        ],
        compiler_params=pltpu.CompilerParams(vmem_limit_bytes=12 * 1024 * 1024),
        cost_estimate=pl.CostEstimate(
            flops=2 * half * din_local * low_rank,
            bytes_accessed=half * din_local * 2 + din_local * low_rank * 2 + 2 * half * low_rank * 4,
            transcendentals=0,
        ),
        name="sketch_first" if first else "sketch_next",
    )(*args)


def project_kernel(n, *refs):
    send_ref, keep_ref = refs[-2:]
    count, _, part = refs[n].shape
    sketch = jnp.concatenate([ref[...] for ref in refs[:n]], axis=0)
    grads = jnp.concatenate(
        [
            jnp.concatenate([ref[j] for j in range(count)], axis=1)
            for ref in refs[n : 2 * n]
        ],
        axis=0,
    )
    total = contract(grads, sketch)
    for j in range(count):
        out_ref = send_ref if j < count // 2 else keep_ref
        out_ref[j % (count // 2)] = total[j * part : (j + 1) * part]


def project(sketches, grads, offsets, count):
    rows, low_rank = sketches[0].shape
    part = grads[0].shape[2]
    n = len(sketches)

    def block_at(offset):
        return pl.BlockSpec((count, rows, part), lambda i: (offset // count, 0, 0))

    out = jax.ShapeDtypeStruct((count // 2, part, low_rank), jnp.float32)
    return pl.pallas_call(
        functools.partial(project_kernel, n),
        grid=(1,),
        in_specs=[pl.BlockSpec((rows, low_rank), lambda i: (0, 0))] * n
        + [block_at(offset) for offset in offsets],
        out_specs=[pl.BlockSpec((count // 2, part, low_rank), lambda i: (0, 0, 0))] * 2,
        out_shape=[out] * 2,
        compiler_params=params(10 * 1024 * 1024),
        cost_estimate=pl.CostEstimate(
            flops=2 * n * count * rows * part * low_rank,
            bytes_accessed=n * (rows * low_rank + count * rows * part) * 2
            + count * low_rank * part * 4,
            transcendentals=0,
        ),
        name="project",
    )(*sketches, *grads)


def prefetch_kernel(*refs):
    n = (len(refs) - 1) // 2
    sources, targets, sem = refs[:n], refs[n : 2 * n], refs[-1]
    pieces = sem.shape[1]
    copies = []
    for at in range(pieces):
        for k, (source, target) in enumerate(zip(sources, targets)):
            rows = source.shape[0] // pieces
            window = pl.ds(at * rows, rows)
            copy = pltpu.make_async_copy(source.at[window], target.at[window], sem.at[k, at])
            copy.start()
            copies.append(copy)
    for copy in copies:
        copy.wait()


def prefetch(*arrays):
    n = len(arrays)
    size = sum(array.size * array.dtype.itemsize for array in arrays)
    return pl.pallas_call(
        prefetch_kernel,
        in_specs=[pl.BlockSpec(memory_space=pl.ANY)] * n,
        out_specs=[pl.BlockSpec(memory_space=pltpu.VMEM)] * n,
        out_shape=[jax.ShapeDtypeStruct(array.shape, array.dtype) for array in arrays],
        scratch_shapes=[pltpu.SemaphoreType.DMA((n, 4))],
        compiler_params=pltpu.CompilerParams(vmem_limit_bytes=size + 2 * 1024 * 1024),
        cost_estimate=pl.CostEstimate(flops=0, bytes_accessed=size, transcendentals=0),
        name="prefetch",
    )(*[pltpu.with_memory_space_constraint(array, pltpu.HBM) for array in arrays])


def update_kernel(where, keep, slabs, tile, *refs):
    n = len(where)
    rows_refs = refs[:n]
    signs_ref, weight_ref, second_ref = refs[n : n + 3]
    new_weight_ref, new_second_ref, new_momentum_ref = refs[-7:-4]
    nw_buf, ns_buf, out_sem, keep_sem = refs[-4:]
    part, low_rank = rows_refs[0].shape
    width = signs_ref.shape[0]
    slab = width // slabs
    gain = math.sqrt(0.05) / math.sqrt(low_rank)
    back = 0.5 / math.sqrt(0.05)
    nt = (((1,), (1,)), ((), ()))
    col = lax.axis_index("col")
    firsts = [pl.multiple_of(((col ^ rel) * 2 + half) * part, part) for rel, half in where]
    stores = []
    if keep:
        half = where[0][1]
        store = pltpu.make_async_copy(
            rows_refs[0], new_momentum_ref.at[pl.ds(half * part, part)], keep_sem.at[0]
        )
        store.start()
        stores.append(store)
    rows = jnp.concatenate([ref[...] for ref in rows_refs], axis=0) * gain
    high = rows.astype(jnp.bfloat16)
    low = (rows - high.astype(jnp.float32)).astype(jnp.bfloat16)
    for k in range(slabs):
        for at in range(k * slab, (k + 1) * slab, tile):
            signs = signs_ref[at : at + tile, :]
            dense = lax.dot_general(high, signs, nt, preferred_element_type=jnp.float32)
            dense += lax.dot_general(low, signs, nt, preferred_element_type=jnp.float32)
            columns = slice(at - k * slab, at - k * slab + tile)
            for b in range(n):
                mine = dense[b * part : (b + 1) * part]
                here = (pl.ds(firsts[b], part), slice(at, at + tile))
                new_second = 0.95 * second_ref[here] + mine * mine
                bottom = new_second * lax.rsqrt(new_second) + 1e-08
                inverse = pl.reciprocal(bottom, approx=True)
                inverse = inverse * (2.0 - bottom * inverse)
                ns_buf[k * n + b, :, columns] = new_second
                nw_buf[k * n + b, :, columns] = weight_ref[here] - (mine * back) * inverse
        for b in range(n):
            slot = k * n + b
            window = (pl.ds(firsts[b], part), pl.ds(k * slab, slab))
            for kind, (buf, ref) in enumerate(
                ((nw_buf, new_weight_ref), (ns_buf, new_second_ref))
            ):
                store = pltpu.make_async_copy(
                    buf.at[slot], ref.at[window], out_sem.at[kind, slot]
                )
                store.start()
                stores.append(store)
    for store in stores:
        store.wait()


def update(row_blocks, where, keep, signs, weight, second, onto):
    part, low_rank = row_blocks[0].shape
    din_local = weight.shape[1]
    n = len(row_blocks)
    slabs = 4
    slab = din_local // slabs
    hbm = pl.BlockSpec(memory_space=pl.ANY)
    vmem = pl.BlockSpec(memory_space=pltpu.VMEM)
    in_specs = [vmem] * (n + 3)
    aliases = {}
    if onto:
        in_specs += [hbm] * 3
        aliases = {n + 3 + k: k for k in range(3)}
    size = n * part * din_local
    buf = pltpu.VMEM((slabs * n, part, slab), jnp.float32)
    return pl.pallas_call(
        functools.partial(update_kernel, where, keep, slabs, min(slab, 256)),
        in_specs=in_specs,
        out_specs=[hbm] * 3,
        out_shape=[
            jax.ShapeDtypeStruct(weight.shape, jnp.float32),
            jax.ShapeDtypeStruct(second.shape, jnp.float32),
            jax.ShapeDtypeStruct((2 * part, low_rank), jnp.float32),
        ],
        scratch_shapes=[
            buf,
            buf,
            pltpu.SemaphoreType.DMA((2, slabs * n)),
            pltpu.SemaphoreType.DMA((1,)),
        ],
        input_output_aliases=aliases,
        compiler_params=pltpu.CompilerParams(
            vmem_limit_bytes=8 * size + 8 * 1024 * 1024
        ),
        cost_estimate=pl.CostEstimate(
            flops=4 * size * low_rank, bytes_accessed=8 * size, transcendentals=2 * size
        ),
        name="update",
    )(*row_blocks, signs, weight, second, *onto)


CORE, X, Y, Z0, Z1 = 1, 2, 4, 8, 16


def exchange(value, mask):
    size = lax.axis_size("dp") * lax.axis_size("col")
    return lax.ppermute(value, AXES, [(i, i ^ mask) for i in range(size)])


def stepped(tokens, out_grad, weight, second, momentum, sign_seed, step_number):
    low_rank = momentum.shape[1]
    owner_rows = momentum.shape[0]
    total_tokens = lax.axis_size("dp") * tokens.shape[0]
    inv_root = 1.0 / jnp.sqrt(jnp.float32(low_rank))
    far0 = [(Z1 | X | Z0, 0), (Z1 | X, 0), (Z1 | Z0, 0), (Z1, 0)]
    near0 = [(Z0 | X, 0), (Z0, 0), (X, 0), (0, 0)]
    far1 = [(Z1 | Y | X, 1), (Z1 | Y, 1), (Z1 | X, 1), (Z1, 1)]
    near1 = [(Y | X, 1), (Y, 1), (X, 1), (0, 1)]

    def toward(mask, pieces):
        return [(rel ^ mask, half) for rel, half in pieces]

    part = owner_rows // 2
    over_y, over_z = far0 + near0, far1 + near1
    columns, og_y, og_z = pack(
        out_grad,
        [toward(Y, over_y), toward(Z0, over_z)],
        owner_rows,
        part,
        (sign_seed.reshape(1, 1), step_number.reshape(1, 1)),
        low_rank,
    )
    og_y = exchange(og_y, Y)
    og_z = exchange(og_z, Z0)
    signs, send_a, keep_a = sketch_parts(tokens, low_rank, None, columns)
    og_yc, og_zc = pack(
        out_grad, [toward(Y | CORE, over_y), toward(Z0 | CORE, over_z)], owner_rows, part
    )
    og_c, og_own = pack(
        out_grad,
        [toward(CORE, over_y + over_z), over_y + over_z],
        owner_rows,
        part,
    )
    got_a = exchange(send_a, CORE)
    across = exchange(keep_a + got_a, X)
    og_yc = exchange(og_yc, Y | CORE)
    og_zc = exchange(og_zc, Z0 | CORE)
    og_c = exchange(og_c, CORE)
    send_b, keep_b = sketch_parts(tokens, low_rank, signs, None)
    weight_v, second_v = prefetch(weight, second)
    got_b = exchange(send_b, CORE)
    sketch = (((keep_b + got_b) + across) * inv_root).astype(jnp.bfloat16)

    sk_y = exchange(sketch, Y)
    sk_z = exchange(sketch, Z0)
    sk_c = exchange(sketch, CORE)
    sk_yc = exchange(sk_y, CORE)
    sk_zc = exchange(sk_z, CORE)

    scale = jnp.float32(1.0 / total_tokens)

    def packed(value, extra):
        return (value * (scale * extra)).astype(jnp.float16)

    def unpacked(value, extra):
        return value.astype(jnp.float32) * (1.0 / (scale * extra))

    y_side = (sketch, sk_c, sk_y, sk_yc), (og_own, og_c, og_y, og_yc)
    z_side = (sketch, sk_c, sk_z, sk_zc), (og_own, og_c, og_z, og_zc)

    def begin(side, offsets, axis):
        send, keep = project(*side, offsets, 4)
        return exchange(packed(send, 8.0), axis), keep

    def middle(state, axis):
        got, keep = state
        ahead = exchange(packed(keep[0] + unpacked(got[0], 8.0), 4.0), axis)
        return ahead, keep[1] + unpacked(got[1], 8.0)

    def finish(state):
        got, keep = state
        return keep + unpacked(got, 4.0)

    far0_state = begin(y_side, (0, 0, 0, 0), X)
    far1_state = begin(z_side, (8, 8, 0, 0), Y)
    near0_state = begin(y_side, (4, 4, 4, 4), Z0)
    near1_state = begin(z_side, (12, 12, 4, 4), Y)
    far0_state = middle(far0_state, Z0)
    far1_state = middle(far1_state, X)
    last0 = exchange(packed(finish(far0_state), 2.0), Z1)
    last1 = exchange(packed(finish(far1_state), 2.0), Z1)
    near0_state = middle(near0_state, X)
    near1_state = middle(near1_state, X)

    def momentum_half(half, near, last):
        projected = (near + unpacked(last, 2.0)) * scale
        return 0.8 * momentum[half * part : (half + 1) * part] + 0.2 * projected

    halves, pieces = [], []
    small = None
    for half, near_state, last in ((0, near0_state, last0), (1, near1_state, last1)):
        if small is not None:
            last, _ = lax.optimization_barrier((last, small))
        mine = momentum_half(half, finish(near_state), last)
        small = mine.astype(jnp.float16)
        from_core = exchange(small, CORE)
        from_x = exchange(small, X)
        from_xc = exchange(from_x, CORE)
        halves.append(mine)
        pieces.append([v.astype(jnp.float32) for v in (from_core, from_x, from_xc)])
    rows = (halves[0], pieces[0][0])
    done = update(rows, ((0, 0), (CORE, 0)), True, signs, weight_v, second_v, ())
    rows = (halves[1], pieces[1][0], pieces[0][1], pieces[0][2])
    where = ((0, 1), (CORE, 1), (X, 0), (X | CORE, 0))
    done = update(rows, where, True, signs, weight_v, second_v, tuple(done))
    rows = (pieces[1][1], pieces[1][2])
    where = ((X, 1), (X | CORE, 1))
    done = update(rows, where, False, signs, weight_v, second_v, tuple(done))
    return tuple(done)


def solution(mesh):
    placed = (
        P("dp", "col"),
        P(AXES, None),
        P("dp", "col"),
        P("dp", "col"),
        P(AXES, None),
        P(),
        P(),
    )

    def per_device(tokens, out_grad, weight, second, momentum, sign_seed, step_number):
        args = (tokens, out_grad, weight, second, momentum, sign_seed, step_number)
        cube = mesh.shape["dp"] == Z1 * 2 // (X * 2) and mesh.shape["col"] == X * 2
        if cube and momentum.shape[0] % (2 * LANES) == 0:
            return stepped(*args)
        return general(*args)

    return jax.shard_map(
        per_device,
        mesh=mesh,
        in_specs=placed,
        out_specs=(P("dp", "col"), P("dp", "col"), P(AXES, None)),
        check_vma=False,
    )
```

profile of v0, /device:TPU:0, one launch (start us, length us, event | category | flops | bytes accessed | tf_op | source)
XLA Modules:
  0.0 124.5 jit_solution(1157289054046753717)
XLA Ops:
  1.9 1.5 %pack.3 = (s32[1,512]{1,0:T(1,128)S(1)}, bf16[8,256,128]{2,1,0:T(8,128)(2,1)S(1)}, bf16[8,256,128]{2,1,0:T(8,128)(2,1)S(1)}) custom-call(bf16[256,8192]{1,0:T(8,128)(2,1)} %og_ref.5, s32[1,1]{1,0:T(1,128)} %bitcast.40.refs_0_, s32[1,1]{1,0:T(1,128)} %bitcast.41.refs_1_), custom_call_target="tpu_custom_call" | custom-call | bytes 2097152 | tf_op jit(solution)/shard_map/pack/pallas_call | solution.py:156
  3.4 3.7 %sketch_first.1 = (bf16[2048,512]{1,0:T(8,128)(2,1)S(1)}, f32[256,512]{1,0:T(8,128)S(1)}, f32[256,512]{1,0:T(8,128)S(1)}) custom-call(s32[1,512]{1,0:T(1,128)S(1)} %get-tuple-element.32.refs_0_, bf16[1024,2048]{1,0:T(8,128)(2,1)} %refs_0_.2), custom_call_target="tpu_custom_call" | custom-call | flops 1073741824 | bytes 6291456 | tf_op jit(solution)/shard_map/sketch_first/pallas_call | solution.py:236
  7.1 0.6 collective-permute-start.1
  7.7 2.5 %sketch_next.1 = (f32[256,512]{1,0:T(8,128)S(1)}, f32[256,512]{1,0:T(8,128)S(1)}) custom-call(bf16[1024,2048]{1,0:T(8,128)(2,1)} %refs_0_.2, bf16[2048,512]{1,0:T(8,128)(2,1)S(1)} %get-tuple-element.33.refs_1_.refs_2_.refs_4_), custom_call_target="tpu_custom_call" | custom-call | flops 1073741824 | bytes 6291456 | tf_op jit(solution)/shard_map/sketch_next/pallas_call | solution.py:236
  10.4 3.0 %collective-permute-start.2 = (f32[256,512]{1,0:T(8,128)S(1)}, f32[256,512]{1,0:T(8,128)S(1)}, u32[]{:S(2)}, u32[]{:S(2)}) collective-permute-start(f32[256,512]{1,0:T(8,128)S(1)} %add.74), channel_id=1, source_target_pairs={{0,2},{1,3},{2,0},{3,1},{4,6},{5,7},{6,4},{7,5},{8,10},{9,11},{10,... | collective-permute-start | bytes 1572872 | tf_op jit(solution)/shard_map/ppermute | solution.py:432
  13.4 2.0 %pack.4 = (bf16[16,256,128]{2,1,0:T(8,128)(2,1)S(1)}, bf16[16,256,128]{2,1,0:T(8,128)(2,1)S(1)}) custom-call(bf16[256,8192]{1,0:T(8,128)(2,1)} %og_ref.5), custom_call_target="tpu_custom_call" | custom-call | bytes 4194304 | tf_op jit(solution)/shard_map/pack/pallas_call | solution.py:156
  15.5 1.6 %collective-permute-start.16 = (bf16[8,256,128]{2,1,0:T(8,128)(2,1)S(1)}, bf16[8,256,128]{2,1,0:T(8,128)(2,1)S(1)}, u32[]{:S(2)}, u32[]{:S(2)}) collective-permute-start(bf16[8,256,128]{2,1,0:T(8,128)(2,1)S(1)} %get-tuple-element.46), channel_id=1, source_target_pairs={{0,4},{1,5},{2,6},{3,7},{4,0},{5,1},{6,2},{7,3},{8,12},{9,13},{10,... | collective-permute-start | bytes 1572872 | tf_op jit(solution)/shard_map/ppermute | solution.py:432
  17.1 1.6 %pack.5 = (bf16[8,256,128]{2,1,0:T(8,128)(2,1)S(1)}, bf16[8,256,128]{2,1,0:T(8,128)(2,1)S(1)}) custom-call(bf16[256,8192]{1,0:T(8,128)(2,1)} %og_ref.5), custom_call_target="tpu_custom_call" | custom-call | bytes 2097152 | tf_op jit(solution)/shard_map/pack/pallas_call | solution.py:156
  18.7 0.3 collective-permute-start.17
  19.0 6.5 %collective-permute-done.2 = f32[256,512]{1,0:T(8,128)S(1)} collective-permute-done((f32[256,512]{1,0:T(8,128)S(1)}, f32[256,512]{1,0:T(8,128)S(1)}, u32[]{:S(2)}, u32[]{:S(2)}) %collective-permute-start.2) | collective-permute-done | bytes 524320 | tf_op jit(solution)/shard_map/ppermute | solution.py:432
  25.5 0.2 multiply_convert_fusion.4.refs_0_
  25.7 1.8 %collective-permute-start.14 = (bf16[256,512]{1,0:T(8,128)(2,1)S(1)}, bf16[256,512]{1,0:T(8,128)(2,1)S(1)}, u32[]{:S(2)}, u32[]{:S(2)}) collective-permute-start(bf16[256,512]{1,0:T(8,128)(2,1)S(1)} %multiply_convert_fusion.4.refs_0_), channel_id=1, source_target_pairs={{0,4},{1,5},{2,6},{3,7},{4,0},{5,1},{6,2},{7,3},{8,12},{9,13},{10,... | collective-permute-start | bytes 786440 | tf_op jit(solution)/shard_map/ppermute | solution.py:432
  27.5 1.6 %collective-permute-start.4 = (bf16[256,512]{1,0:T(8,128)(2,1)S(1)}, bf16[256,512]{1,0:T(8,128)(2,1)S(1)}, u32[]{:S(2)}, u32[]{:S(2)}) collective-permute-start(bf16[256,512]{1,0:T(8,128)(2,1)S(1)} %multiply_convert_fusion.4.refs_0_), channel_id=1, source_target_pairs={{0,8},{1,9},{2,10},{3,11},{4,12},{5,13},{6,14},{7,15},{8,0},{9,1},... | collective-permute-start | bytes 786440 | tf_op jit(solution)/shard_map/ppermute | solution.py:432
  29.1 1.2 collective-permute-done.16.refs_6_
  30.3 16.3 %collective-permute-done.14.refs_2_ = bf16[256,512]{1,0:T(8,128)(2,1)S(1)} collective-permute-done((bf16[256,512]{1,0:T(8,128)(2,1)S(1)}, bf16[256,512]{1,0:T(8,128)(2,1)S(1)}, u32[]{:S(2)}, u32[]{:S(2)}) %collective-permute-start.14) | collective-permute-done | bytes 262176 | tf_op jit(solution)/shard_map/ppermute | solution.py:432
  46.6 1.6 %collective-permute-start.7 = (bf16[8,256,128]{2,1,0:T(8,128)(2,1)S(1)}, bf16[8,256,128]{2,1,0:T(8,128)(2,1)S(1)}, u32[]{:S(2)}, u32[]{:S(2)}) collective-permute-start(bf16[8,256,128]{2,1,0:T(8,128)(2,1)S(1)} %get-tuple-element.40), channel_id=1, source_target_pairs={{0,8},{1,9},{2,10},{3,11},{4,12},{5,13},{6,14},{7,15},{8,0},{9,1},... | collective-permute-start | bytes 1572872 | tf_op jit(solution)/shard_map/ppermute | solution.py:432
  48.2 0.3 collective-permute-start.8
  48.5 0.3 collective-permute-start.5
  48.8 0.7 project.6
  49.6 1.6 %collective-permute-start.18 = (f16[2,128,512]{2,1,0:T(8,128)(2,1)S(1)}, f16[2,128,512]{2,1,0:T(8,128)(2,1)S(1)}, u32[]{:S(2)}, u32[]{:S(2)}) collective-permute-start(f16[2,128,512]{2,1,0:T(8,128)(2,1)S(1)} %multiply_convert_fusion.1), channel_id=1, source_target_pairs={{0,8},{1,9},{2,10},{3,11},{4,12},{5,13},{6,14},{7,15},{8,0},{9,1},... | collective-permute-start | bytes 786440 | tf_op jit(solution)/shard_map/ppermute | solution.py:432
  51.3 0.7 project.7
  52.0 0.6 collective-permute-start.20
  52.6 8.8 %collective-permute-done.7.refs_6_ = bf16[8,256,128]{2,1,0:T(8,128)(2,1)S(1)} collective-permute-done((bf16[8,256,128]{2,1,0:T(8,128)(2,1)S(1)}, bf16[8,256,128]{2,1,0:T(8,128)(2,1)S(1)}, u32[]{:S(2)}, u32[]{:S(2)}) %collective-permute-start.7) | collective-permute-done | bytes 524320 | tf_op jit(solution)/shard_map/ppermute | solution.py:432
  61.4 10.3 %collective-permute-done.8.refs_7_ = bf16[8,256,128]{2,1,0:T(8,128)(2,1)S(1)} collective-permute-done((bf16[8,256,128]{2,1,0:T(8,128)(2,1)S(1)}, bf16[8,256,128]{2,1,0:T(8,128)(2,1)S(1)}, u32[]{:S(2)}, u32[]{:S(2)}) %collective-permute-start.8) | collective-permute-done | bytes 524320 | tf_op jit(solution)/shard_map/ppermute | solution.py:432
  71.8 0.7 project.4
  72.6 1.6 %collective-permute-start.9 = (f16[2,128,512]{2,1,0:T(8,128)(2,1)S(1)}, f16[2,128,512]{2,1,0:T(8,128)(2,1)S(1)}, u32[]{:S(2)}, u32[]{:S(2)}) collective-permute-start(f16[2,128,512]{2,1,0:T(8,128)(2,1)S(1)} %multiply_convert_fusion.3), channel_id=1, source_target_pairs={{0,4},{1,5},{2,6},{3,7},{4,0},{5,1},{6,2},{7,3},{8,12},{9,13},{10,... | collective-permute-start | bytes 786440 | tf_op jit(solution)/shard_map/ppermute | solution.py:432
  74.2 0.7 project.5
  74.9 0.6 collective-permute-start.11
  75.5 2.3 %collective-permute-done.18 = f16[2,128,512]{2,1,0:T(8,128)(2,1)S(1)} collective-permute-done((f16[2,128,512]{2,1,0:T(8,128)(2,1)S(1)}, f16[2,128,512]{2,1,0:T(8,128)(2,1)S(1)}, u32[]{:S(2)}, u32[]{:S(2)}) %collective-permute-start.18) | collective-permute-done | bytes 262176 | tf_op jit(solution)/shard_map/ppermute | solution.py:432
  77.9 0.4 collective-permute-start.19
  78.4 1.8 %collective-permute-start.21 = (f16[128,512]{1,0:T(8,128)(2,1)S(1)}, f16[128,512]{1,0:T(8,128)(2,1)S(1)}, u32[]{:S(2)}, u32[]{:S(2)}) collective-permute-start(f16[128,512]{1,0:T(8,128)(2,1)S(1)} %fusion.13), channel_id=1, source_target_pairs={{0,8},{1,9},{2,10},{3,11},{4,12},{5,13},{6,14},{7,15},{8,0},{9,1},... | collective-permute-start | bytes 393224 | tf_op jit(solution)/shard_map/ppermute | solution.py:432
  80.2 1.6 %collective-permute-done.9 = f16[2,128,512]{2,1,0:T(8,128)(2,1)S(1)} collective-permute-done((f16[2,128,512]{2,1,0:T(8,128)(2,1)S(1)}, f16[2,128,512]{2,1,0:T(8,128)(2,1)S(1)}, u32[]{:S(2)}, u32[]{:S(2)}) %collective-permute-start.9) | collective-permute-done | bytes 262176 | tf_op jit(solution)/shard_map/ppermute | solution.py:432
  81.9 0.6 collective-permute-start.10
  82.5 4.7 %collective-permute-done.11 = f16[2,128,512]{2,1,0:T(8,128)(2,1)S(1)} collective-permute-done((f16[2,128,512]{2,1,0:T(8,128)(2,1)S(1)}, f16[2,128,512]{2,1,0:T(8,128)(2,1)S(1)}, u32[]{:S(2)}, u32[]{:S(2)}) %collective-permute-start.11) | collective-permute-done | bytes 262176 | tf_op jit(solution)/shard_map/ppermute | solution.py:432
  87.2 0.4 collective-permute-start.12
  87.7 2.9 %collective-permute-start.22 = (f16[128,512]{1,0:T(8,128)(2,1)S(1)}, f16[128,512]{1,0:T(8,128)(2,1)S(1)}, u32[]{:S(2)}, u32[]{:S(2)}) collective-permute-start(f16[128,512]{1,0:T(8,128)(2,1)S(1)} %fusion.1), channel_id=1, source_target_pairs={{0,16},{1,17},{2,18},{3,19},{4,20},{5,21},{6,22},{7,23},{8,24},{9,... | collective-permute-start | bytes 393224 | tf_op jit(solution)/shard_map/ppermute | solution.py:432
  90.6 2.0 %collective-permute-done.12 = f16[128,512]{1,0:T(8,128)(2,1)S(1)} collective-permute-done((f16[128,512]{1,0:T(8,128)(2,1)S(1)}, f16[128,512]{1,0:T(8,128)(2,1)S(1)}, u32[]{:S(2)}, u32[]{:S(2)}) %collective-permute-start.12) | collective-permute-done | bytes 131104 | tf_op jit(solution)/shard_map/ppermute | solution.py:432
  92.7 2.7 %collective-permute-start.13 = (f16[128,512]{1,0:T(8,128)(2,1)S(1)}, f16[128,512]{1,0:T(8,128)(2,1)S(1)}, u32[]{:S(2)}, u32[]{:S(2)}) collective-permute-start(f16[128,512]{1,0:T(8,128)(2,1)S(1)} %fusion.6), channel_id=1, source_target_pairs={{0,16},{1,17},{2,18},{3,19},{4,20},{5,21},{6,22},{7,23},{8,24},{9,... | collective-permute-start | bytes 393224 | tf_op jit(solution)/shard_map/ppermute | solution.py:432
  95.3 5.3 %collective-permute-done.22 = f16[128,512]{1,0:T(8,128)(2,1)S(1)} collective-permute-done((f16[128,512]{1,0:T(8,128)(2,1)S(1)}, f16[128,512]{1,0:T(8,128)(2,1)S(1)}, u32[]{:S(2)}, u32[]{:S(2)}) %collective-permute-start.22) | collective-permute-done | bytes 131104 | tf_op jit(solution)/shard_map/ppermute | solution.py:432
  100.8 1.6 %collective-permute-start.26 = (f16[128,512]{1,0:T(8,128)(2,1)S(1)}, f16[128,512]{1,0:T(8,128)(2,1)S(1)}, u32[]{:S(2)}, u32[]{:S(2)}) collective-permute-start(f16[128,512]{1,0:T(8,128)(2,1)S(1)} %get-tuple-element.63), channel_id=1, source_target_pairs={{0,2},{1,3},{2,0},{3,1},{4,6},{5,7},{6,4},{7,5},{8,10},{9,11},{10,... | collective-permute-start | bytes 393224 | tf_op jit(solution)/shard_map/ppermute | solution.py:432
  102.5 1.5 %collective-permute-start.23 = (f16[128,512]{1,0:T(8,128)(2,1)S(1)}, f16[128,512]{1,0:T(8,128)(2,1)S(1)}, u32[]{:S(2)}, u32[]{:S(2)}) collective-permute-start(f16[128,512]{1,0:T(8,128)(2,1)S(1)} %get-tuple-element.61), channel_id=1, source_target_pairs={{0,2},{1,3},{2,0},{3,1},{4,6},{5,7},{6,4},{7,5},{8,10},{9,11},{10,... | collective-permute-start | bytes 393224 | tf_op jit(solution)/shard_map/ppermute | solution.py:432
  104.0 0.5 collective-permute-start.25
  104.5 2.3 %collective-permute-done.26 = f16[128,512]{1,0:T(8,128)(2,1)S(1)} collective-permute-done((f16[128,512]{1,0:T(8,128)(2,1)S(1)}, f16[128,512]{1,0:T(8,128)(2,1)S(1)}, u32[]{:S(2)}, u32[]{:S(2)}) %collective-permute-start.26) | collective-permute-done | bytes 131104 | tf_op jit(solution)/shard_map/ppermute | solution.py:432
  106.8 5.9 %prefetch.1 = (f32[1024,2048]{1,0:T(8,128)S(1)}, f32[1024,2048]{1,0:T(8,128)S(1)}) custom-call(f32[1024,2048]{1,0:T(8,128)} %refs_0_.3, f32[1024,2048]{1,0:T(8,128)} %refs_1_.3), custom_call_target="tpu_custom_call" | custom-call | bytes 16777216 | tf_op jit(solution)/shard_map/prefetch/pallas_call | solution.py:319
  112.7 0.6 collective-permute-start.24
  113.4 2.9 %update.3 = (f32[1024,2048]{1,0:T(8,128)}, f32[1024,2048]{1,0:T(8,128)}, f32[256,512]{1,0:T(8,128)}) custom-call(f32[128,512]{1,0:T(8,128)S(1)} %get-tuple-element.64.refs_0_, f32[128,512]{1,0:T(8,128)S(1)} %convert_element_type.127.refs_1_, bf16[2048,512]{1,0:T(8,128)(2,1)S(1)} %get-tuple-element.33.refs_1_.refs_2_.refs_4_, ...), custom_call_target="tpu_custom_call" | custom-call | flops 1073741824 | bytes 4194304 | tf_op jit(solution)/shard_map/update/pallas_call | solution.py:401
  116.4 5.1 %update.4 = (f32[1024,2048]{1,0:T(8,128)}, f32[1024,2048]{1,0:T(8,128)}, f32[256,512]{1,0:T(8,128)}) custom-call(f32[128,512]{1,0:T(8,128)S(1)} %get-tuple-element.62.refs_0_, f32[128,512]{1,0:T(8,128)S(1)} %convert_element_type.124.refs_1_, ...), custom_call_target="tpu_custom_call", output_to_operand_aliasing={{0}: (7, {}), {1}: (8, {}), {2}: (9, {})} | custom-call | flops 2147483648 | bytes 8388608 | tf_op jit(solution)/shard_map/update/pallas_call | solution.py:401
  121.5 2.8 %update.5 = (f32[1024,2048]{1,0:T(8,128)}, f32[1024,2048]{1,0:T(8,128)}, f32[256,512]{1,0:T(8,128)}) custom-call(f32[128,512]{1,0:T(8,128)S(1)} %convert_element_type.122.refs_0_, f32[128,512]{1,0:T(8,128)S(1)} %convert_element_type.123.refs_1_, ...), custom_call_target="tpu_custom_call", output_to_operand_aliasing={{0}: (5, {}), {1}: (6, {}), {2}: (7, {})} | custom-call | flops 1073741824 | bytes 4194304 | tf_op jit(solution)/shard_map/update/pallas_call | solution.py:401
  (45 shorter events, 1.2 us)
Async XLA Ops:
  7.1 3.2 %collective-permute-start.1 = (f32[256,512]{1,0:T(8,128)S(1)}, f32[256,512]{1,0:T(8,128)S(1)}, u32[]{:S(2)}, u32[]{:S(2)}) collective-permute-start(f32[256,512]{1,0:T(8,128)S(1)} %get-tuple-element.37), channel_id=1, source_target_pairs={{0,1},{1,0},{2,3},{3,2},{4,5},{5,4},{6,7},{7,6},{8,9},{9,8},{10,11... | collective-permute-start | bytes 1572872 | tf_op jit(solution)/shard_map/ppermute | solution.py:432
  10.2 8.8 %collective-permute-start = (f32[256,512]{1,0:T(8,128)S(1)}, f32[256,512]{1,0:T(8,128)S(1)}, u32[]{:S(2)}, u32[]{:S(2)}) collective-permute-start(f32[256,512]{1,0:T(8,128)S(1)} %get-tuple-element.35), channel_id=1, source_target_pairs={{0,1},{1,0},{2,3},{3,2},{4,5},{5,4},{6,7},{7,6},{8,9},{9,8},{10,11... | collective-permute-start | bytes 1572872 | tf_op jit(solution)/shard_map/ppermute | solution.py:432
  10.4 15.1 %collective-permute-start.2 = (f32[256,512]{1,0:T(8,128)S(1)}, f32[256,512]{1,0:T(8,128)S(1)}, u32[]{:S(2)}, u32[]{:S(2)}) collective-permute-start(f32[256,512]{1,0:T(8,128)S(1)} %add.74), channel_id=1, source_target_pairs={{0,2},{1,3},{2,0},{3,1},{4,6},{5,7},{6,4},{7,5},{8,10},{9,11},{10,... | collective-permute-start | bytes 1572872 | tf_op jit(solution)/shard_map/ppermute | solution.py:432
  15.4 32.8 %collective-permute-start.6 = (bf16[16,256,128]{2,1,0:T(8,128)(2,1)S(1)}, bf16[16,256,128]{2,1,0:T(8,128)(2,1)S(1)}, u32[]{:S(2)}, u32[]{:S(2)}) collective-permute-start(bf16[16,256,128]{2,1,0:T(8,128)(2,1)S(1)} %get-tuple-element.39), channel_id=1, source_target_pairs={{0,1},{1,0},{2,3},{3,2},{4,5},{5,4},{6,7},{7,6},{8,9},{9,8},{10,11... | collective-permute-start | bytes 3145736 | tf_op jit(solution)/shard_map/ppermute | solution.py:432
  15.5 14.9 %collective-permute-start.16 = (bf16[8,256,128]{2,1,0:T(8,128)(2,1)S(1)}, bf16[8,256,128]{2,1,0:T(8,128)(2,1)S(1)}, u32[]{:S(2)}, u32[]{:S(2)}) collective-permute-start(bf16[8,256,128]{2,1,0:T(8,128)(2,1)S(1)} %get-tuple-element.46), channel_id=1, source_target_pairs={{0,4},{1,5},{2,6},{3,7},{4,0},{5,1},{6,2},{7,3},{8,12},{9,13},{10,... | collective-permute-start | bytes 1572872 | tf_op jit(solution)/shard_map/ppermute | solution.py:432
  18.7 28.0 %collective-permute-start.17 = (bf16[8,256,128]{2,1,0:T(8,128)(2,1)S(1)}, bf16[8,256,128]{2,1,0:T(8,128)(2,1)S(1)}, u32[]{:S(2)}, u32[]{:S(2)}) collective-permute-start(bf16[8,256,128]{2,1,0:T(8,128)(2,1)S(1)} %get-tuple-element.47), channel_id=1, source_target_pairs={{0,5},{1,4},{2,7},{3,6},{4,1},{5,0},{6,3},{7,2},{8,13},{9,12},{10,... | collective-permute-start | bytes 1572872 | tf_op jit(solution)/shard_map/ppermute | solution.py:432
  25.7 21.0 %collective-permute-start.14 = (bf16[256,512]{1,0:T(8,128)(2,1)S(1)}, bf16[256,512]{1,0:T(8,128)(2,1)S(1)}, u32[]{:S(2)}, u32[]{:S(2)}) collective-permute-start(bf16[256,512]{1,0:T(8,128)(2,1)S(1)} %multiply_convert_fusion.4.refs_0_), channel_id=1, source_target_pairs={{0,4},{1,5},{2,6},{3,7},{4,0},{5,1},{6,2},{7,3},{8,12},{9,13},{10,... | collective-permute-start | bytes 786440 | tf_op jit(solution)/shard_map/ppermute | solution.py:432
  27.5 21.0 %collective-permute-start.4 = (bf16[256,512]{1,0:T(8,128)(2,1)S(1)}, bf16[256,512]{1,0:T(8,128)(2,1)S(1)}, u32[]{:S(2)}, u32[]{:S(2)}) collective-permute-start(bf16[256,512]{1,0:T(8,128)(2,1)S(1)} %multiply_convert_fusion.4.refs_0_), channel_id=1, source_target_pairs={{0,8},{1,9},{2,10},{3,11},{4,12},{5,13},{6,14},{7,15},{8,0},{9,1},... | collective-permute-start | bytes 786440 | tf_op jit(solution)/shard_map/ppermute | solution.py:432
  30.3 18.5 %collective-permute-start.3 = (bf16[256,512]{1,0:T(8,128)(2,1)S(1)}, bf16[256,512]{1,0:T(8,128)(2,1)S(1)}, u32[]{:S(2)}, u32[]{:S(2)}) collective-permute-start(bf16[256,512]{1,0:T(8,128)(2,1)S(1)} %multiply_convert_fusion.4.refs_0_), channel_id=1, source_target_pairs={{0,1},{1,0},{2,3},{3,2},{4,5},{5,4},{6,7},{7,6},{8,9},{9,8},{10,11... | collective-permute-start | bytes 786440 | tf_op jit(solution)/shard_map/ppermute | solution.py:432
  46.6 2.2 %collective-permute-start.15 = (bf16[256,512]{1,0:T(8,128)(2,1)S(1)}, bf16[256,512]{1,0:T(8,128)(2,1)S(1)}, u32[]{:S(2)}, u32[]{:S(2)}) collective-permute-start(bf16[256,512]{1,0:T(8,128)(2,1)S(1)} %collective-permute-done.14.refs_2_), channel_id=1, source_target_pairs={{0,1},{1,0},{2,3},{3,2},{4,5},{5,4},{6,7},{7,6},{8,9},{9,8},{10,11... | collective-permute-start | bytes 786440 | tf_op jit(solution)/shard_map/ppermute | solution.py:432
  46.6 14.8 %collective-permute-start.7 = (bf16[8,256,128]{2,1,0:T(8,128)(2,1)S(1)}, bf16[8,256,128]{2,1,0:T(8,128)(2,1)S(1)}, u32[]{:S(2)}, u32[]{:S(2)}) collective-permute-start(bf16[8,256,128]{2,1,0:T(8,128)(2,1)S(1)} %get-tuple-element.40), channel_id=1, source_target_pairs={{0,8},{1,9},{2,10},{3,11},{4,12},{5,13},{6,14},{7,15},{8,0},{9,1},... | collective-permute-start | bytes 1572872 | tf_op jit(solution)/shard_map/ppermute | solution.py:432
  48.2 23.5 %collective-permute-start.8 = (bf16[8,256,128]{2,1,0:T(8,128)(2,1)S(1)}, bf16[8,256,128]{2,1,0:T(8,128)(2,1)S(1)}, u32[]{:S(2)}, u32[]{:S(2)}) collective-permute-start(bf16[8,256,128]{2,1,0:T(8,128)(2,1)S(1)} %get-tuple-element.41), channel_id=1, source_target_pairs={{0,9},{1,8},{2,11},{3,10},{4,13},{5,12},{6,15},{7,14},{8,1},{9,0},... | collective-permute-start | bytes 1572872 | tf_op jit(solution)/shard_map/ppermute | solution.py:432
  48.5 23.3 %collective-permute-start.5 = (bf16[256,512]{1,0:T(8,128)(2,1)S(1)}, bf16[256,512]{1,0:T(8,128)(2,1)S(1)}, u32[]{:S(2)}, u32[]{:S(2)}) collective-permute-start(bf16[256,512]{1,0:T(8,128)(2,1)S(1)} %collective-permute-done.4.refs_2_), channel_id=1, source_target_pairs={{0,1},{1,0},{2,3},{3,2},{4,5},{5,4},{6,7},{7,6},{8,9},{9,8},{10,11... | collective-permute-start | bytes 786440 | tf_op jit(solution)/shard_map/ppermute | solution.py:432
  49.6 51.0 %copy-start = (f32[256,512]{1,0:T(8,128)S(1)}, f32[256,512]{1,0:T(8,128)}, u32[]{:S(2)}) copy-start(f32[256,512]{1,0:T(8,128)} %param.11) | copy-start | bytes 1572868
  49.6 28.2 %collective-permute-start.18 = (f16[2,128,512]{2,1,0:T(8,128)(2,1)S(1)}, f16[2,128,512]{2,1,0:T(8,128)(2,1)S(1)}, u32[]{:S(2)}, u32[]{:S(2)}) collective-permute-start(f16[2,128,512]{2,1,0:T(8,128)(2,1)S(1)} %multiply_convert_fusion.1), channel_id=1, source_target_pairs={{0,8},{1,9},{2,10},{3,11},{4,12},{5,13},{6,14},{7,15},{8,0},{9,1},... | collective-permute-start | bytes 786440 | tf_op jit(solution)/shard_map/ppermute | solution.py:432
  52.0 26.3 %collective-permute-start.20 = (f16[2,128,512]{2,1,0:T(8,128)(2,1)S(1)}, f16[2,128,512]{2,1,0:T(8,128)(2,1)S(1)}, u32[]{:S(2)}, u32[]{:S(2)}) collective-permute-start(f16[2,128,512]{2,1,0:T(8,128)(2,1)S(1)} %multiply_convert_fusion), channel_id=1, source_target_pairs={{0,2},{1,3},{2,0},{3,1},{4,6},{5,7},{6,4},{7,5},{8,10},{9,11},{10,... | collective-permute-start | bytes 786440 | tf_op jit(solution)/shard_map/ppermute | solution.py:432
  72.6 9.2 %collective-permute-start.9 = (f16[2,128,512]{2,1,0:T(8,128)(2,1)S(1)}, f16[2,128,512]{2,1,0:T(8,128)(2,1)S(1)}, u32[]{:S(2)}, u32[]{:S(2)}) collective-permute-start(f16[2,128,512]{2,1,0:T(8,128)(2,1)S(1)} %multiply_convert_fusion.3), channel_id=1, source_target_pairs={{0,4},{1,5},{2,6},{3,7},{4,0},{5,1},{6,2},{7,3},{8,12},{9,13},{10,... | collective-permute-start | bytes 786440 | tf_op jit(solution)/shard_map/ppermute | solution.py:432
  74.9 12.2 %collective-permute-start.11 = (f16[2,128,512]{2,1,0:T(8,128)(2,1)S(1)}, f16[2,128,512]{2,1,0:T(8,128)(2,1)S(1)}, u32[]{:S(2)}, u32[]{:S(2)}) collective-permute-start(f16[2,128,512]{2,1,0:T(8,128)(2,1)S(1)} %multiply_convert_fusion.2), channel_id=1, source_target_pairs={{0,4},{1,5},{2,6},{3,7},{4,0},{5,1},{6,2},{7,3},{8,12},{9,13},{10,... | collective-permute-start | bytes 786440 | tf_op jit(solution)/shard_map/ppermute | solution.py:432
  77.9 17.4 %collective-permute-start.19 = (f16[128,512]{1,0:T(8,128)(2,1)S(1)}, f16[128,512]{1,0:T(8,128)(2,1)S(1)}, u32[]{:S(2)}, u32[]{:S(2)}) collective-permute-start(f16[128,512]{1,0:T(8,128)(2,1)S(1)} %fusion.12), channel_id=1, source_target_pairs={{0,2},{1,3},{2,0},{3,1},{4,6},{5,7},{6,4},{7,5},{8,10},{9,11},{10,... | collective-permute-start | bytes 393224 | tf_op jit(solution)/shard_map/ppermute | solution.py:432
  78.4 9.2 %collective-permute-start.21 = (f16[128,512]{1,0:T(8,128)(2,1)S(1)}, f16[128,512]{1,0:T(8,128)(2,1)S(1)}, u32[]{:S(2)}, u32[]{:S(2)}) collective-permute-start(f16[128,512]{1,0:T(8,128)(2,1)S(1)} %fusion.13), channel_id=1, source_target_pairs={{0,8},{1,9},{2,10},{3,11},{4,12},{5,13},{6,14},{7,15},{8,0},{9,1},... | collective-permute-start | bytes 393224 | tf_op jit(solution)/shard_map/ppermute | solution.py:432
  81.9 20.5 %collective-permute-start.10 = (f16[128,512]{1,0:T(8,128)(2,1)S(1)}, f16[128,512]{1,0:T(8,128)(2,1)S(1)}, u32[]{:S(2)}, u32[]{:S(2)}) collective-permute-start(f16[128,512]{1,0:T(8,128)(2,1)S(1)} %fusion.10), channel_id=1, source_target_pairs={{0,2},{1,3},{2,0},{3,1},{4,6},{5,7},{6,4},{7,5},{8,10},{9,11},{10,... | collective-permute-start | bytes 393224 | tf_op jit(solution)/shard_map/ppermute | solution.py:432
  87.2 5.3 %collective-permute-start.12 = (f16[128,512]{1,0:T(8,128)(2,1)S(1)}, f16[128,512]{1,0:T(8,128)(2,1)S(1)}, u32[]{:S(2)}, u32[]{:S(2)}) collective-permute-start(f16[128,512]{1,0:T(8,128)(2,1)S(1)} %fusion.11), channel_id=1, source_target_pairs={{0,2},{1,3},{2,0},{3,1},{4,6},{5,7},{6,4},{7,5},{8,10},{9,11},{10,... | collective-permute-start | bytes 393224 | tf_op jit(solution)/shard_map/ppermute | solution.py:432
  87.7 12.9 %collective-permute-start.22 = (f16[128,512]{1,0:T(8,128)(2,1)S(1)}, f16[128,512]{1,0:T(8,128)(2,1)S(1)}, u32[]{:S(2)}, u32[]{:S(2)}) collective-permute-start(f16[128,512]{1,0:T(8,128)(2,1)S(1)} %fusion.1), channel_id=1, source_target_pairs={{0,16},{1,17},{2,18},{3,19},{4,20},{5,21},{6,22},{7,23},{8,24},{9,... | collective-permute-start | bytes 393224 | tf_op jit(solution)/shard_map/ppermute | solution.py:432
  92.7 9.7 %collective-permute-start.13 = (f16[128,512]{1,0:T(8,128)(2,1)S(1)}, f16[128,512]{1,0:T(8,128)(2,1)S(1)}, u32[]{:S(2)}, u32[]{:S(2)}) collective-permute-start(f16[128,512]{1,0:T(8,128)(2,1)S(1)} %fusion.6), channel_id=1, source_target_pairs={{0,16},{1,17},{2,18},{3,19},{4,20},{5,21},{6,22},{7,23},{8,24},{9,... | collective-permute-start | bytes 393224 | tf_op jit(solution)/shard_map/ppermute | solution.py:432
  100.8 6.0 %collective-permute-start.26 = (f16[128,512]{1,0:T(8,128)(2,1)S(1)}, f16[128,512]{1,0:T(8,128)(2,1)S(1)}, u32[]{:S(2)}, u32[]{:S(2)}) collective-permute-start(f16[128,512]{1,0:T(8,128)(2,1)S(1)} %get-tuple-element.63), channel_id=1, source_target_pairs={{0,2},{1,3},{2,0},{3,1},{4,6},{5,7},{6,4},{7,5},{8,10},{9,11},{10,... | collective-permute-start | bytes 393224 | tf_op jit(solution)/shard_map/ppermute | solution.py:432
  102.5 10.3 %collective-permute-start.23 = (f16[128,512]{1,0:T(8,128)(2,1)S(1)}, f16[128,512]{1,0:T(8,128)(2,1)S(1)}, u32[]{:S(2)}, u32[]{:S(2)}) collective-permute-start(f16[128,512]{1,0:T(8,128)(2,1)S(1)} %get-tuple-element.61), channel_id=1, source_target_pairs={{0,2},{1,3},{2,0},{3,1},{4,6},{5,7},{6,4},{7,5},{8,10},{9,11},{10,... | collective-permute-start | bytes 393224 | tf_op jit(solution)/shard_map/ppermute | solution.py:432
  104.0 9.3 %collective-permute-start.28 = (f16[128,512]{1,0:T(8,128)(2,1)S(1)}, f16[128,512]{1,0:T(8,128)(2,1)S(1)}, u32[]{:S(2)}, u32[]{:S(2)}) collective-permute-start(f16[128,512]{1,0:T(8,128)(2,1)S(1)} %get-tuple-element.63), channel_id=1, source_target_pairs={{0,1},{1,0},{2,3},{3,2},{4,5},{5,4},{6,7},{7,6},{8,9},{9,8},{10,11... | collective-permute-start | bytes 393224 | tf_op jit(solution)/shard_map/ppermute | solution.py:432
  104.0 9.4 %collective-permute-start.25 = (f16[128,512]{1,0:T(8,128)(2,1)S(1)}, f16[128,512]{1,0:T(8,128)(2,1)S(1)}, u32[]{:S(2)}, u32[]{:S(2)}) collective-permute-start(f16[128,512]{1,0:T(8,128)(2,1)S(1)} %get-tuple-element.61), channel_id=1, source_target_pairs={{0,1},{1,0},{2,3},{3,2},{4,5},{5,4},{6,7},{7,6},{8,9},{9,8},{10,11... | collective-permute-start | bytes 393224 | tf_op jit(solution)/shard_map/ppermute | solution.py:432
  106.8 9.6 %collective-permute-start.27 = (f16[128,512]{1,0:T(8,128)(2,1)S(1)}, f16[128,512]{1,0:T(8,128)(2,1)S(1)}, u32[]{:S(2)}, u32[]{:S(2)}) collective-permute-start(f16[128,512]{1,0:T(8,128)(2,1)S(1)} %collective-permute-done.26), channel_id=1, source_target_pairs={{0,1},{1,0},{2,3},{3,2},{4,5},{5,4},{6,7},{7,6},{8,9},{9,8},{10,11... | collective-permute-start | bytes 393224 | tf_op jit(solution)/shard_map/ppermute | solution.py:432
  112.7 8.8 %collective-permute-start.24 = (f16[128,512]{1,0:T(8,128)(2,1)S(1)}, f16[128,512]{1,0:T(8,128)(2,1)S(1)}, u32[]{:S(2)}, u32[]{:S(2)}) collective-permute-start(f16[128,512]{1,0:T(8,128)(2,1)S(1)} %collective-permute-done.23), channel_id=1, source_target_pairs={{0,1},{1,0},{2,3},{3,2},{4,5},{5,4},{6,7},{7,6},{8,9},{9,8},{10,11... | collective-permute-start | bytes 393224 | tf_op jit(solution)/shard_map/ppermute | solution.py:432
where the time goes:
time: 125 us
  waiting for transfers between devices  61.4 us (49%)
  Pallas kernels  31 us (25%)
  starting transfers between devices  28.6 us (23%)
  between operations  2.35 us (2%)
    ppermute x29, waiting for transfers between devices, exchange(): return lax.ppermute(value, AXES, [(i, i ^ mask) for i in range(size)])  61.4 us
    ppermute x29, starting transfers between devices, exchange(): return lax.ppermute(value, AXES, [(i, i ^ mask) for i in range(size)])  28.6 us
    pallas_call x3, Pallas kernels, update(): pl.pallas_call(functools.partial(update_kernel, where, keep, slabs, min(s...  10.8 us
    pallas_call x2, Pallas kernels, sketch_parts(): pl.pallas_call(functools.partial(sketch_kernel, first, din_local), in_spe...  6.19 us
    pallas_call x1, Pallas kernels, prefetch(): pl.pallas_call(prefetch_kernel, in_specs=[pl.BlockSpec(memory_space=pl.AN...  5.92 us
    pallas_call x3, Pallas kernels, pack(): pl.pallas_call(functools.partial(pack_kernel, groups, width, part, bool(s...  5.12 us
    pallas_call x4, Pallas kernels, project(): pl.pallas_call(functools.partial(project_kernel, n), grid=(1,), in_specs=...  2.91 us
  transfers between devices with their start and end apart: 29, of which 11 were waited for; matrix products, arithmetic and copies ran while one was open for 1% of the time, Pallas kernels for 18%

commit v1 on v0

--- a/solution.py
+++ b/solution.py
@@ -87,17 +87,7 @@
     )
 
 
-def pack_kernel(groups, width, part, seeded, og_ref, *refs):
-    if seeded:
-        seed_ref, step_ref, *refs = refs
-        columns_ref, *refs = refs
-        *refs, seed, step, seed_sem = refs
-        copies = [
-            pltpu.make_async_copy(seed_ref, seed, seed_sem.at[0]),
-            pltpu.make_async_copy(step_ref, step, seed_sem.at[1]),
-        ]
-        for copy in copies:
-            copy.start()
+def pack_kernel(groups, width, part, og_ref, *refs):
     n_out = len(groups)
     outs = refs[:n_out]
     stage, in_sem, out_sem = refs[n_out:]
@@ -115,12 +105,6 @@
             mine.append(copy)
             slot += 1
         loads.append(mine)
-    if seeded:
-        for copy in copies:
-            copy.wait()
-        constant = seed[...] * 1664525 + step[...] * 1013904223
-        ids = lax.broadcasted_iota(jnp.int32, columns_ref.shape, 1)
-        columns_ref[...] = ids * 747796405 + constant
     stores = []
     slot = 0
     for index, group in enumerate(groups):
@@ -136,35 +120,28 @@
         store.wait()
 
 
-def pack(out_grad, groups, width, part, seeds=(), low_rank=None):
+def pack(out_grad, groups, width, part):
     rows = out_grad.shape[0]
     count = sum(len(group) for group in groups)
     hbm = pl.BlockSpec(memory_space=pl.ANY)
-    out_specs = [hbm] * len(groups)
-    out_shape = [
-        jax.ShapeDtypeStruct((len(group), rows, part), out_grad.dtype) for group in groups
-    ]
-    scratch = [
-        pltpu.VMEM((count, rows, part), out_grad.dtype),
-        pltpu.SemaphoreType.DMA((count,)),
-        pltpu.SemaphoreType.DMA((len(groups),)),
-    ]
-    if seeds:
-        out_specs = [pl.BlockSpec(memory_space=pltpu.VMEM)] + out_specs
-        out_shape = [jax.ShapeDtypeStruct((1, low_rank), jnp.int32)] + out_shape
-        scratch += [pltpu.VMEM((1, 1), jnp.int32)] * 2 + [pltpu.SemaphoreType.DMA((2,))]
     return pl.pallas_call(
-        functools.partial(pack_kernel, groups, width, part, bool(seeds)),
-        in_specs=[hbm] * (1 + len(seeds)),
-        out_specs=out_specs,
-        out_shape=out_shape,
-        scratch_shapes=scratch,
+        functools.partial(pack_kernel, groups, width, part),
+        in_specs=[hbm],
+        out_specs=[hbm] * len(groups),
+        out_shape=[
+            jax.ShapeDtypeStruct((len(group), rows, part), out_grad.dtype) for group in groups
+        ],
+        scratch_shapes=[
+            pltpu.VMEM((count, rows, part), out_grad.dtype),
+            pltpu.SemaphoreType.DMA((count,)),
+            pltpu.SemaphoreType.DMA((len(groups),)),
+        ],
         compiler_params=pltpu.CompilerParams(vmem_limit_bytes=8 * 1024 * 1024),
         cost_estimate=pl.CostEstimate(
             flops=0, bytes_accessed=4 * count * rows * part, transcendentals=0
         ),
         name="pack",
-    )(pltpu.with_memory_space_constraint(out_grad, pltpu.HBM), *seeds)
+    )(pltpu.with_memory_space_constraint(out_grad, pltpu.HBM))
 
 
 CHUNKS = 4
@@ -173,7 +150,14 @@
 
 def sketch_kernel(first, din_local, *refs):
     if first:
-        columns_ref, tok_ref, signs_ref, send_ref, keep_ref, tok, acc, sem = refs
+        seed_ref, step_ref, *refs, seed, step, seed_sem = refs
+        seed_copies = [
+            pltpu.make_async_copy(seed_ref, seed, seed_sem.at[0]),
+            pltpu.make_async_copy(step_ref, step, seed_sem.at[1]),
+        ]
+        for copy in seed_copies:
+            copy.start()
+        tok_ref, signs_ref, send_ref, keep_ref, tok, acc, sem = refs
     else:
         tok_ref, signs_ref, send_ref, keep_ref, tok, acc, sem = refs
     quarter, low_rank = keep_ref.shape
@@ -198,7 +182,11 @@
         row_factor = low_rank * 747796405
         row_factor = (row_factor + (1 << 31)) % (1 << 32) - (1 << 31)
         local = lax.broadcasted_iota(jnp.int32, (STRIP, low_rank), 0) * row_factor
-        local = local + columns_ref[...]
+        columns = lax.broadcasted_iota(jnp.int32, (1, low_rank), 1) * 747796405
+        for copy in seed_copies:
+            copy.wait()
+        columns = columns + (seed[...] * 1664525 + step[...] * 1013904223)
+        local = local + columns
     for part in range(CHUNKS):
         at = slice(part * chunk, (part + 1) * chunk)
         if first:
@@ -218,7 +206,7 @@
             keep_ref[...] = product[quarter:]
 
 
-def sketch_parts(tokens, low_rank, signs, columns):
+def sketch_parts(tokens, low_rank, signs, seeds):
     local_tokens, din_local = tokens.shape
     half = local_tokens // 2
     quarter = half // 2
@@ -228,7 +216,7 @@
     parts = [jax.ShapeDtypeStruct((quarter, low_rank), jnp.float32)] * 2
     tokens = pltpu.with_memory_space_constraint(tokens, pltpu.HBM)
     if first:
-        in_specs, args = [vmem, hbm], (columns, tokens)
+        in_specs, args = [hbm, hbm, hbm], (*seeds, tokens)
         out_shape = [jax.ShapeDtypeStruct((din_local, low_rank), jnp.bfloat16)] + parts
     else:
         in_specs, args = [hbm, vmem], (tokens, signs)
@@ -242,7 +230,8 @@
             pltpu.VMEM((half, din_local), tokens.dtype),
             pltpu.VMEM((half, low_rank), jnp.float32),
             pltpu.SemaphoreType.DMA((CHUNKS, 2)),
-        ],
+        ]
+        + ([pltpu.VMEM((1, 1), jnp.int32)] * 2 + [pltpu.SemaphoreType.DMA((2,))]) * first,
         compiler_params=pltpu.CompilerParams(vmem_limit_bytes=12 * 1024 * 1024),
         cost_estimate=pl.CostEstimate(
             flops=2 * half * din_local * low_rank,
@@ -439,42 +428,38 @@
     inv_root = 1.0 / jnp.sqrt(jnp.float32(low_rank))
     far0 = [(Z1 | X | Z0, 0), (Z1 | X, 0), (Z1 | Z0, 0), (Z1, 0)]
     near0 = [(Z0 | X, 0), (Z0, 0), (X, 0), (0, 0)]
-    far1 = [(Z1 | Y | X, 1), (Z1 | Y, 1), (Z1 | X, 1), (Z1, 1)]
+    far1 = [(Z1 | X | Y, 1), (Z1 | X, 1), (Z1 | Y, 1), (Z1, 1)]
     near1 = [(Y | X, 1), (Y, 1), (X, 1), (0, 1)]
 
     def toward(mask, pieces):
         return [(rel ^ mask, half) for rel, half in pieces]
 
     part = owner_rows // 2
-    over_y, over_z = far0 + near0, far1 + near1
-    columns, og_y, og_z = pack(
-        out_grad,
-        [toward(Y, over_y), toward(Z0, over_z)],
-        owner_rows,
-        part,
-        (sign_seed.reshape(1, 1), step_number.reshape(1, 1)),
-        low_rank,
-    )
-    og_y = exchange(og_y, Y)
-    og_z = exchange(og_z, Z0)
-    signs, send_a, keep_a = sketch_parts(tokens, low_rank, None, columns)
-    og_yc, og_zc = pack(
-        out_grad, [toward(Y | CORE, over_y), toward(Z0 | CORE, over_z)], owner_rows, part
-    )
-    og_c, og_own = pack(
-        out_grad,
-        [toward(CORE, over_y + over_z), over_y + over_z],
-        owner_rows,
-        part,
-    )
+    pieces = far0 + near0 + far1 + near1
+    seeds = (sign_seed.reshape(1, 1), step_number.reshape(1, 1))
+    signs, send_a, keep_a = sketch_parts(tokens, low_rank, None, seeds)
     got_a = exchange(send_a, CORE)
+
+    def messages(over_y, over_z):
+        return [
+            toward(Y, over_y),
+            toward(Z0, over_z),
+            toward(Y | CORE, over_y),
+            toward(Z0 | CORE, over_z),
+        ]
+
+    far_out = pack(out_grad, messages(far0, far1), owner_rows, part)
+    *near_out, og_c, og_own = pack(
+        out_grad, messages(near0, near1) + [toward(CORE, pieces), pieces], owner_rows, part
+    )
     across = exchange(keep_a + got_a, X)
-    og_yc = exchange(og_yc, Y | CORE)
-    og_zc = exchange(og_zc, Z0 | CORE)
+    routes = (("y", Y), ("z", Z0), ("yc", Y | CORE), ("zc", Z0 | CORE))
+    far_og = {name: exchange(value, mask) for value, (name, mask) in zip(far_out, routes)}
     og_c = exchange(og_c, CORE)
     send_b, keep_b = sketch_parts(tokens, low_rank, signs, None)
-    weight_v, second_v = prefetch(weight, second)
     got_b = exchange(send_b, CORE)
+    (weight_v,) = prefetch(weight)
+    (second_v,) = prefetch(second)
     sketch = (((keep_b + got_b) + across) * inv_root).astype(jnp.bfloat16)
 
     sk_y = exchange(sketch, Y)
@@ -482,6 +467,7 @@
     sk_c = exchange(sketch, CORE)
     sk_yc = exchange(sk_y, CORE)
     sk_zc = exchange(sk_z, CORE)
+    near_og = {name: exchange(value, mask) for value, (name, mask) in zip(near_out, routes)}
 
     scale = jnp.float32(1.0 / total_tokens)
 
@@ -491,11 +477,12 @@
     def unpacked(value, extra):
         return value.astype(jnp.float32) * (1.0 / (scale * extra))
 
-    y_side = (sketch, sk_c, sk_y, sk_yc), (og_own, og_c, og_y, og_yc)
-    z_side = (sketch, sk_c, sk_z, sk_zc), (og_own, og_c, og_z, og_zc)
-
-    def begin(side, offsets, axis):
-        send, keep = project(*side, offsets, 4)
+    def side(axis, og):
+        got = {"y": (sk_y, sk_yc), "z": (sk_z, sk_zc)}[axis]
+        return (sketch, sk_c, *got), (og_own, og_c, og[axis], og[axis + "c"])
+
+    def begin(terms, first, axis):
+        send, keep = project(*terms, (first, first, 0, 0), 4)
         return exchange(packed(send, 8.0), axis), keep
 
     def middle(state, axis):
@@ -507,12 +494,12 @@
         got, keep = state
         return keep + unpacked(got, 4.0)
 
-    far0_state = begin(y_side, (0, 0, 0, 0), X)
-    far1_state = begin(z_side, (8, 8, 0, 0), Y)
-    near0_state = begin(y_side, (4, 4, 4, 4), Z0)
-    near1_state = begin(z_side, (12, 12, 4, 4), Y)
+    far0_state = begin(side("y", far_og), 0, X)
+    far1_state = begin(side("z", far_og), 8, X)
+    near0_state = begin(side("y", near_og), 4, Z0)
+    near1_state = begin(side("z", near_og), 12, Y)
     far0_state = middle(far0_state, Z0)
-    far1_state = middle(far1_state, X)
+    far1_state = middle(far1_state, Y)
     last0 = exchange(packed(finish(far0_state), 2.0), Z1)
     last1 = exchange(packed(finish(far1_state), 2.0), Z1)
     near0_state = middle(near0_state, X)
@@ -522,7 +509,7 @@
         projected = (near + unpacked(last, 2.0)) * scale
         return 0.8 * momentum[half * part : (half + 1) * part] + 0.2 * projected
 
-    halves, pieces = [], []
+    halves, others = [], []
     small = None
     for half, near_state, last in ((0, near0_state, last0), (1, near1_state, last1)):
         if small is not None:
@@ -533,15 +520,17 @@
         from_x = exchange(small, X)
         from_xc = exchange(from_x, CORE)
         halves.append(mine)
-        pieces.append([v.astype(jnp.float32) for v in (from_core, from_x, from_xc)])
-    rows = (halves[0], pieces[0][0])
-    done = update(rows, ((0, 0), (CORE, 0)), True, signs, weight_v, second_v, ())
-    rows = (halves[1], pieces[1][0], pieces[0][1], pieces[0][2])
-    where = ((0, 1), (CORE, 1), (X, 0), (X | CORE, 0))
-    done = update(rows, where, True, signs, weight_v, second_v, tuple(done))
-    rows = (pieces[1][1], pieces[1][2])
-    where = ((X, 1), (X | CORE, 1))
-    done = update(rows, where, False, signs, weight_v, second_v, tuple(done))
+        others.append([v.astype(jnp.float32) for v in (from_core, from_x, from_xc)])
+    done = ()
+    for half, rows, relatives in (
+        (0, (halves[0], others[0][0]), (0, CORE)),
+        (0, others[0][1:], (X, X | CORE)),
+        (1, (halves[1], others[1][0]), (0, CORE)),
+        (1, others[1][1:], (X, X | CORE)),
+    ):
+        where = tuple((rel, half) for rel in relatives)
+        keep = 0 in relatives
+        done = update(rows, where, keep, signs, weight_v, second_v, tuple(done))
     return tuple(done)
 
 

time: 125 us -> 124 us (level)
  waiting for transfers between devices: 61.4 us -> 53.6 us
  starting transfers between devices: 28.6 us -> 34.6 us
    ppermute x29 -> x33, waiting for transfers between devices: 61.4 us -> 53.6 us  [exchange(): return lax.ppermute(value, AXES, [(i, i ^ mask) for i in range(size)])]
    ppermute x29 -> x33, starting transfers between devices: 28.6 us -> 34.6 us  [exchange(): return lax.ppermute(value, AXES, [(i, i ^ mask) for i in range(size)])]
    pallas_call x3 -> x2, Pallas kernels: 5.12 us -> 3.99 us  [pack(): pl.pallas_call(functools.partial(pack_kernel, groups, width, part), in_sp...]
    pallas_call x1 -> x2, Pallas kernels: 5.92 us -> 7.01 us  [prefetch(): pl.pallas_call(prefetch_kernel, in_specs=[pl.BlockSpec(memory_space=pl.AN...]
    pallas_call x3 -> x4, Pallas kernels: 10.8 us -> 11.5 us  [update(): pl.pallas_call(functools.partial(update_kernel, where, keep, slabs, min(s...]
  transfers between devices with their start and end apart: 29 -> 33, of which waited for: 11 -> 14; matrix products, arithmetic and copies ran while one was open for 1% -> 1% of each run, Pallas kernels for 18% -> 20%
where the time goes in v1:
time: 124 us; the launch traced here: 123 us
  waiting for transfers between devices  53.6 us (43%)
  starting transfers between devices  34.6 us (28%)
  Pallas kernels  31.6 us (25%)
  between operations  2.38 us (2%)
    ppermute x33, waiting for transfers between devices, exchange(): return lax.ppermute(value, AXES, [(i, i ^ mask) for i in range(size)])  53.6 us
    ppermute x33, starting transfers between devices, exchange(): return lax.ppermute(value, AXES, [(i, i ^ mask) for i in range(size)])  34.6 us
    pallas_call x4, Pallas kernels, update(): pl.pallas_call(functools.partial(update_kernel, where, keep, slabs, min(s...  11.5 us
    pallas_call x2, Pallas kernels, prefetch(): pl.pallas_call(prefetch_kernel, in_specs=[pl.BlockSpec(memory_space=pl.AN...  7.01 us
    pallas_call x2, Pallas kernels, sketch_parts(): pl.pallas_call(functools.partial(sketch_kernel, first, din_local), in_spe...  6.2 us
    pallas_call x2, Pallas kernels, pack(): pl.pallas_call(functools.partial(pack_kernel, groups, width, part), in_sp...  3.99 us
    pallas_call x4, Pallas kernels, project(): pl.pallas_call(functools.partial(project_kernel, n), grid=(1,), in_specs=...  2.91 us
  transfers between devices with their start and end apart: 33, of which 14 were waited for; matrix products, arithmetic and copies ran while one was open for 1% of the time, Pallas kernels for 20%

profile of v1, /device:TPU:0, one launch (start us, length us, event | category | flops | bytes accessed | tf_op | source)
XLA Modules:
  0.0 123.4 jit_solution(10600618027783040041)
XLA Ops:
  1.9 3.7 %sketch_first.1 = (bf16[2048,512]{1,0:T(8,128)(2,1)S(1)}, f32[256,512]{1,0:T(8,128)S(1)}, f32[256,512]{1,0:T(8,128)S(1)}) custom-call(s32[1,1]{1,0:T(1,128)} %bitcast.40.refs_0_, s32[1,1]{1,0:T(1,128)} %bitcast.41.refs_1_, bf16[1024,2048]{1,0:T(8,128)(2,1)} %refs_0_.3), custom_call_target="tpu_custom_call" | custom-call | flops 1073741824 | bytes 6291456 | tf_op jit(solution)/shard_map/sketch_first/pallas_call | solution.py:224
  5.6 0.6 collective-permute-start.1
  6.2 2.5 %sketch_next.1 = (f32[256,512]{1,0:T(8,128)S(1)}, f32[256,512]{1,0:T(8,128)S(1)}) custom-call(bf16[1024,2048]{1,0:T(8,128)(2,1)} %refs_0_.3, bf16[2048,512]{1,0:T(8,128)(2,1)S(1)} %get-tuple-element.36.refs_1_.refs_2_), custom_call_target="tpu_custom_call" | custom-call | flops 1073741824 | bytes 6291456 | tf_op jit(solution)/shard_map/sketch_next/pallas_call | solution.py:224
  8.9 3.0 %collective-permute-start.2 = (f32[256,512]{1,0:T(8,128)S(1)}, f32[256,512]{1,0:T(8,128)S(1)}, u32[]{:S(2)}, u32[]{:S(2)}) collective-permute-start(f32[256,512]{1,0:T(8,128)S(1)} %add.74), channel_id=1, source_target_pairs={{0,2},{1,3},{2,0},{3,1},{4,6},{5,7},{6,4},{7,5},{8,10},{9,11},{10,... | collective-permute-start | bytes 1572872 | tf_op jit(solution)/shard_map/ppermute | solution.py:421
  11.9 2.5 %pack.2 = (bf16[4,256,128]{2,1,0:T(8,128)(2,1)S(1)}, bf16[4,256,128]{2,1,0:T(8,128)(2,1)S(1)}, bf16[4,256,128]{2,1,0:T(8,128)(2,1)S(1)}, bf16[4,256,128]{2,1,0:T...) custom-call(bf16[256,8192]{1,0:T(8,128)(2,1)} %og_ref.3), custom_call_target="tpu_custom_call" | custom-call | bytes 6291456 | tf_op jit(solution)/shard_map/pack/pallas_call | solution.py:127
  14.5 9.5 %collective-permute-done.2 = f32[256,512]{1,0:T(8,128)S(1)} collective-permute-done((f32[256,512]{1,0:T(8,128)S(1)}, f32[256,512]{1,0:T(8,128)S(1)}, u32[]{:S(2)}, u32[]{:S(2)}) %collective-permute-start.2) | collective-permute-done | bytes 524320 | tf_op jit(solution)/shard_map/ppermute | solution.py:421
  24.2 1.8 %collective-permute-start.16 = (bf16[256,512]{1,0:T(8,128)(2,1)S(1)}, bf16[256,512]{1,0:T(8,128)(2,1)S(1)}, u32[]{:S(2)}, u32[]{:S(2)}) collective-permute-start(bf16[256,512]{1,0:T(8,128)(2,1)S(1)} %multiply_convert_fusion.4.refs_0_), channel_id=1, source_target_pairs={{0,4},{1,5},{2,6},{3,7},{4,0},{5,1},{6,2},{7,3},{8,12},{9,13},{10,... | collective-permute-start | bytes 786440 | tf_op jit(solution)/shard_map/ppermute | solution.py:421
  26.0 1.5 %pack.3 = (bf16[4,256,128]{2,1,0:T(8,128)(2,1)S(1)}, bf16[4,256,128]{2,1,0:T(8,128)(2,1)S(1)}, bf16[4,256,128]{2,1,0:T(8,128)(2,1)S(1)}, bf16[4,256,128]{2,1,0:T(8,128)(2,1)S(1)}) custom-call(bf16[256,8192]{1,0:T(8,128)(2,1)} %og_ref.3), custom_call_target="tpu_custom_call" | custom-call | bytes 2097152 | tf_op jit(solution)/shard_map/pack/pallas_call | solution.py:127
  27.8 1.9 %collective-permute-start.3 = (bf16[256,512]{1,0:T(8,128)(2,1)S(1)}, bf16[256,512]{1,0:T(8,128)(2,1)S(1)}, u32[]{:S(2)}, u32[]{:S(2)}) collective-permute-start(bf16[256,512]{1,0:T(8,128)(2,1)S(1)} %multiply_convert_fusion.4.refs_0_), channel_id=1, source_target_pairs={{0,1},{1,0},{2,3},{3,2},{4,5},{5,4},{6,7},{7,6},{8,9},{9,8},{10,11... | collective-permute-start | bytes 786440 | tf_op jit(solution)/shard_map/ppermute | solution.py:421
  29.7 3.7 %collective-permute-done.16.refs_2_ = bf16[256,512]{1,0:T(8,128)(2,1)S(1)} collective-permute-done((bf16[256,512]{1,0:T(8,128)(2,1)S(1)}, bf16[256,512]{1,0:T(8,128)(2,1)S(1)}, u32[]{:S(2)}, u32[]{:S(2)}) %collective-permute-start.16) | collective-permute-done | bytes 262176 | tf_op jit(solution)/shard_map/ppermute | solution.py:421
  33.5 5.6 %collective-permute-done.22.refs_6_ = bf16[4,256,128]{2,1,0:T(8,128)(2,1)S(1)} collective-permute-done((bf16[4,256,128]{2,1,0:T(8,128)(2,1)S(1)}, bf16[4,256,128]{2,1,0:T(8,128)(2,1)S(1)}, u32[]{:S(2)}, u32[]{:S(2)}) %collective-permute-start.22) | collective-permute-done | bytes 262176 | tf_op jit(solution)/shard_map/ppermute | solution.py:421
  39.1 1.8 %collective-permute-start.11 = (bf16[4,256,128]{2,1,0:T(8,128)(2,1)S(1)}, bf16[4,256,128]{2,1,0:T(8,128)(2,1)S(1)}, u32[]{:S(2)}, u32[]{:S(2)}) collective-permute-start(bf16[4,256,128]{2,1,0:T(8,128)(2,1)S(1)} %get-tuple-element.47), channel_id=1, source_target_pairs={{0,8},{1,9},{2,10},{3,11},{4,12},{5,13},{6,14},{7,15},{8,0},{9,1},... | collective-permute-start | bytes 786440 | tf_op jit(solution)/shard_map/ppermute | solution.py:421
  40.9 1.3 %collective-permute-done.23.refs_7_ = bf16[4,256,128]{2,1,0:T(8,128)(2,1)S(1)} collective-permute-done((bf16[4,256,128]{2,1,0:T(8,128)(2,1)S(1)}, bf16[4,256,128]{2,1,0:T(8,128)(2,1)S(1)}, u32[]{:S(2)}, u32[]{:S(2)}) %collective-permute-start.23) | collective-permute-done | bytes 262176 | tf_op jit(solution)/shard_map/ppermute | solution.py:421
  42.2 2.3 %collective-permute-start.12 = (bf16[4,256,128]{2,1,0:T(8,128)(2,1)S(1)}, bf16[4,256,128]{2,1,0:T(8,128)(2,1)S(1)}, u32[]{:S(2)}, u32[]{:S(2)}) collective-permute-start(bf16[4,256,128]{2,1,0:T(8,128)(2,1)S(1)} %get-tuple-element.48), channel_id=1, source_target_pairs={{0,9},{1,8},{2,11},{3,10},{4,13},{5,12},{6,15},{7,14},{8,1},{9,0},... | collective-permute-start | bytes 786440 | tf_op jit(solution)/shard_map/ppermute | solution.py:421
  44.4 1.5 %collective-permute-start.18 = (bf16[4,256,128]{2,1,0:T(8,128)(2,1)S(1)}, bf16[4,256,128]{2,1,0:T(8,128)(2,1)S(1)}, u32[]{:S(2)}, u32[]{:S(2)}) collective-permute-start(bf16[4,256,128]{2,1,0:T(8,128)(2,1)S(1)} %get-tuple-element.51), channel_id=1, source_target_pairs={{0,4},{1,5},{2,6},{3,7},{4,0},{5,1},{6,2},{7,3},{8,12},{9,13},{10,... | collective-permute-start | bytes 786440 | tf_op jit(solution)/shard_map/ppermute | solution.py:421
  46.5 0.7 project.7
  47.3 6.3 %collective-permute-done.18.refs_6_ = bf16[4,256,128]{2,1,0:T(8,128)(2,1)S(1)} collective-permute-done((bf16[4,256,128]{2,1,0:T(8,128)(2,1)S(1)}, bf16[4,256,128]{2,1,0:T(8,128)(2,1)S(1)}, u32[]{:S(2)}, u32[]{:S(2)}) %collective-permute-start.18) | collective-permute-done | bytes 262176 | tf_op jit(solution)/shard_map/ppermute | solution.py:421
  54.1 2.1 %collective-permute-done.19.refs_7_ = bf16[4,256,128]{2,1,0:T(8,128)(2,1)S(1)} collective-permute-done((bf16[4,256,128]{2,1,0:T(8,128)(2,1)S(1)}, bf16[4,256,128]{2,1,0:T(8,128)(2,1)S(1)}, u32[]{:S(2)}, u32[]{:S(2)}) %collective-permute-start.19) | collective-permute-done | bytes 262176 | tf_op jit(solution)/shard_map/ppermute | solution.py:421
  56.2 2.2 %collective-permute-start.8 = (bf16[4,256,128]{2,1,0:T(8,128)(2,1)S(1)}, bf16[4,256,128]{2,1,0:T(8,128)(2,1)S(1)}, u32[]{:S(2)}, u32[]{:S(2)}) collective-permute-start(bf16[4,256,128]{2,1,0:T(8,128)(2,1)S(1)} %get-tuple-element.44), channel_id=1, source_target_pairs={{0,9},{1,8},{2,11},{3,10},{4,13},{5,12},{6,15},{7,14},{8,1},{9,0},... | collective-permute-start | bytes 786440 | tf_op jit(solution)/shard_map/ppermute | solution.py:421
  58.4 0.7 project.6
  59.2 4.1 %collective-permute-done.7.refs_6_ = bf16[4,256,128]{2,1,0:T(8,128)(2,1)S(1)} collective-permute-done((bf16[4,256,128]{2,1,0:T(8,128)(2,1)S(1)}, bf16[4,256,128]{2,1,0:T(8,128)(2,1)S(1)}, u32[]{:S(2)}, u32[]{:S(2)}) %collective-permute-start.7) | collective-permute-done | bytes 262176 | tf_op jit(solution)/shard_map/ppermute | solution.py:421
  63.3 1.5 %collective-permute-start.20 = (f16[2,128,512]{2,1,0:T(8,128)(2,1)S(1)}, f16[2,128,512]{2,1,0:T(8,128)(2,1)S(1)}, u32[]{:S(2)}, u32[]{:S(2)}) collective-permute-start(f16[2,128,512]{2,1,0:T(8,128)(2,1)S(1)} %multiply_convert_fusion.1), channel_id=1, source_target_pairs={{0,8},{1,9},{2,10},{3,11},{4,12},{5,13},{6,14},{7,15},{8,0},{9,1},... | collective-permute-start | bytes 786440 | tf_op jit(solution)/shard_map/ppermute | solution.py:421
  64.8 3.1 %collective-permute-done.8.refs_7_ = bf16[4,256,128]{2,1,0:T(8,128)(2,1)S(1)} collective-permute-done((bf16[4,256,128]{2,1,0:T(8,128)(2,1)S(1)}, bf16[4,256,128]{2,1,0:T(8,128)(2,1)S(1)}, u32[]{:S(2)}, u32[]{:S(2)}) %collective-permute-start.8) | collective-permute-done | bytes 262176 | tf_op jit(solution)/shard_map/ppermute | solution.py:421
  68.0 1.5 %collective-permute-start.24 = (f16[2,128,512]{2,1,0:T(8,128)(2,1)S(1)}, f16[2,128,512]{2,1,0:T(8,128)(2,1)S(1)}, u32[]{:S(2)}, u32[]{:S(2)}) collective-permute-start(f16[2,128,512]{2,1,0:T(8,128)(2,1)S(1)} %multiply_convert_fusion), channel_id=1, source_target_pairs={{0,2},{1,3},{2,0},{3,1},{4,6},{5,7},{6,4},{7,5},{8,10},{9,11},{10,... | collective-permute-start | bytes 786440 | tf_op jit(solution)/shard_map/ppermute | solution.py:421
  69.5 0.7 project.4
  70.3 0.7 project.5
  71.1 0.6 collective-permute-start.13
  71.7 2.0 %collective-permute-start.9 = (f16[2,128,512]{2,1,0:T(8,128)(2,1)S(1)}, f16[2,128,512]{2,1,0:T(8,128)(2,1)S(1)}, u32[]{:S(2)}, u32[]{:S(2)}) collective-permute-start(f16[2,128,512]{2,1,0:T(8,128)(2,1)S(1)} %multiply_convert_fusion.3), channel_id=1, source_target_pairs={{0,4},{1,5},{2,6},{3,7},{4,0},{5,1},{6,2},{7,3},{8,12},{9,13},{10,... | collective-permute-start | bytes 786440 | tf_op jit(solution)/shard_map/ppermute | solution.py:421
  73.8 1.6 %collective-permute-start.21 = (f16[128,512]{1,0:T(8,128)(2,1)S(1)}, f16[128,512]{1,0:T(8,128)(2,1)S(1)}, u32[]{:S(2)}, u32[]{:S(2)}) collective-permute-start(f16[128,512]{1,0:T(8,128)(2,1)S(1)} %fusion.12), channel_id=1, source_target_pairs={{0,2},{1,3},{2,0},{3,1},{4,6},{5,7},{6,4},{7,5},{8,10},{9,11},{10,... | collective-permute-start | bytes 393224 | tf_op jit(solution)/shard_map/ppermute | solution.py:421
  75.4 1.8 %collective-permute-done.24 = f16[2,128,512]{2,1,0:T(8,128)(2,1)S(1)} collective-permute-done((f16[2,128,512]{2,1,0:T(8,128)(2,1)S(1)}, f16[2,128,512]{2,1,0:T(8,128)(2,1)S(1)}, u32[]{:S(2)}, u32[]{:S(2)}) %collective-permute-start.24) | collective-permute-done | bytes 262176 | tf_op jit(solution)/shard_map/ppermute | solution.py:421
  77.2 0.8 collective-permute-start.25
  78.0 4.8 %collective-permute-done.13 = f16[2,128,512]{2,1,0:T(8,128)(2,1)S(1)} collective-permute-done((f16[2,128,512]{2,1,0:T(8,128)(2,1)S(1)}, f16[2,128,512]{2,1,0:T(8,128)(2,1)S(1)}, u32[]{:S(2)}, u32[]{:S(2)}) %collective-permute-start.13) | collective-permute-done | bytes 262176 | tf_op jit(solution)/shard_map/ppermute | solution.py:421
  82.8 2.0 %collective-permute-start.14 = (f16[128,512]{1,0:T(8,128)(2,1)S(1)}, f16[128,512]{1,0:T(8,128)(2,1)S(1)}, u32[]{:S(2)}, u32[]{:S(2)}) collective-permute-start(f16[128,512]{1,0:T(8,128)(2,1)S(1)} %fusion.11), channel_id=1, source_target_pairs={{0,4},{1,5},{2,6},{3,7},{4,0},{5,1},{6,2},{7,3},{8,12},{9,13},{10,... | collective-permute-start | bytes 393224 | tf_op jit(solution)/shard_map/ppermute | solution.py:421
  84.9 1.5 %collective-permute-start.10 = (f16[128,512]{1,0:T(8,128)(2,1)S(1)}, f16[128,512]{1,0:T(8,128)(2,1)S(1)}, u32[]{:S(2)}, u32[]{:S(2)}) collective-permute-start(f16[128,512]{1,0:T(8,128)(2,1)S(1)} %fusion.10), channel_id=1, source_target_pairs={{0,2},{1,3},{2,0},{3,1},{4,6},{5,7},{6,4},{7,5},{8,10},{9,11},{10,... | collective-permute-start | bytes 393224 | tf_op jit(solution)/shard_map/ppermute | solution.py:421
  86.5 2.7 %collective-permute-start.26 = (f16[128,512]{1,0:T(8,128)(2,1)S(1)}, f16[128,512]{1,0:T(8,128)(2,1)S(1)}, u32[]{:S(2)}, u32[]{:S(2)}) collective-permute-start(f16[128,512]{1,0:T(8,128)(2,1)S(1)} %fusion.1), channel_id=1, source_target_pairs={{0,16},{1,17},{2,18},{3,19},{4,20},{5,21},{6,22},{7,23},{8,24},{9,... | collective-permute-start | bytes 393224 | tf_op jit(solution)/shard_map/ppermute | solution.py:421
  89.3 1.4 %collective-permute-start.15 = (f16[128,512]{1,0:T(8,128)(2,1)S(1)}, f16[128,512]{1,0:T(8,128)(2,1)S(1)}, u32[]{:S(2)}, u32[]{:S(2)}) collective-permute-start(f16[128,512]{1,0:T(8,128)(2,1)S(1)} %fusion.6), channel_id=1, source_target_pairs={{0,16},{1,17},{2,18},{3,19},{4,20},{5,21},{6,22},{7,23},{8,24},{9,... | collective-permute-start | bytes 393224 | tf_op jit(solution)/shard_map/ppermute | solution.py:421
  90.7 7.4 %collective-permute-done.26 = f16[128,512]{1,0:T(8,128)(2,1)S(1)} collective-permute-done((f16[128,512]{1,0:T(8,128)(2,1)S(1)}, f16[128,512]{1,0:T(8,128)(2,1)S(1)}, u32[]{:S(2)}, u32[]{:S(2)}) %collective-permute-start.26) | collective-permute-done | bytes 131104 | tf_op jit(solution)/shard_map/ppermute | solution.py:421
  98.2 0.6 collective-permute-start.30
  98.8 0.8 collective-permute-done.15
  99.7 0.8 collective-permute-start.27
  101.1 2.9 %collective-permute-done.30 = f16[128,512]{1,0:T(8,128)(2,1)S(1)} collective-permute-done((f16[128,512]{1,0:T(8,128)(2,1)S(1)}, f16[128,512]{1,0:T(8,128)(2,1)S(1)}, u32[]{:S(2)}, u32[]{:S(2)}) %collective-permute-start.30) | collective-permute-done | bytes 131104 | tf_op jit(solution)/shard_map/ppermute | solution.py:421
  104.0 3.5 %prefetch.2.refs_3_ = f32[1024,2048]{1,0:T(8,128)S(1)} custom-call(f32[1024,2048]{1,0:T(8,128)} %refs_0_.4), custom_call_target="tpu_custom_call" | custom-call | bytes 8388608 | tf_op jit(solution)/shard_map/prefetch/pallas_call | solution.py:308
  107.5 3.5 %prefetch.3.refs_4_ = f32[1024,2048]{1,0:T(8,128)S(1)} custom-call(f32[1024,2048]{1,0:T(8,128)} %refs_0_.5), custom_call_target="tpu_custom_call" | custom-call | bytes 8388608 | tf_op jit(solution)/shard_map/prefetch/pallas_call | solution.py:308
  111.0 0.6 collective-permute-start.28
  111.7 2.9 %update.4 = (f32[1024,2048]{1,0:T(8,128)}, f32[1024,2048]{1,0:T(8,128)}, f32[256,512]{1,0:T(8,128)}) custom-call(f32[128,512]{1,0:T(8,128)S(1)} %get-tuple-element.72.refs_0_, f32[128,512]{1,0:T(8,128)S(1)} %convert_element_type.127.refs_1_, bf16[2048,512]{1,0:T(8,128)(2,1)S(1)} %get-tuple-element.36.refs_1_.refs_2_, f32[1024,2048]{1,0:T(8,128)S(1)} %prefetch.2.refs_3_, ...), custom_call_target="tpu_custom_call" | custom-call | flops 1073741824 | bytes 4194304 | tf_op jit(solution)/shard_map/update/pallas_call | solution.py:390
  114.6 2.8 %update.5 = (f32[1024,2048]{1,0:T(8,128)}, f32[1024,2048]{1,0:T(8,128)}, f32[256,512]{1,0:T(8,128)}) custom-call(f32[128,512]{1,0:T(8,128)S(1)} %convert_element_type.125.refs_0_, f32[128,512]{1,0:T(8,128)S(1)} %convert_element_type.126.refs_1_, ...), custom_call_target="tpu_custom_call", output_to_operand_aliasing={{0}: (5, {}), {1}: (6, {}), {2}: (7, {})} | custom-call | flops 1073741824 | bytes 4194304 | tf_op jit(solution)/shard_map/update/pallas_call | solution.py:390
  117.5 2.9 %update.6 = (f32[1024,2048]{1,0:T(8,128)}, f32[1024,2048]{1,0:T(8,128)}, f32[256,512]{1,0:T(8,128)}) custom-call(f32[128,512]{1,0:T(8,128)S(1)} %get-tuple-element.70.refs_0_, f32[128,512]{1,0:T(8,128)S(1)} %convert_element_type.124.refs_1_, ...), custom_call_target="tpu_custom_call", output_to_operand_aliasing={{0}: (5, {}), {1}: (6, {}), {2}: (7, {})} | custom-call | flops 1073741824 | bytes 4194304 | tf_op jit(solution)/shard_map/update/pallas_call | solution.py:390
  120.4 2.8 %update.7 = (f32[1024,2048]{1,0:T(8,128)}, f32[1024,2048]{1,0:T(8,128)}, f32[256,512]{1,0:T(8,128)}) custom-call(f32[128,512]{1,0:T(8,128)S(1)} %convert_element_type.122.refs_0_, f32[128,512]{1,0:T(8,128)S(1)} %convert_element_type.123.refs_1_, ...), custom_call_target="tpu_custom_call", output_to_operand_aliasing={{0}: (5, {}), {1}: (6, {}), {2}: (7, {})} | custom-call | flops 1073741824 | bytes 4194304 | tf_op jit(solution)/shard_map/update/pallas_call | solution.py:390
  (54 shorter events, 3.4 us)
Async XLA Ops:
  5.6 3.2 %collective-permute-start.1 = (f32[256,512]{1,0:T(8,128)S(1)}, f32[256,512]{1,0:T(8,128)S(1)}, u32[]{:S(2)}, u32[]{:S(2)}) collective-permute-start(f32[256,512]{1,0:T(8,128)S(1)} %get-tuple-element.40), channel_id=1, source_target_pairs={{0,1},{1,0},{2,3},{3,2},{4,5},{5,4},{6,7},{7,6},{8,9},{9,8},{10,11... | collective-permute-start | bytes 1572872 | tf_op jit(solution)/shard_map/ppermute | solution.py:421
  8.7 5.8 %collective-permute-start = (f32[256,512]{1,0:T(8,128)S(1)}, f32[256,512]{1,0:T(8,128)S(1)}, u32[]{:S(2)}, u32[]{:S(2)}) collective-permute-start(f32[256,512]{1,0:T(8,128)S(1)} %get-tuple-element.38), channel_id=1, source_target_pairs={{0,1},{1,0},{2,3},{3,2},{4,5},{5,4},{6,7},{7,6},{8,9},{9,8},{10,11... | collective-permute-start | bytes 1572872 | tf_op jit(solution)/shard_map/ppermute | solution.py:421
  8.9 15.1 %collective-permute-start.2 = (f32[256,512]{1,0:T(8,128)S(1)}, f32[256,512]{1,0:T(8,128)S(1)}, u32[]{:S(2)}, u32[]{:S(2)}) collective-permute-start(f32[256,512]{1,0:T(8,128)S(1)} %add.74), channel_id=1, source_target_pairs={{0,2},{1,3},{2,0},{3,1},{4,6},{5,7},{6,4},{7,5},{8,10},{9,11},{10,... | collective-permute-start | bytes 1572872 | tf_op jit(solution)/shard_map/ppermute | solution.py:421
  14.4 30.0 %collective-permute-start.6 = (bf16[16,256,128]{2,1,0:T(8,128)(2,1)S(1)}, bf16[16,256,128]{2,1,0:T(8,128)(2,1)S(1)}, u32[]{:S(2)}, u32[]{:S(2)}) collective-permute-start(bf16[16,256,128]{2,1,0:T(8,128)(2,1)S(1)} %get-tuple-element.42), channel_id=1, source_target_pairs={{0,1},{1,0},{2,3},{3,2},{4,5},{5,4},{6,7},{7,6},{8,9},{9,8},{10,11... | collective-permute-start | bytes 3145736 | tf_op jit(solution)/shard_map/ppermute | solution.py:421
  24.2 9.2 %collective-permute-start.16 = (bf16[256,512]{1,0:T(8,128)(2,1)S(1)}, bf16[256,512]{1,0:T(8,128)(2,1)S(1)}, u32[]{:S(2)}, u32[]{:S(2)}) collective-permute-start(bf16[256,512]{1,0:T(8,128)(2,1)S(1)} %multiply_convert_fusion.4.refs_0_), channel_id=1, source_target_pairs={{0,4},{1,5},{2,6},{3,7},{4,0},{5,1},{6,2},{7,3},{8,12},{9,13},{10,... | collective-permute-start | bytes 786440 | tf_op jit(solution)/shard_map/ppermute | solution.py:421
  27.5 11.6 %collective-permute-start.22 = (bf16[4,256,128]{2,1,0:T(8,128)(2,1)S(1)}, bf16[4,256,128]{2,1,0:T(8,128)(2,1)S(1)}, u32[]{:S(2)}, u32[]{:S(2)}) collective-permute-start(bf16[4,256,128]{2,1,0:T(8,128)(2,1)S(1)} %get-tuple-element.55), channel_id=1, source_target_pairs={{0,4},{1,5},{2,6},{3,7},{4,0},{5,1},{6,2},{7,3},{8,12},{9,13},{10,... | collective-permute-start | bytes 786440 | tf_op jit(solution)/shard_map/ppermute | solution.py:421
  27.8 14.3 %collective-permute-start.23 = (bf16[4,256,128]{2,1,0:T(8,128)(2,1)S(1)}, bf16[4,256,128]{2,1,0:T(8,128)(2,1)S(1)}, u32[]{:S(2)}, u32[]{:S(2)}) collective-permute-start(bf16[4,256,128]{2,1,0:T(8,128)(2,1)S(1)} %get-tuple-element.56), channel_id=1, source_target_pairs={{0,5},{1,4},{2,7},{3,6},{4,1},{5,0},{6,3},{7,2},{8,13},{9,12},{10,... | collective-permute-start | bytes 786440 | tf_op jit(solution)/shard_map/ppermute | solution.py:421
  27.8 18.1 %collective-permute-start.3 = (bf16[256,512]{1,0:T(8,128)(2,1)S(1)}, bf16[256,512]{1,0:T(8,128)(2,1)S(1)}, u32[]{:S(2)}, u32[]{:S(2)}) collective-permute-start(bf16[256,512]{1,0:T(8,128)(2,1)S(1)} %multiply_convert_fusion.4.refs_0_), channel_id=1, source_target_pairs={{0,1},{1,0},{2,3},{3,2},{4,5},{5,4},{6,7},{7,6},{8,9},{9,8},{10,11... | collective-permute-start | bytes 786440 | tf_op jit(solution)/shard_map/ppermute | solution.py:421
  33.4 12.5 %collective-permute-start.17 = (bf16[256,512]{1,0:T(8,128)(2,1)S(1)}, bf16[256,512]{1,0:T(8,128)(2,1)S(1)}, u32[]{:S(2)}, u32[]{:S(2)}) collective-permute-start(bf16[256,512]{1,0:T(8,128)(2,1)S(1)} %collective-permute-done.16.refs_2_), channel_id=1, source_target_pairs={{0,1},{1,0},{2,3},{3,2},{4,5},{5,4},{6,7},{7,6},{8,9},{9,8},{10,11... | collective-permute-start | bytes 786440 | tf_op jit(solution)/shard_map/ppermute | solution.py:421
  39.1 31.2 %collective-permute-start.11 = (bf16[4,256,128]{2,1,0:T(8,128)(2,1)S(1)}, bf16[4,256,128]{2,1,0:T(8,128)(2,1)S(1)}, u32[]{:S(2)}, u32[]{:S(2)}) collective-permute-start(bf16[4,256,128]{2,1,0:T(8,128)(2,1)S(1)} %get-tuple-element.47), channel_id=1, source_target_pairs={{0,8},{1,9},{2,10},{3,11},{4,12},{5,13},{6,14},{7,15},{8,0},{9,1},... | collective-permute-start | bytes 786440 | tf_op jit(solution)/shard_map/ppermute | solution.py:421
  42.2 28.1 %collective-permute-start.12 = (bf16[4,256,128]{2,1,0:T(8,128)(2,1)S(1)}, bf16[4,256,128]{2,1,0:T(8,128)(2,1)S(1)}, u32[]{:S(2)}, u32[]{:S(2)}) collective-permute-start(bf16[4,256,128]{2,1,0:T(8,128)(2,1)S(1)} %get-tuple-element.48), channel_id=1, source_target_pairs={{0,9},{1,8},{2,11},{3,10},{4,13},{5,12},{6,15},{7,14},{8,1},{9,0},... | collective-permute-start | bytes 786440 | tf_op jit(solution)/shard_map/ppermute | solution.py:421
  44.4 9.2 %collective-permute-start.18 = (bf16[4,256,128]{2,1,0:T(8,128)(2,1)S(1)}, bf16[4,256,128]{2,1,0:T(8,128)(2,1)S(1)}, u32[]{:S(2)}, u32[]{:S(2)}) collective-permute-start(bf16[4,256,128]{2,1,0:T(8,128)(2,1)S(1)} %get-tuple-element.51), channel_id=1, source_target_pairs={{0,4},{1,5},{2,6},{3,7},{4,0},{5,1},{6,2},{7,3},{8,12},{9,13},{10,... | collective-permute-start | bytes 786440 | tf_op jit(solution)/shard_map/ppermute | solution.py:421
  46.0 10.2 %collective-permute-start.19 = (bf16[4,256,128]{2,1,0:T(8,128)(2,1)S(1)}, bf16[4,256,128]{2,1,0:T(8,128)(2,1)S(1)}, u32[]{:S(2)}, u32[]{:S(2)}) collective-permute-start(bf16[4,256,128]{2,1,0:T(8,128)(2,1)S(1)} %get-tuple-element.52), channel_id=1, source_target_pairs={{0,5},{1,4},{2,7},{3,6},{4,1},{5,0},{6,3},{7,2},{8,13},{9,12},{10,... | collective-permute-start | bytes 786440 | tf_op jit(solution)/shard_map/ppermute | solution.py:421
  46.0 12.4 %collective-permute-start.4 = (bf16[256,512]{1,0:T(8,128)(2,1)S(1)}, bf16[256,512]{1,0:T(8,128)(2,1)S(1)}, u32[]{:S(2)}, u32[]{:S(2)}) collective-permute-start(bf16[256,512]{1,0:T(8,128)(2,1)S(1)} %multiply_convert_fusion.4.refs_0_), channel_id=1, source_target_pairs={{0,8},{1,9},{2,10},{3,11},{4,12},{5,13},{6,14},{7,15},{8,0},{9,1},... | collective-permute-start | bytes 786440 | tf_op jit(solution)/shard_map/ppermute | solution.py:421
  53.6 9.7 %collective-permute-start.7 = (bf16[4,256,128]{2,1,0:T(8,128)(2,1)S(1)}, bf16[4,256,128]{2,1,0:T(8,128)(2,1)S(1)}, u32[]{:S(2)}, u32[]{:S(2)}) collective-permute-start(bf16[4,256,128]{2,1,0:T(8,128)(2,1)S(1)} %get-tuple-element.43), channel_id=1, source_target_pairs={{0,8},{1,9},{2,10},{3,11},{4,12},{5,13},{6,14},{7,15},{8,0},{9,1},... | collective-permute-start | bytes 786440 | tf_op jit(solution)/shard_map/ppermute | solution.py:421
  56.2 41.9 %copy-start = (f32[256,512]{1,0:T(8,128)S(1)}, f32[256,512]{1,0:T(8,128)}, u32[]{:S(2)}) copy-start(f32[256,512]{1,0:T(8,128)} %param.11) | copy-start | bytes 1572868
  56.2 11.8 %collective-permute-start.8 = (bf16[4,256,128]{2,1,0:T(8,128)(2,1)S(1)}, bf16[4,256,128]{2,1,0:T(8,128)(2,1)S(1)}, u32[]{:S(2)}, u32[]{:S(2)}) collective-permute-start(bf16[4,256,128]{2,1,0:T(8,128)(2,1)S(1)} %get-tuple-element.44), channel_id=1, source_target_pairs={{0,9},{1,8},{2,11},{3,10},{4,13},{5,12},{6,15},{7,14},{8,1},{9,0},... | collective-permute-start | bytes 786440 | tf_op jit(solution)/shard_map/ppermute | solution.py:421
  58.4 11.1 %collective-permute-start.5 = (bf16[256,512]{1,0:T(8,128)(2,1)S(1)}, bf16[256,512]{1,0:T(8,128)(2,1)S(1)}, u32[]{:S(2)}, u32[]{:S(2)}) collective-permute-start(bf16[256,512]{1,0:T(8,128)(2,1)S(1)} %collective-permute-done.4.refs_2_), channel_id=1, source_target_pairs={{0,1},{1,0},{2,3},{3,2},{4,5},{5,4},{6,7},{7,6},{8,9},{9,8},{10,11... | collective-permute-start | bytes 786440 | tf_op jit(solution)/shard_map/ppermute | solution.py:421
  63.3 10.5 %collective-permute-start.20 = (f16[2,128,512]{2,1,0:T(8,128)(2,1)S(1)}, f16[2,128,512]{2,1,0:T(8,128)(2,1)S(1)}, u32[]{:S(2)}, u32[]{:S(2)}) collective-permute-start(f16[2,128,512]{2,1,0:T(8,128)(2,1)S(1)} %multiply_convert_fusion.1), channel_id=1, source_target_pairs={{0,8},{1,9},{2,10},{3,11},{4,12},{5,13},{6,14},{7,15},{8,0},{9,1},... | collective-permute-start | bytes 786440 | tf_op jit(solution)/shard_map/ppermute | solution.py:421
  68.0 9.2 %collective-permute-start.24 = (f16[2,128,512]{2,1,0:T(8,128)(2,1)S(1)}, f16[2,128,512]{2,1,0:T(8,128)(2,1)S(1)}, u32[]{:S(2)}, u32[]{:S(2)}) collective-permute-start(f16[2,128,512]{2,1,0:T(8,128)(2,1)S(1)} %multiply_convert_fusion), channel_id=1, source_target_pairs={{0,2},{1,3},{2,0},{3,1},{4,6},{5,7},{6,4},{7,5},{8,10},{9,11},{10,... | collective-permute-start | bytes 786440 | tf_op jit(solution)/shard_map/ppermute | solution.py:421
  71.1 11.7 %collective-permute-start.13 = (f16[2,128,512]{2,1,0:T(8,128)(2,1)S(1)}, f16[2,128,512]{2,1,0:T(8,128)(2,1)S(1)}, u32[]{:S(2)}, u32[]{:S(2)}) collective-permute-start(f16[2,128,512]{2,1,0:T(8,128)(2,1)S(1)} %multiply_convert_fusion.2), channel_id=1, source_target_pairs={{0,2},{1,3},{2,0},{3,1},{4,6},{5,7},{6,4},{7,5},{8,10},{9,11},{10,... | collective-permute-start | bytes 786440 | tf_op jit(solution)/shard_map/ppermute | solution.py:421
  71.7 13.2 %collective-permute-start.9 = (f16[2,128,512]{2,1,0:T(8,128)(2,1)S(1)}, f16[2,128,512]{2,1,0:T(8,128)(2,1)S(1)}, u32[]{:S(2)}, u32[]{:S(2)}) collective-permute-start(f16[2,128,512]{2,1,0:T(8,128)(2,1)S(1)} %multiply_convert_fusion.3), channel_id=1, source_target_pairs={{0,4},{1,5},{2,6},{3,7},{4,0},{5,1},{6,2},{7,3},{8,12},{9,13},{10,... | collective-permute-start | bytes 786440 | tf_op jit(solution)/shard_map/ppermute | solution.py:421
  73.8 16.8 %collective-permute-start.21 = (f16[128,512]{1,0:T(8,128)(2,1)S(1)}, f16[128,512]{1,0:T(8,128)(2,1)S(1)}, u32[]{:S(2)}, u32[]{:S(2)}) collective-permute-start(f16[128,512]{1,0:T(8,128)(2,1)S(1)} %fusion.12), channel_id=1, source_target_pairs={{0,2},{1,3},{2,0},{3,1},{4,6},{5,7},{6,4},{7,5},{8,10},{9,11},{10,... | collective-permute-start | bytes 393224 | tf_op jit(solution)/shard_map/ppermute | solution.py:421
  77.2 9.2 %collective-permute-start.25 = (f16[128,512]{1,0:T(8,128)(2,1)S(1)}, f16[128,512]{1,0:T(8,128)(2,1)S(1)}, u32[]{:S(2)}, u32[]{:S(2)}) collective-permute-start(f16[128,512]{1,0:T(8,128)(2,1)S(1)} %fusion.13), channel_id=1, source_target_pairs={{0,8},{1,9},{2,10},{3,11},{4,12},{5,13},{6,14},{7,15},{8,0},{9,1},... | collective-permute-start | bytes 393224 | tf_op jit(solution)/shard_map/ppermute | solution.py:421
  82.8 6.4 %collective-permute-start.14 = (f16[128,512]{1,0:T(8,128)(2,1)S(1)}, f16[128,512]{1,0:T(8,128)(2,1)S(1)}, u32[]{:S(2)}, u32[]{:S(2)}) collective-permute-start(f16[128,512]{1,0:T(8,128)(2,1)S(1)} %fusion.11), channel_id=1, source_target_pairs={{0,4},{1,5},{2,6},{3,7},{4,0},{5,1},{6,2},{7,3},{8,12},{9,13},{10,... | collective-permute-start | bytes 393224 | tf_op jit(solution)/shard_map/ppermute | solution.py:421
  84.9 14.7 %collective-permute-start.10 = (f16[128,512]{1,0:T(8,128)(2,1)S(1)}, f16[128,512]{1,0:T(8,128)(2,1)S(1)}, u32[]{:S(2)}, u32[]{:S(2)}) collective-permute-start(f16[128,512]{1,0:T(8,128)(2,1)S(1)} %fusion.10), channel_id=1, source_target_pairs={{0,2},{1,3},{2,0},{3,1},{4,6},{5,7},{6,4},{7,5},{8,10},{9,11},{10,... | collective-permute-start | bytes 393224 | tf_op jit(solution)/shard_map/ppermute | solution.py:421
  86.5 11.6 %collective-permute-start.26 = (f16[128,512]{1,0:T(8,128)(2,1)S(1)}, f16[128,512]{1,0:T(8,128)(2,1)S(1)}, u32[]{:S(2)}, u32[]{:S(2)}) collective-permute-start(f16[128,512]{1,0:T(8,128)(2,1)S(1)} %fusion.1), channel_id=1, source_target_pairs={{0,16},{1,17},{2,18},{3,19},{4,20},{5,21},{6,22},{7,23},{8,24},{9,... | collective-permute-start | bytes 393224 | tf_op jit(solution)/shard_map/ppermute | solution.py:421
  89.3 10.3 %collective-permute-start.15 = (f16[128,512]{1,0:T(8,128)(2,1)S(1)}, f16[128,512]{1,0:T(8,128)(2,1)S(1)}, u32[]{:S(2)}, u32[]{:S(2)}) collective-permute-start(f16[128,512]{1,0:T(8,128)(2,1)S(1)} %fusion.6), channel_id=1, source_target_pairs={{0,16},{1,17},{2,18},{3,19},{4,20},{5,21},{6,22},{7,23},{8,24},{9,... | collective-permute-start | bytes 393224 | tf_op jit(solution)/shard_map/ppermute | solution.py:421
  98.2 5.7 %collective-permute-start.30 = (f16[128,512]{1,0:T(8,128)(2,1)S(1)}, f16[128,512]{1,0:T(8,128)(2,1)S(1)}, u32[]{:S(2)}, u32[]{:S(2)}) collective-permute-start(f16[128,512]{1,0:T(8,128)(2,1)S(1)} %get-tuple-element.71), channel_id=1, source_target_pairs={{0,2},{1,3},{2,0},{3,1},{4,6},{5,7},{6,4},{7,5},{8,10},{9,11},{10,... | collective-permute-start | bytes 393224 | tf_op jit(solution)/shard_map/ppermute | solution.py:421
  99.7 11.3 %collective-permute-start.27 = (f16[128,512]{1,0:T(8,128)(2,1)S(1)}, f16[128,512]{1,0:T(8,128)(2,1)S(1)}, u32[]{:S(2)}, u32[]{:S(2)}) collective-permute-start(f16[128,512]{1,0:T(8,128)(2,1)S(1)} %get-tuple-element.69), channel_id=1, source_target_pairs={{0,2},{1,3},{2,0},{3,1},{4,6},{5,7},{6,4},{7,5},{8,10},{9,11},{10,... | collective-permute-start | bytes 393224 | tf_op jit(solution)/shard_map/ppermute | solution.py:421
  100.5 11.1 %collective-permute-start.32 = (f16[128,512]{1,0:T(8,128)(2,1)S(1)}, f16[128,512]{1,0:T(8,128)(2,1)S(1)}, u32[]{:S(2)}, u32[]{:S(2)}) collective-permute-start(f16[128,512]{1,0:T(8,128)(2,1)S(1)} %get-tuple-element.71), channel_id=1, source_target_pairs={{0,1},{1,0},{2,3},{3,2},{4,5},{5,4},{6,7},{7,6},{8,9},{9,8},{10,11... | collective-permute-start | bytes 393224 | tf_op jit(solution)/shard_map/ppermute | solution.py:421
  100.5 11.1 %collective-permute-start.29 = (f16[128,512]{1,0:T(8,128)(2,1)S(1)}, f16[128,512]{1,0:T(8,128)(2,1)S(1)}, u32[]{:S(2)}, u32[]{:S(2)}) collective-permute-start(f16[128,512]{1,0:T(8,128)(2,1)S(1)} %get-tuple-element.69), channel_id=1, source_target_pairs={{0,1},{1,0},{2,3},{3,2},{4,5},{5,4},{6,7},{7,6},{8,9},{9,8},{10,11... | collective-permute-start | bytes 393224 | tf_op jit(solution)/shard_map/ppermute | solution.py:421
  104.0 10.7 %collective-permute-start.31 = (f16[128,512]{1,0:T(8,128)(2,1)S(1)}, f16[128,512]{1,0:T(8,128)(2,1)S(1)}, u32[]{:S(2)}, u32[]{:S(2)}) collective-permute-start(f16[128,512]{1,0:T(8,128)(2,1)S(1)} %collective-permute-done.30), channel_id=1, source_target_pairs={{0,1},{1,0},{2,3},{3,2},{4,5},{5,4},{6,7},{7,6},{8,9},{9,8},{10,11... | collective-permute-start | bytes 393224 | tf_op jit(solution)/shard_map/ppermute | solution.py:421
  111.0 9.4 %collective-permute-start.28 = (f16[128,512]{1,0:T(8,128)(2,1)S(1)}, f16[128,512]{1,0:T(8,128)(2,1)S(1)}, u32[]{:S(2)}, u32[]{:S(2)}) collective-permute-start(f16[128,512]{1,0:T(8,128)(2,1)S(1)} %collective-permute-done.27), channel_id=1, source_target_pairs={{0,1},{1,0},{2,3},{3,2},{4,5},{5,4},{6,7},{7,6},{8,9},{9,8},{10,11... | collective-permute-start | bytes 393224 | tf_op jit(solution)/shard_map/ppermute | solution.py:421

commit v2 on v1

--- a/solution.py
+++ b/solution.py
@@ -238,7 +238,7 @@
             bytes_accessed=half * din_local * 2 + din_local * low_rank * 2 + 2 * half * low_rank * 4,
             transcendentals=0,
         ),
-        name="sketch_first" if first else "sketch_next",
+        name="sketch",
     )(*args)
 
 
@@ -428,38 +428,36 @@
     inv_root = 1.0 / jnp.sqrt(jnp.float32(low_rank))
     far0 = [(Z1 | X | Z0, 0), (Z1 | X, 0), (Z1 | Z0, 0), (Z1, 0)]
     near0 = [(Z0 | X, 0), (Z0, 0), (X, 0), (0, 0)]
-    far1 = [(Z1 | X | Y, 1), (Z1 | X, 1), (Z1 | Y, 1), (Z1, 1)]
+    far1 = [(Z1 | Y | X, 1), (Z1 | Y, 1), (Z1 | X, 1), (Z1, 1)]
     near1 = [(Y | X, 1), (Y, 1), (X, 1), (0, 1)]
 
     def toward(mask, pieces):
         return [(rel ^ mask, half) for rel, half in pieces]
 
     part = owner_rows // 2
-    pieces = far0 + near0 + far1 + near1
+    over_y, over_z = far0 + near0, far1 + near1
+    og_y, og_z = pack(out_grad, [toward(Y, over_y), toward(Z0, over_z)], owner_rows, part)
+    og_y = exchange(og_y, Y)
+    og_z = exchange(og_z, Z0)
     seeds = (sign_seed.reshape(1, 1), step_number.reshape(1, 1))
     signs, send_a, keep_a = sketch_parts(tokens, low_rank, None, seeds)
     got_a = exchange(send_a, CORE)
-
-    def messages(over_y, over_z):
-        return [
-            toward(Y, over_y),
-            toward(Z0, over_z),
-            toward(Y | CORE, over_y),
-            toward(Z0 | CORE, over_z),
-        ]
-
-    far_out = pack(out_grad, messages(far0, far1), owner_rows, part)
-    *near_out, og_c, og_own = pack(
-        out_grad, messages(near0, near1) + [toward(CORE, pieces), pieces], owner_rows, part
+    og_yc, og_zc = pack(
+        out_grad, [toward(Y | CORE, over_y), toward(Z0 | CORE, over_z)], owner_rows, part
+    )
+    og_c, og_own = pack(
+        out_grad,
+        [toward(CORE, over_y + over_z), over_y + over_z],
+        owner_rows,
+        part,
     )
     across = exchange(keep_a + got_a, X)
-    routes = (("y", Y), ("z", Z0), ("yc", Y | CORE), ("zc", Z0 | CORE))
-    far_og = {name: exchange(value, mask) for value, (name, mask) in zip(far_out, routes)}
+    og_yc = exchange(og_yc, Y | CORE)
+    og_zc = exchange(og_zc, Z0 | CORE)
     og_c = exchange(og_c, CORE)
     send_b, keep_b = sketch_parts(tokens, low_rank, signs, None)
     got_b = exchange(send_b, CORE)
-    (weight_v,) = prefetch(weight)
-    (second_v,) = prefetch(second)
+    weight_v, second_v = prefetch(weight, second)
     sketch = (((keep_b + got_b) + across) * inv_root).astype(jnp.bfloat16)
 
     sk_y = exchange(sketch, Y)
@@ -467,7 +465,6 @@
     sk_c = exchange(sketch, CORE)
     sk_yc = exchange(sk_y, CORE)
     sk_zc = exchange(sk_z, CORE)
-    near_og = {name: exchange(value, mask) for value, (name, mask) in zip(near_out, routes)}
 
     scale = jnp.float32(1.0 / total_tokens)
 
@@ -477,29 +474,28 @@
     def unpacked(value, extra):
         return value.astype(jnp.float32) * (1.0 / (scale * extra))
 
-    def side(axis, og):
-        got = {"y": (sk_y, sk_yc), "z": (sk_z, sk_zc)}[axis]
-        return (sketch, sk_c, *got), (og_own, og_c, og[axis], og[axis + "c"])
-
-    def begin(terms, first, axis):
-        send, keep = project(*terms, (first, first, 0, 0), 4)
+    y_side = (sketch, sk_c, sk_y, sk_yc), (og_own, og_c, og_y, og_yc)
+    z_side = (sketch, sk_c, sk_z, sk_zc), (og_own, og_c, og_z, og_zc)
+
+    def begin(terms, offsets, axis):
+        send, keep = project(*terms, offsets, 4)
         return exchange(packed(send, 8.0), axis), keep
 
     def middle(state, axis):
         got, keep = state
-        ahead = exchange(packed(keep[0] + unpacked(got[0], 8.0), 4.0), axis)
-        return ahead, keep[1] + unpacked(got[1], 8.0)
+        ahead = packed(keep[0] + unpacked(got[0], 8.0), 4.0)
+        return exchange(ahead, axis), keep[1] + unpacked(got[1], 8.0)
 
     def finish(state):
         got, keep = state
         return keep + unpacked(got, 4.0)
 
-    far0_state = begin(side("y", far_og), 0, X)
-    far1_state = begin(side("z", far_og), 8, X)
-    near0_state = begin(side("y", near_og), 4, Z0)
-    near1_state = begin(side("z", near_og), 12, Y)
+    far0_state = begin(y_side, (0, 0, 0, 0), X)
+    far1_state = begin(z_side, (8, 8, 0, 0), Y)
+    near0_state = begin(y_side, (4, 4, 4, 4), Z0)
+    near1_state = begin(z_side, (12, 12, 4, 4), Y)
     far0_state = middle(far0_state, Z0)
-    far1_state = middle(far1_state, Y)
+    far1_state = middle(far1_state, X)
     last0 = exchange(packed(finish(far0_state), 2.0), Z1)
     last1 = exchange(packed(finish(far1_state), 2.0), Z1)
     near0_state = middle(near0_state, X)

time: 124 us -> 123 us (level)
  starting transfers between devices: 34.6 us -> 28.7 us
  waiting for transfers between devices: 53.6 us -> 58.9 us
    ppermute x33 -> x29, starting transfers between devices: 34.6 us -> 28.7 us  [exchange(): return lax.ppermute(value, AXES, [(i, i ^ mask) for i in range(size)])]
    ppermute x33 -> x29, waiting for transfers between devices: 53.6 us -> 58.9 us  [exchange(): return lax.ppermute(value, AXES, [(i, i ^ mask) for i in range(size)])]
    pallas_call x2 -> x1, Pallas kernels: 7.01 us -> 5.92 us  [prefetch(): pl.pallas_call(prefetch_kernel, in_specs=[pl.BlockSpec(memory_space=pl.AN...]
    pallas_call x2 -> x3, Pallas kernels: 3.99 us -> 4.92 us  [pack(): pl.pallas_call(functools.partial(pack_kernel, groups, width, part), in_sp...]
  transfers between devices with their start and end apart: 33 -> 29, of which waited for: 14 -> 9; matrix products, arithmetic and copies ran while one was open for 1% -> 1% of each run, Pallas kernels for 20% -> 20%
where the time goes in v2:
time: 123 us
  waiting for transfers between devices  58.9 us (48%)
  Pallas kernels  31.4 us (26%)
  starting transfers between devices  28.7 us (23%)
  between operations  2.37 us (2%)
    ppermute x29, waiting for transfers between devices, exchange(): return lax.ppermute(value, AXES, [(i, i ^ mask) for i in range(size)])  58.9 us
    ppermute x29, starting transfers between devices, exchange(): return lax.ppermute(value, AXES, [(i, i ^ mask) for i in range(size)])  28.7 us
    pallas_call x4, Pallas kernels, update(): pl.pallas_call(functools.partial(update_kernel, where, keep, slabs, min(s...  11.4 us
    pallas_call x2, Pallas kernels, sketch_parts(): pl.pallas_call(functools.partial(sketch_kernel, first, din_local), in_spe...  6.2 us
    pallas_call x1, Pallas kernels, prefetch(): pl.pallas_call(prefetch_kernel, in_specs=[pl.BlockSpec(memory_space=pl.AN...  5.92 us
    pallas_call x3, Pallas kernels, pack(): pl.pallas_call(functools.partial(pack_kernel, groups, width, part), in_sp...  4.92 us
    pallas_call x4, Pallas kernels, project(): pl.pallas_call(functools.partial(project_kernel, n), grid=(1,), in_specs=...  2.92 us
  transfers between devices with their start and end apart: 29, of which 9 were waited for; matrix products, arithmetic and copies ran while one was open for 1% of the time, Pallas kernels for 20%

profile of v2, /device:TPU:0, one launch (start us, length us, event | category | flops | bytes accessed | tf_op | source)
XLA Modules:
  0.0 122.6 jit_solution(16760793639470797817)
XLA Ops:
  1.9 3.7 %sketch.2 = (bf16[2048,512]{1,0:T(8,128)(2,1)S(1)}, f32[256,512]{1,0:T(8,128)S(1)}, f32[256,512]{1,0:T(8,128)S(1)}) custom-call(s32[1,1]{1,0:T(1,128)} %bitcast.40.refs_0_, s32[1,1]{1,0:T(1,128)} %bitcast.41.refs_1_, bf16[1024,2048]{1,0:T(8,128)(2,1)} %refs_0_.2), custom_call_target="tpu_custom_call" | custom-call | flops 1073741824 | bytes 6291456 | tf_op jit(solution)/shard_map/sketch/pallas_call | solution.py:224
  5.6 0.6 collective-permute-start.1
  6.2 2.5 %sketch.3 = (f32[256,512]{1,0:T(8,128)S(1)}, f32[256,512]{1,0:T(8,128)S(1)}) custom-call(bf16[1024,2048]{1,0:T(8,128)(2,1)} %refs_0_.2, bf16[2048,512]{1,0:T(8,128)(2,1)S(1)} %get-tuple-element.34.refs_1_.refs_2_), custom_call_target="tpu_custom_call" | custom-call | flops 1073741824 | bytes 6291456 | tf_op jit(solution)/shard_map/sketch/pallas_call | solution.py:224
  8.9 3.0 %collective-permute-start.2 = (f32[256,512]{1,0:T(8,128)S(1)}, f32[256,512]{1,0:T(8,128)S(1)}, u32[]{:S(2)}, u32[]{:S(2)}) collective-permute-start(f32[256,512]{1,0:T(8,128)S(1)} %add.74), channel_id=1, source_target_pairs={{0,2},{1,3},{2,0},{3,1},{4,6},{5,7},{6,4},{7,5},{8,10},{9,11},{10,... | collective-permute-start | bytes 1572872 | tf_op jit(solution)/shard_map/ppermute | solution.py:421
  11.9 2.0 %pack.3 = (bf16[16,256,128]{2,1,0:T(8,128)(2,1)S(1)}, bf16[16,256,128]{2,1,0:T(8,128)(2,1)S(1)}) custom-call(bf16[256,8192]{1,0:T(8,128)(2,1)} %og_ref.5), custom_call_target="tpu_custom_call" | custom-call | bytes 4194304 | tf_op jit(solution)/shard_map/pack/pallas_call | solution.py:127
  14.0 1.5 %pack.5 = (bf16[8,256,128]{2,1,0:T(8,128)(2,1)S(1)}, bf16[8,256,128]{2,1,0:T(8,128)(2,1)S(1)}) custom-call(bf16[256,8192]{1,0:T(8,128)(2,1)} %og_ref.5), custom_call_target="tpu_custom_call" | custom-call | bytes 2097152 | tf_op jit(solution)/shard_map/pack/pallas_call | solution.py:127
  15.5 1.7 %collective-permute-start.17 = (bf16[8,256,128]{2,1,0:T(8,128)(2,1)S(1)}, bf16[8,256,128]{2,1,0:T(8,128)(2,1)S(1)}, u32[]{:S(2)}, u32[]{:S(2)}) collective-permute-start(bf16[8,256,128]{2,1,0:T(8,128)(2,1)S(1)} %get-tuple-element.48), channel_id=1, source_target_pairs={{0,5},{1,4},{2,7},{3,6},{4,1},{5,0},{6,3},{7,2},{8,13},{9,12},{10,... | collective-permute-start | bytes 1572872 | tf_op jit(solution)/shard_map/ppermute | solution.py:421
  17.1 1.5 %pack.4 = (bf16[8,256,128]{2,1,0:T(8,128)(2,1)S(1)}, bf16[8,256,128]{2,1,0:T(8,128)(2,1)S(1)}) custom-call(bf16[256,8192]{1,0:T(8,128)(2,1)} %og_ref.5), custom_call_target="tpu_custom_call" | custom-call | bytes 2097152 | tf_op jit(solution)/shard_map/pack/pallas_call | solution.py:127
  18.6 0.6 collective-permute-start.16
  19.2 4.8 %collective-permute-done.2 = f32[256,512]{1,0:T(8,128)S(1)} collective-permute-done((f32[256,512]{1,0:T(8,128)S(1)}, f32[256,512]{1,0:T(8,128)S(1)}, u32[]{:S(2)}, u32[]{:S(2)}) %collective-permute-start.2) | collective-permute-done | bytes 524320 | tf_op jit(solution)/shard_map/ppermute | solution.py:421
  24.0 0.2 multiply_convert_fusion.4.refs_0_
  24.2 1.8 %collective-permute-start.14 = (bf16[256,512]{1,0:T(8,128)(2,1)S(1)}, bf16[256,512]{1,0:T(8,128)(2,1)S(1)}, u32[]{:S(2)}, u32[]{:S(2)}) collective-permute-start(bf16[256,512]{1,0:T(8,128)(2,1)S(1)} %multiply_convert_fusion.4.refs_0_), channel_id=1, source_target_pairs={{0,4},{1,5},{2,6},{3,7},{4,0},{5,1},{6,2},{7,3},{8,12},{9,13},{10,... | collective-permute-start | bytes 786440 | tf_op jit(solution)/shard_map/ppermute | solution.py:421
  26.0 1.6 %collective-permute-start.4 = (bf16[256,512]{1,0:T(8,128)(2,1)S(1)}, bf16[256,512]{1,0:T(8,128)(2,1)S(1)}, u32[]{:S(2)}, u32[]{:S(2)}) collective-permute-start(bf16[256,512]{1,0:T(8,128)(2,1)S(1)} %multiply_convert_fusion.4.refs_0_), channel_id=1, source_target_pairs={{0,8},{1,9},{2,10},{3,11},{4,12},{5,13},{6,14},{7,15},{8,0},{9,1},... | collective-permute-start | bytes 786440 | tf_op jit(solution)/shard_map/ppermute | solution.py:421
  27.6 1.8 %collective-permute-done.17.refs_7_ = bf16[8,256,128]{2,1,0:T(8,128)(2,1)S(1)} collective-permute-done((bf16[8,256,128]{2,1,0:T(8,128)(2,1)S(1)}, bf16[8,256,128]{2,1,0:T(8,128)(2,1)S(1)}, u32[]{:S(2)}, u32[]{:S(2)}) %collective-permute-start.17) | collective-permute-done | bytes 524320 | tf_op jit(solution)/shard_map/ppermute | solution.py:421
  29.4 1.1 collective-permute-start.3
  30.5 16.1 %collective-permute-done.14.refs_2_ = bf16[256,512]{1,0:T(8,128)(2,1)S(1)} collective-permute-done((bf16[256,512]{1,0:T(8,128)(2,1)S(1)}, bf16[256,512]{1,0:T(8,128)(2,1)S(1)}, u32[]{:S(2)}, u32[]{:S(2)}) %collective-permute-start.14) | collective-permute-done | bytes 262176 | tf_op jit(solution)/shard_map/ppermute | solution.py:421
  46.6 1.7 %collective-permute-start.8 = (bf16[8,256,128]{2,1,0:T(8,128)(2,1)S(1)}, bf16[8,256,128]{2,1,0:T(8,128)(2,1)S(1)}, u32[]{:S(2)}, u32[]{:S(2)}) collective-permute-start(bf16[8,256,128]{2,1,0:T(8,128)(2,1)S(1)} %get-tuple-element.42), channel_id=1, source_target_pairs={{0,9},{1,8},{2,11},{3,10},{4,13},{5,12},{6,15},{7,14},{8,1},{9,0},... | collective-permute-start | bytes 1572872 | tf_op jit(solution)/shard_map/ppermute | solution.py:421
  48.3 0.4 collective-permute-start.7
  48.8 0.7 project.7
  49.6 0.5 collective-permute-start.20
  50.0 0.7 project.6
  50.8 1.8 %collective-permute-start.18 = (f16[2,128,512]{2,1,0:T(8,128)(2,1)S(1)}, f16[2,128,512]{2,1,0:T(8,128)(2,1)S(1)}, u32[]{:S(2)}, u32[]{:S(2)}) collective-permute-start(f16[2,128,512]{2,1,0:T(8,128)(2,1)S(1)} %multiply_convert_fusion.1), channel_id=1, source_target_pairs={{0,8},{1,9},{2,10},{3,11},{4,12},{5,13},{6,14},{7,15},{8,0},{9,1},... | collective-permute-start | bytes 786440 | tf_op jit(solution)/shard_map/ppermute | solution.py:421
  52.6 8.0 %collective-permute-done.8.refs_7_ = bf16[8,256,128]{2,1,0:T(8,128)(2,1)S(1)} collective-permute-done((bf16[8,256,128]{2,1,0:T(8,128)(2,1)S(1)}, bf16[8,256,128]{2,1,0:T(8,128)(2,1)S(1)}, u32[]{:S(2)}, u32[]{:S(2)}) %collective-permute-start.8) | collective-permute-done | bytes 524320 | tf_op jit(solution)/shard_map/ppermute | solution.py:421
  60.6 12.1 %collective-permute-done.7.refs_6_ = bf16[8,256,128]{2,1,0:T(8,128)(2,1)S(1)} collective-permute-done((bf16[8,256,128]{2,1,0:T(8,128)(2,1)S(1)}, bf16[8,256,128]{2,1,0:T(8,128)(2,1)S(1)}, u32[]{:S(2)}, u32[]{:S(2)}) %collective-permute-start.7) | collective-permute-done | bytes 524320 | tf_op jit(solution)/shard_map/ppermute | solution.py:421
  72.8 0.7 project.4
  73.6 0.7 project.5
  74.3 1.6 %collective-permute-start.11 = (f16[2,128,512]{2,1,0:T(8,128)(2,1)S(1)}, f16[2,128,512]{2,1,0:T(8,128)(2,1)S(1)}, u32[]{:S(2)}, u32[]{:S(2)}) collective-permute-start(f16[2,128,512]{2,1,0:T(8,128)(2,1)S(1)} %multiply_convert_fusion.2), channel_id=1, source_target_pairs={{0,4},{1,5},{2,6},{3,7},{4,0},{5,1},{6,2},{7,3},{8,12},{9,13},{10,... | collective-permute-start | bytes 786440 | tf_op jit(solution)/shard_map/ppermute | solution.py:421
  75.9 0.5 collective-permute-start.9
  76.5 1.6 %collective-permute-start.21 = (f16[128,512]{1,0:T(8,128)(2,1)S(1)}, f16[128,512]{1,0:T(8,128)(2,1)S(1)}, u32[]{:S(2)}, u32[]{:S(2)}) collective-permute-start(f16[128,512]{1,0:T(8,128)(2,1)S(1)} %fusion.13), channel_id=1, source_target_pairs={{0,8},{1,9},{2,10},{3,11},{4,12},{5,13},{6,14},{7,15},{8,0},{9,1},... | collective-permute-start | bytes 393224 | tf_op jit(solution)/shard_map/ppermute | solution.py:421
  78.2 0.6 collective-permute-start.19
  78.8 4.8 %collective-permute-done.11 = f16[2,128,512]{2,1,0:T(8,128)(2,1)S(1)} collective-permute-done((f16[2,128,512]{2,1,0:T(8,128)(2,1)S(1)}, f16[2,128,512]{2,1,0:T(8,128)(2,1)S(1)}, u32[]{:S(2)}, u32[]{:S(2)}) %collective-permute-start.11) | collective-permute-done | bytes 262176 | tf_op jit(solution)/shard_map/ppermute | solution.py:421
  83.7 0.5 collective-permute-start.12
  84.1 2.9 %collective-permute-done.9 = f16[2,128,512]{2,1,0:T(8,128)(2,1)S(1)} collective-permute-done((f16[2,128,512]{2,1,0:T(8,128)(2,1)S(1)}, f16[2,128,512]{2,1,0:T(8,128)(2,1)S(1)}, u32[]{:S(2)}, u32[]{:S(2)}) %collective-permute-start.9) | collective-permute-done | bytes 262176 | tf_op jit(solution)/shard_map/ppermute | solution.py:421
  87.0 0.6 collective-permute-start.10
  87.7 2.6 %collective-permute-start.22 = (f16[128,512]{1,0:T(8,128)(2,1)S(1)}, f16[128,512]{1,0:T(8,128)(2,1)S(1)}, u32[]{:S(2)}, u32[]{:S(2)}) collective-permute-start(f16[128,512]{1,0:T(8,128)(2,1)S(1)} %fusion.1), channel_id=1, source_target_pairs={{0,16},{1,17},{2,18},{3,19},{4,20},{5,21},{6,22},{7,23},{8,24},{9,... | collective-permute-start | bytes 393224 | tf_op jit(solution)/shard_map/ppermute | solution.py:421
  90.5 2.1 %collective-permute-start.13 = (f16[128,512]{1,0:T(8,128)(2,1)S(1)}, f16[128,512]{1,0:T(8,128)(2,1)S(1)}, u32[]{:S(2)}, u32[]{:S(2)}) collective-permute-start(f16[128,512]{1,0:T(8,128)(2,1)S(1)} %fusion.6), channel_id=1, source_target_pairs={{0,16},{1,17},{2,18},{3,19},{4,20},{5,21},{6,22},{7,23},{8,24},{9,... | collective-permute-start | bytes 393224 | tf_op jit(solution)/shard_map/ppermute | solution.py:421
  92.5 6.3 %collective-permute-done.22 = f16[128,512]{1,0:T(8,128)(2,1)S(1)} collective-permute-done((f16[128,512]{1,0:T(8,128)(2,1)S(1)}, f16[128,512]{1,0:T(8,128)(2,1)S(1)}, u32[]{:S(2)}, u32[]{:S(2)}) %collective-permute-start.22) | collective-permute-done | bytes 131104 | tf_op jit(solution)/shard_map/ppermute | solution.py:421
  99.0 1.4 %collective-permute-start.26 = (f16[128,512]{1,0:T(8,128)(2,1)S(1)}, f16[128,512]{1,0:T(8,128)(2,1)S(1)}, u32[]{:S(2)}, u32[]{:S(2)}) collective-permute-start(f16[128,512]{1,0:T(8,128)(2,1)S(1)} %get-tuple-element.67), channel_id=1, source_target_pairs={{0,2},{1,3},{2,0},{3,1},{4,6},{5,7},{6,4},{7,5},{8,10},{9,11},{10,... | collective-permute-start | bytes 393224 | tf_op jit(solution)/shard_map/ppermute | solution.py:421
  100.4 0.1 fusion.14
  100.5 1.3 %collective-permute-start.23 = (f16[128,512]{1,0:T(8,128)(2,1)S(1)}, f16[128,512]{1,0:T(8,128)(2,1)S(1)}, u32[]{:S(2)}, u32[]{:S(2)}) collective-permute-start(f16[128,512]{1,0:T(8,128)(2,1)S(1)} %get-tuple-element.65), channel_id=1, source_target_pairs={{0,2},{1,3},{2,0},{3,1},{4,6},{5,7},{6,4},{7,5},{8,10},{9,11},{10,... | collective-permute-start | bytes 393224 | tf_op jit(solution)/shard_map/ppermute | solution.py:421
  101.8 0.5 collective-permute-start.25
  102.3 1.9 %collective-permute-done.26 = f16[128,512]{1,0:T(8,128)(2,1)S(1)} collective-permute-done((f16[128,512]{1,0:T(8,128)(2,1)S(1)}, f16[128,512]{1,0:T(8,128)(2,1)S(1)}, u32[]{:S(2)}, u32[]{:S(2)}) %collective-permute-start.26) | collective-permute-done | bytes 131104 | tf_op jit(solution)/shard_map/ppermute | solution.py:421
  104.2 5.9 %prefetch.1 = (f32[1024,2048]{1,0:T(8,128)S(1)}, f32[1024,2048]{1,0:T(8,128)S(1)}) custom-call(f32[1024,2048]{1,0:T(8,128)} %refs_0_.3, f32[1024,2048]{1,0:T(8,128)} %refs_1_.1), custom_call_target="tpu_custom_call" | custom-call | bytes 16777216 | tf_op jit(solution)/shard_map/prefetch/pallas_call | solution.py:308
  110.2 0.6 collective-permute-start.24
  110.9 2.9 %update.4 = (f32[1024,2048]{1,0:T(8,128)}, f32[1024,2048]{1,0:T(8,128)}, f32[256,512]{1,0:T(8,128)}) custom-call(f32[128,512]{1,0:T(8,128)S(1)} %get-tuple-element.68.refs_0_, f32[128,512]{1,0:T(8,128)S(1)} %convert_element_type.127.refs_1_, bf16[2048,512]{1,0:T(8,128)(2,1)S(1)} %get-tuple-element.34.refs_1_.refs_2_, ...), custom_call_target="tpu_custom_call" | custom-call | flops 1073741824 | bytes 4194304 | tf_op jit(solution)/shard_map/update/pallas_call | solution.py:390
  113.8 2.8 %update.5 = (f32[1024,2048]{1,0:T(8,128)}, f32[1024,2048]{1,0:T(8,128)}, f32[256,512]{1,0:T(8,128)}) custom-call(f32[128,512]{1,0:T(8,128)S(1)} %convert_element_type.125.refs_0_, f32[128,512]{1,0:T(8,128)S(1)} %convert_element_type.126.refs_1_, ...), custom_call_target="tpu_custom_call", output_to_operand_aliasing={{0}: (5, {}), {1}: (6, {}), {2}: (7, {})} | custom-call | flops 1073741824 | bytes 4194304 | tf_op jit(solution)/shard_map/update/pallas_call | solution.py:390
  116.6 2.9 %update.6 = (f32[1024,2048]{1,0:T(8,128)}, f32[1024,2048]{1,0:T(8,128)}, f32[256,512]{1,0:T(8,128)}) custom-call(f32[128,512]{1,0:T(8,128)S(1)} %get-tuple-element.66.refs_0_, f32[128,512]{1,0:T(8,128)S(1)} %convert_element_type.124.refs_1_, ...), custom_call_target="tpu_custom_call", output_to_operand_aliasing={{0}: (5, {}), {1}: (6, {}), {2}: (7, {})} | custom-call | flops 1073741824 | bytes 4194304 | tf_op jit(solution)/shard_map/update/pallas_call | solution.py:390
  119.6 2.8 %update.7 = (f32[1024,2048]{1,0:T(8,128)}, f32[1024,2048]{1,0:T(8,128)}, f32[256,512]{1,0:T(8,128)}) custom-call(f32[128,512]{1,0:T(8,128)S(1)} %convert_element_type.122.refs_0_, f32[128,512]{1,0:T(8,128)S(1)} %convert_element_type.123.refs_1_, ...), custom_call_target="tpu_custom_call", output_to_operand_aliasing={{0}: (5, {}), {1}: (6, {}), {2}: (7, {})} | custom-call | flops 1073741824 | bytes 4194304 | tf_op jit(solution)/shard_map/update/pallas_call | solution.py:390
  (46 shorter events, 1.1 us)
Async XLA Ops:
  5.6 3.2 %collective-permute-start.1 = (f32[256,512]{1,0:T(8,128)S(1)}, f32[256,512]{1,0:T(8,128)S(1)}, u32[]{:S(2)}, u32[]{:S(2)}) collective-permute-start(f32[256,512]{1,0:T(8,128)S(1)} %get-tuple-element.38), channel_id=1, source_target_pairs={{0,1},{1,0},{2,3},{3,2},{4,5},{5,4},{6,7},{7,6},{8,9},{9,8},{10,11... | collective-permute-start | bytes 1572872 | tf_op jit(solution)/shard_map/ppermute | solution.py:421
  8.7 10.5 %collective-permute-start = (f32[256,512]{1,0:T(8,128)S(1)}, f32[256,512]{1,0:T(8,128)S(1)}, u32[]{:S(2)}, u32[]{:S(2)}) collective-permute-start(f32[256,512]{1,0:T(8,128)S(1)} %get-tuple-element.36), channel_id=1, source_target_pairs={{0,1},{1,0},{2,3},{3,2},{4,5},{5,4},{6,7},{7,6},{8,9},{9,8},{10,11... | collective-permute-start | bytes 1572872 | tf_op jit(solution)/shard_map/ppermute | solution.py:421
  8.9 15.1 %collective-permute-start.2 = (f32[256,512]{1,0:T(8,128)S(1)}, f32[256,512]{1,0:T(8,128)S(1)}, u32[]{:S(2)}, u32[]{:S(2)}) collective-permute-start(f32[256,512]{1,0:T(8,128)S(1)} %add.74), channel_id=1, source_target_pairs={{0,2},{1,3},{2,0},{3,1},{4,6},{5,7},{6,4},{7,5},{8,10},{9,11},{10,... | collective-permute-start | bytes 1572872 | tf_op jit(solution)/shard_map/ppermute | solution.py:421
  13.9 34.4 %collective-permute-start.6 = (bf16[16,256,128]{2,1,0:T(8,128)(2,1)S(1)}, bf16[16,256,128]{2,1,0:T(8,128)(2,1)S(1)}, u32[]{:S(2)}, u32[]{:S(2)}) collective-permute-start(bf16[16,256,128]{2,1,0:T(8,128)(2,1)S(1)} %get-tuple-element.40), channel_id=1, source_target_pairs={{0,1},{1,0},{2,3},{3,2},{4,5},{5,4},{6,7},{7,6},{8,9},{9,8},{10,11... | collective-permute-start | bytes 3145736 | tf_op jit(solution)/shard_map/ppermute | solution.py:421
  15.5 14.0 %collective-permute-start.17 = (bf16[8,256,128]{2,1,0:T(8,128)(2,1)S(1)}, bf16[8,256,128]{2,1,0:T(8,128)(2,1)S(1)}, u32[]{:S(2)}, u32[]{:S(2)}) collective-permute-start(bf16[8,256,128]{2,1,0:T(8,128)(2,1)S(1)} %get-tuple-element.48), channel_id=1, source_target_pairs={{0,5},{1,4},{2,7},{3,6},{4,1},{5,0},{6,3},{7,2},{8,13},{9,12},{10,... | collective-permute-start | bytes 1572872 | tf_op jit(solution)/shard_map/ppermute | solution.py:421
  18.6 28.0 %collective-permute-start.16 = (bf16[8,256,128]{2,1,0:T(8,128)(2,1)S(1)}, bf16[8,256,128]{2,1,0:T(8,128)(2,1)S(1)}, u32[]{:S(2)}, u32[]{:S(2)}) collective-permute-start(bf16[8,256,128]{2,1,0:T(8,128)(2,1)S(1)} %get-tuple-element.47), channel_id=1, source_target_pairs={{0,4},{1,5},{2,6},{3,7},{4,0},{5,1},{6,2},{7,3},{8,12},{9,13},{10,... | collective-permute-start | bytes 1572872 | tf_op jit(solution)/shard_map/ppermute | solution.py:421
  24.2 22.4 %collective-permute-start.14 = (bf16[256,512]{1,0:T(8,128)(2,1)S(1)}, bf16[256,512]{1,0:T(8,128)(2,1)S(1)}, u32[]{:S(2)}, u32[]{:S(2)}) collective-permute-start(bf16[256,512]{1,0:T(8,128)(2,1)S(1)} %multiply_convert_fusion.4.refs_0_), channel_id=1, source_target_pairs={{0,4},{1,5},{2,6},{3,7},{4,0},{5,1},{6,2},{7,3},{8,12},{9,13},{10,... | collective-permute-start | bytes 786440 | tf_op jit(solution)/shard_map/ppermute | solution.py:421
  26.0 22.7 %collective-permute-start.4 = (bf16[256,512]{1,0:T(8,128)(2,1)S(1)}, bf16[256,512]{1,0:T(8,128)(2,1)S(1)}, u32[]{:S(2)}, u32[]{:S(2)}) collective-permute-start(bf16[256,512]{1,0:T(8,128)(2,1)S(1)} %multiply_convert_fusion.4.refs_0_), channel_id=1, source_target_pairs={{0,8},{1,9},{2,10},{3,11},{4,12},{5,13},{6,14},{7,15},{8,0},{9,1},... | collective-permute-start | bytes 786440 | tf_op jit(solution)/shard_map/ppermute | solution.py:421
  29.4 19.3 %collective-permute-start.3 = (bf16[256,512]{1,0:T(8,128)(2,1)S(1)}, bf16[256,512]{1,0:T(8,128)(2,1)S(1)}, u32[]{:S(2)}, u32[]{:S(2)}) collective-permute-start(bf16[256,512]{1,0:T(8,128)(2,1)S(1)} %multiply_convert_fusion.4.refs_0_), channel_id=1, source_target_pairs={{0,1},{1,0},{2,3},{3,2},{4,5},{5,4},{6,7},{7,6},{8,9},{9,8},{10,11... | collective-permute-start | bytes 786440 | tf_op jit(solution)/shard_map/ppermute | solution.py:421
  46.6 2.2 %collective-permute-start.15 = (bf16[256,512]{1,0:T(8,128)(2,1)S(1)}, bf16[256,512]{1,0:T(8,128)(2,1)S(1)}, u32[]{:S(2)}, u32[]{:S(2)}) collective-permute-start(bf16[256,512]{1,0:T(8,128)(2,1)S(1)} %collective-permute-done.14.refs_2_), channel_id=1, source_target_pairs={{0,1},{1,0},{2,3},{3,2},{4,5},{5,4},{6,7},{7,6},{8,9},{9,8},{10,11... | collective-permute-start | bytes 786440 | tf_op jit(solution)/shard_map/ppermute | solution.py:421
  46.6 14.0 %collective-permute-start.8 = (bf16[8,256,128]{2,1,0:T(8,128)(2,1)S(1)}, bf16[8,256,128]{2,1,0:T(8,128)(2,1)S(1)}, u32[]{:S(2)}, u32[]{:S(2)}) collective-permute-start(bf16[8,256,128]{2,1,0:T(8,128)(2,1)S(1)} %get-tuple-element.42), channel_id=1, source_target_pairs={{0,9},{1,8},{2,11},{3,10},{4,13},{5,12},{6,15},{7,14},{8,1},{9,0},... | collective-permute-start | bytes 1572872 | tf_op jit(solution)/shard_map/ppermute | solution.py:421
  48.3 24.5 %collective-permute-start.7 = (bf16[8,256,128]{2,1,0:T(8,128)(2,1)S(1)}, bf16[8,256,128]{2,1,0:T(8,128)(2,1)S(1)}, u32[]{:S(2)}, u32[]{:S(2)}) collective-permute-start(bf16[8,256,128]{2,1,0:T(8,128)(2,1)S(1)} %get-tuple-element.41), channel_id=1, source_target_pairs={{0,8},{1,9},{2,10},{3,11},{4,12},{5,13},{6,14},{7,15},{8,0},{9,1},... | collective-permute-start | bytes 1572872 | tf_op jit(solution)/shard_map/ppermute | solution.py:421
  48.8 24.0 %collective-permute-start.5 = (bf16[256,512]{1,0:T(8,128)(2,1)S(1)}, bf16[256,512]{1,0:T(8,128)(2,1)S(1)}, u32[]{:S(2)}, u32[]{:S(2)}) collective-permute-start(bf16[256,512]{1,0:T(8,128)(2,1)S(1)} %collective-permute-done.4.refs_2_), channel_id=1, source_target_pairs={{0,1},{1,0},{2,3},{3,2},{4,5},{5,4},{6,7},{7,6},{8,9},{9,8},{10,11... | collective-permute-start | bytes 786440 | tf_op jit(solution)/shard_map/ppermute | solution.py:421
  49.6 49.3 %copy-start = (f32[256,512]{1,0:T(8,128)S(1)}, f32[256,512]{1,0:T(8,128)}, u32[]{:S(2)}) copy-start(f32[256,512]{1,0:T(8,128)} %param.11) | copy-start | bytes 1572868
  49.6 26.9 %collective-permute-start.20 = (f16[2,128,512]{2,1,0:T(8,128)(2,1)S(1)}, f16[2,128,512]{2,1,0:T(8,128)(2,1)S(1)}, u32[]{:S(2)}, u32[]{:S(2)}) collective-permute-start(f16[2,128,512]{2,1,0:T(8,128)(2,1)S(1)} %multiply_convert_fusion), channel_id=1, source_target_pairs={{0,2},{1,3},{2,0},{3,1},{4,6},{5,7},{6,4},{7,5},{8,10},{9,11},{10,... | collective-permute-start | bytes 786440 | tf_op jit(solution)/shard_map/ppermute | solution.py:421
  50.8 27.3 %collective-permute-start.18 = (f16[2,128,512]{2,1,0:T(8,128)(2,1)S(1)}, f16[2,128,512]{2,1,0:T(8,128)(2,1)S(1)}, u32[]{:S(2)}, u32[]{:S(2)}) collective-permute-start(f16[2,128,512]{2,1,0:T(8,128)(2,1)S(1)} %multiply_convert_fusion.1), channel_id=1, source_target_pairs={{0,8},{1,9},{2,10},{3,11},{4,12},{5,13},{6,14},{7,15},{8,0},{9,1},... | collective-permute-start | bytes 786440 | tf_op jit(solution)/shard_map/ppermute | solution.py:421
  74.3 9.2 %collective-permute-start.11 = (f16[2,128,512]{2,1,0:T(8,128)(2,1)S(1)}, f16[2,128,512]{2,1,0:T(8,128)(2,1)S(1)}, u32[]{:S(2)}, u32[]{:S(2)}) collective-permute-start(f16[2,128,512]{2,1,0:T(8,128)(2,1)S(1)} %multiply_convert_fusion.2), channel_id=1, source_target_pairs={{0,4},{1,5},{2,6},{3,7},{4,0},{5,1},{6,2},{7,3},{8,12},{9,13},{10,... | collective-permute-start | bytes 786440 | tf_op jit(solution)/shard_map/ppermute | solution.py:421
  75.9 11.0 %collective-permute-start.9 = (f16[2,128,512]{2,1,0:T(8,128)(2,1)S(1)}, f16[2,128,512]{2,1,0:T(8,128)(2,1)S(1)}, u32[]{:S(2)}, u32[]{:S(2)}) collective-permute-start(f16[2,128,512]{2,1,0:T(8,128)(2,1)S(1)} %multiply_convert_fusion.3), channel_id=1, source_target_pairs={{0,4},{1,5},{2,6},{3,7},{4,0},{5,1},{6,2},{7,3},{8,12},{9,13},{10,... | collective-permute-start | bytes 786440 | tf_op jit(solution)/shard_map/ppermute | solution.py:421
  76.5 11.2 %collective-permute-start.21 = (f16[128,512]{1,0:T(8,128)(2,1)S(1)}, f16[128,512]{1,0:T(8,128)(2,1)S(1)}, u32[]{:S(2)}, u32[]{:S(2)}) collective-permute-start(f16[128,512]{1,0:T(8,128)(2,1)S(1)} %fusion.13), channel_id=1, source_target_pairs={{0,8},{1,9},{2,10},{3,11},{4,12},{5,13},{6,14},{7,15},{8,0},{9,1},... | collective-permute-start | bytes 393224 | tf_op jit(solution)/shard_map/ppermute | solution.py:421
  78.2 14.3 %collective-permute-start.19 = (f16[128,512]{1,0:T(8,128)(2,1)S(1)}, f16[128,512]{1,0:T(8,128)(2,1)S(1)}, u32[]{:S(2)}, u32[]{:S(2)}) collective-permute-start(f16[128,512]{1,0:T(8,128)(2,1)S(1)} %fusion.12), channel_id=1, source_target_pairs={{0,2},{1,3},{2,0},{3,1},{4,6},{5,7},{6,4},{7,5},{8,10},{9,11},{10,... | collective-permute-start | bytes 393224 | tf_op jit(solution)/shard_map/ppermute | solution.py:421
  83.7 6.7 %collective-permute-start.12 = (f16[128,512]{1,0:T(8,128)(2,1)S(1)}, f16[128,512]{1,0:T(8,128)(2,1)S(1)}, u32[]{:S(2)}, u32[]{:S(2)}) collective-permute-start(f16[128,512]{1,0:T(8,128)(2,1)S(1)} %fusion.11), channel_id=1, source_target_pairs={{0,2},{1,3},{2,0},{3,1},{4,6},{5,7},{6,4},{7,5},{8,10},{9,11},{10,... | collective-permute-start | bytes 393224 | tf_op jit(solution)/shard_map/ppermute | solution.py:421
  87.0 13.4 %collective-permute-start.10 = (f16[128,512]{1,0:T(8,128)(2,1)S(1)}, f16[128,512]{1,0:T(8,128)(2,1)S(1)}, u32[]{:S(2)}, u32[]{:S(2)}) collective-permute-start(f16[128,512]{1,0:T(8,128)(2,1)S(1)} %fusion.10), channel_id=1, source_target_pairs={{0,2},{1,3},{2,0},{3,1},{4,6},{5,7},{6,4},{7,5},{8,10},{9,11},{10,... | collective-permute-start | bytes 393224 | tf_op jit(solution)/shard_map/ppermute | solution.py:421
  87.7 11.2 %collective-permute-start.22 = (f16[128,512]{1,0:T(8,128)(2,1)S(1)}, f16[128,512]{1,0:T(8,128)(2,1)S(1)}, u32[]{:S(2)}, u32[]{:S(2)}) collective-permute-start(f16[128,512]{1,0:T(8,128)(2,1)S(1)} %fusion.1), channel_id=1, source_target_pairs={{0,16},{1,17},{2,18},{3,19},{4,20},{5,21},{6,22},{7,23},{8,24},{9,... | collective-permute-start | bytes 393224 | tf_op jit(solution)/shard_map/ppermute | solution.py:421
  90.5 9.9 %collective-permute-start.13 = (f16[128,512]{1,0:T(8,128)(2,1)S(1)}, f16[128,512]{1,0:T(8,128)(2,1)S(1)}, u32[]{:S(2)}, u32[]{:S(2)}) collective-permute-start(f16[128,512]{1,0:T(8,128)(2,1)S(1)} %fusion.6), channel_id=1, source_target_pairs={{0,16},{1,17},{2,18},{3,19},{4,20},{5,21},{6,22},{7,23},{8,24},{9,... | collective-permute-start | bytes 393224 | tf_op jit(solution)/shard_map/ppermute | solution.py:421
  99.0 5.2 %collective-permute-start.26 = (f16[128,512]{1,0:T(8,128)(2,1)S(1)}, f16[128,512]{1,0:T(8,128)(2,1)S(1)}, u32[]{:S(2)}, u32[]{:S(2)}) collective-permute-start(f16[128,512]{1,0:T(8,128)(2,1)S(1)} %get-tuple-element.67), channel_id=1, source_target_pairs={{0,2},{1,3},{2,0},{3,1},{4,6},{5,7},{6,4},{7,5},{8,10},{9,11},{10,... | collective-permute-start | bytes 393224 | tf_op jit(solution)/shard_map/ppermute | solution.py:421
  100.5 9.6 %collective-permute-start.23 = (f16[128,512]{1,0:T(8,128)(2,1)S(1)}, f16[128,512]{1,0:T(8,128)(2,1)S(1)}, u32[]{:S(2)}, u32[]{:S(2)}) collective-permute-start(f16[128,512]{1,0:T(8,128)(2,1)S(1)} %get-tuple-element.65), channel_id=1, source_target_pairs={{0,2},{1,3},{2,0},{3,1},{4,6},{5,7},{6,4},{7,5},{8,10},{9,11},{10,... | collective-permute-start | bytes 393224 | tf_op jit(solution)/shard_map/ppermute | solution.py:421
  101.8 9.0 %collective-permute-start.28 = (f16[128,512]{1,0:T(8,128)(2,1)S(1)}, f16[128,512]{1,0:T(8,128)(2,1)S(1)}, u32[]{:S(2)}, u32[]{:S(2)}) collective-permute-start(f16[128,512]{1,0:T(8,128)(2,1)S(1)} %get-tuple-element.67), channel_id=1, source_target_pairs={{0,1},{1,0},{2,3},{3,2},{4,5},{5,4},{6,7},{7,6},{8,9},{9,8},{10,11... | collective-permute-start | bytes 393224 | tf_op jit(solution)/shard_map/ppermute | solution.py:421
  101.8 9.0 %collective-permute-start.25 = (f16[128,512]{1,0:T(8,128)(2,1)S(1)}, f16[128,512]{1,0:T(8,128)(2,1)S(1)}, u32[]{:S(2)}, u32[]{:S(2)}) collective-permute-start(f16[128,512]{1,0:T(8,128)(2,1)S(1)} %get-tuple-element.65), channel_id=1, source_target_pairs={{0,1},{1,0},{2,3},{3,2},{4,5},{5,4},{6,7},{7,6},{8,9},{9,8},{10,11... | collective-permute-start | bytes 393224 | tf_op jit(solution)/shard_map/ppermute | solution.py:421
  104.2 9.6 %collective-permute-start.27 = (f16[128,512]{1,0:T(8,128)(2,1)S(1)}, f16[128,512]{1,0:T(8,128)(2,1)S(1)}, u32[]{:S(2)}, u32[]{:S(2)}) collective-permute-start(f16[128,512]{1,0:T(8,128)(2,1)S(1)} %collective-permute-done.26), channel_id=1, source_target_pairs={{0,1},{1,0},{2,3},{3,2},{4,5},{5,4},{6,7},{7,6},{8,9},{9,8},{10,11... | collective-permute-start | bytes 393224 | tf_op jit(solution)/shard_map/ppermute | solution.py:421
  110.2 9.3 %collective-permute-start.24 = (f16[128,512]{1,0:T(8,128)(2,1)S(1)}, f16[128,512]{1,0:T(8,128)(2,1)S(1)}, u32[]{:S(2)}, u32[]{:S(2)}) collective-permute-start(f16[128,512]{1,0:T(8,128)(2,1)S(1)} %collective-permute-done.23), channel_id=1, source_target_pairs={{0,1},{1,0},{2,3},{3,2},{4,5},{5,4},{6,7},{7,6},{8,9},{9,8},{10,11... | collective-permute-start | bytes 393224 | tf_op jit(solution)/shard_map/ppermute | solution.py:421

commit v3 on v2

--- a/solution.py
+++ b/solution.py
@@ -254,12 +254,13 @@
         axis=0,
     )
     total = contract(grads, sketch)
+    away = send_ref.shape[0]
     for j in range(count):
-        out_ref = send_ref if j < count // 2 else keep_ref
-        out_ref[j % (count // 2)] = total[j * part : (j + 1) * part]
-
-
-def project(sketches, grads, offsets, count):
+        out_ref, at = (send_ref, j) if j < away else (keep_ref, j - away)
+        out_ref[at] = total[j * part : (j + 1) * part]
+
+
+def project(sketches, grads, offsets, count, away):
     rows, low_rank = sketches[0].shape
     part = grads[0].shape[2]
     n = len(sketches)
@@ -267,14 +268,14 @@
     def block_at(offset):
         return pl.BlockSpec((count, rows, part), lambda i: (offset // count, 0, 0))
 
-    out = jax.ShapeDtypeStruct((count // 2, part, low_rank), jnp.float32)
+    shapes = [(away, part, low_rank), (count - away, part, low_rank)]
     return pl.pallas_call(
         functools.partial(project_kernel, n),
         grid=(1,),
         in_specs=[pl.BlockSpec((rows, low_rank), lambda i: (0, 0))] * n
         + [block_at(offset) for offset in offsets],
-        out_specs=[pl.BlockSpec((count // 2, part, low_rank), lambda i: (0, 0, 0))] * 2,
-        out_shape=[out] * 2,
+        out_specs=[pl.BlockSpec(shape, lambda i: (0, 0, 0)) for shape in shapes],
+        out_shape=[jax.ShapeDtypeStruct(shape, jnp.float32) for shape in shapes],
         compiler_params=params(10 * 1024 * 1024),
         cost_estimate=pl.CostEstimate(
             flops=2 * n * count * rows * part * low_rank,
@@ -457,7 +458,8 @@
     og_c = exchange(og_c, CORE)
     send_b, keep_b = sketch_parts(tokens, low_rank, signs, None)
     got_b = exchange(send_b, CORE)
-    weight_v, second_v = prefetch(weight, second)
+    (weight_v,) = prefetch(weight)
+    (second_v,) = prefetch(second)
     sketch = (((keep_b + got_b) + across) * inv_root).astype(jnp.bfloat16)
 
     sk_y = exchange(sketch, Y)
@@ -478,8 +480,16 @@
     z_side = (sketch, sk_c, sk_z, sk_zc), (og_own, og_c, og_z, og_zc)
 
     def begin(terms, offsets, axis):
-        send, keep = project(*terms, offsets, 4)
+        send, keep = project(*terms, offsets, 4, 2)
         return exchange(packed(send, 8.0), axis), keep
+
+    def direct(terms, offsets, masks):
+        send, keep = project(*terms, offsets, 4, 3)
+        total = keep[0]
+        for at, mask in enumerate(masks):
+            got = exchange(packed(send[at], 8.0), mask)
+            total += unpacked(got, 8.0)
+        return total
 
     def middle(state, axis):
         got, keep = state
@@ -490,14 +500,12 @@
         got, keep = state
         return keep + unpacked(got, 4.0)
 
-    far0_state = begin(y_side, (0, 0, 0, 0), X)
-    far1_state = begin(z_side, (8, 8, 0, 0), Y)
+    far0_total = direct(y_side, (0, 0, 0, 0), (X | Z0, X, Z0))
+    far1_total = direct(z_side, (8, 8, 0, 0), (Y | X, Y, X))
     near0_state = begin(y_side, (4, 4, 4, 4), Z0)
     near1_state = begin(z_side, (12, 12, 4, 4), Y)
-    far0_state = middle(far0_state, Z0)
-    far1_state = middle(far1_state, X)
-    last0 = exchange(packed(finish(far0_state), 2.0), Z1)
-    last1 = exchange(packed(finish(far1_state), 2.0), Z1)
+    last0 = exchange(packed(far0_total, 2.0), Z1)
+    last1 = exchange(packed(far1_total, 2.0), Z1)
     near0_state = middle(near0_state, X)
     near1_state = middle(near1_state, X)
 
@@ -518,15 +526,17 @@
         halves.append(mine)
         others.append([v.astype(jnp.float32) for v in (from_core, from_x, from_xc)])
     done = ()
-    for half, rows, relatives in (
-        (0, (halves[0], others[0][0]), (0, CORE)),
-        (0, others[0][1:], (X, X | CORE)),
-        (1, (halves[1], others[1][0]), (0, CORE)),
-        (1, others[1][1:], (X, X | CORE)),
+    near, far = (0, CORE), (X, X | CORE)
+    for rows, where in (
+        ((halves[0], others[0][0]), [(rel, 0) for rel in near]),
+        (
+            (halves[1], others[1][0], *others[0][1:]),
+            [(rel, 1) for rel in near] + [(rel, 0) for rel in far],
+        ),
+        (others[1][1:], [(rel, 1) for rel in far]),
     ):
-        where = tuple((rel, half) for rel in relatives)
-        keep = 0 in relatives
-        done = update(rows, where, keep, signs, weight_v, second_v, tuple(done))
+        keep = where[0][0] == 0
+        done = update(rows, tuple(where), keep, signs, weight_v, second_v, tuple(done))
     return tuple(done)
 
 

time: 123 us -> 125 us (1.016)
  starting transfers between devices: 28.7 us -> 32.8 us
  waiting for transfers between devices: 58.9 us -> 55.8 us
    ppermute x29 -> x31, starting transfers between devices: 28.7 us -> 32.8 us  [exchange(): return lax.ppermute(value, AXES, [(i, i ^ mask) for i in range(size)])]
    ppermute x29 -> x31, waiting for transfers between devices: 58.9 us -> 55.8 us  [exchange(): return lax.ppermute(value, AXES, [(i, i ^ mask) for i in range(size)])]
    pallas_call x1 -> x2, Pallas kernels: 5.92 us -> 7.01 us  [prefetch(): pl.pallas_call(prefetch_kernel, in_specs=[pl.BlockSpec(memory_space=pl.AN...]
    pallas_call x4 -> x3, Pallas kernels: 11.4 us -> 10.8 us  [update(): pl.pallas_call(functools.partial(update_kernel, where, keep, slabs, min(s...]
  transfers between devices with their start and end apart: 29 -> 31, of which waited for: 9 -> 10; matrix products, arithmetic and copies ran while one was open for 1% -> 1% of each run, Pallas kernels for 20% -> 20%
where the time goes in v3:
time: 125 us; the launch traced here: 124 us
  waiting for transfers between devices  55.8 us (45%)
  starting transfers between devices  32.8 us (26%)
  Pallas kernels  31.9 us (26%)
  between operations  2.36 us (2%)
    ppermute x31, waiting for transfers between devices, exchange(): return lax.ppermute(value, AXES, [(i, i ^ mask) for i in range(size)])  55.8 us
    ppermute x31, starting transfers between devices, exchange(): return lax.ppermute(value, AXES, [(i, i ^ mask) for i in range(size)])  32.8 us
    pallas_call x3, Pallas kernels, update(): pl.pallas_call(functools.partial(update_kernel, where, keep, slabs, min(s...  10.8 us
    pallas_call x2, Pallas kernels, prefetch(): pl.pallas_call(prefetch_kernel, in_specs=[pl.BlockSpec(memory_space=pl.AN...  7.01 us
    pallas_call x2, Pallas kernels, sketch_parts(): pl.pallas_call(functools.partial(sketch_kernel, first, din_local), in_spe...  6.2 us
    pallas_call x3, Pallas kernels, pack(): pl.pallas_call(functools.partial(pack_kernel, groups, width, part), in_sp...  4.92 us
    pallas_call x4, Pallas kernels, project(): pl.pallas_call(functools.partial(project_kernel, n), grid=(1,), in_specs=...  2.91 us
  transfers between devices with their start and end apart: 31, of which 10 were waited for; matrix products, arithmetic and copies ran while one was open for 1% of the time, Pallas kernels for 20%

profile of v3, /device:TPU:0, one launch (start us, length us, event | category | flops | bytes accessed | tf_op | source)
XLA Modules:
  0.0 124.1 jit_solution(8610095373322546072)
XLA Ops:
  1.9 3.7 %sketch.2 = (bf16[2048,512]{1,0:T(8,128)(2,1)S(1)}, f32[256,512]{1,0:T(8,128)S(1)}, f32[256,512]{1,0:T(8,128)S(1)}) custom-call(s32[1,1]{1,0:T(1,128)} %bitcast.56.refs_0_, s32[1,1]{1,0:T(1,128)} %bitcast.57.refs_1_, bf16[1024,2048]{1,0:T(8,128)(2,1)} %refs_0_.3), custom_call_target="tpu_custom_call" | custom-call | flops 1073741824 | bytes 6291456 | tf_op jit(solution)/shard_map/sketch/pallas_call | solution.py:224
  5.6 0.6 collective-permute-start.1
  6.2 2.5 %sketch.3 = (f32[256,512]{1,0:T(8,128)S(1)}, f32[256,512]{1,0:T(8,128)S(1)}) custom-call(bf16[1024,2048]{1,0:T(8,128)(2,1)} %refs_0_.3, bf16[2048,512]{1,0:T(8,128)(2,1)S(1)} %get-tuple-element.29.refs_1_.refs_2_.refs_4_), custom_call_target="tpu_custom_call" | custom-call | flops 1073741824 | bytes 6291456 | tf_op jit(solution)/shard_map/sketch/pallas_call | solution.py:224
  8.9 3.0 %collective-permute-start.2 = (f32[256,512]{1,0:T(8,128)S(1)}, f32[256,512]{1,0:T(8,128)S(1)}, u32[]{:S(2)}, u32[]{:S(2)}) collective-permute-start(f32[256,512]{1,0:T(8,128)S(1)} %add.66), channel_id=1, source_target_pairs={{0,2},{1,3},{2,0},{3,1},{4,6},{5,7},{6,4},{7,5},{8,10},{9,11},{10,... | collective-permute-start | bytes 1572872 | tf_op jit(solution)/shard_map/ppermute | solution.py:422
  11.9 2.0 %pack.3 = (bf16[16,256,128]{2,1,0:T(8,128)(2,1)S(1)}, bf16[16,256,128]{2,1,0:T(8,128)(2,1)S(1)}) custom-call(bf16[256,8192]{1,0:T(8,128)(2,1)} %og_ref.5), custom_call_target="tpu_custom_call" | custom-call | bytes 4194304 | tf_op jit(solution)/shard_map/pack/pallas_call | solution.py:127
  14.0 1.5 %pack.4 = (bf16[8,256,128]{2,1,0:T(8,128)(2,1)S(1)}, bf16[8,256,128]{2,1,0:T(8,128)(2,1)S(1)}) custom-call(bf16[256,8192]{1,0:T(8,128)(2,1)} %og_ref.5), custom_call_target="tpu_custom_call" | custom-call | bytes 2097152 | tf_op jit(solution)/shard_map/pack/pallas_call | solution.py:127
  15.5 1.6 %collective-permute-start.17 = (bf16[8,256,128]{2,1,0:T(8,128)(2,1)S(1)}, bf16[8,256,128]{2,1,0:T(8,128)(2,1)S(1)}, u32[]{:S(2)}, u32[]{:S(2)}) collective-permute-start(bf16[8,256,128]{2,1,0:T(8,128)(2,1)S(1)} %get-tuple-element.42), channel_id=1, source_target_pairs={{0,4},{1,5},{2,6},{3,7},{4,0},{5,1},{6,2},{7,3},{8,12},{9,13},{10,... | collective-permute-start | bytes 1572872 | tf_op jit(solution)/shard_map/ppermute | solution.py:422
  17.1 1.5 %pack.5 = (bf16[8,256,128]{2,1,0:T(8,128)(2,1)S(1)}, bf16[8,256,128]{2,1,0:T(8,128)(2,1)S(1)}) custom-call(bf16[256,8192]{1,0:T(8,128)(2,1)} %og_ref.5), custom_call_target="tpu_custom_call" | custom-call | bytes 2097152 | tf_op jit(solution)/shard_map/pack/pallas_call | solution.py:127
  18.5 0.4 collective-permute-start.18
  18.9 5.1 %collective-permute-done.2 = f32[256,512]{1,0:T(8,128)S(1)} collective-permute-done((f32[256,512]{1,0:T(8,128)S(1)}, f32[256,512]{1,0:T(8,128)S(1)}, u32[]{:S(2)}, u32[]{:S(2)}) %collective-permute-start.2) | collective-permute-done | bytes 524320 | tf_op jit(solution)/shard_map/ppermute | solution.py:422
  24.2 1.9 %collective-permute-start.15 = (bf16[256,512]{1,0:T(8,128)(2,1)S(1)}, bf16[256,512]{1,0:T(8,128)(2,1)S(1)}, u32[]{:S(2)}, u32[]{:S(2)}) collective-permute-start(bf16[256,512]{1,0:T(8,128)(2,1)S(1)} %multiply_convert_fusion.2.refs_0_), channel_id=1, source_target_pairs={{0,4},{1,5},{2,6},{3,7},{4,0},{5,1},{6,2},{7,3},{8,12},{9,13},{10,... | collective-permute-start | bytes 786440 | tf_op jit(solution)/shard_map/ppermute | solution.py:422
  26.1 1.6 %collective-permute-start.4 = (bf16[256,512]{1,0:T(8,128)(2,1)S(1)}, bf16[256,512]{1,0:T(8,128)(2,1)S(1)}, u32[]{:S(2)}, u32[]{:S(2)}) collective-permute-start(bf16[256,512]{1,0:T(8,128)(2,1)S(1)} %multiply_convert_fusion.2.refs_0_), channel_id=1, source_target_pairs={{0,8},{1,9},{2,10},{3,11},{4,12},{5,13},{6,14},{7,15},{8,0},{9,1},... | collective-permute-start | bytes 786440 | tf_op jit(solution)/shard_map/ppermute | solution.py:422
  27.6 2.7 %collective-permute-done.17.refs_6_ = bf16[8,256,128]{2,1,0:T(8,128)(2,1)S(1)} collective-permute-done((bf16[8,256,128]{2,1,0:T(8,128)(2,1)S(1)}, bf16[8,256,128]{2,1,0:T(8,128)(2,1)S(1)}, u32[]{:S(2)}, u32[]{:S(2)}) %collective-permute-start.17) | collective-permute-done | bytes 524320 | tf_op jit(solution)/shard_map/ppermute | solution.py:422
  30.3 16.4 %collective-permute-done.15.refs_2_ = bf16[256,512]{1,0:T(8,128)(2,1)S(1)} collective-permute-done((bf16[256,512]{1,0:T(8,128)(2,1)S(1)}, bf16[256,512]{1,0:T(8,128)(2,1)S(1)}, u32[]{:S(2)}, u32[]{:S(2)}) %collective-permute-start.15) | collective-permute-done | bytes 262176 | tf_op jit(solution)/shard_map/ppermute | solution.py:422
  46.7 1.6 %collective-permute-start.7 = (bf16[8,256,128]{2,1,0:T(8,128)(2,1)S(1)}, bf16[8,256,128]{2,1,0:T(8,128)(2,1)S(1)}, u32[]{:S(2)}, u32[]{:S(2)}) collective-permute-start(bf16[8,256,128]{2,1,0:T(8,128)(2,1)S(1)} %get-tuple-element.36), channel_id=1, source_target_pairs={{0,8},{1,9},{2,10},{3,11},{4,12},{5,13},{6,14},{7,15},{8,0},{9,1},... | collective-permute-start | bytes 1572872 | tf_op jit(solution)/shard_map/ppermute | solution.py:422
  48.6 0.3 collective-permute-start.5
  48.9 0.7 project.6
  49.7 1.7 %collective-permute-start.19 = (f16[2,128,512]{2,1,0:T(8,128)(2,1)S(1)}, f16[2,128,512]{2,1,0:T(8,128)(2,1)S(1)}, u32[]{:S(2)}, u32[]{:S(2)}) collective-permute-start(f16[2,128,512]{2,1,0:T(8,128)(2,1)S(1)} %multiply_convert_fusion), channel_id=1, source_target_pairs={{0,8},{1,9},{2,10},{3,11},{4,12},{5,13},{6,14},{7,15},{8,0},{9,1},... | collective-permute-start | bytes 786440 | tf_op jit(solution)/shard_map/ppermute | solution.py:422
  51.3 0.7 project.7
  52.1 0.3 collective-permute-start.21
  52.4 9.1 %collective-permute-done.7.refs_6_ = bf16[8,256,128]{2,1,0:T(8,128)(2,1)S(1)} collective-permute-done((bf16[8,256,128]{2,1,0:T(8,128)(2,1)S(1)}, bf16[8,256,128]{2,1,0:T(8,128)(2,1)S(1)}, u32[]{:S(2)}, u32[]{:S(2)}) %collective-permute-start.7) | collective-permute-done | bytes 524320 | tf_op jit(solution)/shard_map/ppermute | solution.py:422
  61.5 0.3 collective-permute-start.22
  61.8 10.0 %collective-permute-done.8.refs_7_ = bf16[8,256,128]{2,1,0:T(8,128)(2,1)S(1)} collective-permute-done((bf16[8,256,128]{2,1,0:T(8,128)(2,1)S(1)}, bf16[8,256,128]{2,1,0:T(8,128)(2,1)S(1)}, u32[]{:S(2)}, u32[]{:S(2)}) %collective-permute-start.8) | collective-permute-done | bytes 524320 | tf_op jit(solution)/shard_map/ppermute | solution.py:422
  71.8 1.6 %collective-permute-start.23 = (f16[128,512]{1,0:T(8,128)(2,1)S(1)}, f16[128,512]{1,0:T(8,128)(2,1)S(1)}, u32[]{:S(2)}, u32[]{:S(2)}) collective-permute-start(f16[128,512]{1,0:T(8,128)(2,1)S(1)} %get-tuple-element.60), channel_id=1, source_target_pairs={{0,8},{1,9},{2,10},{3,11},{4,12},{5,13},{6,14},{7,15},{8,0},{9,1},... | collective-permute-start | bytes 393224 | tf_op jit(solution)/shard_map/ppermute | solution.py:422
  73.4 0.7 project.4
  74.2 1.6 %collective-permute-start.9 = (f16[2,128,512]{2,1,0:T(8,128)(2,1)S(1)}, f16[2,128,512]{2,1,0:T(8,128)(2,1)S(1)}, u32[]{:S(2)}, u32[]{:S(2)}) collective-permute-start(f16[2,128,512]{2,1,0:T(8,128)(2,1)S(1)} %multiply_convert_fusion.1), channel_id=1, source_target_pairs={{0,4},{1,5},{2,6},{3,7},{4,0},{5,1},{6,2},{7,3},{8,12},{9,13},{10,... | collective-permute-start | bytes 786440 | tf_op jit(solution)/shard_map/ppermute | solution.py:422
  75.8 0.7 project.5
  76.6 4.4 %collective-permute-done.21 = f16[128,512]{1,0:T(8,128)(2,1)S(1)} collective-permute-done((f16[128,512]{1,0:T(8,128)(2,1)S(1)}, f16[128,512]{1,0:T(8,128)(2,1)S(1)}, u32[]{:S(2)}, u32[]{:S(2)}) %collective-permute-start.21) | collective-permute-done | bytes 131104 | tf_op jit(solution)/shard_map/ppermute | solution.py:422
  80.9 2.7 %collective-permute-start.11 = (f16[128,512]{1,0:T(8,128)(2,1)S(1)}, f16[128,512]{1,0:T(8,128)(2,1)S(1)}, u32[]{:S(2)}, u32[]{:S(2)}) collective-permute-start(f16[128,512]{1,0:T(8,128)(2,1)S(1)} %get-tuple-element.62), channel_id=1, source_target_pairs={{0,6},{1,7},{2,4},{3,5},{4,2},{5,3},{6,0},{7,1},{8,14},{9,15},{10,... | collective-permute-start | bytes 393224 | tf_op jit(solution)/shard_map/ppermute | solution.py:422
  83.6 0.5 collective-permute-start.12
  84.1 0.3 collective-permute-start.13
  84.5 2.6 %collective-permute-done.11 = f16[128,512]{1,0:T(8,128)(2,1)S(1)} collective-permute-done((f16[128,512]{1,0:T(8,128)(2,1)S(1)}, f16[128,512]{1,0:T(8,128)(2,1)S(1)}, u32[]{:S(2)}, u32[]{:S(2)}) %collective-permute-start.11) | collective-permute-done | bytes 131104 | tf_op jit(solution)/shard_map/ppermute | solution.py:422
  87.1 2.7 %collective-permute-start.24 = (f16[128,512]{1,0:T(8,128)(2,1)S(1)}, f16[128,512]{1,0:T(8,128)(2,1)S(1)}, u32[]{:S(2)}, u32[]{:S(2)}) collective-permute-start(f16[128,512]{1,0:T(8,128)(2,1)S(1)} %fusion.3), channel_id=1, source_target_pairs={{0,16},{1,17},{2,18},{3,19},{4,20},{5,21},{6,22},{7,23},{8,24},{9,... | collective-permute-start | bytes 393224 | tf_op jit(solution)/shard_map/ppermute | solution.py:422
  90.0 2.6 %collective-permute-start.14 = (f16[128,512]{1,0:T(8,128)(2,1)S(1)}, f16[128,512]{1,0:T(8,128)(2,1)S(1)}, u32[]{:S(2)}, u32[]{:S(2)}) collective-permute-start(f16[128,512]{1,0:T(8,128)(2,1)S(1)} %fusion.10), channel_id=1, source_target_pairs={{0,16},{1,17},{2,18},{3,19},{4,20},{5,21},{6,22},{7,23},{8,24},{9,... | collective-permute-start | bytes 393224 | tf_op jit(solution)/shard_map/ppermute | solution.py:422
  92.7 1.2 %collective-permute-start.20 = (f16[128,512]{1,0:T(8,128)(2,1)S(1)}, f16[128,512]{1,0:T(8,128)(2,1)S(1)}, u32[]{:S(2)}, u32[]{:S(2)}) collective-permute-start(f16[128,512]{1,0:T(8,128)(2,1)S(1)} %fusion.18), channel_id=1, source_target_pairs={{0,2},{1,3},{2,0},{3,1},{4,6},{5,7},{6,4},{7,5},{8,10},{9,11},{10,... | collective-permute-start | bytes 393224 | tf_op jit(solution)/shard_map/ppermute | solution.py:422
  94.0 0.9 collective-permute-start.10
  94.9 2.8 %collective-permute-done.24 = f16[128,512]{1,0:T(8,128)(2,1)S(1)} collective-permute-done((f16[128,512]{1,0:T(8,128)(2,1)S(1)}, f16[128,512]{1,0:T(8,128)(2,1)S(1)}, u32[]{:S(2)}, u32[]{:S(2)}) %collective-permute-start.24) | collective-permute-done | bytes 131104 | tf_op jit(solution)/shard_map/ppermute | solution.py:422
  97.7 0.7 collective-permute-done.20
  98.5 2.8 %collective-permute-start.28 = (f16[128,512]{1,0:T(8,128)(2,1)S(1)}, f16[128,512]{1,0:T(8,128)(2,1)S(1)}, u32[]{:S(2)}, u32[]{:S(2)}) collective-permute-start(f16[128,512]{1,0:T(8,128)(2,1)S(1)} %get-tuple-element.57), channel_id=1, source_target_pairs={{0,2},{1,3},{2,0},{3,1},{4,6},{5,7},{6,4},{7,5},{8,10},{9,11},{10,... | collective-permute-start | bytes 393224 | tf_op jit(solution)/shard_map/ppermute | solution.py:422
  101.5 1.3 %collective-permute-start.25 = (f16[128,512]{1,0:T(8,128)(2,1)S(1)}, f16[128,512]{1,0:T(8,128)(2,1)S(1)}, u32[]{:S(2)}, u32[]{:S(2)}) collective-permute-start(f16[128,512]{1,0:T(8,128)(2,1)S(1)} %get-tuple-element.55), channel_id=1, source_target_pairs={{0,2},{1,3},{2,0},{3,1},{4,6},{5,7},{6,4},{7,5},{8,10},{9,11},{10,... | collective-permute-start | bytes 393224 | tf_op jit(solution)/shard_map/ppermute | solution.py:422
  102.8 0.5 collective-permute-start.27
  103.3 2.0 %collective-permute-done.28 = f16[128,512]{1,0:T(8,128)(2,1)S(1)} collective-permute-done((f16[128,512]{1,0:T(8,128)(2,1)S(1)}, f16[128,512]{1,0:T(8,128)(2,1)S(1)}, u32[]{:S(2)}, u32[]{:S(2)}) %collective-permute-start.28) | collective-permute-done | bytes 131104 | tf_op jit(solution)/shard_map/ppermute | solution.py:422
  105.3 3.5 %prefetch.2.refs_3_.refs_5_ = f32[1024,2048]{1,0:T(8,128)S(1)} custom-call(f32[1024,2048]{1,0:T(8,128)} %refs_0_.4), custom_call_target="tpu_custom_call" | custom-call | bytes 8388608 | tf_op jit(solution)/shard_map/prefetch/pallas_call | solution.py:309
  108.8 3.5 %prefetch.3.refs_4_.refs_6_ = f32[1024,2048]{1,0:T(8,128)S(1)} custom-call(f32[1024,2048]{1,0:T(8,128)} %refs_0_.5), custom_call_target="tpu_custom_call" | custom-call | bytes 8388608 | tf_op jit(solution)/shard_map/prefetch/pallas_call | solution.py:309
  112.4 0.6 collective-permute-start.26
  113.0 2.9 %update.3 = (f32[1024,2048]{1,0:T(8,128)}, f32[1024,2048]{1,0:T(8,128)}, f32[256,512]{1,0:T(8,128)}) custom-call(f32[128,512]{1,0:T(8,128)S(1)} %get-tuple-element.58.refs_0_, f32[128,512]{1,0:T(8,128)S(1)} %convert_element_type.161.refs_1_, bf16[2048,512]{1,0:T(8,128)(2,1)S(1)} %get-tuple-element.29.refs_1_.refs_2_.refs_4_, ...), custom_call_target="tpu_custom_call" | custom-call | flops 1073741824 | bytes 4194304 | tf_op jit(solution)/shard_map/update/pallas_call | solution.py:391
  116.0 5.1 %update.4 = (f32[1024,2048]{1,0:T(8,128)}, f32[1024,2048]{1,0:T(8,128)}, f32[256,512]{1,0:T(8,128)}) custom-call(f32[128,512]{1,0:T(8,128)S(1)} %get-tuple-element.56.refs_0_, f32[128,512]{1,0:T(8,128)S(1)} %convert_element_type.158.refs_1_, ...), custom_call_target="tpu_custom_call", output_to_operand_aliasing={{0}: (7, {}), {1}: (8, {}), {2}: (9, {})} | custom-call | flops 2147483648 | bytes 8388608 | tf_op jit(solution)/shard_map/update/pallas_call | solution.py:391
  121.1 2.8 %update.5 = (f32[1024,2048]{1,0:T(8,128)}, f32[1024,2048]{1,0:T(8,128)}, f32[256,512]{1,0:T(8,128)}) custom-call(f32[128,512]{1,0:T(8,128)S(1)} %convert_element_type.156.refs_0_, f32[128,512]{1,0:T(8,128)S(1)} %convert_element_type.157.refs_1_, ...), custom_call_target="tpu_custom_call", output_to_operand_aliasing={{0}: (5, {}), {1}: (6, {}), {2}: (7, {})} | custom-call | flops 1073741824 | bytes 4194304 | tf_op jit(solution)/shard_map/update/pallas_call | solution.py:391
  (48 shorter events, 1.7 us)
Async XLA Ops:
  5.6 3.2 %collective-permute-start.1 = (f32[256,512]{1,0:T(8,128)S(1)}, f32[256,512]{1,0:T(8,128)S(1)}, u32[]{:S(2)}, u32[]{:S(2)}) collective-permute-start(f32[256,512]{1,0:T(8,128)S(1)} %get-tuple-element.33), channel_id=1, source_target_pairs={{0,1},{1,0},{2,3},{3,2},{4,5},{5,4},{6,7},{7,6},{8,9},{9,8},{10,11... | collective-permute-start | bytes 1572872 | tf_op jit(solution)/shard_map/ppermute | solution.py:422
  8.7 10.2 %collective-permute-start = (f32[256,512]{1,0:T(8,128)S(1)}, f32[256,512]{1,0:T(8,128)S(1)}, u32[]{:S(2)}, u32[]{:S(2)}) collective-permute-start(f32[256,512]{1,0:T(8,128)S(1)} %get-tuple-element.31), channel_id=1, source_target_pairs={{0,1},{1,0},{2,3},{3,2},{4,5},{5,4},{6,7},{7,6},{8,9},{9,8},{10,11... | collective-permute-start | bytes 1572872 | tf_op jit(solution)/shard_map/ppermute | solution.py:422
  8.9 15.1 %collective-permute-start.2 = (f32[256,512]{1,0:T(8,128)S(1)}, f32[256,512]{1,0:T(8,128)S(1)}, u32[]{:S(2)}, u32[]{:S(2)}) collective-permute-start(f32[256,512]{1,0:T(8,128)S(1)} %add.66), channel_id=1, source_target_pairs={{0,2},{1,3},{2,0},{3,1},{4,6},{5,7},{6,4},{7,5},{8,10},{9,11},{10,... | collective-permute-start | bytes 1572872 | tf_op jit(solution)/shard_map/ppermute | solution.py:422
  13.9 34.4 %collective-permute-start.6 = (bf16[16,256,128]{2,1,0:T(8,128)(2,1)S(1)}, bf16[16,256,128]{2,1,0:T(8,128)(2,1)S(1)}, u32[]{:S(2)}, u32[]{:S(2)}) collective-permute-start(bf16[16,256,128]{2,1,0:T(8,128)(2,1)S(1)} %get-tuple-element.35), channel_id=1, source_target_pairs={{0,1},{1,0},{2,3},{3,2},{4,5},{5,4},{6,7},{7,6},{8,9},{9,8},{10,11... | collective-permute-start | bytes 3145736 | tf_op jit(solution)/shard_map/ppermute | solution.py:422
  15.5 14.9 %collective-permute-start.17 = (bf16[8,256,128]{2,1,0:T(8,128)(2,1)S(1)}, bf16[8,256,128]{2,1,0:T(8,128)(2,1)S(1)}, u32[]{:S(2)}, u32[]{:S(2)}) collective-permute-start(bf16[8,256,128]{2,1,0:T(8,128)(2,1)S(1)} %get-tuple-element.42), channel_id=1, source_target_pairs={{0,4},{1,5},{2,6},{3,7},{4,0},{5,1},{6,2},{7,3},{8,12},{9,13},{10,... | collective-permute-start | bytes 1572872 | tf_op jit(solution)/shard_map/ppermute | solution.py:422
  18.5 28.2 %collective-permute-start.18 = (bf16[8,256,128]{2,1,0:T(8,128)(2,1)S(1)}, bf16[8,256,128]{2,1,0:T(8,128)(2,1)S(1)}, u32[]{:S(2)}, u32[]{:S(2)}) collective-permute-start(bf16[8,256,128]{2,1,0:T(8,128)(2,1)S(1)} %get-tuple-element.43), channel_id=1, source_target_pairs={{0,5},{1,4},{2,7},{3,6},{4,1},{5,0},{6,3},{7,2},{8,13},{9,12},{10,... | collective-permute-start | bytes 1572872 | tf_op jit(solution)/shard_map/ppermute | solution.py:422
  24.2 22.5 %collective-permute-start.15 = (bf16[256,512]{1,0:T(8,128)(2,1)S(1)}, bf16[256,512]{1,0:T(8,128)(2,1)S(1)}, u32[]{:S(2)}, u32[]{:S(2)}) collective-permute-start(bf16[256,512]{1,0:T(8,128)(2,1)S(1)} %multiply_convert_fusion.2.refs_0_), channel_id=1, source_target_pairs={{0,4},{1,5},{2,6},{3,7},{4,0},{5,1},{6,2},{7,3},{8,12},{9,13},{10,... | collective-permute-start | bytes 786440 | tf_op jit(solution)/shard_map/ppermute | solution.py:422
  26.1 22.5 %collective-permute-start.4 = (bf16[256,512]{1,0:T(8,128)(2,1)S(1)}, bf16[256,512]{1,0:T(8,128)(2,1)S(1)}, u32[]{:S(2)}, u32[]{:S(2)}) collective-permute-start(bf16[256,512]{1,0:T(8,128)(2,1)S(1)} %multiply_convert_fusion.2.refs_0_), channel_id=1, source_target_pairs={{0,8},{1,9},{2,10},{3,11},{4,12},{5,13},{6,14},{7,15},{8,0},{9,1},... | collective-permute-start | bytes 786440 | tf_op jit(solution)/shard_map/ppermute | solution.py:422
  30.3 18.5 %collective-permute-start.3 = (bf16[256,512]{1,0:T(8,128)(2,1)S(1)}, bf16[256,512]{1,0:T(8,128)(2,1)S(1)}, u32[]{:S(2)}, u32[]{:S(2)}) collective-permute-start(bf16[256,512]{1,0:T(8,128)(2,1)S(1)} %multiply_convert_fusion.2.refs_0_), channel_id=1, source_target_pairs={{0,1},{1,0},{2,3},{3,2},{4,5},{5,4},{6,7},{7,6},{8,9},{9,8},{10,11... | collective-permute-start | bytes 786440 | tf_op jit(solution)/shard_map/ppermute | solution.py:422
  46.7 2.2 %collective-permute-start.16 = (bf16[256,512]{1,0:T(8,128)(2,1)S(1)}, bf16[256,512]{1,0:T(8,128)(2,1)S(1)}, u32[]{:S(2)}, u32[]{:S(2)}) collective-permute-start(bf16[256,512]{1,0:T(8,128)(2,1)S(1)} %collective-permute-done.15.refs_2_), channel_id=1, source_target_pairs={{0,1},{1,0},{2,3},{3,2},{4,5},{5,4},{6,7},{7,6},{8,9},{9,8},{10,11... | collective-permute-start | bytes 786440 | tf_op jit(solution)/shard_map/ppermute | solution.py:422
  46.7 14.8 %collective-permute-start.7 = (bf16[8,256,128]{2,1,0:T(8,128)(2,1)S(1)}, bf16[8,256,128]{2,1,0:T(8,128)(2,1)S(1)}, u32[]{:S(2)}, u32[]{:S(2)}) collective-permute-start(bf16[8,256,128]{2,1,0:T(8,128)(2,1)S(1)} %get-tuple-element.36), channel_id=1, source_target_pairs={{0,8},{1,9},{2,10},{3,11},{4,12},{5,13},{6,14},{7,15},{8,0},{9,1},... | collective-permute-start | bytes 1572872 | tf_op jit(solution)/shard_map/ppermute | solution.py:422
  48.3 23.5 %collective-permute-start.8 = (bf16[8,256,128]{2,1,0:T(8,128)(2,1)S(1)}, bf16[8,256,128]{2,1,0:T(8,128)(2,1)S(1)}, u32[]{:S(2)}, u32[]{:S(2)}) collective-permute-start(bf16[8,256,128]{2,1,0:T(8,128)(2,1)S(1)} %get-tuple-element.37), channel_id=1, source_target_pairs={{0,9},{1,8},{2,11},{3,10},{4,13},{5,12},{6,15},{7,14},{8,1},{9,0},... | collective-permute-start | bytes 1572872 | tf_op jit(solution)/shard_map/ppermute | solution.py:422
  48.6 24.8 %collective-permute-start.5 = (bf16[256,512]{1,0:T(8,128)(2,1)S(1)}, bf16[256,512]{1,0:T(8,128)(2,1)S(1)}, u32[]{:S(2)}, u32[]{:S(2)}) collective-permute-start(bf16[256,512]{1,0:T(8,128)(2,1)S(1)} %collective-permute-done.4.refs_2_), channel_id=1, source_target_pairs={{0,1},{1,0},{2,3},{3,2},{4,5},{5,4},{6,7},{7,6},{8,9},{9,8},{10,11... | collective-permute-start | bytes 786440 | tf_op jit(solution)/shard_map/ppermute | solution.py:422
  49.6 48.7 %copy-start = (f32[256,512]{1,0:T(8,128)S(1)}, f32[256,512]{1,0:T(8,128)}, u32[]{:S(2)}) copy-start(f32[256,512]{1,0:T(8,128)} %param.11) | copy-start | bytes 1572868
  49.7 43.0 %collective-permute-start.19 = (f16[2,128,512]{2,1,0:T(8,128)(2,1)S(1)}, f16[2,128,512]{2,1,0:T(8,128)(2,1)S(1)}, u32[]{:S(2)}, u32[]{:S(2)}) collective-permute-start(f16[2,128,512]{2,1,0:T(8,128)(2,1)S(1)} %multiply_convert_fusion), channel_id=1, source_target_pairs={{0,8},{1,9},{2,10},{3,11},{4,12},{5,13},{6,14},{7,15},{8,0},{9,1},... | collective-permute-start | bytes 786440 | tf_op jit(solution)/shard_map/ppermute | solution.py:422
  52.1 28.8 %collective-permute-start.21 = (f16[128,512]{1,0:T(8,128)(2,1)S(1)}, f16[128,512]{1,0:T(8,128)(2,1)S(1)}, u32[]{:S(2)}, u32[]{:S(2)}) collective-permute-start(f16[128,512]{1,0:T(8,128)(2,1)S(1)} %get-tuple-element.59), channel_id=1, source_target_pairs={{0,10},{1,11},{2,8},{3,9},{4,14},{5,15},{6,12},{7,13},{8,2},{9,3},... | collective-permute-start | bytes 393224 | tf_op jit(solution)/shard_map/ppermute | solution.py:422
  61.5 22.1 %collective-permute-start.22 = (f16[128,512]{1,0:T(8,128)(2,1)S(1)}, f16[128,512]{1,0:T(8,128)(2,1)S(1)}, u32[]{:S(2)}, u32[]{:S(2)}) collective-permute-start(f16[128,512]{1,0:T(8,128)(2,1)S(1)} %get-tuple-element.61), channel_id=1, source_target_pairs={{0,2},{1,3},{2,0},{3,1},{4,6},{5,7},{6,4},{7,5},{8,10},{9,11},{10,... | collective-permute-start | bytes 393224 | tf_op jit(solution)/shard_map/ppermute | solution.py:422
  71.8 12.2 %collective-permute-start.23 = (f16[128,512]{1,0:T(8,128)(2,1)S(1)}, f16[128,512]{1,0:T(8,128)(2,1)S(1)}, u32[]{:S(2)}, u32[]{:S(2)}) collective-permute-start(f16[128,512]{1,0:T(8,128)(2,1)S(1)} %get-tuple-element.60), channel_id=1, source_target_pairs={{0,8},{1,9},{2,10},{3,11},{4,12},{5,13},{6,14},{7,15},{8,0},{9,1},... | collective-permute-start | bytes 393224 | tf_op jit(solution)/shard_map/ppermute | solution.py:422
  74.2 19.7 %collective-permute-start.9 = (f16[2,128,512]{2,1,0:T(8,128)(2,1)S(1)}, f16[2,128,512]{2,1,0:T(8,128)(2,1)S(1)}, u32[]{:S(2)}, u32[]{:S(2)}) collective-permute-start(f16[2,128,512]{2,1,0:T(8,128)(2,1)S(1)} %multiply_convert_fusion.1), channel_id=1, source_target_pairs={{0,4},{1,5},{2,6},{3,7},{4,0},{5,1},{6,2},{7,3},{8,12},{9,13},{10,... | collective-permute-start | bytes 786440 | tf_op jit(solution)/shard_map/ppermute | solution.py:422
  80.9 6.2 %collective-permute-start.11 = (f16[128,512]{1,0:T(8,128)(2,1)S(1)}, f16[128,512]{1,0:T(8,128)(2,1)S(1)}, u32[]{:S(2)}, u32[]{:S(2)}) collective-permute-start(f16[128,512]{1,0:T(8,128)(2,1)S(1)} %get-tuple-element.62), channel_id=1, source_target_pairs={{0,6},{1,7},{2,4},{3,5},{4,2},{5,3},{6,0},{7,1},{8,14},{9,15},{10,... | collective-permute-start | bytes 393224 | tf_op jit(solution)/shard_map/ppermute | solution.py:422
  83.6 6.3 %collective-permute-start.12 = (f16[128,512]{1,0:T(8,128)(2,1)S(1)}, f16[128,512]{1,0:T(8,128)(2,1)S(1)}, u32[]{:S(2)}, u32[]{:S(2)}) collective-permute-start(f16[128,512]{1,0:T(8,128)(2,1)S(1)} %get-tuple-element.64), channel_id=1, source_target_pairs={{0,4},{1,5},{2,6},{3,7},{4,0},{5,1},{6,2},{7,3},{8,12},{9,13},{10,... | collective-permute-start | bytes 393224 | tf_op jit(solution)/shard_map/ppermute | solution.py:422
  84.1 5.8 %collective-permute-start.13 = (f16[128,512]{1,0:T(8,128)(2,1)S(1)}, f16[128,512]{1,0:T(8,128)(2,1)S(1)}, u32[]{:S(2)}, u32[]{:S(2)}) collective-permute-start(f16[128,512]{1,0:T(8,128)(2,1)S(1)} %get-tuple-element.63), channel_id=1, source_target_pairs={{0,2},{1,3},{2,0},{3,1},{4,6},{5,7},{6,4},{7,5},{8,10},{9,11},{10,... | collective-permute-start | bytes 393224 | tf_op jit(solution)/shard_map/ppermute | solution.py:422
  87.1 10.5 %collective-permute-start.24 = (f16[128,512]{1,0:T(8,128)(2,1)S(1)}, f16[128,512]{1,0:T(8,128)(2,1)S(1)}, u32[]{:S(2)}, u32[]{:S(2)}) collective-permute-start(f16[128,512]{1,0:T(8,128)(2,1)S(1)} %fusion.3), channel_id=1, source_target_pairs={{0,16},{1,17},{2,18},{3,19},{4,20},{5,21},{6,22},{7,23},{8,24},{9,... | collective-permute-start | bytes 393224 | tf_op jit(solution)/shard_map/ppermute | solution.py:422
  90.0 11.3 %collective-permute-start.14 = (f16[128,512]{1,0:T(8,128)(2,1)S(1)}, f16[128,512]{1,0:T(8,128)(2,1)S(1)}, u32[]{:S(2)}, u32[]{:S(2)}) collective-permute-start(f16[128,512]{1,0:T(8,128)(2,1)S(1)} %fusion.10), channel_id=1, source_target_pairs={{0,16},{1,17},{2,18},{3,19},{4,20},{5,21},{6,22},{7,23},{8,24},{9,... | collective-permute-start | bytes 393224 | tf_op jit(solution)/shard_map/ppermute | solution.py:422
  92.7 5.7 %collective-permute-start.20 = (f16[128,512]{1,0:T(8,128)(2,1)S(1)}, f16[128,512]{1,0:T(8,128)(2,1)S(1)}, u32[]{:S(2)}, u32[]{:S(2)}) collective-permute-start(f16[128,512]{1,0:T(8,128)(2,1)S(1)} %fusion.18), channel_id=1, source_target_pairs={{0,2},{1,3},{2,0},{3,1},{4,6},{5,7},{6,4},{7,5},{8,10},{9,11},{10,... | collective-permute-start | bytes 393224 | tf_op jit(solution)/shard_map/ppermute | solution.py:422
  94.0 7.3 %collective-permute-start.10 = (f16[128,512]{1,0:T(8,128)(2,1)S(1)}, f16[128,512]{1,0:T(8,128)(2,1)S(1)}, u32[]{:S(2)}, u32[]{:S(2)}) collective-permute-start(f16[128,512]{1,0:T(8,128)(2,1)S(1)} %fusion.14), channel_id=1, source_target_pairs={{0,2},{1,3},{2,0},{3,1},{4,6},{5,7},{6,4},{7,5},{8,10},{9,11},{10,... | collective-permute-start | bytes 393224 | tf_op jit(solution)/shard_map/ppermute | solution.py:422
  98.5 6.8 %collective-permute-start.28 = (f16[128,512]{1,0:T(8,128)(2,1)S(1)}, f16[128,512]{1,0:T(8,128)(2,1)S(1)}, u32[]{:S(2)}, u32[]{:S(2)}) collective-permute-start(f16[128,512]{1,0:T(8,128)(2,1)S(1)} %get-tuple-element.57), channel_id=1, source_target_pairs={{0,2},{1,3},{2,0},{3,1},{4,6},{5,7},{6,4},{7,5},{8,10},{9,11},{10,... | collective-permute-start | bytes 393224 | tf_op jit(solution)/shard_map/ppermute | solution.py:422
  101.5 10.9 %collective-permute-start.25 = (f16[128,512]{1,0:T(8,128)(2,1)S(1)}, f16[128,512]{1,0:T(8,128)(2,1)S(1)}, u32[]{:S(2)}, u32[]{:S(2)}) collective-permute-start(f16[128,512]{1,0:T(8,128)(2,1)S(1)} %get-tuple-element.55), channel_id=1, source_target_pairs={{0,2},{1,3},{2,0},{3,1},{4,6},{5,7},{6,4},{7,5},{8,10},{9,11},{10,... | collective-permute-start | bytes 393224 | tf_op jit(solution)/shard_map/ppermute | solution.py:422
  102.8 10.2 %collective-permute-start.30 = (f16[128,512]{1,0:T(8,128)(2,1)S(1)}, f16[128,512]{1,0:T(8,128)(2,1)S(1)}, u32[]{:S(2)}, u32[]{:S(2)}) collective-permute-start(f16[128,512]{1,0:T(8,128)(2,1)S(1)} %get-tuple-element.57), channel_id=1, source_target_pairs={{0,1},{1,0},{2,3},{3,2},{4,5},{5,4},{6,7},{7,6},{8,9},{9,8},{10,11... | collective-permute-start | bytes 393224 | tf_op jit(solution)/shard_map/ppermute | solution.py:422
  102.8 10.2 %collective-permute-start.27 = (f16[128,512]{1,0:T(8,128)(2,1)S(1)}, f16[128,512]{1,0:T(8,128)(2,1)S(1)}, u32[]{:S(2)}, u32[]{:S(2)}) collective-permute-start(f16[128,512]{1,0:T(8,128)(2,1)S(1)} %get-tuple-element.55), channel_id=1, source_target_pairs={{0,1},{1,0},{2,3},{3,2},{4,5},{5,4},{6,7},{7,6},{8,9},{9,8},{10,11... | collective-permute-start | bytes 393224 | tf_op jit(solution)/shard_map/ppermute | solution.py:422
  105.3 10.6 %collective-permute-start.29 = (f16[128,512]{1,0:T(8,128)(2,1)S(1)}, f16[128,512]{1,0:T(8,128)(2,1)S(1)}, u32[]{:S(2)}, u32[]{:S(2)}) collective-permute-start(f16[128,512]{1,0:T(8,128)(2,1)S(1)} %collective-permute-done.28), channel_id=1, source_target_pairs={{0,1},{1,0},{2,3},{3,2},{4,5},{5,4},{6,7},{7,6},{8,9},{9,8},{10,11... | collective-permute-start | bytes 393224 | tf_op jit(solution)/shard_map/ppermute | solution.py:422
  112.4 8.8 %collective-permute-start.26 = (f16[128,512]{1,0:T(8,128)(2,1)S(1)}, f16[128,512]{1,0:T(8,128)(2,1)S(1)}, u32[]{:S(2)}, u32[]{:S(2)}) collective-permute-start(f16[128,512]{1,0:T(8,128)(2,1)S(1)} %collective-permute-done.25), channel_id=1, source_target_pairs={{0,1},{1,0},{2,3},{3,2},{4,5},{5,4},{6,7},{7,6},{8,9},{9,8},{10,11... | collective-permute-start | bytes 393224 | tf_op jit(solution)/shard_map/ppermute | solution.py:422

commit v4 on v3

--- a/solution.py
+++ b/solution.py
@@ -428,15 +428,15 @@
     total_tokens = lax.axis_size("dp") * tokens.shape[0]
     inv_root = 1.0 / jnp.sqrt(jnp.float32(low_rank))
     far0 = [(Z1 | X | Z0, 0), (Z1 | X, 0), (Z1 | Z0, 0), (Z1, 0)]
-    near0 = [(Z0 | X, 0), (Z0, 0), (X, 0), (0, 0)]
+    near0 = [(Y | X, 0), (Y, 0), (X, 0), (0, 0)]
     far1 = [(Z1 | Y | X, 1), (Z1 | Y, 1), (Z1 | X, 1), (Z1, 1)]
-    near1 = [(Y | X, 1), (Y, 1), (X, 1), (0, 1)]
+    near1 = [(Z0 | X, 1), (Z0, 1), (X, 1), (0, 1)]
 
     def toward(mask, pieces):
         return [(rel ^ mask, half) for rel, half in pieces]
 
     part = owner_rows // 2
-    over_y, over_z = far0 + near0, far1 + near1
+    over_y, over_z = far0 + near1, far1 + near0
     og_y, og_z = pack(out_grad, [toward(Y, over_y), toward(Z0, over_z)], owner_rows, part)
     og_y = exchange(og_y, Y)
     og_z = exchange(og_z, Z0)
@@ -502,8 +502,8 @@
 
     far0_total = direct(y_side, (0, 0, 0, 0), (X | Z0, X, Z0))
     far1_total = direct(z_side, (8, 8, 0, 0), (Y | X, Y, X))
-    near0_state = begin(y_side, (4, 4, 4, 4), Z0)
-    near1_state = begin(z_side, (12, 12, 4, 4), Y)
+    near0_state = begin(z_side, (12, 12, 4, 4), Y)
+    near1_state = begin(y_side, (4, 4, 4, 4), Z0)
     last0 = exchange(packed(far0_total, 2.0), Z1)
     last1 = exchange(packed(far1_total, 2.0), Z1)
     near0_state = middle(near0_state, X)

time: 125 us -> 124 us (level)
  transfers between devices with their start and end apart: 31 -> 31, of which waited for: 10 -> 14; matrix products, arithmetic and copies ran while one was open for 1% -> 1% of each run, Pallas kernels for 20% -> 21%
where the time goes in v4:
time: 124 us
  waiting for transfers between devices  56.4 us (45%)
  Pallas kernels  31.9 us (26%)
  starting transfers between devices  31.8 us (26%)
  between operations  2.36 us (2%)
    ppermute x31, waiting for transfers between devices, exchange(): return lax.ppermute(value, AXES, [(i, i ^ mask) for i in range(size)])  56.4 us
    ppermute x31, starting transfers between devices, exchange(): return lax.ppermute(value, AXES, [(i, i ^ mask) for i in range(size)])  31.8 us
    pallas_call x3, Pallas kernels, update(): pl.pallas_call(functools.partial(update_kernel, where, keep, slabs, min(s...  10.8 us
    pallas_call x2, Pallas kernels, prefetch(): pl.pallas_call(prefetch_kernel, in_specs=[pl.BlockSpec(memory_space=pl.AN...  7.01 us
    pallas_call x2, Pallas kernels, sketch_parts(): pl.pallas_call(functools.partial(sketch_kernel, first, din_local), in_spe...  6.2 us
    pallas_call x3, Pallas kernels, pack(): pl.pallas_call(functools.partial(pack_kernel, groups, width, part), in_sp...  4.92 us
    pallas_call x4, Pallas kernels, project(): pl.pallas_call(functools.partial(project_kernel, n), grid=(1,), in_specs=...  2.91 us
  transfers between devices with their start and end apart: 31, of which 14 were waited for; matrix products, arithmetic and copies ran while one was open for 1% of the time, Pallas kernels for 21%

profile of v4, /device:TPU:0, one launch (start us, length us, event | category | flops | bytes accessed | tf_op | source)
XLA Modules:
  0.0 123.7 jit_solution(4709263201502844854)
XLA Ops:
  1.9 3.7 %sketch.2 = (bf16[2048,512]{1,0:T(8,128)(2,1)S(1)}, f32[256,512]{1,0:T(8,128)S(1)}, f32[256,512]{1,0:T(8,128)S(1)}) custom-call(s32[1,1]{1,0:T(1,128)} %bitcast.56.refs_0_, s32[1,1]{1,0:T(1,128)} %bitcast.57.refs_1_, bf16[1024,2048]{1,0:T(8,128)(2,1)} %refs_0_.3), custom_call_target="tpu_custom_call" | custom-call | flops 1073741824 | bytes 6291456 | tf_op jit(solution)/shard_map/sketch/pallas_call | solution.py:224
  5.6 0.6 collective-permute-start.1
  6.2 2.5 %sketch.3 = (f32[256,512]{1,0:T(8,128)S(1)}, f32[256,512]{1,0:T(8,128)S(1)}) custom-call(bf16[1024,2048]{1,0:T(8,128)(2,1)} %refs_0_.3, bf16[2048,512]{1,0:T(8,128)(2,1)S(1)} %get-tuple-element.29.refs_1_.refs_2_.refs_4_), custom_call_target="tpu_custom_call" | custom-call | flops 1073741824 | bytes 6291456 | tf_op jit(solution)/shard_map/sketch/pallas_call | solution.py:224
  8.9 3.0 %collective-permute-start.2 = (f32[256,512]{1,0:T(8,128)S(1)}, f32[256,512]{1,0:T(8,128)S(1)}, u32[]{:S(2)}, u32[]{:S(2)}) collective-permute-start(f32[256,512]{1,0:T(8,128)S(1)} %add.66), channel_id=1, source_target_pairs={{0,2},{1,3},{2,0},{3,1},{4,6},{5,7},{6,4},{7,5},{8,10},{9,11},{10,... | collective-permute-start | bytes 1572872 | tf_op jit(solution)/shard_map/ppermute | solution.py:422
  11.9 2.0 %pack.3 = (bf16[16,256,128]{2,1,0:T(8,128)(2,1)S(1)}, bf16[16,256,128]{2,1,0:T(8,128)(2,1)S(1)}) custom-call(bf16[256,8192]{1,0:T(8,128)(2,1)} %og_ref.5), custom_call_target="tpu_custom_call" | custom-call | bytes 4194304 | tf_op jit(solution)/shard_map/pack/pallas_call | solution.py:127
  14.0 1.5 %pack.4 = (bf16[8,256,128]{2,1,0:T(8,128)(2,1)S(1)}, bf16[8,256,128]{2,1,0:T(8,128)(2,1)S(1)}) custom-call(bf16[256,8192]{1,0:T(8,128)(2,1)} %og_ref.5), custom_call_target="tpu_custom_call" | custom-call | bytes 2097152 | tf_op jit(solution)/shard_map/pack/pallas_call | solution.py:127
  15.5 1.7 %collective-permute-start.13 = (bf16[8,256,128]{2,1,0:T(8,128)(2,1)S(1)}, bf16[8,256,128]{2,1,0:T(8,128)(2,1)S(1)}, u32[]{:S(2)}, u32[]{:S(2)}) collective-permute-start(bf16[8,256,128]{2,1,0:T(8,128)(2,1)S(1)} %get-tuple-element.40), channel_id=1, source_target_pairs={{0,8},{1,9},{2,10},{3,11},{4,12},{5,13},{6,14},{7,15},{8,0},{9,1},... | collective-permute-start | bytes 1572872 | tf_op jit(solution)/shard_map/ppermute | solution.py:422
  17.1 1.5 %pack.5 = (bf16[8,256,128]{2,1,0:T(8,128)(2,1)S(1)}, bf16[8,256,128]{2,1,0:T(8,128)(2,1)S(1)}) custom-call(bf16[256,8192]{1,0:T(8,128)(2,1)} %og_ref.5), custom_call_target="tpu_custom_call" | custom-call | bytes 2097152 | tf_op jit(solution)/shard_map/pack/pallas_call | solution.py:127
  18.9 5.1 %collective-permute-done.2 = f32[256,512]{1,0:T(8,128)S(1)} collective-permute-done((f32[256,512]{1,0:T(8,128)S(1)}, f32[256,512]{1,0:T(8,128)S(1)}, u32[]{:S(2)}, u32[]{:S(2)}) %collective-permute-start.2) | collective-permute-done | bytes 524320 | tf_op jit(solution)/shard_map/ppermute | solution.py:422
  24.2 1.9 %collective-permute-start.11 = (bf16[256,512]{1,0:T(8,128)(2,1)S(1)}, bf16[256,512]{1,0:T(8,128)(2,1)S(1)}, u32[]{:S(2)}, u32[]{:S(2)}) collective-permute-start(bf16[256,512]{1,0:T(8,128)(2,1)S(1)} %multiply_convert_fusion.2.refs_0_), channel_id=1, source_target_pairs={{0,8},{1,9},{2,10},{3,11},{4,12},{5,13},{6,14},{7,15},{8,0},{9,1},... | collective-permute-start | bytes 786440 | tf_op jit(solution)/shard_map/ppermute | solution.py:422
  26.1 1.5 %collective-permute-start.4 = (bf16[256,512]{1,0:T(8,128)(2,1)S(1)}, bf16[256,512]{1,0:T(8,128)(2,1)S(1)}, u32[]{:S(2)}, u32[]{:S(2)}) collective-permute-start(bf16[256,512]{1,0:T(8,128)(2,1)S(1)} %multiply_convert_fusion.2.refs_0_), channel_id=1, source_target_pairs={{0,4},{1,5},{2,6},{3,7},{4,0},{5,1},{6,2},{7,3},{8,12},{9,13},{10,... | collective-permute-start | bytes 786440 | tf_op jit(solution)/shard_map/ppermute | solution.py:422
  27.6 2.7 %collective-permute-done.13.refs_6_ = bf16[8,256,128]{2,1,0:T(8,128)(2,1)S(1)} collective-permute-done((bf16[8,256,128]{2,1,0:T(8,128)(2,1)S(1)}, bf16[8,256,128]{2,1,0:T(8,128)(2,1)S(1)}, u32[]{:S(2)}, u32[]{:S(2)}) %collective-permute-start.13) | collective-permute-done | bytes 524320 | tf_op jit(solution)/shard_map/ppermute | solution.py:422
  30.3 16.4 %collective-permute-done.11.refs_2_ = bf16[256,512]{1,0:T(8,128)(2,1)S(1)} collective-permute-done((bf16[256,512]{1,0:T(8,128)(2,1)S(1)}, bf16[256,512]{1,0:T(8,128)(2,1)S(1)}, u32[]{:S(2)}, u32[]{:S(2)}) %collective-permute-start.11) | collective-permute-done | bytes 262176 | tf_op jit(solution)/shard_map/ppermute | solution.py:422
  46.7 1.5 %collective-permute-start.7 = (bf16[8,256,128]{2,1,0:T(8,128)(2,1)S(1)}, bf16[8,256,128]{2,1,0:T(8,128)(2,1)S(1)}, u32[]{:S(2)}, u32[]{:S(2)}) collective-permute-start(bf16[8,256,128]{2,1,0:T(8,128)(2,1)S(1)} %get-tuple-element.36), channel_id=1, source_target_pairs={{0,4},{1,5},{2,6},{3,7},{4,0},{5,1},{6,2},{7,3},{8,12},{9,13},{10,... | collective-permute-start | bytes 1572872 | tf_op jit(solution)/shard_map/ppermute | solution.py:422
  48.9 0.7 project.6
  49.7 1.6 %collective-permute-start.19 = (f16[2,128,512]{2,1,0:T(8,128)(2,1)S(1)}, f16[2,128,512]{2,1,0:T(8,128)(2,1)S(1)}, u32[]{:S(2)}, u32[]{:S(2)}) collective-permute-start(f16[2,128,512]{2,1,0:T(8,128)(2,1)S(1)} %multiply_convert_fusion), channel_id=1, source_target_pairs={{0,4},{1,5},{2,6},{3,7},{4,0},{5,1},{6,2},{7,3},{8,12},{9,13},{10,... | collective-permute-start | bytes 786440 | tf_op jit(solution)/shard_map/ppermute | solution.py:422
  51.2 10.3 %collective-permute-done.7.refs_6_ = bf16[8,256,128]{2,1,0:T(8,128)(2,1)S(1)} collective-permute-done((bf16[8,256,128]{2,1,0:T(8,128)(2,1)S(1)}, bf16[8,256,128]{2,1,0:T(8,128)(2,1)S(1)}, u32[]{:S(2)}, u32[]{:S(2)}) %collective-permute-start.7) | collective-permute-done | bytes 524320 | tf_op jit(solution)/shard_map/ppermute | solution.py:422
  61.5 10.3 %collective-permute-done.8.refs_7_ = bf16[8,256,128]{2,1,0:T(8,128)(2,1)S(1)} collective-permute-done((bf16[8,256,128]{2,1,0:T(8,128)(2,1)S(1)}, bf16[8,256,128]{2,1,0:T(8,128)(2,1)S(1)}, u32[]{:S(2)}, u32[]{:S(2)}) %collective-permute-start.8) | collective-permute-done | bytes 524320 | tf_op jit(solution)/shard_map/ppermute | solution.py:422
  71.8 0.7 project.7
  72.6 1.6 %collective-permute-start.21 = (f16[128,512]{1,0:T(8,128)(2,1)S(1)}, f16[128,512]{1,0:T(8,128)(2,1)S(1)}, u32[]{:S(2)}, u32[]{:S(2)}) collective-permute-start(f16[128,512]{1,0:T(8,128)(2,1)S(1)} %get-tuple-element.59), channel_id=1, source_target_pairs={{0,10},{1,11},{2,8},{3,9},{4,14},{5,15},{6,12},{7,13},{8,2},{9,3},... | collective-permute-start | bytes 393224 | tf_op jit(solution)/shard_map/ppermute | solution.py:422
  74.2 1.5 %collective-permute-start.22 = (f16[128,512]{1,0:T(8,128)(2,1)S(1)}, f16[128,512]{1,0:T(8,128)(2,1)S(1)}, u32[]{:S(2)}, u32[]{:S(2)}) collective-permute-start(f16[128,512]{1,0:T(8,128)(2,1)S(1)} %get-tuple-element.61), channel_id=1, source_target_pairs={{0,2},{1,3},{2,0},{3,1},{4,6},{5,7},{6,4},{7,5},{8,10},{9,11},{10,... | collective-permute-start | bytes 393224 | tf_op jit(solution)/shard_map/ppermute | solution.py:422
  75.7 0.4 collective-permute-start.23
  76.2 0.7 project.4
  77.0 1.7 %collective-permute-start.9 = (f16[2,128,512]{2,1,0:T(8,128)(2,1)S(1)}, f16[2,128,512]{2,1,0:T(8,128)(2,1)S(1)}, u32[]{:S(2)}, u32[]{:S(2)}) collective-permute-start(f16[2,128,512]{2,1,0:T(8,128)(2,1)S(1)} %multiply_convert_fusion.1), channel_id=1, source_target_pairs={{0,8},{1,9},{2,10},{3,11},{4,12},{5,13},{6,14},{7,15},{8,0},{9,1},... | collective-permute-start | bytes 786440 | tf_op jit(solution)/shard_map/ppermute | solution.py:422
  78.6 0.7 project.5
  79.4 0.6 collective-permute-done.21
  80.0 1.5 %collective-permute-start.15 = (f16[128,512]{1,0:T(8,128)(2,1)S(1)}, f16[128,512]{1,0:T(8,128)(2,1)S(1)}, u32[]{:S(2)}, u32[]{:S(2)}) collective-permute-start(f16[128,512]{1,0:T(8,128)(2,1)S(1)} %get-tuple-element.62), channel_id=1, source_target_pairs={{0,6},{1,7},{2,4},{3,5},{4,2},{5,3},{6,0},{7,1},{8,14},{9,15},{10,... | collective-permute-start | bytes 393224 | tf_op jit(solution)/shard_map/ppermute | solution.py:422
  81.5 1.1 collective-permute-done.22
  82.5 1.6 %collective-permute-start.16 = (f16[128,512]{1,0:T(8,128)(2,1)S(1)}, f16[128,512]{1,0:T(8,128)(2,1)S(1)}, u32[]{:S(2)}, u32[]{:S(2)}) collective-permute-start(f16[128,512]{1,0:T(8,128)(2,1)S(1)} %get-tuple-element.64), channel_id=1, source_target_pairs={{0,4},{1,5},{2,6},{3,7},{4,0},{5,1},{6,2},{7,3},{8,12},{9,13},{10,... | collective-permute-start | bytes 393224 | tf_op jit(solution)/shard_map/ppermute | solution.py:422
  84.1 0.6 collective-permute-start.17
  84.8 1.6 %collective-permute-done.15 = f16[128,512]{1,0:T(8,128)(2,1)S(1)} collective-permute-done((f16[128,512]{1,0:T(8,128)(2,1)S(1)}, f16[128,512]{1,0:T(8,128)(2,1)S(1)}, u32[]{:S(2)}, u32[]{:S(2)}) %collective-permute-start.15) | collective-permute-done | bytes 131104 | tf_op jit(solution)/shard_map/ppermute | solution.py:422
  86.4 2.6 %collective-permute-start.24 = (f16[128,512]{1,0:T(8,128)(2,1)S(1)}, f16[128,512]{1,0:T(8,128)(2,1)S(1)}, u32[]{:S(2)}, u32[]{:S(2)}) collective-permute-start(f16[128,512]{1,0:T(8,128)(2,1)S(1)} %fusion.3), channel_id=1, source_target_pairs={{0,16},{1,17},{2,18},{3,19},{4,20},{5,21},{6,22},{7,23},{8,24},{9,... | collective-permute-start | bytes 393224 | tf_op jit(solution)/shard_map/ppermute | solution.py:422
  89.4 2.7 %collective-permute-start.18 = (f16[128,512]{1,0:T(8,128)(2,1)S(1)}, f16[128,512]{1,0:T(8,128)(2,1)S(1)}, u32[]{:S(2)}, u32[]{:S(2)}) collective-permute-start(f16[128,512]{1,0:T(8,128)(2,1)S(1)} %fusion.10), channel_id=1, source_target_pairs={{0,16},{1,17},{2,18},{3,19},{4,20},{5,21},{6,22},{7,23},{8,24},{9,... | collective-permute-start | bytes 393224 | tf_op jit(solution)/shard_map/ppermute | solution.py:422
  92.1 0.6 collective-permute-start.20
  92.7 1.6 %collective-permute-start.10 = (f16[128,512]{1,0:T(8,128)(2,1)S(1)}, f16[128,512]{1,0:T(8,128)(2,1)S(1)}, u32[]{:S(2)}, u32[]{:S(2)}) collective-permute-start(f16[128,512]{1,0:T(8,128)(2,1)S(1)} %fusion.14), channel_id=1, source_target_pairs={{0,2},{1,3},{2,0},{3,1},{4,6},{5,7},{6,4},{7,5},{8,10},{9,11},{10,... | collective-permute-start | bytes 393224 | tf_op jit(solution)/shard_map/ppermute | solution.py:422
  94.3 3.6 %collective-permute-done.24 = f16[128,512]{1,0:T(8,128)(2,1)S(1)} collective-permute-done((f16[128,512]{1,0:T(8,128)(2,1)S(1)}, f16[128,512]{1,0:T(8,128)(2,1)S(1)}, u32[]{:S(2)}, u32[]{:S(2)}) %collective-permute-start.24) | collective-permute-done | bytes 131104 | tf_op jit(solution)/shard_map/ppermute | solution.py:422
  97.9 0.7 collective-permute-done.20
  98.7 0.8 collective-permute-start.28
  99.5 0.7 collective-permute-done.18
  100.3 0.8 collective-permute-start.25
  101.2 0.5 collective-permute-start.27
  101.7 3.1 %collective-permute-done.28 = f16[128,512]{1,0:T(8,128)(2,1)S(1)} collective-permute-done((f16[128,512]{1,0:T(8,128)(2,1)S(1)}, f16[128,512]{1,0:T(8,128)(2,1)S(1)}, u32[]{:S(2)}, u32[]{:S(2)}) %collective-permute-start.28) | collective-permute-done | bytes 131104 | tf_op jit(solution)/shard_map/ppermute | solution.py:422
  104.8 3.5 %prefetch.2.refs_3_.refs_5_ = f32[1024,2048]{1,0:T(8,128)S(1)} custom-call(f32[1024,2048]{1,0:T(8,128)} %refs_0_.4), custom_call_target="tpu_custom_call" | custom-call | bytes 8388608 | tf_op jit(solution)/shard_map/prefetch/pallas_call | solution.py:309
  108.3 3.5 %prefetch.3.refs_4_.refs_6_ = f32[1024,2048]{1,0:T(8,128)S(1)} custom-call(f32[1024,2048]{1,0:T(8,128)} %refs_0_.5), custom_call_target="tpu_custom_call" | custom-call | bytes 8388608 | tf_op jit(solution)/shard_map/prefetch/pallas_call | solution.py:309
  111.9 0.6 collective-permute-start.26
  112.6 2.9 %update.3 = (f32[1024,2048]{1,0:T(8,128)}, f32[1024,2048]{1,0:T(8,128)}, f32[256,512]{1,0:T(8,128)}) custom-call(f32[128,512]{1,0:T(8,128)S(1)} %get-tuple-element.58.refs_0_, f32[128,512]{1,0:T(8,128)S(1)} %convert_element_type.161.refs_1_, bf16[2048,512]{1,0:T(8,128)(2,1)S(1)} %get-tuple-element.29.refs_1_.refs_2_.refs_4_, ...), custom_call_target="tpu_custom_call" | custom-call | flops 1073741824 | bytes 4194304 | tf_op jit(solution)/shard_map/update/pallas_call | solution.py:391
  115.5 5.1 %update.4 = (f32[1024,2048]{1,0:T(8,128)}, f32[1024,2048]{1,0:T(8,128)}, f32[256,512]{1,0:T(8,128)}) custom-call(f32[128,512]{1,0:T(8,128)S(1)} %get-tuple-element.56.refs_0_, f32[128,512]{1,0:T(8,128)S(1)} %convert_element_type.158.refs_1_, ...), custom_call_target="tpu_custom_call", output_to_operand_aliasing={{0}: (7, {}), {1}: (8, {}), {2}: (9, {})} | custom-call | flops 2147483648 | bytes 8388608 | tf_op jit(solution)/shard_map/update/pallas_call | solution.py:391
  120.7 2.8 %update.5 = (f32[1024,2048]{1,0:T(8,128)}, f32[1024,2048]{1,0:T(8,128)}, f32[256,512]{1,0:T(8,128)}) custom-call(f32[128,512]{1,0:T(8,128)S(1)} %convert_element_type.156.refs_0_, f32[128,512]{1,0:T(8,128)S(1)} %convert_element_type.157.refs_1_, ...), custom_call_target="tpu_custom_call", output_to_operand_aliasing={{0}: (5, {}), {1}: (6, {}), {2}: (7, {})} | custom-call | flops 1073741824 | bytes 4194304 | tf_op jit(solution)/shard_map/update/pallas_call | solution.py:391
  (48 shorter events, 2.6 us)
Async XLA Ops:
  5.6 3.2 %collective-permute-start.1 = (f32[256,512]{1,0:T(8,128)S(1)}, f32[256,512]{1,0:T(8,128)S(1)}, u32[]{:S(2)}, u32[]{:S(2)}) collective-permute-start(f32[256,512]{1,0:T(8,128)S(1)} %get-tuple-element.33), channel_id=1, source_target_pairs={{0,1},{1,0},{2,3},{3,2},{4,5},{5,4},{6,7},{7,6},{8,9},{9,8},{10,11... | collective-permute-start | bytes 1572872 | tf_op jit(solution)/shard_map/ppermute | solution.py:422
  8.7 10.2 %collective-permute-start = (f32[256,512]{1,0:T(8,128)S(1)}, f32[256,512]{1,0:T(8,128)S(1)}, u32[]{:S(2)}, u32[]{:S(2)}) collective-permute-start(f32[256,512]{1,0:T(8,128)S(1)} %get-tuple-element.31), channel_id=1, source_target_pairs={{0,1},{1,0},{2,3},{3,2},{4,5},{5,4},{6,7},{7,6},{8,9},{9,8},{10,11... | collective-permute-start | bytes 1572872 | tf_op jit(solution)/shard_map/ppermute | solution.py:422
  8.9 15.1 %collective-permute-start.2 = (f32[256,512]{1,0:T(8,128)S(1)}, f32[256,512]{1,0:T(8,128)S(1)}, u32[]{:S(2)}, u32[]{:S(2)}) collective-permute-start(f32[256,512]{1,0:T(8,128)S(1)} %add.66), channel_id=1, source_target_pairs={{0,2},{1,3},{2,0},{3,1},{4,6},{5,7},{6,4},{7,5},{8,10},{9,11},{10,... | collective-permute-start | bytes 1572872 | tf_op jit(solution)/shard_map/ppermute | solution.py:422
  13.9 34.3 %collective-permute-start.6 = (bf16[16,256,128]{2,1,0:T(8,128)(2,1)S(1)}, bf16[16,256,128]{2,1,0:T(8,128)(2,1)S(1)}, u32[]{:S(2)}, u32[]{:S(2)}) collective-permute-start(bf16[16,256,128]{2,1,0:T(8,128)(2,1)S(1)} %get-tuple-element.35), channel_id=1, source_target_pairs={{0,1},{1,0},{2,3},{3,2},{4,5},{5,4},{6,7},{7,6},{8,9},{9,8},{10,11... | collective-permute-start | bytes 3145736 | tf_op jit(solution)/shard_map/ppermute | solution.py:422
  15.5 14.9 %collective-permute-start.13 = (bf16[8,256,128]{2,1,0:T(8,128)(2,1)S(1)}, bf16[8,256,128]{2,1,0:T(8,128)(2,1)S(1)}, u32[]{:S(2)}, u32[]{:S(2)}) collective-permute-start(bf16[8,256,128]{2,1,0:T(8,128)(2,1)S(1)} %get-tuple-element.40), channel_id=1, source_target_pairs={{0,8},{1,9},{2,10},{3,11},{4,12},{5,13},{6,14},{7,15},{8,0},{9,1},... | collective-permute-start | bytes 1572872 | tf_op jit(solution)/shard_map/ppermute | solution.py:422
  18.6 28.1 %collective-permute-start.14 = (bf16[8,256,128]{2,1,0:T(8,128)(2,1)S(1)}, bf16[8,256,128]{2,1,0:T(8,128)(2,1)S(1)}, u32[]{:S(2)}, u32[]{:S(2)}) collective-permute-start(bf16[8,256,128]{2,1,0:T(8,128)(2,1)S(1)} %get-tuple-element.41), channel_id=1, source_target_pairs={{0,9},{1,8},{2,11},{3,10},{4,13},{5,12},{6,15},{7,14},{8,1},{9,0},... | collective-permute-start | bytes 1572872 | tf_op jit(solution)/shard_map/ppermute | solution.py:422
  24.2 22.5 %collective-permute-start.11 = (bf16[256,512]{1,0:T(8,128)(2,1)S(1)}, bf16[256,512]{1,0:T(8,128)(2,1)S(1)}, u32[]{:S(2)}, u32[]{:S(2)}) collective-permute-start(bf16[256,512]{1,0:T(8,128)(2,1)S(1)} %multiply_convert_fusion.2.refs_0_), channel_id=1, source_target_pairs={{0,8},{1,9},{2,10},{3,11},{4,12},{5,13},{6,14},{7,15},{8,0},{9,1},... | collective-permute-start | bytes 786440 | tf_op jit(solution)/shard_map/ppermute | solution.py:422
  26.1 22.5 %collective-permute-start.4 = (bf16[256,512]{1,0:T(8,128)(2,1)S(1)}, bf16[256,512]{1,0:T(8,128)(2,1)S(1)}, u32[]{:S(2)}, u32[]{:S(2)}) collective-permute-start(bf16[256,512]{1,0:T(8,128)(2,1)S(1)} %multiply_convert_fusion.2.refs_0_), channel_id=1, source_target_pairs={{0,4},{1,5},{2,6},{3,7},{4,0},{5,1},{6,2},{7,3},{8,12},{9,13},{10,... | collective-permute-start | bytes 786440 | tf_op jit(solution)/shard_map/ppermute | solution.py:422
  30.3 18.5 %collective-permute-start.3 = (bf16[256,512]{1,0:T(8,128)(2,1)S(1)}, bf16[256,512]{1,0:T(8,128)(2,1)S(1)}, u32[]{:S(2)}, u32[]{:S(2)}) collective-permute-start(bf16[256,512]{1,0:T(8,128)(2,1)S(1)} %multiply_convert_fusion.2.refs_0_), channel_id=1, source_target_pairs={{0,1},{1,0},{2,3},{3,2},{4,5},{5,4},{6,7},{7,6},{8,9},{9,8},{10,11... | collective-permute-start | bytes 786440 | tf_op jit(solution)/shard_map/ppermute | solution.py:422
  46.7 2.2 %collective-permute-start.12 = (bf16[256,512]{1,0:T(8,128)(2,1)S(1)}, bf16[256,512]{1,0:T(8,128)(2,1)S(1)}, u32[]{:S(2)}, u32[]{:S(2)}) collective-permute-start(bf16[256,512]{1,0:T(8,128)(2,1)S(1)} %collective-permute-done.11.refs_2_), channel_id=1, source_target_pairs={{0,1},{1,0},{2,3},{3,2},{4,5},{5,4},{6,7},{7,6},{8,9},{9,8},{10,11... | collective-permute-start | bytes 786440 | tf_op jit(solution)/shard_map/ppermute | solution.py:422
  46.7 14.8 %collective-permute-start.7 = (bf16[8,256,128]{2,1,0:T(8,128)(2,1)S(1)}, bf16[8,256,128]{2,1,0:T(8,128)(2,1)S(1)}, u32[]{:S(2)}, u32[]{:S(2)}) collective-permute-start(bf16[8,256,128]{2,1,0:T(8,128)(2,1)S(1)} %get-tuple-element.36), channel_id=1, source_target_pairs={{0,4},{1,5},{2,6},{3,7},{4,0},{5,1},{6,2},{7,3},{8,12},{9,13},{10,... | collective-permute-start | bytes 1572872 | tf_op jit(solution)/shard_map/ppermute | solution.py:422
  48.2 23.6 %collective-permute-start.8 = (bf16[8,256,128]{2,1,0:T(8,128)(2,1)S(1)}, bf16[8,256,128]{2,1,0:T(8,128)(2,1)S(1)}, u32[]{:S(2)}, u32[]{:S(2)}) collective-permute-start(bf16[8,256,128]{2,1,0:T(8,128)(2,1)S(1)} %get-tuple-element.37), channel_id=1, source_target_pairs={{0,5},{1,4},{2,7},{3,6},{4,1},{5,0},{6,3},{7,2},{8,13},{9,12},{10,... | collective-permute-start | bytes 1572872 | tf_op jit(solution)/shard_map/ppermute | solution.py:422
  48.6 23.2 %collective-permute-start.5 = (bf16[256,512]{1,0:T(8,128)(2,1)S(1)}, bf16[256,512]{1,0:T(8,128)(2,1)S(1)}, u32[]{:S(2)}, u32[]{:S(2)}) collective-permute-start(bf16[256,512]{1,0:T(8,128)(2,1)S(1)} %collective-permute-done.4.refs_2_), channel_id=1, source_target_pairs={{0,1},{1,0},{2,3},{3,2},{4,5},{5,4},{6,7},{7,6},{8,9},{9,8},{10,11... | collective-permute-start | bytes 786440 | tf_op jit(solution)/shard_map/ppermute | solution.py:422
  49.6 48.9 %copy-start = (f32[256,512]{1,0:T(8,128)S(1)}, f32[256,512]{1,0:T(8,128)}, u32[]{:S(2)}) copy-start(f32[256,512]{1,0:T(8,128)} %param.11) | copy-start | bytes 1572868
  49.7 42.4 %collective-permute-start.19 = (f16[2,128,512]{2,1,0:T(8,128)(2,1)S(1)}, f16[2,128,512]{2,1,0:T(8,128)(2,1)S(1)}, u32[]{:S(2)}, u32[]{:S(2)}) collective-permute-start(f16[2,128,512]{2,1,0:T(8,128)(2,1)S(1)} %multiply_convert_fusion), channel_id=1, source_target_pairs={{0,4},{1,5},{2,6},{3,7},{4,0},{5,1},{6,2},{7,3},{8,12},{9,13},{10,... | collective-permute-start | bytes 786440 | tf_op jit(solution)/shard_map/ppermute | solution.py:422
  72.6 7.4 %collective-permute-start.21 = (f16[128,512]{1,0:T(8,128)(2,1)S(1)}, f16[128,512]{1,0:T(8,128)(2,1)S(1)}, u32[]{:S(2)}, u32[]{:S(2)}) collective-permute-start(f16[128,512]{1,0:T(8,128)(2,1)S(1)} %get-tuple-element.59), channel_id=1, source_target_pairs={{0,10},{1,11},{2,8},{3,9},{4,14},{5,15},{6,12},{7,13},{8,2},{9,3},... | collective-permute-start | bytes 393224 | tf_op jit(solution)/shard_map/ppermute | solution.py:422
  74.2 8.3 %collective-permute-start.22 = (f16[128,512]{1,0:T(8,128)(2,1)S(1)}, f16[128,512]{1,0:T(8,128)(2,1)S(1)}, u32[]{:S(2)}, u32[]{:S(2)}) collective-permute-start(f16[128,512]{1,0:T(8,128)(2,1)S(1)} %get-tuple-element.61), channel_id=1, source_target_pairs={{0,2},{1,3},{2,0},{3,1},{4,6},{5,7},{6,4},{7,5},{8,10},{9,11},{10,... | collective-permute-start | bytes 393224 | tf_op jit(solution)/shard_map/ppermute | solution.py:422
  75.7 8.4 %collective-permute-start.23 = (f16[128,512]{1,0:T(8,128)(2,1)S(1)}, f16[128,512]{1,0:T(8,128)(2,1)S(1)}, u32[]{:S(2)}, u32[]{:S(2)}) collective-permute-start(f16[128,512]{1,0:T(8,128)(2,1)S(1)} %get-tuple-element.60), channel_id=1, source_target_pairs={{0,8},{1,9},{2,10},{3,11},{4,12},{5,13},{6,14},{7,15},{8,0},{9,1},... | collective-permute-start | bytes 393224 | tf_op jit(solution)/shard_map/ppermute | solution.py:422
  77.0 15.7 %collective-permute-start.9 = (f16[2,128,512]{2,1,0:T(8,128)(2,1)S(1)}, f16[2,128,512]{2,1,0:T(8,128)(2,1)S(1)}, u32[]{:S(2)}, u32[]{:S(2)}) collective-permute-start(f16[2,128,512]{2,1,0:T(8,128)(2,1)S(1)} %multiply_convert_fusion.1), channel_id=1, source_target_pairs={{0,8},{1,9},{2,10},{3,11},{4,12},{5,13},{6,14},{7,15},{8,0},{9,1},... | collective-permute-start | bytes 786440 | tf_op jit(solution)/shard_map/ppermute | solution.py:422
  80.0 6.4 %collective-permute-start.15 = (f16[128,512]{1,0:T(8,128)(2,1)S(1)}, f16[128,512]{1,0:T(8,128)(2,1)S(1)}, u32[]{:S(2)}, u32[]{:S(2)}) collective-permute-start(f16[128,512]{1,0:T(8,128)(2,1)S(1)} %get-tuple-element.62), channel_id=1, source_target_pairs={{0,6},{1,7},{2,4},{3,5},{4,2},{5,3},{6,0},{7,1},{8,14},{9,15},{10,... | collective-permute-start | bytes 393224 | tf_op jit(solution)/shard_map/ppermute | solution.py:422
  82.5 6.6 %collective-permute-start.16 = (f16[128,512]{1,0:T(8,128)(2,1)S(1)}, f16[128,512]{1,0:T(8,128)(2,1)S(1)}, u32[]{:S(2)}, u32[]{:S(2)}) collective-permute-start(f16[128,512]{1,0:T(8,128)(2,1)S(1)} %get-tuple-element.64), channel_id=1, source_target_pairs={{0,4},{1,5},{2,6},{3,7},{4,0},{5,1},{6,2},{7,3},{8,12},{9,13},{10,... | collective-permute-start | bytes 393224 | tf_op jit(solution)/shard_map/ppermute | solution.py:422
  84.1 5.1 %collective-permute-start.17 = (f16[128,512]{1,0:T(8,128)(2,1)S(1)}, f16[128,512]{1,0:T(8,128)(2,1)S(1)}, u32[]{:S(2)}, u32[]{:S(2)}) collective-permute-start(f16[128,512]{1,0:T(8,128)(2,1)S(1)} %get-tuple-element.63), channel_id=1, source_target_pairs={{0,2},{1,3},{2,0},{3,1},{4,6},{5,7},{6,4},{7,5},{8,10},{9,11},{10,... | collective-permute-start | bytes 393224 | tf_op jit(solution)/shard_map/ppermute | solution.py:422
  86.4 11.5 %collective-permute-start.24 = (f16[128,512]{1,0:T(8,128)(2,1)S(1)}, f16[128,512]{1,0:T(8,128)(2,1)S(1)}, u32[]{:S(2)}, u32[]{:S(2)}) collective-permute-start(f16[128,512]{1,0:T(8,128)(2,1)S(1)} %fusion.3), channel_id=1, source_target_pairs={{0,16},{1,17},{2,18},{3,19},{4,20},{5,21},{6,22},{7,23},{8,24},{9,... | collective-permute-start | bytes 393224 | tf_op jit(solution)/shard_map/ppermute | solution.py:422
  89.4 10.8 %collective-permute-start.18 = (f16[128,512]{1,0:T(8,128)(2,1)S(1)}, f16[128,512]{1,0:T(8,128)(2,1)S(1)}, u32[]{:S(2)}, u32[]{:S(2)}) collective-permute-start(f16[128,512]{1,0:T(8,128)(2,1)S(1)} %fusion.10), channel_id=1, source_target_pairs={{0,16},{1,17},{2,18},{3,19},{4,20},{5,21},{6,22},{7,23},{8,24},{9,... | collective-permute-start | bytes 393224 | tf_op jit(solution)/shard_map/ppermute | solution.py:422
  92.1 6.4 %collective-permute-start.20 = (f16[128,512]{1,0:T(8,128)(2,1)S(1)}, f16[128,512]{1,0:T(8,128)(2,1)S(1)}, u32[]{:S(2)}, u32[]{:S(2)}) collective-permute-start(f16[128,512]{1,0:T(8,128)(2,1)S(1)} %fusion.18), channel_id=1, source_target_pairs={{0,2},{1,3},{2,0},{3,1},{4,6},{5,7},{6,4},{7,5},{8,10},{9,11},{10,... | collective-permute-start | bytes 393224 | tf_op jit(solution)/shard_map/ppermute | solution.py:422
  92.7 7.5 %collective-permute-start.10 = (f16[128,512]{1,0:T(8,128)(2,1)S(1)}, f16[128,512]{1,0:T(8,128)(2,1)S(1)}, u32[]{:S(2)}, u32[]{:S(2)}) collective-permute-start(f16[128,512]{1,0:T(8,128)(2,1)S(1)} %fusion.14), channel_id=1, source_target_pairs={{0,2},{1,3},{2,0},{3,1},{4,6},{5,7},{6,4},{7,5},{8,10},{9,11},{10,... | collective-permute-start | bytes 393224 | tf_op jit(solution)/shard_map/ppermute | solution.py:422
  98.7 6.2 %collective-permute-start.28 = (f16[128,512]{1,0:T(8,128)(2,1)S(1)}, f16[128,512]{1,0:T(8,128)(2,1)S(1)}, u32[]{:S(2)}, u32[]{:S(2)}) collective-permute-start(f16[128,512]{1,0:T(8,128)(2,1)S(1)} %get-tuple-element.57), channel_id=1, source_target_pairs={{0,2},{1,3},{2,0},{3,1},{4,6},{5,7},{6,4},{7,5},{8,10},{9,11},{10,... | collective-permute-start | bytes 393224 | tf_op jit(solution)/shard_map/ppermute | solution.py:422
  100.3 11.5 %collective-permute-start.25 = (f16[128,512]{1,0:T(8,128)(2,1)S(1)}, f16[128,512]{1,0:T(8,128)(2,1)S(1)}, u32[]{:S(2)}, u32[]{:S(2)}) collective-permute-start(f16[128,512]{1,0:T(8,128)(2,1)S(1)} %get-tuple-element.55), channel_id=1, source_target_pairs={{0,2},{1,3},{2,0},{3,1},{4,6},{5,7},{6,4},{7,5},{8,10},{9,11},{10,... | collective-permute-start | bytes 393224 | tf_op jit(solution)/shard_map/ppermute | solution.py:422
  101.2 11.3 %collective-permute-start.30 = (f16[128,512]{1,0:T(8,128)(2,1)S(1)}, f16[128,512]{1,0:T(8,128)(2,1)S(1)}, u32[]{:S(2)}, u32[]{:S(2)}) collective-permute-start(f16[128,512]{1,0:T(8,128)(2,1)S(1)} %get-tuple-element.57), channel_id=1, source_target_pairs={{0,1},{1,0},{2,3},{3,2},{4,5},{5,4},{6,7},{7,6},{8,9},{9,8},{10,11... | collective-permute-start | bytes 393224 | tf_op jit(solution)/shard_map/ppermute | solution.py:422
  101.2 11.4 %collective-permute-start.27 = (f16[128,512]{1,0:T(8,128)(2,1)S(1)}, f16[128,512]{1,0:T(8,128)(2,1)S(1)}, u32[]{:S(2)}, u32[]{:S(2)}) collective-permute-start(f16[128,512]{1,0:T(8,128)(2,1)S(1)} %get-tuple-element.55), channel_id=1, source_target_pairs={{0,1},{1,0},{2,3},{3,2},{4,5},{5,4},{6,7},{7,6},{8,9},{9,8},{10,11... | collective-permute-start | bytes 393224 | tf_op jit(solution)/shard_map/ppermute | solution.py:422
  104.8 10.6 %collective-permute-start.29 = (f16[128,512]{1,0:T(8,128)(2,1)S(1)}, f16[128,512]{1,0:T(8,128)(2,1)S(1)}, u32[]{:S(2)}, u32[]{:S(2)}) collective-permute-start(f16[128,512]{1,0:T(8,128)(2,1)S(1)} %collective-permute-done.28), channel_id=1, source_target_pairs={{0,1},{1,0},{2,3},{3,2},{4,5},{5,4},{6,7},{7,6},{8,9},{9,8},{10,11... | collective-permute-start | bytes 393224 | tf_op jit(solution)/shard_map/ppermute | solution.py:422
  111.9 8.8 %collective-permute-start.26 = (f16[128,512]{1,0:T(8,128)(2,1)S(1)}, f16[128,512]{1,0:T(8,128)(2,1)S(1)}, u32[]{:S(2)}, u32[]{:S(2)}) collective-permute-start(f16[128,512]{1,0:T(8,128)(2,1)S(1)} %collective-permute-done.25), channel_id=1, source_target_pairs={{0,1},{1,0},{2,3},{3,2},{4,5},{5,4},{6,7},{7,6},{8,9},{9,8},{10,11... | collective-permute-start | bytes 393224 | tf_op jit(solution)/shard_map/ppermute | solution.py:422

commit v5 on v3

--- a/solution.py
+++ b/solution.py
@@ -428,7 +428,7 @@
     total_tokens = lax.axis_size("dp") * tokens.shape[0]
     inv_root = 1.0 / jnp.sqrt(jnp.float32(low_rank))
     far0 = [(Z1 | X | Z0, 0), (Z1 | X, 0), (Z1 | Z0, 0), (Z1, 0)]
-    near0 = [(Z0 | X, 0), (Z0, 0), (X, 0), (0, 0)]
+    near0 = [(Z0 | X, 0), (X, 0), (Z0, 0), (0, 0)]
     far1 = [(Z1 | Y | X, 1), (Z1 | Y, 1), (Z1 | X, 1), (Z1, 1)]
     near1 = [(Y | X, 1), (Y, 1), (X, 1), (0, 1)]
 
@@ -502,11 +502,12 @@
 
     far0_total = direct(y_side, (0, 0, 0, 0), (X | Z0, X, Z0))
     far1_total = direct(z_side, (8, 8, 0, 0), (Y | X, Y, X))
-    near0_state = begin(y_side, (4, 4, 4, 4), Z0)
+    near0_state = begin(y_side, (4, 4, 4, 4), X)
     near1_state = begin(z_side, (12, 12, 4, 4), Y)
     last0 = exchange(packed(far0_total, 2.0), Z1)
-    last1 = exchange(packed(far1_total, 2.0), Z1)
-    near0_state = middle(near0_state, X)
+    far1_small = packed(far1_total, 2.0)
+    last1 = exchange(far1_small, Z1)
+    near0_state = middle(near0_state, Z0)
     near1_state = middle(near1_state, X)
 
     def momentum_half(half, near, last):
@@ -527,14 +528,13 @@
         others.append([v.astype(jnp.float32) for v in (from_core, from_x, from_xc)])
     done = ()
     near, far = (0, CORE), (X, X | CORE)
-    for rows, where in (
-        ((halves[0], others[0][0]), [(rel, 0) for rel in near]),
-        (
-            (halves[1], others[1][0], *others[0][1:]),
-            [(rel, 1) for rel in near] + [(rel, 0) for rel in far],
-        ),
-        (others[1][1:], [(rel, 1) for rel in far]),
+    for half, rows, relatives in (
+        (0, (halves[0], others[0][0]), near),
+        (0, others[0][1:], far),
+        (1, (halves[1], others[1][0]), near),
+        (1, others[1][1:], far),
     ):
+        where = [(rel, half) for rel in relatives]
         keep = where[0][0] == 0
         done = update(rows, tuple(where), keep, signs, weight_v, second_v, tuple(done))
     return tuple(done)

time: 125 us -> 122 us (0.976)
  waiting for transfers between devices: 55.8 us -> 51.2 us
  starting transfers between devices: 32.8 us -> 34.2 us
    ppermute x31, waiting for transfers between devices: 55.8 us -> 51.2 us  [exchange(): return lax.ppermute(value, AXES, [(i, i ^ mask) for i in range(size)])]
    ppermute x31, starting transfers between devices: 32.8 us -> 34.2 us  [exchange(): return lax.ppermute(value, AXES, [(i, i ^ mask) for i in range(size)])]
    pallas_call x3 -> x4, Pallas kernels: 10.8 us -> 11.5 us  [update(): pl.pallas_call(functools.partial(update_kernel, where, keep, slabs, min(s...]
  transfers between devices with their start and end apart: 31 -> 31, of which waited for: 10 -> 10; matrix products, arithmetic and copies ran while one was open for 1% -> 1% of each run, Pallas kernels for 20% -> 21%
where the time goes in v5:
time: 122 us
  waiting for transfers between devices  51.2 us (42%)
  starting transfers between devices  34.2 us (28%)
  Pallas kernels  32.5 us (27%)
  between operations  2.38 us (2%)
    ppermute x31, waiting for transfers between devices, exchange(): return lax.ppermute(value, AXES, [(i, i ^ mask) for i in range(size)])  51.2 us
    ppermute x31, starting transfers between devices, exchange(): return lax.ppermute(value, AXES, [(i, i ^ mask) for i in range(size)])  34.2 us
    pallas_call x4, Pallas kernels, update(): pl.pallas_call(functools.partial(update_kernel, where, keep, slabs, min(s...  11.5 us
    pallas_call x2, Pallas kernels, prefetch(): pl.pallas_call(prefetch_kernel, in_specs=[pl.BlockSpec(memory_space=pl.AN...  7.01 us
    pallas_call x2, Pallas kernels, sketch_parts(): pl.pallas_call(functools.partial(sketch_kernel, first, din_local), in_spe...  6.2 us
    pallas_call x3, Pallas kernels, pack(): pl.pallas_call(functools.partial(pack_kernel, groups, width, part), in_sp...  4.92 us
    pallas_call x4, Pallas kernels, project(): pl.pallas_call(functools.partial(project_kernel, n), grid=(1,), in_specs=...  2.91 us
  transfers between devices with their start and end apart: 31, of which 10 were waited for; matrix products, arithmetic and copies ran while one was open for 1% of the time, Pallas kernels for 21%

profile of v5, /device:TPU:0, one launch (start us, length us, event | category | flops | bytes accessed | tf_op | source)
XLA Modules:
  0.0 121.5 jit_solution(16763958588544641335)
XLA Ops:
  1.9 3.7 %sketch.2 = (bf16[2048,512]{1,0:T(8,128)(2,1)S(1)}, f32[256,512]{1,0:T(8,128)S(1)}, f32[256,512]{1,0:T(8,128)S(1)}) custom-call(s32[1,1]{1,0:T(1,128)} %bitcast.56.refs_0_, s32[1,1]{1,0:T(1,128)} %bitcast.57.refs_1_, bf16[1024,2048]{1,0:T(8,128)(2,1)} %refs_0_.3), custom_call_target="tpu_custom_call" | custom-call | flops 1073741824 | bytes 6291456 | tf_op jit(solution)/shard_map/sketch/pallas_call | solution.py:224
  5.6 0.6 collective-permute-start.1
  6.2 2.5 %sketch.3 = (f32[256,512]{1,0:T(8,128)S(1)}, f32[256,512]{1,0:T(8,128)S(1)}) custom-call(bf16[1024,2048]{1,0:T(8,128)(2,1)} %refs_0_.3, bf16[2048,512]{1,0:T(8,128)(2,1)S(1)} %get-tuple-element.32.refs_1_.refs_2_), custom_call_target="tpu_custom_call" | custom-call | flops 1073741824 | bytes 6291456 | tf_op jit(solution)/shard_map/sketch/pallas_call | solution.py:224
  8.9 3.0 %collective-permute-start.2 = (f32[256,512]{1,0:T(8,128)S(1)}, f32[256,512]{1,0:T(8,128)S(1)}, u32[]{:S(2)}, u32[]{:S(2)}) collective-permute-start(f32[256,512]{1,0:T(8,128)S(1)} %add.66), channel_id=1, source_target_pairs={{0,2},{1,3},{2,0},{3,1},{4,6},{5,7},{6,4},{7,5},{8,10},{9,11},{10,... | collective-permute-start | bytes 1572872 | tf_op jit(solution)/shard_map/ppermute | solution.py:422
  11.9 2.0 %pack.3 = (bf16[16,256,128]{2,1,0:T(8,128)(2,1)S(1)}, bf16[16,256,128]{2,1,0:T(8,128)(2,1)S(1)}) custom-call(bf16[256,8192]{1,0:T(8,128)(2,1)} %og_ref.5), custom_call_target="tpu_custom_call" | custom-call | bytes 4194304 | tf_op jit(solution)/shard_map/pack/pallas_call | solution.py:127
  14.0 1.5 %pack.5 = (bf16[8,256,128]{2,1,0:T(8,128)(2,1)S(1)}, bf16[8,256,128]{2,1,0:T(8,128)(2,1)S(1)}) custom-call(bf16[256,8192]{1,0:T(8,128)(2,1)} %og_ref.5), custom_call_target="tpu_custom_call" | custom-call | bytes 2097152 | tf_op jit(solution)/shard_map/pack/pallas_call | solution.py:127
  15.5 1.7 %collective-permute-start.18 = (bf16[8,256,128]{2,1,0:T(8,128)(2,1)S(1)}, bf16[8,256,128]{2,1,0:T(8,128)(2,1)S(1)}, u32[]{:S(2)}, u32[]{:S(2)}) collective-permute-start(bf16[8,256,128]{2,1,0:T(8,128)(2,1)S(1)} %get-tuple-element.46), channel_id=1, source_target_pairs={{0,5},{1,4},{2,7},{3,6},{4,1},{5,0},{6,3},{7,2},{8,13},{9,12},{10,... | collective-permute-start | bytes 1572872 | tf_op jit(solution)/shard_map/ppermute | solution.py:422
  17.1 1.5 %pack.4 = (bf16[8,256,128]{2,1,0:T(8,128)(2,1)S(1)}, bf16[8,256,128]{2,1,0:T(8,128)(2,1)S(1)}) custom-call(bf16[256,8192]{1,0:T(8,128)(2,1)} %og_ref.5), custom_call_target="tpu_custom_call" | custom-call | bytes 2097152 | tf_op jit(solution)/shard_map/pack/pallas_call | solution.py:127
  18.6 0.6 collective-permute-start.17
  19.2 4.8 %collective-permute-done.2 = f32[256,512]{1,0:T(8,128)S(1)} collective-permute-done((f32[256,512]{1,0:T(8,128)S(1)}, f32[256,512]{1,0:T(8,128)S(1)}, u32[]{:S(2)}, u32[]{:S(2)}) %collective-permute-start.2) | collective-permute-done | bytes 524320 | tf_op jit(solution)/shard_map/ppermute | solution.py:422
  24.2 1.8 %collective-permute-start.15 = (bf16[256,512]{1,0:T(8,128)(2,1)S(1)}, bf16[256,512]{1,0:T(8,128)(2,1)S(1)}, u32[]{:S(2)}, u32[]{:S(2)}) collective-permute-start(bf16[256,512]{1,0:T(8,128)(2,1)S(1)} %multiply_convert_fusion.2.refs_0_), channel_id=1, source_target_pairs={{0,4},{1,5},{2,6},{3,7},{4,0},{5,1},{6,2},{7,3},{8,12},{9,13},{10,... | collective-permute-start | bytes 786440 | tf_op jit(solution)/shard_map/ppermute | solution.py:422
  26.0 1.6 %collective-permute-start.4 = (bf16[256,512]{1,0:T(8,128)(2,1)S(1)}, bf16[256,512]{1,0:T(8,128)(2,1)S(1)}, u32[]{:S(2)}, u32[]{:S(2)}) collective-permute-start(bf16[256,512]{1,0:T(8,128)(2,1)S(1)} %multiply_convert_fusion.2.refs_0_), channel_id=1, source_target_pairs={{0,8},{1,9},{2,10},{3,11},{4,12},{5,13},{6,14},{7,15},{8,0},{9,1},... | collective-permute-start | bytes 786440 | tf_op jit(solution)/shard_map/ppermute | solution.py:422
  27.6 1.8 %collective-permute-done.18.refs_7_ = bf16[8,256,128]{2,1,0:T(8,128)(2,1)S(1)} collective-permute-done((bf16[8,256,128]{2,1,0:T(8,128)(2,1)S(1)}, bf16[8,256,128]{2,1,0:T(8,128)(2,1)S(1)}, u32[]{:S(2)}, u32[]{:S(2)}) %collective-permute-start.18) | collective-permute-done | bytes 524320 | tf_op jit(solution)/shard_map/ppermute | solution.py:422
  29.4 1.1 collective-permute-start.3
  30.5 16.1 %collective-permute-done.15.refs_2_ = bf16[256,512]{1,0:T(8,128)(2,1)S(1)} collective-permute-done((bf16[256,512]{1,0:T(8,128)(2,1)S(1)}, bf16[256,512]{1,0:T(8,128)(2,1)S(1)}, u32[]{:S(2)}, u32[]{:S(2)}) %collective-permute-start.15) | collective-permute-done | bytes 262176 | tf_op jit(solution)/shard_map/ppermute | solution.py:422
  46.6 1.7 %collective-permute-start.8 = (bf16[8,256,128]{2,1,0:T(8,128)(2,1)S(1)}, bf16[8,256,128]{2,1,0:T(8,128)(2,1)S(1)}, u32[]{:S(2)}, u32[]{:S(2)}) collective-permute-start(bf16[8,256,128]{2,1,0:T(8,128)(2,1)S(1)} %get-tuple-element.40), channel_id=1, source_target_pairs={{0,9},{1,8},{2,11},{3,10},{4,13},{5,12},{6,15},{7,14},{8,1},{9,0},... | collective-permute-start | bytes 1572872 | tf_op jit(solution)/shard_map/ppermute | solution.py:422
  48.3 0.4 collective-permute-start.7
  48.8 0.7 project.6
  49.6 0.5 collective-permute-start.19
  50.0 0.7 project.7
  50.9 2.7 %collective-permute-start.21 = (f16[128,512]{1,0:T(8,128)(2,1)S(1)}, f16[128,512]{1,0:T(8,128)(2,1)S(1)}, u32[]{:S(2)}, u32[]{:S(2)}) collective-permute-start(f16[128,512]{1,0:T(8,128)(2,1)S(1)} %get-tuple-element.65), channel_id=1, source_target_pairs={{0,10},{1,11},{2,8},{3,9},{4,14},{5,15},{6,12},{7,13},{8,2},{9,3},... | collective-permute-start | bytes 393224 | tf_op jit(solution)/shard_map/ppermute | solution.py:422
  53.6 7.1 %collective-permute-done.8.refs_7_ = bf16[8,256,128]{2,1,0:T(8,128)(2,1)S(1)} collective-permute-done((bf16[8,256,128]{2,1,0:T(8,128)(2,1)S(1)}, bf16[8,256,128]{2,1,0:T(8,128)(2,1)S(1)}, u32[]{:S(2)}, u32[]{:S(2)}) %collective-permute-start.8) | collective-permute-done | bytes 524320 | tf_op jit(solution)/shard_map/ppermute | solution.py:422
  60.6 1.1 collective-permute-start.23
  61.7 11.0 %collective-permute-done.7.refs_6_ = bf16[8,256,128]{2,1,0:T(8,128)(2,1)S(1)} collective-permute-done((bf16[8,256,128]{2,1,0:T(8,128)(2,1)S(1)}, bf16[8,256,128]{2,1,0:T(8,128)(2,1)S(1)}, u32[]{:S(2)}, u32[]{:S(2)}) %collective-permute-start.7) | collective-permute-done | bytes 524320 | tf_op jit(solution)/shard_map/ppermute | solution.py:422
  73.2 0.7 project.4
  73.9 1.7 %collective-permute-start.9 = (f16[2,128,512]{2,1,0:T(8,128)(2,1)S(1)}, f16[2,128,512]{2,1,0:T(8,128)(2,1)S(1)}, u32[]{:S(2)}, u32[]{:S(2)}) collective-permute-start(f16[2,128,512]{2,1,0:T(8,128)(2,1)S(1)} %multiply_convert_fusion.1), channel_id=1, source_target_pairs={{0,4},{1,5},{2,6},{3,7},{4,0},{5,1},{6,2},{7,3},{8,12},{9,13},{10,... | collective-permute-start | bytes 786440 | tf_op jit(solution)/shard_map/ppermute | solution.py:422
  75.7 0.7 project.5
  76.5 1.5 %collective-permute-start.11 = (f16[128,512]{1,0:T(8,128)(2,1)S(1)}, f16[128,512]{1,0:T(8,128)(2,1)S(1)}, u32[]{:S(2)}, u32[]{:S(2)}) collective-permute-start(f16[128,512]{1,0:T(8,128)(2,1)S(1)} %get-tuple-element.68), channel_id=1, source_target_pairs={{0,6},{1,7},{2,4},{3,5},{4,2},{5,3},{6,0},{7,1},{8,14},{9,15},{10,... | collective-permute-start | bytes 393224 | tf_op jit(solution)/shard_map/ppermute | solution.py:422
  78.0 0.5 collective-permute-start.13
  78.5 1.5 %collective-permute-start.12 = (f16[128,512]{1,0:T(8,128)(2,1)S(1)}, f16[128,512]{1,0:T(8,128)(2,1)S(1)}, u32[]{:S(2)}, u32[]{:S(2)}) collective-permute-start(f16[128,512]{1,0:T(8,128)(2,1)S(1)} %get-tuple-element.70), channel_id=1, source_target_pairs={{0,4},{1,5},{2,6},{3,7},{4,0},{5,1},{6,2},{7,3},{8,12},{9,13},{10,... | collective-permute-start | bytes 393224 | tf_op jit(solution)/shard_map/ppermute | solution.py:422
  80.2 3.4 %collective-permute-done.11 = f16[128,512]{1,0:T(8,128)(2,1)S(1)} collective-permute-done((f16[128,512]{1,0:T(8,128)(2,1)S(1)}, f16[128,512]{1,0:T(8,128)(2,1)S(1)}, u32[]{:S(2)}, u32[]{:S(2)}) %collective-permute-start.11) | collective-permute-done | bytes 131104 | tf_op jit(solution)/shard_map/ppermute | solution.py:422
  83.6 2.6 %collective-permute-start.24 = (f16[128,512]{1,0:T(8,128)(2,1)S(1)}, f16[128,512]{1,0:T(8,128)(2,1)S(1)}, u32[]{:S(2)}, u32[]{:S(2)}) collective-permute-start(f16[128,512]{1,0:T(8,128)(2,1)S(1)} %fusion.3), channel_id=1, source_target_pairs={{0,16},{1,17},{2,18},{3,19},{4,20},{5,21},{6,22},{7,23},{8,24},{9,... | collective-permute-start | bytes 393224 | tf_op jit(solution)/shard_map/ppermute | solution.py:422
  86.6 2.6 %collective-permute-start.14 = (f16[128,512]{1,0:T(8,128)(2,1)S(1)}, f16[128,512]{1,0:T(8,128)(2,1)S(1)}, u32[]{:S(2)}, u32[]{:S(2)}) collective-permute-start(f16[128,512]{1,0:T(8,128)(2,1)S(1)} %fusion.10), channel_id=1, source_target_pairs={{0,16},{1,17},{2,18},{3,19},{4,20},{5,21},{6,22},{7,23},{8,24},{9,... | collective-permute-start | bytes 393224 | tf_op jit(solution)/shard_map/ppermute | solution.py:422
  89.3 1.6 %collective-permute-start.20 = (f16[128,512]{1,0:T(8,128)(2,1)S(1)}, f16[128,512]{1,0:T(8,128)(2,1)S(1)}, u32[]{:S(2)}, u32[]{:S(2)}) collective-permute-start(f16[128,512]{1,0:T(8,128)(2,1)S(1)} %fusion.18), channel_id=1, source_target_pairs={{0,8},{1,9},{2,10},{3,11},{4,12},{5,13},{6,14},{7,15},{8,0},{9,1},... | collective-permute-start | bytes 393224 | tf_op jit(solution)/shard_map/ppermute | solution.py:422
  91.0 1.6 %collective-permute-start.10 = (f16[128,512]{1,0:T(8,128)(2,1)S(1)}, f16[128,512]{1,0:T(8,128)(2,1)S(1)}, u32[]{:S(2)}, u32[]{:S(2)}) collective-permute-start(f16[128,512]{1,0:T(8,128)(2,1)S(1)} %fusion.14), channel_id=1, source_target_pairs={{0,2},{1,3},{2,0},{3,1},{4,6},{5,7},{6,4},{7,5},{8,10},{9,11},{10,... | collective-permute-start | bytes 393224 | tf_op jit(solution)/shard_map/ppermute | solution.py:422
  92.5 2.5 %collective-permute-done.24 = f16[128,512]{1,0:T(8,128)(2,1)S(1)} collective-permute-done((f16[128,512]{1,0:T(8,128)(2,1)S(1)}, f16[128,512]{1,0:T(8,128)(2,1)S(1)}, u32[]{:S(2)}, u32[]{:S(2)}) %collective-permute-start.24) | collective-permute-done | bytes 131104 | tf_op jit(solution)/shard_map/ppermute | solution.py:422
  95.0 1.8 %collective-permute-done.20 = f16[128,512]{1,0:T(8,128)(2,1)S(1)} collective-permute-done((f16[128,512]{1,0:T(8,128)(2,1)S(1)}, f16[128,512]{1,0:T(8,128)(2,1)S(1)}, u32[]{:S(2)}, u32[]{:S(2)}) %collective-permute-start.20) | collective-permute-done | bytes 131104 | tf_op jit(solution)/shard_map/ppermute | solution.py:422
  97.0 1.0 collective-permute-start.28
  98.1 1.2 collective-permute-start.25
  99.3 0.5 collective-permute-start.27
  99.8 2.2 %collective-permute-done.28 = f16[128,512]{1,0:T(8,128)(2,1)S(1)} collective-permute-done((f16[128,512]{1,0:T(8,128)(2,1)S(1)}, f16[128,512]{1,0:T(8,128)(2,1)S(1)}, u32[]{:S(2)}, u32[]{:S(2)}) %collective-permute-start.28) | collective-permute-done | bytes 131104 | tf_op jit(solution)/shard_map/ppermute | solution.py:422
  102.0 3.5 %prefetch.2.refs_3_ = f32[1024,2048]{1,0:T(8,128)S(1)} custom-call(f32[1024,2048]{1,0:T(8,128)} %refs_0_.4), custom_call_target="tpu_custom_call" | custom-call | bytes 8388608 | tf_op jit(solution)/shard_map/prefetch/pallas_call | solution.py:309
  105.6 3.5 %prefetch.3.refs_4_ = f32[1024,2048]{1,0:T(8,128)S(1)} custom-call(f32[1024,2048]{1,0:T(8,128)} %refs_0_.5), custom_call_target="tpu_custom_call" | custom-call | bytes 8388608 | tf_op jit(solution)/shard_map/prefetch/pallas_call | solution.py:309
  109.1 0.6 collective-permute-start.26
  109.8 2.9 %update.4 = (f32[1024,2048]{1,0:T(8,128)}, f32[1024,2048]{1,0:T(8,128)}, f32[256,512]{1,0:T(8,128)}) custom-call(f32[128,512]{1,0:T(8,128)S(1)} %get-tuple-element.64.refs_0_, f32[128,512]{1,0:T(8,128)S(1)} %convert_element_type.161.refs_1_, bf16[2048,512]{1,0:T(8,128)(2,1)S(1)} %get-tuple-element.32.refs_1_.refs_2_, f32[1024,2048]{1,0:T(8,128)S(1)} %prefetch.2.refs_3_, ...), custom_call_target="tpu_custom_call" | custom-call | flops 1073741824 | bytes 4194304 | tf_op jit(solution)/shard_map/update/pallas_call | solution.py:391
  112.7 2.8 %update.5 = (f32[1024,2048]{1,0:T(8,128)}, f32[1024,2048]{1,0:T(8,128)}, f32[256,512]{1,0:T(8,128)}) custom-call(f32[128,512]{1,0:T(8,128)S(1)} %convert_element_type.159.refs_0_, f32[128,512]{1,0:T(8,128)S(1)} %convert_element_type.160.refs_1_, ...), custom_call_target="tpu_custom_call", output_to_operand_aliasing={{0}: (5, {}), {1}: (6, {}), {2}: (7, {})} | custom-call | flops 1073741824 | bytes 4194304 | tf_op jit(solution)/shard_map/update/pallas_call | solution.py:391
  115.6 2.9 %update.6 = (f32[1024,2048]{1,0:T(8,128)}, f32[1024,2048]{1,0:T(8,128)}, f32[256,512]{1,0:T(8,128)}) custom-call(f32[128,512]{1,0:T(8,128)S(1)} %get-tuple-element.62.refs_0_, f32[128,512]{1,0:T(8,128)S(1)} %convert_element_type.158.refs_1_, ...), custom_call_target="tpu_custom_call", output_to_operand_aliasing={{0}: (5, {}), {1}: (6, {}), {2}: (7, {})} | custom-call | flops 1073741824 | bytes 4194304 | tf_op jit(solution)/shard_map/update/pallas_call | solution.py:391
  118.5 2.8 %update.7 = (f32[1024,2048]{1,0:T(8,128)}, f32[1024,2048]{1,0:T(8,128)}, f32[256,512]{1,0:T(8,128)}) custom-call(f32[128,512]{1,0:T(8,128)S(1)} %convert_element_type.156.refs_0_, f32[128,512]{1,0:T(8,128)S(1)} %convert_element_type.157.refs_1_, ...), custom_call_target="tpu_custom_call", output_to_operand_aliasing={{0}: (5, {}), {1}: (6, {}), {2}: (7, {})} | custom-call | flops 1073741824 | bytes 4194304 | tf_op jit(solution)/shard_map/update/pallas_call | solution.py:391
  (49 shorter events, 2.1 us)
Async XLA Ops:
  5.6 3.2 %collective-permute-start.1 = (f32[256,512]{1,0:T(8,128)S(1)}, f32[256,512]{1,0:T(8,128)S(1)}, u32[]{:S(2)}, u32[]{:S(2)}) collective-permute-start(f32[256,512]{1,0:T(8,128)S(1)} %get-tuple-element.36), channel_id=1, source_target_pairs={{0,1},{1,0},{2,3},{3,2},{4,5},{5,4},{6,7},{7,6},{8,9},{9,8},{10,11... | collective-permute-start | bytes 1572872 | tf_op jit(solution)/shard_map/ppermute | solution.py:422
  8.7 10.5 %collective-permute-start = (f32[256,512]{1,0:T(8,128)S(1)}, f32[256,512]{1,0:T(8,128)S(1)}, u32[]{:S(2)}, u32[]{:S(2)}) collective-permute-start(f32[256,512]{1,0:T(8,128)S(1)} %get-tuple-element.34), channel_id=1, source_target_pairs={{0,1},{1,0},{2,3},{3,2},{4,5},{5,4},{6,7},{7,6},{8,9},{9,8},{10,11... | collective-permute-start | bytes 1572872 | tf_op jit(solution)/shard_map/ppermute | solution.py:422
  8.9 15.1 %collective-permute-start.2 = (f32[256,512]{1,0:T(8,128)S(1)}, f32[256,512]{1,0:T(8,128)S(1)}, u32[]{:S(2)}, u32[]{:S(2)}) collective-permute-start(f32[256,512]{1,0:T(8,128)S(1)} %add.66), channel_id=1, source_target_pairs={{0,2},{1,3},{2,0},{3,1},{4,6},{5,7},{6,4},{7,5},{8,10},{9,11},{10,... | collective-permute-start | bytes 1572872 | tf_op jit(solution)/shard_map/ppermute | solution.py:422
  13.9 34.4 %collective-permute-start.6 = (bf16[16,256,128]{2,1,0:T(8,128)(2,1)S(1)}, bf16[16,256,128]{2,1,0:T(8,128)(2,1)S(1)}, u32[]{:S(2)}, u32[]{:S(2)}) collective-permute-start(bf16[16,256,128]{2,1,0:T(8,128)(2,1)S(1)} %get-tuple-element.38), channel_id=1, source_target_pairs={{0,1},{1,0},{2,3},{3,2},{4,5},{5,4},{6,7},{7,6},{8,9},{9,8},{10,11... | collective-permute-start | bytes 3145736 | tf_op jit(solution)/shard_map/ppermute | solution.py:422
  15.5 14.0 %collective-permute-start.18 = (bf16[8,256,128]{2,1,0:T(8,128)(2,1)S(1)}, bf16[8,256,128]{2,1,0:T(8,128)(2,1)S(1)}, u32[]{:S(2)}, u32[]{:S(2)}) collective-permute-start(bf16[8,256,128]{2,1,0:T(8,128)(2,1)S(1)} %get-tuple-element.46), channel_id=1, source_target_pairs={{0,5},{1,4},{2,7},{3,6},{4,1},{5,0},{6,3},{7,2},{8,13},{9,12},{10,... | collective-permute-start | bytes 1572872 | tf_op jit(solution)/shard_map/ppermute | solution.py:422
  18.6 28.0 %collective-permute-start.17 = (bf16[8,256,128]{2,1,0:T(8,128)(2,1)S(1)}, bf16[8,256,128]{2,1,0:T(8,128)(2,1)S(1)}, u32[]{:S(2)}, u32[]{:S(2)}) collective-permute-start(bf16[8,256,128]{2,1,0:T(8,128)(2,1)S(1)} %get-tuple-element.45), channel_id=1, source_target_pairs={{0,4},{1,5},{2,6},{3,7},{4,0},{5,1},{6,2},{7,3},{8,12},{9,13},{10,... | collective-permute-start | bytes 1572872 | tf_op jit(solution)/shard_map/ppermute | solution.py:422
  24.2 22.4 %collective-permute-start.15 = (bf16[256,512]{1,0:T(8,128)(2,1)S(1)}, bf16[256,512]{1,0:T(8,128)(2,1)S(1)}, u32[]{:S(2)}, u32[]{:S(2)}) collective-permute-start(bf16[256,512]{1,0:T(8,128)(2,1)S(1)} %multiply_convert_fusion.2.refs_0_), channel_id=1, source_target_pairs={{0,4},{1,5},{2,6},{3,7},{4,0},{5,1},{6,2},{7,3},{8,12},{9,13},{10,... | collective-permute-start | bytes 786440 | tf_op jit(solution)/shard_map/ppermute | solution.py:422
  26.0 22.7 %collective-permute-start.4 = (bf16[256,512]{1,0:T(8,128)(2,1)S(1)}, bf16[256,512]{1,0:T(8,128)(2,1)S(1)}, u32[]{:S(2)}, u32[]{:S(2)}) collective-permute-start(bf16[256,512]{1,0:T(8,128)(2,1)S(1)} %multiply_convert_fusion.2.refs_0_), channel_id=1, source_target_pairs={{0,8},{1,9},{2,10},{3,11},{4,12},{5,13},{6,14},{7,15},{8,0},{9,1},... | collective-permute-start | bytes 786440 | tf_op jit(solution)/shard_map/ppermute | solution.py:422
  29.4 19.3 %collective-permute-start.3 = (bf16[256,512]{1,0:T(8,128)(2,1)S(1)}, bf16[256,512]{1,0:T(8,128)(2,1)S(1)}, u32[]{:S(2)}, u32[]{:S(2)}) collective-permute-start(bf16[256,512]{1,0:T(8,128)(2,1)S(1)} %multiply_convert_fusion.2.refs_0_), channel_id=1, source_target_pairs={{0,1},{1,0},{2,3},{3,2},{4,5},{5,4},{6,7},{7,6},{8,9},{9,8},{10,11... | collective-permute-start | bytes 786440 | tf_op jit(solution)/shard_map/ppermute | solution.py:422
  46.6 2.2 %collective-permute-start.16 = (bf16[256,512]{1,0:T(8,128)(2,1)S(1)}, bf16[256,512]{1,0:T(8,128)(2,1)S(1)}, u32[]{:S(2)}, u32[]{:S(2)}) collective-permute-start(bf16[256,512]{1,0:T(8,128)(2,1)S(1)} %collective-permute-done.15.refs_2_), channel_id=1, source_target_pairs={{0,1},{1,0},{2,3},{3,2},{4,5},{5,4},{6,7},{7,6},{8,9},{9,8},{10,11... | collective-permute-start | bytes 786440 | tf_op jit(solution)/shard_map/ppermute | solution.py:422
  46.6 14.0 %collective-permute-start.8 = (bf16[8,256,128]{2,1,0:T(8,128)(2,1)S(1)}, bf16[8,256,128]{2,1,0:T(8,128)(2,1)S(1)}, u32[]{:S(2)}, u32[]{:S(2)}) collective-permute-start(bf16[8,256,128]{2,1,0:T(8,128)(2,1)S(1)} %get-tuple-element.40), channel_id=1, source_target_pairs={{0,9},{1,8},{2,11},{3,10},{4,13},{5,12},{6,15},{7,14},{8,1},{9,0},... | collective-permute-start | bytes 1572872 | tf_op jit(solution)/shard_map/ppermute | solution.py:422
  48.3 24.5 %collective-permute-start.7 = (bf16[8,256,128]{2,1,0:T(8,128)(2,1)S(1)}, bf16[8,256,128]{2,1,0:T(8,128)(2,1)S(1)}, u32[]{:S(2)}, u32[]{:S(2)}) collective-permute-start(bf16[8,256,128]{2,1,0:T(8,128)(2,1)S(1)} %get-tuple-element.39), channel_id=1, source_target_pairs={{0,8},{1,9},{2,10},{3,11},{4,12},{5,13},{6,14},{7,15},{8,0},{9,1},... | collective-permute-start | bytes 1572872 | tf_op jit(solution)/shard_map/ppermute | solution.py:422
  48.8 24.4 %collective-permute-start.5 = (bf16[256,512]{1,0:T(8,128)(2,1)S(1)}, bf16[256,512]{1,0:T(8,128)(2,1)S(1)}, u32[]{:S(2)}, u32[]{:S(2)}) collective-permute-start(bf16[256,512]{1,0:T(8,128)(2,1)S(1)} %collective-permute-done.4.refs_2_), channel_id=1, source_target_pairs={{0,1},{1,0},{2,3},{3,2},{4,5},{5,4},{6,7},{7,6},{8,9},{9,8},{10,11... | collective-permute-start | bytes 786440 | tf_op jit(solution)/shard_map/ppermute | solution.py:422
  49.6 47.3 %copy-start = (f32[256,512]{1,0:T(8,128)S(1)}, f32[256,512]{1,0:T(8,128)}, u32[]{:S(2)}) copy-start(f32[256,512]{1,0:T(8,128)} %param.11) | copy-start | bytes 1572868
  49.6 39.6 %collective-permute-start.19 = (f16[2,128,512]{2,1,0:T(8,128)(2,1)S(1)}, f16[2,128,512]{2,1,0:T(8,128)(2,1)S(1)}, u32[]{:S(2)}, u32[]{:S(2)}) collective-permute-start(f16[2,128,512]{2,1,0:T(8,128)(2,1)S(1)} %multiply_convert_fusion), channel_id=1, source_target_pairs={{0,2},{1,3},{2,0},{3,1},{4,6},{5,7},{6,4},{7,5},{8,10},{9,11},{10,... | collective-permute-start | bytes 786440 | tf_op jit(solution)/shard_map/ppermute | solution.py:422
  50.9 25.6 %collective-permute-start.21 = (f16[128,512]{1,0:T(8,128)(2,1)S(1)}, f16[128,512]{1,0:T(8,128)(2,1)S(1)}, u32[]{:S(2)}, u32[]{:S(2)}) collective-permute-start(f16[128,512]{1,0:T(8,128)(2,1)S(1)} %get-tuple-element.65), channel_id=1, source_target_pairs={{0,10},{1,11},{2,8},{3,9},{4,14},{5,15},{6,12},{7,13},{8,2},{9,3},... | collective-permute-start | bytes 393224 | tf_op jit(solution)/shard_map/ppermute | solution.py:422
  60.6 17.4 %collective-permute-start.23 = (f16[128,512]{1,0:T(8,128)(2,1)S(1)}, f16[128,512]{1,0:T(8,128)(2,1)S(1)}, u32[]{:S(2)}, u32[]{:S(2)}) collective-permute-start(f16[128,512]{1,0:T(8,128)(2,1)S(1)} %get-tuple-element.66), channel_id=1, source_target_pairs={{0,8},{1,9},{2,10},{3,11},{4,12},{5,13},{6,14},{7,15},{8,0},{9,1},... | collective-permute-start | bytes 393224 | tf_op jit(solution)/shard_map/ppermute | solution.py:422
  72.8 5.8 %collective-permute-start.22 = (f16[128,512]{1,0:T(8,128)(2,1)S(1)}, f16[128,512]{1,0:T(8,128)(2,1)S(1)}, u32[]{:S(2)}, u32[]{:S(2)}) collective-permute-start(f16[128,512]{1,0:T(8,128)(2,1)S(1)} %get-tuple-element.67), channel_id=1, source_target_pairs={{0,2},{1,3},{2,0},{3,1},{4,6},{5,7},{6,4},{7,5},{8,10},{9,11},{10,... | collective-permute-start | bytes 393224 | tf_op jit(solution)/shard_map/ppermute | solution.py:422
  73.9 17.0 %collective-permute-start.9 = (f16[2,128,512]{2,1,0:T(8,128)(2,1)S(1)}, f16[2,128,512]{2,1,0:T(8,128)(2,1)S(1)}, u32[]{:S(2)}, u32[]{:S(2)}) collective-permute-start(f16[2,128,512]{2,1,0:T(8,128)(2,1)S(1)} %multiply_convert_fusion.1), channel_id=1, source_target_pairs={{0,4},{1,5},{2,6},{3,7},{4,0},{5,1},{6,2},{7,3},{8,12},{9,13},{10,... | collective-permute-start | bytes 786440 | tf_op jit(solution)/shard_map/ppermute | solution.py:422
  76.5 7.1 %collective-permute-start.11 = (f16[128,512]{1,0:T(8,128)(2,1)S(1)}, f16[128,512]{1,0:T(8,128)(2,1)S(1)}, u32[]{:S(2)}, u32[]{:S(2)}) collective-permute-start(f16[128,512]{1,0:T(8,128)(2,1)S(1)} %get-tuple-element.68), channel_id=1, source_target_pairs={{0,6},{1,7},{2,4},{3,5},{4,2},{5,3},{6,0},{7,1},{8,14},{9,15},{10,... | collective-permute-start | bytes 393224 | tf_op jit(solution)/shard_map/ppermute | solution.py:422
  78.0 8.2 %collective-permute-start.13 = (f16[128,512]{1,0:T(8,128)(2,1)S(1)}, f16[128,512]{1,0:T(8,128)(2,1)S(1)}, u32[]{:S(2)}, u32[]{:S(2)}) collective-permute-start(f16[128,512]{1,0:T(8,128)(2,1)S(1)} %get-tuple-element.69), channel_id=1, source_target_pairs={{0,2},{1,3},{2,0},{3,1},{4,6},{5,7},{6,4},{7,5},{8,10},{9,11},{10,... | collective-permute-start | bytes 393224 | tf_op jit(solution)/shard_map/ppermute | solution.py:422
  78.5 7.9 %collective-permute-start.12 = (f16[128,512]{1,0:T(8,128)(2,1)S(1)}, f16[128,512]{1,0:T(8,128)(2,1)S(1)}, u32[]{:S(2)}, u32[]{:S(2)}) collective-permute-start(f16[128,512]{1,0:T(8,128)(2,1)S(1)} %get-tuple-element.70), channel_id=1, source_target_pairs={{0,4},{1,5},{2,6},{3,7},{4,0},{5,1},{6,2},{7,3},{8,12},{9,13},{10,... | collective-permute-start | bytes 393224 | tf_op jit(solution)/shard_map/ppermute | solution.py:422
  83.6 11.4 %collective-permute-start.24 = (f16[128,512]{1,0:T(8,128)(2,1)S(1)}, f16[128,512]{1,0:T(8,128)(2,1)S(1)}, u32[]{:S(2)}, u32[]{:S(2)}) collective-permute-start(f16[128,512]{1,0:T(8,128)(2,1)S(1)} %fusion.3), channel_id=1, source_target_pairs={{0,16},{1,17},{2,18},{3,19},{4,20},{5,21},{6,22},{7,23},{8,24},{9,... | collective-permute-start | bytes 393224 | tf_op jit(solution)/shard_map/ppermute | solution.py:422
  86.6 11.4 %collective-permute-start.14 = (f16[128,512]{1,0:T(8,128)(2,1)S(1)}, f16[128,512]{1,0:T(8,128)(2,1)S(1)}, u32[]{:S(2)}, u32[]{:S(2)}) collective-permute-start(f16[128,512]{1,0:T(8,128)(2,1)S(1)} %fusion.10), channel_id=1, source_target_pairs={{0,16},{1,17},{2,18},{3,19},{4,20},{5,21},{6,22},{7,23},{8,24},{9,... | collective-permute-start | bytes 393224 | tf_op jit(solution)/shard_map/ppermute | solution.py:422
  89.3 7.6 %collective-permute-start.20 = (f16[128,512]{1,0:T(8,128)(2,1)S(1)}, f16[128,512]{1,0:T(8,128)(2,1)S(1)}, u32[]{:S(2)}, u32[]{:S(2)}) collective-permute-start(f16[128,512]{1,0:T(8,128)(2,1)S(1)} %fusion.18), channel_id=1, source_target_pairs={{0,8},{1,9},{2,10},{3,11},{4,12},{5,13},{6,14},{7,15},{8,0},{9,1},... | collective-permute-start | bytes 393224 | tf_op jit(solution)/shard_map/ppermute | solution.py:422
  91.0 7.0 %collective-permute-start.10 = (f16[128,512]{1,0:T(8,128)(2,1)S(1)}, f16[128,512]{1,0:T(8,128)(2,1)S(1)}, u32[]{:S(2)}, u32[]{:S(2)}) collective-permute-start(f16[128,512]{1,0:T(8,128)(2,1)S(1)} %fusion.14), channel_id=1, source_target_pairs={{0,2},{1,3},{2,0},{3,1},{4,6},{5,7},{6,4},{7,5},{8,10},{9,11},{10,... | collective-permute-start | bytes 393224 | tf_op jit(solution)/shard_map/ppermute | solution.py:422
  97.0 5.0 %collective-permute-start.28 = (f16[128,512]{1,0:T(8,128)(2,1)S(1)}, f16[128,512]{1,0:T(8,128)(2,1)S(1)}, u32[]{:S(2)}, u32[]{:S(2)}) collective-permute-start(f16[128,512]{1,0:T(8,128)(2,1)S(1)} %get-tuple-element.63), channel_id=1, source_target_pairs={{0,2},{1,3},{2,0},{3,1},{4,6},{5,7},{6,4},{7,5},{8,10},{9,11},{10,... | collective-permute-start | bytes 393224 | tf_op jit(solution)/shard_map/ppermute | solution.py:422
  98.1 11.0 %collective-permute-start.25 = (f16[128,512]{1,0:T(8,128)(2,1)S(1)}, f16[128,512]{1,0:T(8,128)(2,1)S(1)}, u32[]{:S(2)}, u32[]{:S(2)}) collective-permute-start(f16[128,512]{1,0:T(8,128)(2,1)S(1)} %get-tuple-element.61), channel_id=1, source_target_pairs={{0,2},{1,3},{2,0},{3,1},{4,6},{5,7},{6,4},{7,5},{8,10},{9,11},{10,... | collective-permute-start | bytes 393224 | tf_op jit(solution)/shard_map/ppermute | solution.py:422
  99.3 10.4 %collective-permute-start.30 = (f16[128,512]{1,0:T(8,128)(2,1)S(1)}, f16[128,512]{1,0:T(8,128)(2,1)S(1)}, u32[]{:S(2)}, u32[]{:S(2)}) collective-permute-start(f16[128,512]{1,0:T(8,128)(2,1)S(1)} %get-tuple-element.63), channel_id=1, source_target_pairs={{0,1},{1,0},{2,3},{3,2},{4,5},{5,4},{6,7},{7,6},{8,9},{9,8},{10,11... | collective-permute-start | bytes 393224 | tf_op jit(solution)/shard_map/ppermute | solution.py:422
  99.3 10.4 %collective-permute-start.27 = (f16[128,512]{1,0:T(8,128)(2,1)S(1)}, f16[128,512]{1,0:T(8,128)(2,1)S(1)}, u32[]{:S(2)}, u32[]{:S(2)}) collective-permute-start(f16[128,512]{1,0:T(8,128)(2,1)S(1)} %get-tuple-element.61), channel_id=1, source_target_pairs={{0,1},{1,0},{2,3},{3,2},{4,5},{5,4},{6,7},{7,6},{8,9},{9,8},{10,11... | collective-permute-start | bytes 393224 | tf_op jit(solution)/shard_map/ppermute | solution.py:422
  102.0 10.7 %collective-permute-start.29 = (f16[128,512]{1,0:T(8,128)(2,1)S(1)}, f16[128,512]{1,0:T(8,128)(2,1)S(1)}, u32[]{:S(2)}, u32[]{:S(2)}) collective-permute-start(f16[128,512]{1,0:T(8,128)(2,1)S(1)} %collective-permute-done.28), channel_id=1, source_target_pairs={{0,1},{1,0},{2,3},{3,2},{4,5},{5,4},{6,7},{7,6},{8,9},{9,8},{10,11... | collective-permute-start | bytes 393224 | tf_op jit(solution)/shard_map/ppermute | solution.py:422
  109.1 9.4 %collective-permute-start.26 = (f16[128,512]{1,0:T(8,128)(2,1)S(1)}, f16[128,512]{1,0:T(8,128)(2,1)S(1)}, u32[]{:S(2)}, u32[]{:S(2)}) collective-permute-start(f16[128,512]{1,0:T(8,128)(2,1)S(1)} %collective-permute-done.25), channel_id=1, source_target_pairs={{0,1},{1,0},{2,3},{3,2},{4,5},{5,4},{6,7},{7,6},{8,9},{9,8},{10,11... | collective-permute-start | bytes 393224 | tf_op jit(solution)/shard_map/ppermute | solution.py:422

commit v6 on v5

--- a/solution.py
+++ b/solution.py
@@ -428,7 +428,7 @@
     total_tokens = lax.axis_size("dp") * tokens.shape[0]
     inv_root = 1.0 / jnp.sqrt(jnp.float32(low_rank))
     far0 = [(Z1 | X | Z0, 0), (Z1 | X, 0), (Z1 | Z0, 0), (Z1, 0)]
-    near0 = [(Z0 | X, 0), (X, 0), (Z0, 0), (0, 0)]
+    near0 = [(Z0 | X, 0), (Z0, 0), (X, 0), (0, 0)]
     far1 = [(Z1 | Y | X, 1), (Z1 | Y, 1), (Z1 | X, 1), (Z1, 1)]
     near1 = [(Y | X, 1), (Y, 1), (X, 1), (0, 1)]
 
@@ -502,12 +502,11 @@
 
     far0_total = direct(y_side, (0, 0, 0, 0), (X | Z0, X, Z0))
     far1_total = direct(z_side, (8, 8, 0, 0), (Y | X, Y, X))
-    near0_state = begin(y_side, (4, 4, 4, 4), X)
+    near0_state = begin(y_side, (4, 4, 4, 4), Z0)
     near1_state = begin(z_side, (12, 12, 4, 4), Y)
     last0 = exchange(packed(far0_total, 2.0), Z1)
-    far1_small = packed(far1_total, 2.0)
-    last1 = exchange(far1_small, Z1)
-    near0_state = middle(near0_state, Z0)
+    last1 = exchange(packed(far1_total, 2.0), Z1)
+    near0_state = middle(near0_state, X)
     near1_state = middle(near1_state, X)
 
     def momentum_half(half, near, last):
@@ -530,8 +529,8 @@
     near, far = (0, CORE), (X, X | CORE)
     for half, rows, relatives in (
         (0, (halves[0], others[0][0]), near),
+        (1, (halves[1], others[1][0]), near),
         (0, others[0][1:], far),
-        (1, (halves[1], others[1][0]), near),
         (1, others[1][1:], far),
     ):
         where = [(rel, half) for rel in relatives]

time: 122 us -> 123 us (level)
  waiting for transfers between devices: 51.2 us -> 53.8 us
  starting transfers between devices: 34.2 us -> 32.4 us
    ppermute x31, waiting for transfers between devices: 51.2 us -> 53.8 us  [exchange(): return lax.ppermute(value, AXES, [(i, i ^ mask) for i in range(size)])]
    ppermute x31, starting transfers between devices: 34.2 us -> 32.4 us  [exchange(): return lax.ppermute(value, AXES, [(i, i ^ mask) for i in range(size)])]
  transfers between devices with their start and end apart: 31 -> 31, of which waited for: 10 -> 9; matrix products, arithmetic and copies ran while one was open for 1% -> 1% of each run, Pallas kernels for 21% -> 21%
where the time goes in v6:
time: 123 us; the launch traced here: 122 us
  waiting for transfers between devices  53.8 us (44%)
  Pallas kernels  32.5 us (26%)
  starting transfers between devices  32.4 us (26%)
  between operations  2.38 us (2%)
    ppermute x31, waiting for transfers between devices, exchange(): return lax.ppermute(value, AXES, [(i, i ^ mask) for i in range(size)])  53.8 us
    ppermute x31, starting transfers between devices, exchange(): return lax.ppermute(value, AXES, [(i, i ^ mask) for i in range(size)])  32.4 us
    pallas_call x4, Pallas kernels, update(): pl.pallas_call(functools.partial(update_kernel, where, keep, slabs, min(s...  11.4 us
    pallas_call x2, Pallas kernels, prefetch(): pl.pallas_call(prefetch_kernel, in_specs=[pl.BlockSpec(memory_space=pl.AN...  7 us
    pallas_call x2, Pallas kernels, sketch_parts(): pl.pallas_call(functools.partial(sketch_kernel, first, din_local), in_spe...  6.2 us
    pallas_call x3, Pallas kernels, pack(): pl.pallas_call(functools.partial(pack_kernel, groups, width, part), in_sp...  4.92 us
    pallas_call x4, Pallas kernels, project(): pl.pallas_call(functools.partial(project_kernel, n), grid=(1,), in_specs=...  2.91 us
  transfers between devices with their start and end apart: 31, of which 9 were waited for; matrix products, arithmetic and copies ran while one was open for 1% of the time, Pallas kernels for 21%

profile of v6, /device:TPU:0, one launch (start us, length us, event | category | flops | bytes accessed | tf_op | source)
XLA Modules:
  0.0 122.3 jit_solution(6347607994204586858)
XLA Ops:
  1.9 3.7 %sketch.2 = (bf16[2048,512]{1,0:T(8,128)(2,1)S(1)}, f32[256,512]{1,0:T(8,128)S(1)}, f32[256,512]{1,0:T(8,128)S(1)}) custom-call(s32[1,1]{1,0:T(1,128)} %bitcast.56.refs_0_, s32[1,1]{1,0:T(1,128)} %bitcast.57.refs_1_, bf16[1024,2048]{1,0:T(8,128)(2,1)} %refs_0_.3), custom_call_target="tpu_custom_call" | custom-call | flops 1073741824 | bytes 6291456 | tf_op jit(solution)/shard_map/sketch/pallas_call | solution.py:224
  5.6 0.6 collective-permute-start.1
  6.2 2.5 %sketch.3 = (f32[256,512]{1,0:T(8,128)S(1)}, f32[256,512]{1,0:T(8,128)S(1)}) custom-call(bf16[1024,2048]{1,0:T(8,128)(2,1)} %refs_0_.3, bf16[2048,512]{1,0:T(8,128)(2,1)S(1)} %get-tuple-element.32.refs_1_.refs_2_), custom_call_target="tpu_custom_call" | custom-call | flops 1073741824 | bytes 6291456 | tf_op jit(solution)/shard_map/sketch/pallas_call | solution.py:224
  8.9 3.0 %collective-permute-start.2 = (f32[256,512]{1,0:T(8,128)S(1)}, f32[256,512]{1,0:T(8,128)S(1)}, u32[]{:S(2)}, u32[]{:S(2)}) collective-permute-start(f32[256,512]{1,0:T(8,128)S(1)} %add.66), channel_id=1, source_target_pairs={{0,2},{1,3},{2,0},{3,1},{4,6},{5,7},{6,4},{7,5},{8,10},{9,11},{10,... | collective-permute-start | bytes 1572872 | tf_op jit(solution)/shard_map/ppermute | solution.py:422
  11.9 2.0 %pack.3 = (bf16[16,256,128]{2,1,0:T(8,128)(2,1)S(1)}, bf16[16,256,128]{2,1,0:T(8,128)(2,1)S(1)}) custom-call(bf16[256,8192]{1,0:T(8,128)(2,1)} %og_ref.5), custom_call_target="tpu_custom_call" | custom-call | bytes 4194304 | tf_op jit(solution)/shard_map/pack/pallas_call | solution.py:127
  14.0 1.5 %pack.4 = (bf16[8,256,128]{2,1,0:T(8,128)(2,1)S(1)}, bf16[8,256,128]{2,1,0:T(8,128)(2,1)S(1)}) custom-call(bf16[256,8192]{1,0:T(8,128)(2,1)} %og_ref.5), custom_call_target="tpu_custom_call" | custom-call | bytes 2097152 | tf_op jit(solution)/shard_map/pack/pallas_call | solution.py:127
  15.5 1.6 %collective-permute-start.17 = (bf16[8,256,128]{2,1,0:T(8,128)(2,1)S(1)}, bf16[8,256,128]{2,1,0:T(8,128)(2,1)S(1)}, u32[]{:S(2)}, u32[]{:S(2)}) collective-permute-start(bf16[8,256,128]{2,1,0:T(8,128)(2,1)S(1)} %get-tuple-element.45), channel_id=1, source_target_pairs={{0,4},{1,5},{2,6},{3,7},{4,0},{5,1},{6,2},{7,3},{8,12},{9,13},{10,... | collective-permute-start | bytes 1572872 | tf_op jit(solution)/shard_map/ppermute | solution.py:422
  17.1 1.5 %pack.5 = (bf16[8,256,128]{2,1,0:T(8,128)(2,1)S(1)}, bf16[8,256,128]{2,1,0:T(8,128)(2,1)S(1)}) custom-call(bf16[256,8192]{1,0:T(8,128)(2,1)} %og_ref.5), custom_call_target="tpu_custom_call" | custom-call | bytes 2097152 | tf_op jit(solution)/shard_map/pack/pallas_call | solution.py:127
  18.5 0.4 collective-permute-start.18
  18.9 5.1 %collective-permute-done.2 = f32[256,512]{1,0:T(8,128)S(1)} collective-permute-done((f32[256,512]{1,0:T(8,128)S(1)}, f32[256,512]{1,0:T(8,128)S(1)}, u32[]{:S(2)}, u32[]{:S(2)}) %collective-permute-start.2) | collective-permute-done | bytes 524320 | tf_op jit(solution)/shard_map/ppermute | solution.py:422
  24.2 1.9 %collective-permute-start.15 = (bf16[256,512]{1,0:T(8,128)(2,1)S(1)}, bf16[256,512]{1,0:T(8,128)(2,1)S(1)}, u32[]{:S(2)}, u32[]{:S(2)}) collective-permute-start(bf16[256,512]{1,0:T(8,128)(2,1)S(1)} %multiply_convert_fusion.2.refs_0_), channel_id=1, source_target_pairs={{0,4},{1,5},{2,6},{3,7},{4,0},{5,1},{6,2},{7,3},{8,12},{9,13},{10,... | collective-permute-start | bytes 786440 | tf_op jit(solution)/shard_map/ppermute | solution.py:422
  26.1 1.6 %collective-permute-start.4 = (bf16[256,512]{1,0:T(8,128)(2,1)S(1)}, bf16[256,512]{1,0:T(8,128)(2,1)S(1)}, u32[]{:S(2)}, u32[]{:S(2)}) collective-permute-start(bf16[256,512]{1,0:T(8,128)(2,1)S(1)} %multiply_convert_fusion.2.refs_0_), channel_id=1, source_target_pairs={{0,8},{1,9},{2,10},{3,11},{4,12},{5,13},{6,14},{7,15},{8,0},{9,1},... | collective-permute-start | bytes 786440 | tf_op jit(solution)/shard_map/ppermute | solution.py:422
  27.6 2.7 %collective-permute-done.17.refs_6_ = bf16[8,256,128]{2,1,0:T(8,128)(2,1)S(1)} collective-permute-done((bf16[8,256,128]{2,1,0:T(8,128)(2,1)S(1)}, bf16[8,256,128]{2,1,0:T(8,128)(2,1)S(1)}, u32[]{:S(2)}, u32[]{:S(2)}) %collective-permute-start.17) | collective-permute-done | bytes 524320 | tf_op jit(solution)/shard_map/ppermute | solution.py:422
  30.3 16.4 %collective-permute-done.15.refs_2_ = bf16[256,512]{1,0:T(8,128)(2,1)S(1)} collective-permute-done((bf16[256,512]{1,0:T(8,128)(2,1)S(1)}, bf16[256,512]{1,0:T(8,128)(2,1)S(1)}, u32[]{:S(2)}, u32[]{:S(2)}) %collective-permute-start.15) | collective-permute-done | bytes 262176 | tf_op jit(solution)/shard_map/ppermute | solution.py:422
  46.7 1.6 %collective-permute-start.7 = (bf16[8,256,128]{2,1,0:T(8,128)(2,1)S(1)}, bf16[8,256,128]{2,1,0:T(8,128)(2,1)S(1)}, u32[]{:S(2)}, u32[]{:S(2)}) collective-permute-start(bf16[8,256,128]{2,1,0:T(8,128)(2,1)S(1)} %get-tuple-element.39), channel_id=1, source_target_pairs={{0,8},{1,9},{2,10},{3,11},{4,12},{5,13},{6,14},{7,15},{8,0},{9,1},... | collective-permute-start | bytes 1572872 | tf_op jit(solution)/shard_map/ppermute | solution.py:422
  48.3 0.3 collective-permute-start.8
  48.6 0.3 collective-permute-start.5
  48.9 0.7 project.6
  49.7 1.7 %collective-permute-start.19 = (f16[2,128,512]{2,1,0:T(8,128)(2,1)S(1)}, f16[2,128,512]{2,1,0:T(8,128)(2,1)S(1)}, u32[]{:S(2)}, u32[]{:S(2)}) collective-permute-start(f16[2,128,512]{2,1,0:T(8,128)(2,1)S(1)} %multiply_convert_fusion), channel_id=1, source_target_pairs={{0,8},{1,9},{2,10},{3,11},{4,12},{5,13},{6,14},{7,15},{8,0},{9,1},... | collective-permute-start | bytes 786440 | tf_op jit(solution)/shard_map/ppermute | solution.py:422
  51.3 0.7 project.7
  52.1 0.3 collective-permute-start.21
  52.4 9.1 %collective-permute-done.7.refs_6_ = bf16[8,256,128]{2,1,0:T(8,128)(2,1)S(1)} collective-permute-done((bf16[8,256,128]{2,1,0:T(8,128)(2,1)S(1)}, bf16[8,256,128]{2,1,0:T(8,128)(2,1)S(1)}, u32[]{:S(2)}, u32[]{:S(2)}) %collective-permute-start.7) | collective-permute-done | bytes 524320 | tf_op jit(solution)/shard_map/ppermute | solution.py:422
  61.5 0.3 collective-permute-start.22
  61.8 10.0 %collective-permute-done.8.refs_7_ = bf16[8,256,128]{2,1,0:T(8,128)(2,1)S(1)} collective-permute-done((bf16[8,256,128]{2,1,0:T(8,128)(2,1)S(1)}, bf16[8,256,128]{2,1,0:T(8,128)(2,1)S(1)}, u32[]{:S(2)}, u32[]{:S(2)}) %collective-permute-start.8) | collective-permute-done | bytes 524320 | tf_op jit(solution)/shard_map/ppermute | solution.py:422
  71.8 1.6 %collective-permute-start.23 = (f16[128,512]{1,0:T(8,128)(2,1)S(1)}, f16[128,512]{1,0:T(8,128)(2,1)S(1)}, u32[]{:S(2)}, u32[]{:S(2)}) collective-permute-start(f16[128,512]{1,0:T(8,128)(2,1)S(1)} %get-tuple-element.66), channel_id=1, source_target_pairs={{0,8},{1,9},{2,10},{3,11},{4,12},{5,13},{6,14},{7,15},{8,0},{9,1},... | collective-permute-start | bytes 393224 | tf_op jit(solution)/shard_map/ppermute | solution.py:422
  73.4 0.7 project.4
  74.2 1.6 %collective-permute-start.9 = (f16[2,128,512]{2,1,0:T(8,128)(2,1)S(1)}, f16[2,128,512]{2,1,0:T(8,128)(2,1)S(1)}, u32[]{:S(2)}, u32[]{:S(2)}) collective-permute-start(f16[2,128,512]{2,1,0:T(8,128)(2,1)S(1)} %multiply_convert_fusion.1), channel_id=1, source_target_pairs={{0,4},{1,5},{2,6},{3,7},{4,0},{5,1},{6,2},{7,3},{8,12},{9,13},{10,... | collective-permute-start | bytes 786440 | tf_op jit(solution)/shard_map/ppermute | solution.py:422
  75.8 0.7 project.5
  76.6 4.4 %collective-permute-done.21 = f16[128,512]{1,0:T(8,128)(2,1)S(1)} collective-permute-done((f16[128,512]{1,0:T(8,128)(2,1)S(1)}, f16[128,512]{1,0:T(8,128)(2,1)S(1)}, u32[]{:S(2)}, u32[]{:S(2)}) %collective-permute-start.21) | collective-permute-done | bytes 131104 | tf_op jit(solution)/shard_map/ppermute | solution.py:422
  80.9 2.7 %collective-permute-start.11 = (f16[128,512]{1,0:T(8,128)(2,1)S(1)}, f16[128,512]{1,0:T(8,128)(2,1)S(1)}, u32[]{:S(2)}, u32[]{:S(2)}) collective-permute-start(f16[128,512]{1,0:T(8,128)(2,1)S(1)} %get-tuple-element.68), channel_id=1, source_target_pairs={{0,6},{1,7},{2,4},{3,5},{4,2},{5,3},{6,0},{7,1},{8,14},{9,15},{10,... | collective-permute-start | bytes 393224 | tf_op jit(solution)/shard_map/ppermute | solution.py:422
  83.6 0.5 collective-permute-start.12
  84.1 0.3 collective-permute-start.13
  84.5 2.6 %collective-permute-done.11 = f16[128,512]{1,0:T(8,128)(2,1)S(1)} collective-permute-done((f16[128,512]{1,0:T(8,128)(2,1)S(1)}, f16[128,512]{1,0:T(8,128)(2,1)S(1)}, u32[]{:S(2)}, u32[]{:S(2)}) %collective-permute-start.11) | collective-permute-done | bytes 131104 | tf_op jit(solution)/shard_map/ppermute | solution.py:422
  87.1 2.7 %collective-permute-start.24 = (f16[128,512]{1,0:T(8,128)(2,1)S(1)}, f16[128,512]{1,0:T(8,128)(2,1)S(1)}, u32[]{:S(2)}, u32[]{:S(2)}) collective-permute-start(f16[128,512]{1,0:T(8,128)(2,1)S(1)} %fusion.3), channel_id=1, source_target_pairs={{0,16},{1,17},{2,18},{3,19},{4,20},{5,21},{6,22},{7,23},{8,24},{9,... | collective-permute-start | bytes 393224 | tf_op jit(solution)/shard_map/ppermute | solution.py:422
  90.0 2.6 %collective-permute-start.14 = (f16[128,512]{1,0:T(8,128)(2,1)S(1)}, f16[128,512]{1,0:T(8,128)(2,1)S(1)}, u32[]{:S(2)}, u32[]{:S(2)}) collective-permute-start(f16[128,512]{1,0:T(8,128)(2,1)S(1)} %fusion.10), channel_id=1, source_target_pairs={{0,16},{1,17},{2,18},{3,19},{4,20},{5,21},{6,22},{7,23},{8,24},{9,... | collective-permute-start | bytes 393224 | tf_op jit(solution)/shard_map/ppermute | solution.py:422
  92.7 1.2 %collective-permute-start.20 = (f16[128,512]{1,0:T(8,128)(2,1)S(1)}, f16[128,512]{1,0:T(8,128)(2,1)S(1)}, u32[]{:S(2)}, u32[]{:S(2)}) collective-permute-start(f16[128,512]{1,0:T(8,128)(2,1)S(1)} %fusion.18), channel_id=1, source_target_pairs={{0,2},{1,3},{2,0},{3,1},{4,6},{5,7},{6,4},{7,5},{8,10},{9,11},{10,... | collective-permute-start | bytes 393224 | tf_op jit(solution)/shard_map/ppermute | solution.py:422
  94.0 0.9 collective-permute-start.10
  94.9 2.8 %collective-permute-done.24 = f16[128,512]{1,0:T(8,128)(2,1)S(1)} collective-permute-done((f16[128,512]{1,0:T(8,128)(2,1)S(1)}, f16[128,512]{1,0:T(8,128)(2,1)S(1)}, u32[]{:S(2)}, u32[]{:S(2)}) %collective-permute-start.24) | collective-permute-done | bytes 131104 | tf_op jit(solution)/shard_map/ppermute | solution.py:422
  97.7 0.7 collective-permute-done.20
  98.6 2.8 %collective-permute-start.27 = (f16[128,512]{1,0:T(8,128)(2,1)S(1)}, f16[128,512]{1,0:T(8,128)(2,1)S(1)}, u32[]{:S(2)}, u32[]{:S(2)}) collective-permute-start(f16[128,512]{1,0:T(8,128)(2,1)S(1)} %get-tuple-element.63), channel_id=1, source_target_pairs={{0,2},{1,3},{2,0},{3,1},{4,6},{5,7},{6,4},{7,5},{8,10},{9,11},{10,... | collective-permute-start | bytes 393224 | tf_op jit(solution)/shard_map/ppermute | solution.py:422
  101.8 1.0 collective-permute-start.25
  102.8 3.5 %prefetch.2.refs_3_ = f32[1024,2048]{1,0:T(8,128)S(1)} custom-call(f32[1024,2048]{1,0:T(8,128)} %refs_0_.4), custom_call_target="tpu_custom_call" | custom-call | bytes 8388608 | tf_op jit(solution)/shard_map/prefetch/pallas_call | solution.py:309
  106.3 3.5 %prefetch.3.refs_4_ = f32[1024,2048]{1,0:T(8,128)S(1)} custom-call(f32[1024,2048]{1,0:T(8,128)} %refs_0_.5), custom_call_target="tpu_custom_call" | custom-call | bytes 8388608 | tf_op jit(solution)/shard_map/prefetch/pallas_call | solution.py:309
  110.1 2.9 %update.4 = (f32[1024,2048]{1,0:T(8,128)}, f32[1024,2048]{1,0:T(8,128)}, f32[256,512]{1,0:T(8,128)}) custom-call(f32[128,512]{1,0:T(8,128)S(1)} %get-tuple-element.64.refs_0_, f32[128,512]{1,0:T(8,128)S(1)} %convert_element_type.161.refs_1_, bf16[2048,512]{1,0:T(8,128)(2,1)S(1)} %get-tuple-element.32.refs_1_.refs_2_, f32[1024,2048]{1,0:T(8,128)S(1)} %prefetch.2.refs_3_, ...), custom_call_target="tpu_custom_call" | custom-call | flops 1073741824 | bytes 4194304 | tf_op jit(solution)/shard_map/update/pallas_call | solution.py:391
  113.1 0.4 collective-permute-start.26
  113.5 2.9 %update.5 = (f32[1024,2048]{1,0:T(8,128)}, f32[1024,2048]{1,0:T(8,128)}, f32[256,512]{1,0:T(8,128)}) custom-call(f32[128,512]{1,0:T(8,128)S(1)} %get-tuple-element.62.refs_0_, f32[128,512]{1,0:T(8,128)S(1)} %convert_element_type.160.refs_1_, ...), custom_call_target="tpu_custom_call", output_to_operand_aliasing={{0}: (5, {}), {1}: (6, {}), {2}: (7, {})} | custom-call | flops 1073741824 | bytes 4194304 | tf_op jit(solution)/shard_map/update/pallas_call | solution.py:391
  116.5 2.8 %update.6 = (f32[1024,2048]{1,0:T(8,128)}, f32[1024,2048]{1,0:T(8,128)}, f32[256,512]{1,0:T(8,128)}) custom-call(f32[128,512]{1,0:T(8,128)S(1)} %convert_element_type.158.refs_0_, f32[128,512]{1,0:T(8,128)S(1)} %convert_element_type.159.refs_1_, ...), custom_call_target="tpu_custom_call", output_to_operand_aliasing={{0}: (5, {}), {1}: (6, {}), {2}: (7, {})} | custom-call | flops 1073741824 | bytes 4194304 | tf_op jit(solution)/shard_map/update/pallas_call | solution.py:391
  119.4 2.8 %update.7 = (f32[1024,2048]{1,0:T(8,128)}, f32[1024,2048]{1,0:T(8,128)}, f32[256,512]{1,0:T(8,128)}) custom-call(f32[128,512]{1,0:T(8,128)S(1)} %convert_element_type.156.refs_0_, f32[128,512]{1,0:T(8,128)S(1)} %convert_element_type.157.refs_1_, ...), custom_call_target="tpu_custom_call", output_to_operand_aliasing={{0}: (5, {}), {1}: (6, {}), {2}: (7, {})} | custom-call | flops 1073741824 | bytes 4194304 | tf_op jit(solution)/shard_map/update/pallas_call | solution.py:391
  (49 shorter events, 2.0 us)
Async XLA Ops:
  5.6 3.2 %collective-permute-start.1 = (f32[256,512]{1,0:T(8,128)S(1)}, f32[256,512]{1,0:T(8,128)S(1)}, u32[]{:S(2)}, u32[]{:S(2)}) collective-permute-start(f32[256,512]{1,0:T(8,128)S(1)} %get-tuple-element.36), channel_id=1, source_target_pairs={{0,1},{1,0},{2,3},{3,2},{4,5},{5,4},{6,7},{7,6},{8,9},{9,8},{10,11... | collective-permute-start | bytes 1572872 | tf_op jit(solution)/shard_map/ppermute | solution.py:422
  8.7 10.2 %collective-permute-start = (f32[256,512]{1,0:T(8,128)S(1)}, f32[256,512]{1,0:T(8,128)S(1)}, u32[]{:S(2)}, u32[]{:S(2)}) collective-permute-start(f32[256,512]{1,0:T(8,128)S(1)} %get-tuple-element.34), channel_id=1, source_target_pairs={{0,1},{1,0},{2,3},{3,2},{4,5},{5,4},{6,7},{7,6},{8,9},{9,8},{10,11... | collective-permute-start | bytes 1572872 | tf_op jit(solution)/shard_map/ppermute | solution.py:422
  8.9 15.1 %collective-permute-start.2 = (f32[256,512]{1,0:T(8,128)S(1)}, f32[256,512]{1,0:T(8,128)S(1)}, u32[]{:S(2)}, u32[]{:S(2)}) collective-permute-start(f32[256,512]{1,0:T(8,128)S(1)} %add.66), channel_id=1, source_target_pairs={{0,2},{1,3},{2,0},{3,1},{4,6},{5,7},{6,4},{7,5},{8,10},{9,11},{10,... | collective-permute-start | bytes 1572872 | tf_op jit(solution)/shard_map/ppermute | solution.py:422
  13.9 34.4 %collective-permute-start.6 = (bf16[16,256,128]{2,1,0:T(8,128)(2,1)S(1)}, bf16[16,256,128]{2,1,0:T(8,128)(2,1)S(1)}, u32[]{:S(2)}, u32[]{:S(2)}) collective-permute-start(bf16[16,256,128]{2,1,0:T(8,128)(2,1)S(1)} %get-tuple-element.38), channel_id=1, source_target_pairs={{0,1},{1,0},{2,3},{3,2},{4,5},{5,4},{6,7},{7,6},{8,9},{9,8},{10,11... | collective-permute-start | bytes 3145736 | tf_op jit(solution)/shard_map/ppermute | solution.py:422
  15.5 14.9 %collective-permute-start.17 = (bf16[8,256,128]{2,1,0:T(8,128)(2,1)S(1)}, bf16[8,256,128]{2,1,0:T(8,128)(2,1)S(1)}, u32[]{:S(2)}, u32[]{:S(2)}) collective-permute-start(bf16[8,256,128]{2,1,0:T(8,128)(2,1)S(1)} %get-tuple-element.45), channel_id=1, source_target_pairs={{0,4},{1,5},{2,6},{3,7},{4,0},{5,1},{6,2},{7,3},{8,12},{9,13},{10,... | collective-permute-start | bytes 1572872 | tf_op jit(solution)/shard_map/ppermute | solution.py:422
  18.5 28.2 %collective-permute-start.18 = (bf16[8,256,128]{2,1,0:T(8,128)(2,1)S(1)}, bf16[8,256,128]{2,1,0:T(8,128)(2,1)S(1)}, u32[]{:S(2)}, u32[]{:S(2)}) collective-permute-start(bf16[8,256,128]{2,1,0:T(8,128)(2,1)S(1)} %get-tuple-element.46), channel_id=1, source_target_pairs={{0,5},{1,4},{2,7},{3,6},{4,1},{5,0},{6,3},{7,2},{8,13},{9,12},{10,... | collective-permute-start | bytes 1572872 | tf_op jit(solution)/shard_map/ppermute | solution.py:422
  24.2 22.5 %collective-permute-start.15 = (bf16[256,512]{1,0:T(8,128)(2,1)S(1)}, bf16[256,512]{1,0:T(8,128)(2,1)S(1)}, u32[]{:S(2)}, u32[]{:S(2)}) collective-permute-start(bf16[256,512]{1,0:T(8,128)(2,1)S(1)} %multiply_convert_fusion.2.refs_0_), channel_id=1, source_target_pairs={{0,4},{1,5},{2,6},{3,7},{4,0},{5,1},{6,2},{7,3},{8,12},{9,13},{10,... | collective-permute-start | bytes 786440 | tf_op jit(solution)/shard_map/ppermute | solution.py:422
  26.1 22.5 %collective-permute-start.4 = (bf16[256,512]{1,0:T(8,128)(2,1)S(1)}, bf16[256,512]{1,0:T(8,128)(2,1)S(1)}, u32[]{:S(2)}, u32[]{:S(2)}) collective-permute-start(bf16[256,512]{1,0:T(8,128)(2,1)S(1)} %multiply_convert_fusion.2.refs_0_), channel_id=1, source_target_pairs={{0,8},{1,9},{2,10},{3,11},{4,12},{5,13},{6,14},{7,15},{8,0},{9,1},... | collective-permute-start | bytes 786440 | tf_op jit(solution)/shard_map/ppermute | solution.py:422
  30.3 18.5 %collective-permute-start.3 = (bf16[256,512]{1,0:T(8,128)(2,1)S(1)}, bf16[256,512]{1,0:T(8,128)(2,1)S(1)}, u32[]{:S(2)}, u32[]{:S(2)}) collective-permute-start(bf16[256,512]{1,0:T(8,128)(2,1)S(1)} %multiply_convert_fusion.2.refs_0_), channel_id=1, source_target_pairs={{0,1},{1,0},{2,3},{3,2},{4,5},{5,4},{6,7},{7,6},{8,9},{9,8},{10,11... | collective-permute-start | bytes 786440 | tf_op jit(solution)/shard_map/ppermute | solution.py:422
  46.7 2.2 %collective-permute-start.16 = (bf16[256,512]{1,0:T(8,128)(2,1)S(1)}, bf16[256,512]{1,0:T(8,128)(2,1)S(1)}, u32[]{:S(2)}, u32[]{:S(2)}) collective-permute-start(bf16[256,512]{1,0:T(8,128)(2,1)S(1)} %collective-permute-done.15.refs_2_), channel_id=1, source_target_pairs={{0,1},{1,0},{2,3},{3,2},{4,5},{5,4},{6,7},{7,6},{8,9},{9,8},{10,11... | collective-permute-start | bytes 786440 | tf_op jit(solution)/shard_map/ppermute | solution.py:422
  46.7 14.8 %collective-permute-start.7 = (bf16[8,256,128]{2,1,0:T(8,128)(2,1)S(1)}, bf16[8,256,128]{2,1,0:T(8,128)(2,1)S(1)}, u32[]{:S(2)}, u32[]{:S(2)}) collective-permute-start(bf16[8,256,128]{2,1,0:T(8,128)(2,1)S(1)} %get-tuple-element.39), channel_id=1, source_target_pairs={{0,8},{1,9},{2,10},{3,11},{4,12},{5,13},{6,14},{7,15},{8,0},{9,1},... | collective-permute-start | bytes 1572872 | tf_op jit(solution)/shard_map/ppermute | solution.py:422
  48.3 23.5 %collective-permute-start.8 = (bf16[8,256,128]{2,1,0:T(8,128)(2,1)S(1)}, bf16[8,256,128]{2,1,0:T(8,128)(2,1)S(1)}, u32[]{:S(2)}, u32[]{:S(2)}) collective-permute-start(bf16[8,256,128]{2,1,0:T(8,128)(2,1)S(1)} %get-tuple-element.40), channel_id=1, source_target_pairs={{0,9},{1,8},{2,11},{3,10},{4,13},{5,12},{6,15},{7,14},{8,1},{9,0},... | collective-permute-start | bytes 1572872 | tf_op jit(solution)/shard_map/ppermute | solution.py:422
  48.6 24.8 %collective-permute-start.5 = (bf16[256,512]{1,0:T(8,128)(2,1)S(1)}, bf16[256,512]{1,0:T(8,128)(2,1)S(1)}, u32[]{:S(2)}, u32[]{:S(2)}) collective-permute-start(bf16[256,512]{1,0:T(8,128)(2,1)S(1)} %collective-permute-done.4.refs_2_), channel_id=1, source_target_pairs={{0,1},{1,0},{2,3},{3,2},{4,5},{5,4},{6,7},{7,6},{8,9},{9,8},{10,11... | collective-permute-start | bytes 786440 | tf_op jit(solution)/shard_map/ppermute | solution.py:422
  49.6 48.7 %copy-start = (f32[256,512]{1,0:T(8,128)S(1)}, f32[256,512]{1,0:T(8,128)}, u32[]{:S(2)}) copy-start(f32[256,512]{1,0:T(8,128)} %param.11) | copy-start | bytes 1572868
  49.7 43.0 %collective-permute-start.19 = (f16[2,128,512]{2,1,0:T(8,128)(2,1)S(1)}, f16[2,128,512]{2,1,0:T(8,128)(2,1)S(1)}, u32[]{:S(2)}, u32[]{:S(2)}) collective-permute-start(f16[2,128,512]{2,1,0:T(8,128)(2,1)S(1)} %multiply_convert_fusion), channel_id=1, source_target_pairs={{0,8},{1,9},{2,10},{3,11},{4,12},{5,13},{6,14},{7,15},{8,0},{9,1},... | collective-permute-start | bytes 786440 | tf_op jit(solution)/shard_map/ppermute | solution.py:422
  52.1 28.8 %collective-permute-start.21 = (f16[128,512]{1,0:T(8,128)(2,1)S(1)}, f16[128,512]{1,0:T(8,128)(2,1)S(1)}, u32[]{:S(2)}, u32[]{:S(2)}) collective-permute-start(f16[128,512]{1,0:T(8,128)(2,1)S(1)} %get-tuple-element.65), channel_id=1, source_target_pairs={{0,10},{1,11},{2,8},{3,9},{4,14},{5,15},{6,12},{7,13},{8,2},{9,3},... | collective-permute-start | bytes 393224 | tf_op jit(solution)/shard_map/ppermute | solution.py:422
  61.5 22.1 %collective-permute-start.22 = (f16[128,512]{1,0:T(8,128)(2,1)S(1)}, f16[128,512]{1,0:T(8,128)(2,1)S(1)}, u32[]{:S(2)}, u32[]{:S(2)}) collective-permute-start(f16[128,512]{1,0:T(8,128)(2,1)S(1)} %get-tuple-element.67), channel_id=1, source_target_pairs={{0,2},{1,3},{2,0},{3,1},{4,6},{5,7},{6,4},{7,5},{8,10},{9,11},{10,... | collective-permute-start | bytes 393224 | tf_op jit(solution)/shard_map/ppermute | solution.py:422
  71.8 12.2 %collective-permute-start.23 = (f16[128,512]{1,0:T(8,128)(2,1)S(1)}, f16[128,512]{1,0:T(8,128)(2,1)S(1)}, u32[]{:S(2)}, u32[]{:S(2)}) collective-permute-start(f16[128,512]{1,0:T(8,128)(2,1)S(1)} %get-tuple-element.66), channel_id=1, source_target_pairs={{0,8},{1,9},{2,10},{3,11},{4,12},{5,13},{6,14},{7,15},{8,0},{9,1},... | collective-permute-start | bytes 393224 | tf_op jit(solution)/shard_map/ppermute | solution.py:422
  74.2 19.7 %collective-permute-start.9 = (f16[2,128,512]{2,1,0:T(8,128)(2,1)S(1)}, f16[2,128,512]{2,1,0:T(8,128)(2,1)S(1)}, u32[]{:S(2)}, u32[]{:S(2)}) collective-permute-start(f16[2,128,512]{2,1,0:T(8,128)(2,1)S(1)} %multiply_convert_fusion.1), channel_id=1, source_target_pairs={{0,4},{1,5},{2,6},{3,7},{4,0},{5,1},{6,2},{7,3},{8,12},{9,13},{10,... | collective-permute-start | bytes 786440 | tf_op jit(solution)/shard_map/ppermute | solution.py:422
  80.9 6.2 %collective-permute-start.11 = (f16[128,512]{1,0:T(8,128)(2,1)S(1)}, f16[128,512]{1,0:T(8,128)(2,1)S(1)}, u32[]{:S(2)}, u32[]{:S(2)}) collective-permute-start(f16[128,512]{1,0:T(8,128)(2,1)S(1)} %get-tuple-element.68), channel_id=1, source_target_pairs={{0,6},{1,7},{2,4},{3,5},{4,2},{5,3},{6,0},{7,1},{8,14},{9,15},{10,... | collective-permute-start | bytes 393224 | tf_op jit(solution)/shard_map/ppermute | solution.py:422
  83.6 6.3 %collective-permute-start.12 = (f16[128,512]{1,0:T(8,128)(2,1)S(1)}, f16[128,512]{1,0:T(8,128)(2,1)S(1)}, u32[]{:S(2)}, u32[]{:S(2)}) collective-permute-start(f16[128,512]{1,0:T(8,128)(2,1)S(1)} %get-tuple-element.70), channel_id=1, source_target_pairs={{0,4},{1,5},{2,6},{3,7},{4,0},{5,1},{6,2},{7,3},{8,12},{9,13},{10,... | collective-permute-start | bytes 393224 | tf_op jit(solution)/shard_map/ppermute | solution.py:422
  84.1 5.8 %collective-permute-start.13 = (f16[128,512]{1,0:T(8,128)(2,1)S(1)}, f16[128,512]{1,0:T(8,128)(2,1)S(1)}, u32[]{:S(2)}, u32[]{:S(2)}) collective-permute-start(f16[128,512]{1,0:T(8,128)(2,1)S(1)} %get-tuple-element.69), channel_id=1, source_target_pairs={{0,2},{1,3},{2,0},{3,1},{4,6},{5,7},{6,4},{7,5},{8,10},{9,11},{10,... | collective-permute-start | bytes 393224 | tf_op jit(solution)/shard_map/ppermute | solution.py:422
  87.1 10.5 %collective-permute-start.24 = (f16[128,512]{1,0:T(8,128)(2,1)S(1)}, f16[128,512]{1,0:T(8,128)(2,1)S(1)}, u32[]{:S(2)}, u32[]{:S(2)}) collective-permute-start(f16[128,512]{1,0:T(8,128)(2,1)S(1)} %fusion.3), channel_id=1, source_target_pairs={{0,16},{1,17},{2,18},{3,19},{4,20},{5,21},{6,22},{7,23},{8,24},{9,... | collective-permute-start | bytes 393224 | tf_op jit(solution)/shard_map/ppermute | solution.py:422
  90.0 11.4 %collective-permute-start.14 = (f16[128,512]{1,0:T(8,128)(2,1)S(1)}, f16[128,512]{1,0:T(8,128)(2,1)S(1)}, u32[]{:S(2)}, u32[]{:S(2)}) collective-permute-start(f16[128,512]{1,0:T(8,128)(2,1)S(1)} %fusion.10), channel_id=1, source_target_pairs={{0,16},{1,17},{2,18},{3,19},{4,20},{5,21},{6,22},{7,23},{8,24},{9,... | collective-permute-start | bytes 393224 | tf_op jit(solution)/shard_map/ppermute | solution.py:422
  92.7 5.7 %collective-permute-start.20 = (f16[128,512]{1,0:T(8,128)(2,1)S(1)}, f16[128,512]{1,0:T(8,128)(2,1)S(1)}, u32[]{:S(2)}, u32[]{:S(2)}) collective-permute-start(f16[128,512]{1,0:T(8,128)(2,1)S(1)} %fusion.18), channel_id=1, source_target_pairs={{0,2},{1,3},{2,0},{3,1},{4,6},{5,7},{6,4},{7,5},{8,10},{9,11},{10,... | collective-permute-start | bytes 393224 | tf_op jit(solution)/shard_map/ppermute | solution.py:422
  94.0 7.4 %collective-permute-start.10 = (f16[128,512]{1,0:T(8,128)(2,1)S(1)}, f16[128,512]{1,0:T(8,128)(2,1)S(1)}, u32[]{:S(2)}, u32[]{:S(2)}) collective-permute-start(f16[128,512]{1,0:T(8,128)(2,1)S(1)} %fusion.14), channel_id=1, source_target_pairs={{0,2},{1,3},{2,0},{3,1},{4,6},{5,7},{6,4},{7,5},{8,10},{9,11},{10,... | collective-permute-start | bytes 393224 | tf_op jit(solution)/shard_map/ppermute | solution.py:422
  98.5 11.3 %collective-permute-start.30 = (f16[128,512]{1,0:T(8,128)(2,1)S(1)}, f16[128,512]{1,0:T(8,128)(2,1)S(1)}, u32[]{:S(2)}, u32[]{:S(2)}) collective-permute-start(f16[128,512]{1,0:T(8,128)(2,1)S(1)} %get-tuple-element.63), channel_id=1, source_target_pairs={{0,1},{1,0},{2,3},{3,2},{4,5},{5,4},{6,7},{7,6},{8,9},{9,8},{10,11... | collective-permute-start | bytes 393224 | tf_op jit(solution)/shard_map/ppermute | solution.py:422
  98.6 11.3 %collective-permute-start.27 = (f16[128,512]{1,0:T(8,128)(2,1)S(1)}, f16[128,512]{1,0:T(8,128)(2,1)S(1)}, u32[]{:S(2)}, u32[]{:S(2)}) collective-permute-start(f16[128,512]{1,0:T(8,128)(2,1)S(1)} %get-tuple-element.63), channel_id=1, source_target_pairs={{0,2},{1,3},{2,0},{3,1},{4,6},{5,7},{6,4},{7,5},{8,10},{9,11},{10,... | collective-permute-start | bytes 393224 | tf_op jit(solution)/shard_map/ppermute | solution.py:422
  101.6 11.5 %collective-permute-start.29 = (f16[128,512]{1,0:T(8,128)(2,1)S(1)}, f16[128,512]{1,0:T(8,128)(2,1)S(1)}, u32[]{:S(2)}, u32[]{:S(2)}) collective-permute-start(f16[128,512]{1,0:T(8,128)(2,1)S(1)} %get-tuple-element.61), channel_id=1, source_target_pairs={{0,1},{1,0},{2,3},{3,2},{4,5},{5,4},{6,7},{7,6},{8,9},{9,8},{10,11... | collective-permute-start | bytes 393224 | tf_op jit(solution)/shard_map/ppermute | solution.py:422
  101.8 11.3 %collective-permute-start.25 = (f16[128,512]{1,0:T(8,128)(2,1)S(1)}, f16[128,512]{1,0:T(8,128)(2,1)S(1)}, u32[]{:S(2)}, u32[]{:S(2)}) collective-permute-start(f16[128,512]{1,0:T(8,128)(2,1)S(1)} %get-tuple-element.61), channel_id=1, source_target_pairs={{0,2},{1,3},{2,0},{3,1},{4,6},{5,7},{6,4},{7,5},{8,10},{9,11},{10,... | collective-permute-start | bytes 393224 | tf_op jit(solution)/shard_map/ppermute | solution.py:422
  109.9 6.6 %collective-permute-start.28 = (f16[128,512]{1,0:T(8,128)(2,1)S(1)}, f16[128,512]{1,0:T(8,128)(2,1)S(1)}, u32[]{:S(2)}, u32[]{:S(2)}) collective-permute-start(f16[128,512]{1,0:T(8,128)(2,1)S(1)} %collective-permute-done.27), channel_id=1, source_target_pairs={{0,1},{1,0},{2,3},{3,2},{4,5},{5,4},{6,7},{7,6},{8,9},{9,8},{10,11... | collective-permute-start | bytes 393224 | tf_op jit(solution)/shard_map/ppermute | solution.py:422
  113.1 6.3 %collective-permute-start.26 = (f16[128,512]{1,0:T(8,128)(2,1)S(1)}, f16[128,512]{1,0:T(8,128)(2,1)S(1)}, u32[]{:S(2)}, u32[]{:S(2)}) collective-permute-start(f16[128,512]{1,0:T(8,128)(2,1)S(1)} %collective-permute-done.25), channel_id=1, source_target_pairs={{0,1},{1,0},{2,3},{3,2},{4,5},{5,4},{6,7},{7,6},{8,9},{9,8},{10,11... | collective-permute-start | bytes 393224 | tf_op jit(solution)/shard_map/ppermute | solution.py:422

commit v7 on v5

--- a/solution.py
+++ b/solution.py
@@ -479,10 +479,6 @@
     y_side = (sketch, sk_c, sk_y, sk_yc), (og_own, og_c, og_y, og_yc)
     z_side = (sketch, sk_c, sk_z, sk_zc), (og_own, og_c, og_z, og_zc)
 
-    def begin(terms, offsets, axis):
-        send, keep = project(*terms, offsets, 4, 2)
-        return exchange(packed(send, 8.0), axis), keep
-
     def direct(terms, offsets, masks):
         send, keep = project(*terms, offsets, 4, 3)
         total = keep[0]
@@ -491,24 +487,13 @@
             total += unpacked(got, 8.0)
         return total
 
-    def middle(state, axis):
-        got, keep = state
-        ahead = packed(keep[0] + unpacked(got[0], 8.0), 4.0)
-        return exchange(ahead, axis), keep[1] + unpacked(got[1], 8.0)
-
-    def finish(state):
-        got, keep = state
-        return keep + unpacked(got, 4.0)
-
     far0_total = direct(y_side, (0, 0, 0, 0), (X | Z0, X, Z0))
     far1_total = direct(z_side, (8, 8, 0, 0), (Y | X, Y, X))
-    near0_state = begin(y_side, (4, 4, 4, 4), X)
-    near1_state = begin(z_side, (12, 12, 4, 4), Y)
+    near0_total = direct(y_side, (4, 4, 4, 4), (X | Z0, X, Z0))
+    near1_total = direct(z_side, (12, 12, 4, 4), (Y | X, Y, X))
     last0 = exchange(packed(far0_total, 2.0), Z1)
     far1_small = packed(far1_total, 2.0)
     last1 = exchange(far1_small, Z1)
-    near0_state = middle(near0_state, Z0)
-    near1_state = middle(near1_state, X)
 
     def momentum_half(half, near, last):
         projected = (near + unpacked(last, 2.0)) * scale
@@ -516,10 +501,10 @@
 
     halves, others = [], []
     small = None
-    for half, near_state, last in ((0, near0_state, last0), (1, near1_state, last1)):
+    for half, near, last in ((0, near0_total, last0), (1, near1_total, last1)):
         if small is not None:
             last, _ = lax.optimization_barrier((last, small))
-        mine = momentum_half(half, finish(near_state), last)
+        mine = momentum_half(half, near, last)
         small = mine.astype(jnp.float16)
         from_core = exchange(small, CORE)
         from_x = exchange(small, X)
@@ -530,8 +515,8 @@
     near, far = (0, CORE), (X, X | CORE)
     for half, rows, relatives in (
         (0, (halves[0], others[0][0]), near),
+        (1, (halves[1], others[1][0]), near),
         (0, others[0][1:], far),
-        (1, (halves[1], others[1][0]), near),
         (1, others[1][1:], far),
     ):
         where = [(rel, half) for rel in relatives]

time: 122 us -> 124 us (1.016)
  waiting for transfers between devices: 51.2 us -> 54.5 us
    ppermute x31 -> x33, waiting for transfers between devices: 51.2 us -> 54.5 us  [exchange(): return lax.ppermute(value, AXES, [(i, i ^ mask) for i in range(size)])]
    ppermute x31 -> x33, starting transfers between devices: 34.2 us -> 33.5 us  [exchange(): return lax.ppermute(value, AXES, [(i, i ^ mask) for i in range(size)])]
  transfers between devices with their start and end apart: 31 -> 33, of which waited for: 10 -> 9; matrix products, arithmetic and copies ran while one was open for 1% -> 1% of each run, Pallas kernels for 21% -> 21%
where the time goes in v7:
time: 124 us
  waiting for transfers between devices  54.5 us (44%)
  starting transfers between devices  33.5 us (27%)
  Pallas kernels  32.5 us (26%)
  between operations  2.39 us (2%)
    ppermute x33, waiting for transfers between devices, exchange(): return lax.ppermute(value, AXES, [(i, i ^ mask) for i in range(size)])  54.5 us
    ppermute x33, starting transfers between devices, exchange(): return lax.ppermute(value, AXES, [(i, i ^ mask) for i in range(size)])  33.5 us
    pallas_call x4, Pallas kernels, update(): pl.pallas_call(functools.partial(update_kernel, where, keep, slabs, min(s...  11.4 us
    pallas_call x2, Pallas kernels, prefetch(): pl.pallas_call(prefetch_kernel, in_specs=[pl.BlockSpec(memory_space=pl.AN...  7 us
    pallas_call x2, Pallas kernels, sketch_parts(): pl.pallas_call(functools.partial(sketch_kernel, first, din_local), in_spe...  6.2 us
    pallas_call x3, Pallas kernels, pack(): pl.pallas_call(functools.partial(pack_kernel, groups, width, part), in_sp...  4.92 us
    pallas_call x4, Pallas kernels, project(): pl.pallas_call(functools.partial(project_kernel, n), grid=(1,), in_specs=...  2.91 us
  transfers between devices with their start and end apart: 33, of which 9 were waited for; matrix products, arithmetic and copies ran while one was open for 1% of the time, Pallas kernels for 21%

profile of v7, /device:TPU:0, one launch (start us, length us, event | category | flops | bytes accessed | tf_op | source)
XLA Modules:
  0.0 124.0 jit_solution(15043193108497873599)
XLA Ops:
  1.9 3.7 %sketch.2 = (bf16[2048,512]{1,0:T(8,128)(2,1)S(1)}, f32[256,512]{1,0:T(8,128)S(1)}, f32[256,512]{1,0:T(8,128)S(1)}) custom-call(s32[1,1]{1,0:T(1,128)} %bitcast.72.refs_0_, s32[1,1]{1,0:T(1,128)} %bitcast.73.refs_1_, bf16[1024,2048]{1,0:T(8,128)(2,1)} %refs_0_.3), custom_call_target="tpu_custom_call" | custom-call | flops 1073741824 | bytes 6291456 | tf_op jit(solution)/shard_map/sketch/pallas_call | solution.py:224
  5.6 0.6 collective-permute-start.1
  6.2 2.5 %sketch.3 = (f32[256,512]{1,0:T(8,128)S(1)}, f32[256,512]{1,0:T(8,128)S(1)}) custom-call(bf16[1024,2048]{1,0:T(8,128)(2,1)} %refs_0_.3, bf16[2048,512]{1,0:T(8,128)(2,1)S(1)} %get-tuple-element.32.refs_1_.refs_2_), custom_call_target="tpu_custom_call" | custom-call | flops 1073741824 | bytes 6291456 | tf_op jit(solution)/shard_map/sketch/pallas_call | solution.py:224
  8.9 3.0 %collective-permute-start.2 = (f32[256,512]{1,0:T(8,128)S(1)}, f32[256,512]{1,0:T(8,128)S(1)}, u32[]{:S(2)}, u32[]{:S(2)}) collective-permute-start(f32[256,512]{1,0:T(8,128)S(1)} %add.58), channel_id=1, source_target_pairs={{0,2},{1,3},{2,0},{3,1},{4,6},{5,7},{6,4},{7,5},{8,10},{9,11},{10,... | collective-permute-start | bytes 1572872 | tf_op jit(solution)/shard_map/ppermute | solution.py:422
  11.9 2.0 %pack.3 = (bf16[16,256,128]{2,1,0:T(8,128)(2,1)S(1)}, bf16[16,256,128]{2,1,0:T(8,128)(2,1)S(1)}) custom-call(bf16[256,8192]{1,0:T(8,128)(2,1)} %og_ref.5), custom_call_target="tpu_custom_call" | custom-call | bytes 4194304 | tf_op jit(solution)/shard_map/pack/pallas_call | solution.py:127
  14.0 1.5 %pack.4 = (bf16[8,256,128]{2,1,0:T(8,128)(2,1)S(1)}, bf16[8,256,128]{2,1,0:T(8,128)(2,1)S(1)}) custom-call(bf16[256,8192]{1,0:T(8,128)(2,1)} %og_ref.5), custom_call_target="tpu_custom_call" | custom-call | bytes 2097152 | tf_op jit(solution)/shard_map/pack/pallas_call | solution.py:127
  15.5 1.6 %collective-permute-start.18 = (bf16[8,256,128]{2,1,0:T(8,128)(2,1)S(1)}, bf16[8,256,128]{2,1,0:T(8,128)(2,1)S(1)}, u32[]{:S(2)}, u32[]{:S(2)}) collective-permute-start(bf16[8,256,128]{2,1,0:T(8,128)(2,1)S(1)} %get-tuple-element.45), channel_id=1, source_target_pairs={{0,4},{1,5},{2,6},{3,7},{4,0},{5,1},{6,2},{7,3},{8,12},{9,13},{10,... | collective-permute-start | bytes 1572872 | tf_op jit(solution)/shard_map/ppermute | solution.py:422
  17.1 1.5 %pack.5 = (bf16[8,256,128]{2,1,0:T(8,128)(2,1)S(1)}, bf16[8,256,128]{2,1,0:T(8,128)(2,1)S(1)}) custom-call(bf16[256,8192]{1,0:T(8,128)(2,1)} %og_ref.5), custom_call_target="tpu_custom_call" | custom-call | bytes 2097152 | tf_op jit(solution)/shard_map/pack/pallas_call | solution.py:127
  18.5 0.4 collective-permute-start.19
  18.9 5.1 %collective-permute-done.2 = f32[256,512]{1,0:T(8,128)S(1)} collective-permute-done((f32[256,512]{1,0:T(8,128)S(1)}, f32[256,512]{1,0:T(8,128)S(1)}, u32[]{:S(2)}, u32[]{:S(2)}) %collective-permute-start.2) | collective-permute-done | bytes 524320 | tf_op jit(solution)/shard_map/ppermute | solution.py:422
  24.2 1.9 %collective-permute-start.16 = (bf16[256,512]{1,0:T(8,128)(2,1)S(1)}, bf16[256,512]{1,0:T(8,128)(2,1)S(1)}, u32[]{:S(2)}, u32[]{:S(2)}) collective-permute-start(bf16[256,512]{1,0:T(8,128)(2,1)S(1)} %multiply_convert_fusion.refs_0_), channel_id=1, source_target_pairs={{0,4},{1,5},{2,6},{3,7},{4,0},{5,1},{6,2},{7,3},{8,12},{9,13},{10,... | collective-permute-start | bytes 786440 | tf_op jit(solution)/shard_map/ppermute | solution.py:422
  26.1 1.6 %collective-permute-start.4 = (bf16[256,512]{1,0:T(8,128)(2,1)S(1)}, bf16[256,512]{1,0:T(8,128)(2,1)S(1)}, u32[]{:S(2)}, u32[]{:S(2)}) collective-permute-start(bf16[256,512]{1,0:T(8,128)(2,1)S(1)} %multiply_convert_fusion.refs_0_), channel_id=1, source_target_pairs={{0,8},{1,9},{2,10},{3,11},{4,12},{5,13},{6,14},{7,15},{8,0},{9,1},... | collective-permute-start | bytes 786440 | tf_op jit(solution)/shard_map/ppermute | solution.py:422
  27.6 2.7 %collective-permute-done.18.refs_6_ = bf16[8,256,128]{2,1,0:T(8,128)(2,1)S(1)} collective-permute-done((bf16[8,256,128]{2,1,0:T(8,128)(2,1)S(1)}, bf16[8,256,128]{2,1,0:T(8,128)(2,1)S(1)}, u32[]{:S(2)}, u32[]{:S(2)}) %collective-permute-start.18) | collective-permute-done | bytes 524320 | tf_op jit(solution)/shard_map/ppermute | solution.py:422
  30.3 16.4 %collective-permute-done.16.refs_2_ = bf16[256,512]{1,0:T(8,128)(2,1)S(1)} collective-permute-done((bf16[256,512]{1,0:T(8,128)(2,1)S(1)}, bf16[256,512]{1,0:T(8,128)(2,1)S(1)}, u32[]{:S(2)}, u32[]{:S(2)}) %collective-permute-start.16) | collective-permute-done | bytes 262176 | tf_op jit(solution)/shard_map/ppermute | solution.py:422
  46.7 1.6 %collective-permute-start.7 = (bf16[8,256,128]{2,1,0:T(8,128)(2,1)S(1)}, bf16[8,256,128]{2,1,0:T(8,128)(2,1)S(1)}, u32[]{:S(2)}, u32[]{:S(2)}) collective-permute-start(bf16[8,256,128]{2,1,0:T(8,128)(2,1)S(1)} %get-tuple-element.39), channel_id=1, source_target_pairs={{0,8},{1,9},{2,10},{3,11},{4,12},{5,13},{6,14},{7,15},{8,0},{9,1},... | collective-permute-start | bytes 1572872 | tf_op jit(solution)/shard_map/ppermute | solution.py:422
  48.6 0.3 collective-permute-start.5
  48.9 0.7 project.7
  49.7 1.6 %collective-permute-start.23 = (f16[128,512]{1,0:T(8,128)(2,1)S(1)}, f16[128,512]{1,0:T(8,128)(2,1)S(1)}, u32[]{:S(2)}, u32[]{:S(2)}) collective-permute-start(f16[128,512]{1,0:T(8,128)(2,1)S(1)} %get-tuple-element.71), channel_id=1, source_target_pairs={{0,10},{1,11},{2,8},{3,9},{4,14},{5,15},{6,12},{7,13},{8,2},{9,3},... | collective-permute-start | bytes 393224 | tf_op jit(solution)/shard_map/ppermute | solution.py:422
  51.3 1.5 %collective-permute-start.24 = (f16[128,512]{1,0:T(8,128)(2,1)S(1)}, f16[128,512]{1,0:T(8,128)(2,1)S(1)}, u32[]{:S(2)}, u32[]{:S(2)}) collective-permute-start(f16[128,512]{1,0:T(8,128)(2,1)S(1)} %get-tuple-element.73), channel_id=1, source_target_pairs={{0,2},{1,3},{2,0},{3,1},{4,6},{5,7},{6,4},{7,5},{8,10},{9,11},{10,... | collective-permute-start | bytes 393224 | tf_op jit(solution)/shard_map/ppermute | solution.py:422
  52.8 0.7 project.6
  53.6 7.9 %collective-permute-done.7.refs_6_ = bf16[8,256,128]{2,1,0:T(8,128)(2,1)S(1)} collective-permute-done((bf16[8,256,128]{2,1,0:T(8,128)(2,1)S(1)}, bf16[8,256,128]{2,1,0:T(8,128)(2,1)S(1)}, u32[]{:S(2)}, u32[]{:S(2)}) %collective-permute-start.7) | collective-permute-done | bytes 524320 | tf_op jit(solution)/shard_map/ppermute | solution.py:422
  61.5 1.6 %collective-permute-start.25 = (f16[128,512]{1,0:T(8,128)(2,1)S(1)}, f16[128,512]{1,0:T(8,128)(2,1)S(1)}, u32[]{:S(2)}, u32[]{:S(2)}) collective-permute-start(f16[128,512]{1,0:T(8,128)(2,1)S(1)} %get-tuple-element.72), channel_id=1, source_target_pairs={{0,8},{1,9},{2,10},{3,11},{4,12},{5,13},{6,14},{7,15},{8,0},{9,1},... | collective-permute-start | bytes 393224 | tf_op jit(solution)/shard_map/ppermute | solution.py:422
  63.1 8.8 %collective-permute-done.8.refs_7_ = bf16[8,256,128]{2,1,0:T(8,128)(2,1)S(1)} collective-permute-done((bf16[8,256,128]{2,1,0:T(8,128)(2,1)S(1)}, bf16[8,256,128]{2,1,0:T(8,128)(2,1)S(1)}, u32[]{:S(2)}, u32[]{:S(2)}) %collective-permute-start.8) | collective-permute-done | bytes 524320 | tf_op jit(solution)/shard_map/ppermute | solution.py:422
  71.8 1.5 %collective-permute-start.20 = (f16[128,512]{1,0:T(8,128)(2,1)S(1)}, f16[128,512]{1,0:T(8,128)(2,1)S(1)}, u32[]{:S(2)}, u32[]{:S(2)}) collective-permute-start(f16[128,512]{1,0:T(8,128)(2,1)S(1)} %get-tuple-element.68), channel_id=1, source_target_pairs={{0,10},{1,11},{2,8},{3,9},{4,14},{5,15},{6,12},{7,13},{8,2},{9,3},... | collective-permute-start | bytes 393224 | tf_op jit(solution)/shard_map/ppermute | solution.py:422
  73.3 1.5 %collective-permute-start.21 = (f16[128,512]{1,0:T(8,128)(2,1)S(1)}, f16[128,512]{1,0:T(8,128)(2,1)S(1)}, u32[]{:S(2)}, u32[]{:S(2)}) collective-permute-start(f16[128,512]{1,0:T(8,128)(2,1)S(1)} %get-tuple-element.70), channel_id=1, source_target_pairs={{0,2},{1,3},{2,0},{3,1},{4,6},{5,7},{6,4},{7,5},{8,10},{9,11},{10,... | collective-permute-start | bytes 393224 | tf_op jit(solution)/shard_map/ppermute | solution.py:422
  74.9 0.7 project.5
  75.7 0.7 project.4
  76.5 1.5 %collective-permute-start.12 = (f16[128,512]{1,0:T(8,128)(2,1)S(1)}, f16[128,512]{1,0:T(8,128)(2,1)S(1)}, u32[]{:S(2)}, u32[]{:S(2)}) collective-permute-start(f16[128,512]{1,0:T(8,128)(2,1)S(1)} %get-tuple-element.74), channel_id=1, source_target_pairs={{0,6},{1,7},{2,4},{3,5},{4,2},{5,3},{6,0},{7,1},{8,14},{9,15},{10,... | collective-permute-start | bytes 393224 | tf_op jit(solution)/shard_map/ppermute | solution.py:422
  78.0 0.5 collective-permute-start.13
  78.5 1.5 %collective-permute-start.14 = (f16[128,512]{1,0:T(8,128)(2,1)S(1)}, f16[128,512]{1,0:T(8,128)(2,1)S(1)}, u32[]{:S(2)}, u32[]{:S(2)}) collective-permute-start(f16[128,512]{1,0:T(8,128)(2,1)S(1)} %get-tuple-element.75), channel_id=1, source_target_pairs={{0,2},{1,3},{2,0},{3,1},{4,6},{5,7},{6,4},{7,5},{8,10},{9,11},{10,... | collective-permute-start | bytes 393224 | tf_op jit(solution)/shard_map/ppermute | solution.py:422
  80.2 6.2 %collective-permute-done.12 = f16[128,512]{1,0:T(8,128)(2,1)S(1)} collective-permute-done((f16[128,512]{1,0:T(8,128)(2,1)S(1)}, f16[128,512]{1,0:T(8,128)(2,1)S(1)}, u32[]{:S(2)}, u32[]{:S(2)}) %collective-permute-start.12) | collective-permute-done | bytes 131104 | tf_op jit(solution)/shard_map/ppermute | solution.py:422
  86.3 0.5 collective-permute-start.22
  86.8 0.5 collective-permute-start.10
  87.3 0.4 collective-permute-done.14
  87.8 2.6 %collective-permute-start.26 = (f16[128,512]{1,0:T(8,128)(2,1)S(1)}, f16[128,512]{1,0:T(8,128)(2,1)S(1)}, u32[]{:S(2)}, u32[]{:S(2)}) collective-permute-start(f16[128,512]{1,0:T(8,128)(2,1)S(1)} %fusion.3), channel_id=1, source_target_pairs={{0,16},{1,17},{2,18},{3,19},{4,20},{5,21},{6,22},{7,23},{8,24},{9,... | collective-permute-start | bytes 393224 | tf_op jit(solution)/shard_map/ppermute | solution.py:422
  90.5 1.8 %collective-permute-start.11 = (f16[128,512]{1,0:T(8,128)(2,1)S(1)}, f16[128,512]{1,0:T(8,128)(2,1)S(1)}, u32[]{:S(2)}, u32[]{:S(2)}) collective-permute-start(f16[128,512]{1,0:T(8,128)(2,1)S(1)} %get-tuple-element.66), channel_id=1, source_target_pairs={{0,2},{1,3},{2,0},{3,1},{4,6},{5,7},{6,4},{7,5},{8,10},{9,11},{10,... | collective-permute-start | bytes 393224 | tf_op jit(solution)/shard_map/ppermute | solution.py:422
  92.3 1.2 %collective-permute-start.9 = (f16[128,512]{1,0:T(8,128)(2,1)S(1)}, f16[128,512]{1,0:T(8,128)(2,1)S(1)}, u32[]{:S(2)}, u32[]{:S(2)}) collective-permute-start(f16[128,512]{1,0:T(8,128)(2,1)S(1)} %get-tuple-element.65), channel_id=1, source_target_pairs={{0,6},{1,7},{2,4},{3,5},{4,2},{5,3},{6,0},{7,1},{8,14},{9,15},{10,... | collective-permute-start | bytes 393224 | tf_op jit(solution)/shard_map/ppermute | solution.py:422
  93.5 1.4 %collective-permute-start.15 = (f16[128,512]{1,0:T(8,128)(2,1)S(1)}, f16[128,512]{1,0:T(8,128)(2,1)S(1)}, u32[]{:S(2)}, u32[]{:S(2)}) collective-permute-start(f16[128,512]{1,0:T(8,128)(2,1)S(1)} %fusion.12), channel_id=1, source_target_pairs={{0,16},{1,17},{2,18},{3,19},{4,20},{5,21},{6,22},{7,23},{8,24},{9,... | collective-permute-start | bytes 393224 | tf_op jit(solution)/shard_map/ppermute | solution.py:422
  94.9 3.5 %collective-permute-done.26 = f16[128,512]{1,0:T(8,128)(2,1)S(1)} collective-permute-done((f16[128,512]{1,0:T(8,128)(2,1)S(1)}, f16[128,512]{1,0:T(8,128)(2,1)S(1)}, u32[]{:S(2)}, u32[]{:S(2)}) %collective-permute-start.26) | collective-permute-done | bytes 131104 | tf_op jit(solution)/shard_map/ppermute | solution.py:422
  98.7 3.5 %collective-permute-done.15 = f16[128,512]{1,0:T(8,128)(2,1)S(1)} collective-permute-done((f16[128,512]{1,0:T(8,128)(2,1)S(1)}, f16[128,512]{1,0:T(8,128)(2,1)S(1)}, u32[]{:S(2)}, u32[]{:S(2)}) %collective-permute-start.15) | collective-permute-done | bytes 131104 | tf_op jit(solution)/shard_map/ppermute | solution.py:422
  102.2 2.0 %collective-permute-start.29 = (f16[128,512]{1,0:T(8,128)(2,1)S(1)}, f16[128,512]{1,0:T(8,128)(2,1)S(1)}, u32[]{:S(2)}, u32[]{:S(2)}) collective-permute-start(f16[128,512]{1,0:T(8,128)(2,1)S(1)} %get-tuple-element.63), channel_id=1, source_target_pairs={{0,2},{1,3},{2,0},{3,1},{4,6},{5,7},{6,4},{7,5},{8,10},{9,11},{10,... | collective-permute-start | bytes 393224 | tf_op jit(solution)/shard_map/ppermute | solution.py:422
  104.5 3.5 %prefetch.2.refs_3_ = f32[1024,2048]{1,0:T(8,128)S(1)} custom-call(f32[1024,2048]{1,0:T(8,128)} %refs_0_.4), custom_call_target="tpu_custom_call" | custom-call | bytes 8388608 | tf_op jit(solution)/shard_map/prefetch/pallas_call | solution.py:309
  108.0 3.5 %prefetch.3.refs_4_ = f32[1024,2048]{1,0:T(8,128)S(1)} custom-call(f32[1024,2048]{1,0:T(8,128)} %refs_0_.5), custom_call_target="tpu_custom_call" | custom-call | bytes 8388608 | tf_op jit(solution)/shard_map/prefetch/pallas_call | solution.py:309
  111.6 0.5 collective-permute-start.30
  112.0 2.9 %update.4 = (f32[1024,2048]{1,0:T(8,128)}, f32[1024,2048]{1,0:T(8,128)}, f32[256,512]{1,0:T(8,128)}) custom-call(f32[128,512]{1,0:T(8,128)S(1)} %get-tuple-element.64.refs_0_, f32[128,512]{1,0:T(8,128)S(1)} %convert_element_type.195.refs_1_, bf16[2048,512]{1,0:T(8,128)(2,1)S(1)} %get-tuple-element.32.refs_1_.refs_2_, f32[1024,2048]{1,0:T(8,128)S(1)} %prefetch.2.refs_3_, ...), custom_call_target="tpu_custom_call" | custom-call | flops 1073741824 | bytes 4194304 | tf_op jit(solution)/shard_map/update/pallas_call | solution.py:391
  115.2 2.9 %update.5 = (f32[1024,2048]{1,0:T(8,128)}, f32[1024,2048]{1,0:T(8,128)}, f32[256,512]{1,0:T(8,128)}) custom-call(f32[128,512]{1,0:T(8,128)S(1)} %get-tuple-element.62.refs_0_, f32[128,512]{1,0:T(8,128)S(1)} %convert_element_type.194.refs_1_, ...), custom_call_target="tpu_custom_call", output_to_operand_aliasing={{0}: (5, {}), {1}: (6, {}), {2}: (7, {})} | custom-call | flops 1073741824 | bytes 4194304 | tf_op jit(solution)/shard_map/update/pallas_call | solution.py:391
  118.2 2.8 %update.6 = (f32[1024,2048]{1,0:T(8,128)}, f32[1024,2048]{1,0:T(8,128)}, f32[256,512]{1,0:T(8,128)}) custom-call(f32[128,512]{1,0:T(8,128)S(1)} %convert_element_type.192.refs_0_, f32[128,512]{1,0:T(8,128)S(1)} %convert_element_type.193.refs_1_, ...), custom_call_target="tpu_custom_call", output_to_operand_aliasing={{0}: (5, {}), {1}: (6, {}), {2}: (7, {})} | custom-call | flops 1073741824 | bytes 4194304 | tf_op jit(solution)/shard_map/update/pallas_call | solution.py:391
  121.0 2.8 %update.7 = (f32[1024,2048]{1,0:T(8,128)}, f32[1024,2048]{1,0:T(8,128)}, f32[256,512]{1,0:T(8,128)}) custom-call(f32[128,512]{1,0:T(8,128)S(1)} %convert_element_type.190.refs_0_, f32[128,512]{1,0:T(8,128)S(1)} %convert_element_type.191.refs_1_, ...), custom_call_target="tpu_custom_call", output_to_operand_aliasing={{0}: (5, {}), {1}: (6, {}), {2}: (7, {})} | custom-call | flops 1073741824 | bytes 4194304 | tf_op jit(solution)/shard_map/update/pallas_call | solution.py:391
  (51 shorter events, 2.1 us)
Async XLA Ops:
  5.6 3.2 %collective-permute-start.1 = (f32[256,512]{1,0:T(8,128)S(1)}, f32[256,512]{1,0:T(8,128)S(1)}, u32[]{:S(2)}, u32[]{:S(2)}) collective-permute-start(f32[256,512]{1,0:T(8,128)S(1)} %get-tuple-element.36), channel_id=1, source_target_pairs={{0,1},{1,0},{2,3},{3,2},{4,5},{5,4},{6,7},{7,6},{8,9},{9,8},{10,11... | collective-permute-start | bytes 1572872 | tf_op jit(solution)/shard_map/ppermute | solution.py:422
  8.7 10.2 %collective-permute-start = (f32[256,512]{1,0:T(8,128)S(1)}, f32[256,512]{1,0:T(8,128)S(1)}, u32[]{:S(2)}, u32[]{:S(2)}) collective-permute-start(f32[256,512]{1,0:T(8,128)S(1)} %get-tuple-element.34), channel_id=1, source_target_pairs={{0,1},{1,0},{2,3},{3,2},{4,5},{5,4},{6,7},{7,6},{8,9},{9,8},{10,11... | collective-permute-start | bytes 1572872 | tf_op jit(solution)/shard_map/ppermute | solution.py:422
  8.9 15.1 %collective-permute-start.2 = (f32[256,512]{1,0:T(8,128)S(1)}, f32[256,512]{1,0:T(8,128)S(1)}, u32[]{:S(2)}, u32[]{:S(2)}) collective-permute-start(f32[256,512]{1,0:T(8,128)S(1)} %add.58), channel_id=1, source_target_pairs={{0,2},{1,3},{2,0},{3,1},{4,6},{5,7},{6,4},{7,5},{8,10},{9,11},{10,... | collective-permute-start | bytes 1572872 | tf_op jit(solution)/shard_map/ppermute | solution.py:422
  13.9 34.4 %collective-permute-start.6 = (bf16[16,256,128]{2,1,0:T(8,128)(2,1)S(1)}, bf16[16,256,128]{2,1,0:T(8,128)(2,1)S(1)}, u32[]{:S(2)}, u32[]{:S(2)}) collective-permute-start(bf16[16,256,128]{2,1,0:T(8,128)(2,1)S(1)} %get-tuple-element.38), channel_id=1, source_target_pairs={{0,1},{1,0},{2,3},{3,2},{4,5},{5,4},{6,7},{7,6},{8,9},{9,8},{10,11... | collective-permute-start | bytes 3145736 | tf_op jit(solution)/shard_map/ppermute | solution.py:422
  15.5 14.9 %collective-permute-start.18 = (bf16[8,256,128]{2,1,0:T(8,128)(2,1)S(1)}, bf16[8,256,128]{2,1,0:T(8,128)(2,1)S(1)}, u32[]{:S(2)}, u32[]{:S(2)}) collective-permute-start(bf16[8,256,128]{2,1,0:T(8,128)(2,1)S(1)} %get-tuple-element.45), channel_id=1, source_target_pairs={{0,4},{1,5},{2,6},{3,7},{4,0},{5,1},{6,2},{7,3},{8,12},{9,13},{10,... | collective-permute-start | bytes 1572872 | tf_op jit(solution)/shard_map/ppermute | solution.py:422
  18.5 28.2 %collective-permute-start.19 = (bf16[8,256,128]{2,1,0:T(8,128)(2,1)S(1)}, bf16[8,256,128]{2,1,0:T(8,128)(2,1)S(1)}, u32[]{:S(2)}, u32[]{:S(2)}) collective-permute-start(bf16[8,256,128]{2,1,0:T(8,128)(2,1)S(1)} %get-tuple-element.46), channel_id=1, source_target_pairs={{0,5},{1,4},{2,7},{3,6},{4,1},{5,0},{6,3},{7,2},{8,13},{9,12},{10,... | collective-permute-start | bytes 1572872 | tf_op jit(solution)/shard_map/ppermute | solution.py:422
  24.2 22.5 %collective-permute-start.16 = (bf16[256,512]{1,0:T(8,128)(2,1)S(1)}, bf16[256,512]{1,0:T(8,128)(2,1)S(1)}, u32[]{:S(2)}, u32[]{:S(2)}) collective-permute-start(bf16[256,512]{1,0:T(8,128)(2,1)S(1)} %multiply_convert_fusion.refs_0_), channel_id=1, source_target_pairs={{0,4},{1,5},{2,6},{3,7},{4,0},{5,1},{6,2},{7,3},{8,12},{9,13},{10,... | collective-permute-start | bytes 786440 | tf_op jit(solution)/shard_map/ppermute | solution.py:422
  26.1 22.5 %collective-permute-start.4 = (bf16[256,512]{1,0:T(8,128)(2,1)S(1)}, bf16[256,512]{1,0:T(8,128)(2,1)S(1)}, u32[]{:S(2)}, u32[]{:S(2)}) collective-permute-start(bf16[256,512]{1,0:T(8,128)(2,1)S(1)} %multiply_convert_fusion.refs_0_), channel_id=1, source_target_pairs={{0,8},{1,9},{2,10},{3,11},{4,12},{5,13},{6,14},{7,15},{8,0},{9,1},... | collective-permute-start | bytes 786440 | tf_op jit(solution)/shard_map/ppermute | solution.py:422
  30.3 18.5 %collective-permute-start.3 = (bf16[256,512]{1,0:T(8,128)(2,1)S(1)}, bf16[256,512]{1,0:T(8,128)(2,1)S(1)}, u32[]{:S(2)}, u32[]{:S(2)}) collective-permute-start(bf16[256,512]{1,0:T(8,128)(2,1)S(1)} %multiply_convert_fusion.refs_0_), channel_id=1, source_target_pairs={{0,1},{1,0},{2,3},{3,2},{4,5},{5,4},{6,7},{7,6},{8,9},{9,8},{10,11... | collective-permute-start | bytes 786440 | tf_op jit(solution)/shard_map/ppermute | solution.py:422
  46.7 2.2 %collective-permute-start.17 = (bf16[256,512]{1,0:T(8,128)(2,1)S(1)}, bf16[256,512]{1,0:T(8,128)(2,1)S(1)}, u32[]{:S(2)}, u32[]{:S(2)}) collective-permute-start(bf16[256,512]{1,0:T(8,128)(2,1)S(1)} %collective-permute-done.16.refs_2_), channel_id=1, source_target_pairs={{0,1},{1,0},{2,3},{3,2},{4,5},{5,4},{6,7},{7,6},{8,9},{9,8},{10,11... | collective-permute-start | bytes 786440 | tf_op jit(solution)/shard_map/ppermute | solution.py:422
  46.7 14.8 %collective-permute-start.7 = (bf16[8,256,128]{2,1,0:T(8,128)(2,1)S(1)}, bf16[8,256,128]{2,1,0:T(8,128)(2,1)S(1)}, u32[]{:S(2)}, u32[]{:S(2)}) collective-permute-start(bf16[8,256,128]{2,1,0:T(8,128)(2,1)S(1)} %get-tuple-element.39), channel_id=1, source_target_pairs={{0,8},{1,9},{2,10},{3,11},{4,12},{5,13},{6,14},{7,15},{8,0},{9,1},... | collective-permute-start | bytes 1572872 | tf_op jit(solution)/shard_map/ppermute | solution.py:422
  48.3 23.5 %collective-permute-start.8 = (bf16[8,256,128]{2,1,0:T(8,128)(2,1)S(1)}, bf16[8,256,128]{2,1,0:T(8,128)(2,1)S(1)}, u32[]{:S(2)}, u32[]{:S(2)}) collective-permute-start(bf16[8,256,128]{2,1,0:T(8,128)(2,1)S(1)} %get-tuple-element.40), channel_id=1, source_target_pairs={{0,9},{1,8},{2,11},{3,10},{4,13},{5,12},{6,15},{7,14},{8,1},{9,0},... | collective-permute-start | bytes 1572872 | tf_op jit(solution)/shard_map/ppermute | solution.py:422
  48.6 24.8 %collective-permute-start.5 = (bf16[256,512]{1,0:T(8,128)(2,1)S(1)}, bf16[256,512]{1,0:T(8,128)(2,1)S(1)}, u32[]{:S(2)}, u32[]{:S(2)}) collective-permute-start(bf16[256,512]{1,0:T(8,128)(2,1)S(1)} %collective-permute-done.4.refs_2_), channel_id=1, source_target_pairs={{0,1},{1,0},{2,3},{3,2},{4,5},{5,4},{6,7},{7,6},{8,9},{9,8},{10,11... | collective-permute-start | bytes 786440 | tf_op jit(solution)/shard_map/ppermute | solution.py:422
  49.7 26.8 %collective-permute-start.23 = (f16[128,512]{1,0:T(8,128)(2,1)S(1)}, f16[128,512]{1,0:T(8,128)(2,1)S(1)}, u32[]{:S(2)}, u32[]{:S(2)}) collective-permute-start(f16[128,512]{1,0:T(8,128)(2,1)S(1)} %get-tuple-element.71), channel_id=1, source_target_pairs={{0,10},{1,11},{2,8},{3,9},{4,14},{5,15},{6,12},{7,13},{8,2},{9,3},... | collective-permute-start | bytes 393224 | tf_op jit(solution)/shard_map/ppermute | solution.py:422
  51.3 47.2 %copy-start = (f32[256,512]{1,0:T(8,128)S(1)}, f32[256,512]{1,0:T(8,128)}, u32[]{:S(2)}) copy-start(f32[256,512]{1,0:T(8,128)} %param.11) | copy-start | bytes 1572868
  51.3 26.8 %collective-permute-start.24 = (f16[128,512]{1,0:T(8,128)(2,1)S(1)}, f16[128,512]{1,0:T(8,128)(2,1)S(1)}, u32[]{:S(2)}, u32[]{:S(2)}) collective-permute-start(f16[128,512]{1,0:T(8,128)(2,1)S(1)} %get-tuple-element.73), channel_id=1, source_target_pairs={{0,2},{1,3},{2,0},{3,1},{4,6},{5,7},{6,4},{7,5},{8,10},{9,11},{10,... | collective-permute-start | bytes 393224 | tf_op jit(solution)/shard_map/ppermute | solution.py:422
  61.5 17.0 %collective-permute-start.25 = (f16[128,512]{1,0:T(8,128)(2,1)S(1)}, f16[128,512]{1,0:T(8,128)(2,1)S(1)}, u32[]{:S(2)}, u32[]{:S(2)}) collective-permute-start(f16[128,512]{1,0:T(8,128)(2,1)S(1)} %get-tuple-element.72), channel_id=1, source_target_pairs={{0,8},{1,9},{2,10},{3,11},{4,12},{5,13},{6,14},{7,15},{8,0},{9,1},... | collective-permute-start | bytes 393224 | tf_op jit(solution)/shard_map/ppermute | solution.py:422
  71.8 18.6 %collective-permute-start.20 = (f16[128,512]{1,0:T(8,128)(2,1)S(1)}, f16[128,512]{1,0:T(8,128)(2,1)S(1)}, u32[]{:S(2)}, u32[]{:S(2)}) collective-permute-start(f16[128,512]{1,0:T(8,128)(2,1)S(1)} %get-tuple-element.68), channel_id=1, source_target_pairs={{0,10},{1,11},{2,8},{3,9},{4,14},{5,15},{6,12},{7,13},{8,2},{9,3},... | collective-permute-start | bytes 393224 | tf_op jit(solution)/shard_map/ppermute | solution.py:422
  73.3 18.9 %collective-permute-start.21 = (f16[128,512]{1,0:T(8,128)(2,1)S(1)}, f16[128,512]{1,0:T(8,128)(2,1)S(1)}, u32[]{:S(2)}, u32[]{:S(2)}) collective-permute-start(f16[128,512]{1,0:T(8,128)(2,1)S(1)} %get-tuple-element.70), channel_id=1, source_target_pairs={{0,2},{1,3},{2,0},{3,1},{4,6},{5,7},{6,4},{7,5},{8,10},{9,11},{10,... | collective-permute-start | bytes 393224 | tf_op jit(solution)/shard_map/ppermute | solution.py:422
  76.5 9.8 %collective-permute-start.12 = (f16[128,512]{1,0:T(8,128)(2,1)S(1)}, f16[128,512]{1,0:T(8,128)(2,1)S(1)}, u32[]{:S(2)}, u32[]{:S(2)}) collective-permute-start(f16[128,512]{1,0:T(8,128)(2,1)S(1)} %get-tuple-element.74), channel_id=1, source_target_pairs={{0,6},{1,7},{2,4},{3,5},{4,2},{5,3},{6,0},{7,1},{8,14},{9,15},{10,... | collective-permute-start | bytes 393224 | tf_op jit(solution)/shard_map/ppermute | solution.py:422
  78.0 8.8 %collective-permute-start.13 = (f16[128,512]{1,0:T(8,128)(2,1)S(1)}, f16[128,512]{1,0:T(8,128)(2,1)S(1)}, u32[]{:S(2)}, u32[]{:S(2)}) collective-permute-start(f16[128,512]{1,0:T(8,128)(2,1)S(1)} %get-tuple-element.76), channel_id=1, source_target_pairs={{0,4},{1,5},{2,6},{3,7},{4,0},{5,1},{6,2},{7,3},{8,12},{9,13},{10,... | collective-permute-start | bytes 393224 | tf_op jit(solution)/shard_map/ppermute | solution.py:422
  78.5 9.2 %collective-permute-start.14 = (f16[128,512]{1,0:T(8,128)(2,1)S(1)}, f16[128,512]{1,0:T(8,128)(2,1)S(1)}, u32[]{:S(2)}, u32[]{:S(2)}) collective-permute-start(f16[128,512]{1,0:T(8,128)(2,1)S(1)} %get-tuple-element.75), channel_id=1, source_target_pairs={{0,2},{1,3},{2,0},{3,1},{4,6},{5,7},{6,4},{7,5},{8,10},{9,11},{10,... | collective-permute-start | bytes 393224 | tf_op jit(solution)/shard_map/ppermute | solution.py:422
  86.3 7.2 %collective-permute-start.22 = (f16[128,512]{1,0:T(8,128)(2,1)S(1)}, f16[128,512]{1,0:T(8,128)(2,1)S(1)}, u32[]{:S(2)}, u32[]{:S(2)}) collective-permute-start(f16[128,512]{1,0:T(8,128)(2,1)S(1)} %get-tuple-element.69), channel_id=1, source_target_pairs={{0,8},{1,9},{2,10},{3,11},{4,12},{5,13},{6,14},{7,15},{8,0},{9,1},... | collective-permute-start | bytes 393224 | tf_op jit(solution)/shard_map/ppermute | solution.py:422
  86.8 17.3 %collective-permute-start.10 = (f16[128,512]{1,0:T(8,128)(2,1)S(1)}, f16[128,512]{1,0:T(8,128)(2,1)S(1)}, u32[]{:S(2)}, u32[]{:S(2)}) collective-permute-start(f16[128,512]{1,0:T(8,128)(2,1)S(1)} %get-tuple-element.67), channel_id=1, source_target_pairs={{0,4},{1,5},{2,6},{3,7},{4,0},{5,1},{6,2},{7,3},{8,12},{9,13},{10,... | collective-permute-start | bytes 393224 | tf_op jit(solution)/shard_map/ppermute | solution.py:422
  87.8 10.7 %collective-permute-start.26 = (f16[128,512]{1,0:T(8,128)(2,1)S(1)}, f16[128,512]{1,0:T(8,128)(2,1)S(1)}, u32[]{:S(2)}, u32[]{:S(2)}) collective-permute-start(f16[128,512]{1,0:T(8,128)(2,1)S(1)} %fusion.3), channel_id=1, source_target_pairs={{0,16},{1,17},{2,18},{3,19},{4,20},{5,21},{6,22},{7,23},{8,24},{9,... | collective-permute-start | bytes 393224 | tf_op jit(solution)/shard_map/ppermute | solution.py:422
  90.5 13.7 %collective-permute-start.11 = (f16[128,512]{1,0:T(8,128)(2,1)S(1)}, f16[128,512]{1,0:T(8,128)(2,1)S(1)}, u32[]{:S(2)}, u32[]{:S(2)}) collective-permute-start(f16[128,512]{1,0:T(8,128)(2,1)S(1)} %get-tuple-element.66), channel_id=1, source_target_pairs={{0,2},{1,3},{2,0},{3,1},{4,6},{5,7},{6,4},{7,5},{8,10},{9,11},{10,... | collective-permute-start | bytes 393224 | tf_op jit(solution)/shard_map/ppermute | solution.py:422
  92.3 11.9 %collective-permute-start.9 = (f16[128,512]{1,0:T(8,128)(2,1)S(1)}, f16[128,512]{1,0:T(8,128)(2,1)S(1)}, u32[]{:S(2)}, u32[]{:S(2)}) collective-permute-start(f16[128,512]{1,0:T(8,128)(2,1)S(1)} %get-tuple-element.65), channel_id=1, source_target_pairs={{0,6},{1,7},{2,4},{3,5},{4,2},{5,3},{6,0},{7,1},{8,14},{9,15},{10,... | collective-permute-start | bytes 393224 | tf_op jit(solution)/shard_map/ppermute | solution.py:422
  93.5 8.7 %collective-permute-start.15 = (f16[128,512]{1,0:T(8,128)(2,1)S(1)}, f16[128,512]{1,0:T(8,128)(2,1)S(1)}, u32[]{:S(2)}, u32[]{:S(2)}) collective-permute-start(f16[128,512]{1,0:T(8,128)(2,1)S(1)} %fusion.12), channel_id=1, source_target_pairs={{0,16},{1,17},{2,18},{3,19},{4,20},{5,21},{6,22},{7,23},{8,24},{9,... | collective-permute-start | bytes 393224 | tf_op jit(solution)/shard_map/ppermute | solution.py:422
  98.6 12.9 %collective-permute-start.32 = (f16[128,512]{1,0:T(8,128)(2,1)S(1)}, f16[128,512]{1,0:T(8,128)(2,1)S(1)}, u32[]{:S(2)}, u32[]{:S(2)}) collective-permute-start(f16[128,512]{1,0:T(8,128)(2,1)S(1)} %get-tuple-element.63), channel_id=1, source_target_pairs={{0,1},{1,0},{2,3},{3,2},{4,5},{5,4},{6,7},{7,6},{8,9},{9,8},{10,11... | collective-permute-start | bytes 393224 | tf_op jit(solution)/shard_map/ppermute | solution.py:422
  102.2 9.4 %collective-permute-start.29 = (f16[128,512]{1,0:T(8,128)(2,1)S(1)}, f16[128,512]{1,0:T(8,128)(2,1)S(1)}, u32[]{:S(2)}, u32[]{:S(2)}) collective-permute-start(f16[128,512]{1,0:T(8,128)(2,1)S(1)} %get-tuple-element.63), channel_id=1, source_target_pairs={{0,2},{1,3},{2,0},{3,1},{4,6},{5,7},{6,4},{7,5},{8,10},{9,11},{10,... | collective-permute-start | bytes 393224 | tf_op jit(solution)/shard_map/ppermute | solution.py:422
  104.3 10.6 %collective-permute-start.31 = (f16[128,512]{1,0:T(8,128)(2,1)S(1)}, f16[128,512]{1,0:T(8,128)(2,1)S(1)}, u32[]{:S(2)}, u32[]{:S(2)}) collective-permute-start(f16[128,512]{1,0:T(8,128)(2,1)S(1)} %get-tuple-element.61), channel_id=1, source_target_pairs={{0,1},{1,0},{2,3},{3,2},{4,5},{5,4},{6,7},{7,6},{8,9},{9,8},{10,11... | collective-permute-start | bytes 393224 | tf_op jit(solution)/shard_map/ppermute | solution.py:422
  104.4 10.6 %collective-permute-start.27 = (f16[128,512]{1,0:T(8,128)(2,1)S(1)}, f16[128,512]{1,0:T(8,128)(2,1)S(1)}, u32[]{:S(2)}, u32[]{:S(2)}) collective-permute-start(f16[128,512]{1,0:T(8,128)(2,1)S(1)} %get-tuple-element.61), channel_id=1, source_target_pairs={{0,2},{1,3},{2,0},{3,1},{4,6},{5,7},{6,4},{7,5},{8,10},{9,11},{10,... | collective-permute-start | bytes 393224 | tf_op jit(solution)/shard_map/ppermute | solution.py:422
  111.6 6.6 %collective-permute-start.30 = (f16[128,512]{1,0:T(8,128)(2,1)S(1)}, f16[128,512]{1,0:T(8,128)(2,1)S(1)}, u32[]{:S(2)}, u32[]{:S(2)}) collective-permute-start(f16[128,512]{1,0:T(8,128)(2,1)S(1)} %collective-permute-done.29), channel_id=1, source_target_pairs={{0,1},{1,0},{2,3},{3,2},{4,5},{5,4},{6,7},{7,6},{8,9},{9,8},{10,11... | collective-permute-start | bytes 393224 | tf_op jit(solution)/shard_map/ppermute | solution.py:422
  115.0 6.0 %collective-permute-start.28 = (f16[128,512]{1,0:T(8,128)(2,1)S(1)}, f16[128,512]{1,0:T(8,128)(2,1)S(1)}, u32[]{:S(2)}, u32[]{:S(2)}) collective-permute-start(f16[128,512]{1,0:T(8,128)(2,1)S(1)} %collective-permute-done.27), channel_id=1, source_target_pairs={{0,1},{1,0},{2,3},{3,2},{4,5},{5,4},{6,7},{7,6},{8,9},{9,8},{10,11... | collective-permute-start | bytes 393224 | tf_op jit(solution)/shard_map/ppermute | solution.py:422

commit v8 on v2

--- a/solution.py
+++ b/solution.py
@@ -457,7 +457,8 @@
     og_c = exchange(og_c, CORE)
     send_b, keep_b = sketch_parts(tokens, low_rank, signs, None)
     got_b = exchange(send_b, CORE)
-    weight_v, second_v = prefetch(weight, second)
+    (weight_v,) = prefetch(weight)
+    (second_v,) = prefetch(second)
     sketch = (((keep_b + got_b) + across) * inv_root).astype(jnp.bfloat16)
 
     sk_y = exchange(sketch, Y)
@@ -518,14 +519,15 @@
         halves.append(mine)
         others.append([v.astype(jnp.float32) for v in (from_core, from_x, from_xc)])
     done = ()
+    near, far = (0, CORE), (X, X | CORE)
     for half, rows, relatives in (
-        (0, (halves[0], others[0][0]), (0, CORE)),
-        (0, others[0][1:], (X, X | CORE)),
-        (1, (halves[1], others[1][0]), (0, CORE)),
-        (1, others[1][1:], (X, X | CORE)),
+        (0, (halves[0], others[0][0]), near),
+        (1, (halves[1], others[1][0]), near),
+        (0, others[0][1:], far),
+        (1, others[1][1:], far),
     ):
         where = tuple((rel, half) for rel in relatives)
-        keep = 0 in relatives
+        keep = where[0][0] == 0
         done = update(rows, where, keep, signs, weight_v, second_v, tuple(done))
     return tuple(done)
 

time: 123 us -> 124 us (level)
    pallas_call x1 -> x2, Pallas kernels: 5.92 us -> 7 us  [prefetch(): pl.pallas_call(prefetch_kernel, in_specs=[pl.BlockSpec(memory_space=pl.AN...]
  transfers between devices with their start and end apart: 29 -> 29, of which waited for: 9 -> 10; matrix products, arithmetic and copies ran while one was open for 1% -> 1% of each run, Pallas kernels for 20% -> 21%
where the time goes in v8:
time: 124 us
  waiting for transfers between devices  59.4 us (48%)
  Pallas kernels  32.5 us (26%)
  starting transfers between devices  28.2 us (23%)
  between operations  2.38 us (2%)
    ppermute x29, waiting for transfers between devices, exchange(): return lax.ppermute(value, AXES, [(i, i ^ mask) for i in range(size)])  59.4 us
    ppermute x29, starting transfers between devices, exchange(): return lax.ppermute(value, AXES, [(i, i ^ mask) for i in range(size)])  28.2 us
    pallas_call x4, Pallas kernels, update(): pl.pallas_call(functools.partial(update_kernel, where, keep, slabs, min(s...  11.4 us
    pallas_call x2, Pallas kernels, prefetch(): pl.pallas_call(prefetch_kernel, in_specs=[pl.BlockSpec(memory_space=pl.AN...  7 us
    pallas_call x2, Pallas kernels, sketch_parts(): pl.pallas_call(functools.partial(sketch_kernel, first, din_local), in_spe...  6.2 us
    pallas_call x3, Pallas kernels, pack(): pl.pallas_call(functools.partial(pack_kernel, groups, width, part), in_sp...  4.92 us
    pallas_call x4, Pallas kernels, project(): pl.pallas_call(functools.partial(project_kernel, n), grid=(1,), in_specs=...  2.91 us
  transfers between devices with their start and end apart: 29, of which 10 were waited for; matrix products, arithmetic and copies ran while one was open for 1% of the time, Pallas kernels for 21%

profile of v8, /device:TPU:0, one launch (start us, length us, event | category | flops | bytes accessed | tf_op | source)
XLA Modules:
  0.0 123.6 jit_solution(1246475425473537321)
XLA Ops:
  1.9 3.7 %sketch.2 = (bf16[2048,512]{1,0:T(8,128)(2,1)S(1)}, f32[256,512]{1,0:T(8,128)S(1)}, f32[256,512]{1,0:T(8,128)S(1)}) custom-call(s32[1,1]{1,0:T(1,128)} %bitcast.40.refs_0_, s32[1,1]{1,0:T(1,128)} %bitcast.41.refs_1_, bf16[1024,2048]{1,0:T(8,128)(2,1)} %refs_0_.3), custom_call_target="tpu_custom_call" | custom-call | flops 1073741824 | bytes 6291456 | tf_op jit(solution)/shard_map/sketch/pallas_call | solution.py:224
  5.6 0.6 collective-permute-start.1
  6.2 2.5 %sketch.3 = (f32[256,512]{1,0:T(8,128)S(1)}, f32[256,512]{1,0:T(8,128)S(1)}) custom-call(bf16[1024,2048]{1,0:T(8,128)(2,1)} %refs_0_.3, bf16[2048,512]{1,0:T(8,128)(2,1)S(1)} %get-tuple-element.32.refs_1_.refs_2_), custom_call_target="tpu_custom_call" | custom-call | flops 1073741824 | bytes 6291456 | tf_op jit(solution)/shard_map/sketch/pallas_call | solution.py:224
  8.9 3.0 %collective-permute-start.2 = (f32[256,512]{1,0:T(8,128)S(1)}, f32[256,512]{1,0:T(8,128)S(1)}, u32[]{:S(2)}, u32[]{:S(2)}) collective-permute-start(f32[256,512]{1,0:T(8,128)S(1)} %add.74), channel_id=1, source_target_pairs={{0,2},{1,3},{2,0},{3,1},{4,6},{5,7},{6,4},{7,5},{8,10},{9,11},{10,... | collective-permute-start | bytes 1572872 | tf_op jit(solution)/shard_map/ppermute | solution.py:421
  11.9 2.0 %pack.3 = (bf16[16,256,128]{2,1,0:T(8,128)(2,1)S(1)}, bf16[16,256,128]{2,1,0:T(8,128)(2,1)S(1)}) custom-call(bf16[256,8192]{1,0:T(8,128)(2,1)} %og_ref.5), custom_call_target="tpu_custom_call" | custom-call | bytes 4194304 | tf_op jit(solution)/shard_map/pack/pallas_call | solution.py:127
  14.0 1.5 %pack.4 = (bf16[8,256,128]{2,1,0:T(8,128)(2,1)S(1)}, bf16[8,256,128]{2,1,0:T(8,128)(2,1)S(1)}) custom-call(bf16[256,8192]{1,0:T(8,128)(2,1)} %og_ref.5), custom_call_target="tpu_custom_call" | custom-call | bytes 2097152 | tf_op jit(solution)/shard_map/pack/pallas_call | solution.py:127
  15.5 1.6 %collective-permute-start.16 = (bf16[8,256,128]{2,1,0:T(8,128)(2,1)S(1)}, bf16[8,256,128]{2,1,0:T(8,128)(2,1)S(1)}, u32[]{:S(2)}, u32[]{:S(2)}) collective-permute-start(bf16[8,256,128]{2,1,0:T(8,128)(2,1)S(1)} %get-tuple-element.45), channel_id=1, source_target_pairs={{0,4},{1,5},{2,6},{3,7},{4,0},{5,1},{6,2},{7,3},{8,12},{9,13},{10,... | collective-permute-start | bytes 1572872 | tf_op jit(solution)/shard_map/ppermute | solution.py:421
  17.1 1.5 %pack.5 = (bf16[8,256,128]{2,1,0:T(8,128)(2,1)S(1)}, bf16[8,256,128]{2,1,0:T(8,128)(2,1)S(1)}) custom-call(bf16[256,8192]{1,0:T(8,128)(2,1)} %og_ref.5), custom_call_target="tpu_custom_call" | custom-call | bytes 2097152 | tf_op jit(solution)/shard_map/pack/pallas_call | solution.py:127
  18.5 0.4 collective-permute-start.17
  18.9 5.1 %collective-permute-done.2 = f32[256,512]{1,0:T(8,128)S(1)} collective-permute-done((f32[256,512]{1,0:T(8,128)S(1)}, f32[256,512]{1,0:T(8,128)S(1)}, u32[]{:S(2)}, u32[]{:S(2)}) %collective-permute-start.2) | collective-permute-done | bytes 524320 | tf_op jit(solution)/shard_map/ppermute | solution.py:421
  24.2 1.9 %collective-permute-start.14 = (bf16[256,512]{1,0:T(8,128)(2,1)S(1)}, bf16[256,512]{1,0:T(8,128)(2,1)S(1)}, u32[]{:S(2)}, u32[]{:S(2)}) collective-permute-start(bf16[256,512]{1,0:T(8,128)(2,1)S(1)} %multiply_convert_fusion.4.refs_0_), channel_id=1, source_target_pairs={{0,4},{1,5},{2,6},{3,7},{4,0},{5,1},{6,2},{7,3},{8,12},{9,13},{10,... | collective-permute-start | bytes 786440 | tf_op jit(solution)/shard_map/ppermute | solution.py:421
  26.1 1.6 %collective-permute-start.4 = (bf16[256,512]{1,0:T(8,128)(2,1)S(1)}, bf16[256,512]{1,0:T(8,128)(2,1)S(1)}, u32[]{:S(2)}, u32[]{:S(2)}) collective-permute-start(bf16[256,512]{1,0:T(8,128)(2,1)S(1)} %multiply_convert_fusion.4.refs_0_), channel_id=1, source_target_pairs={{0,8},{1,9},{2,10},{3,11},{4,12},{5,13},{6,14},{7,15},{8,0},{9,1},... | collective-permute-start | bytes 786440 | tf_op jit(solution)/shard_map/ppermute | solution.py:421
  27.6 2.7 %collective-permute-done.16.refs_6_ = bf16[8,256,128]{2,1,0:T(8,128)(2,1)S(1)} collective-permute-done((bf16[8,256,128]{2,1,0:T(8,128)(2,1)S(1)}, bf16[8,256,128]{2,1,0:T(8,128)(2,1)S(1)}, u32[]{:S(2)}, u32[]{:S(2)}) %collective-permute-start.16) | collective-permute-done | bytes 524320 | tf_op jit(solution)/shard_map/ppermute | solution.py:421
  30.3 16.4 %collective-permute-done.14.refs_2_ = bf16[256,512]{1,0:T(8,128)(2,1)S(1)} collective-permute-done((bf16[256,512]{1,0:T(8,128)(2,1)S(1)}, bf16[256,512]{1,0:T(8,128)(2,1)S(1)}, u32[]{:S(2)}, u32[]{:S(2)}) %collective-permute-start.14) | collective-permute-done | bytes 262176 | tf_op jit(solution)/shard_map/ppermute | solution.py:421
  46.7 1.6 %collective-permute-start.7 = (bf16[8,256,128]{2,1,0:T(8,128)(2,1)S(1)}, bf16[8,256,128]{2,1,0:T(8,128)(2,1)S(1)}, u32[]{:S(2)}, u32[]{:S(2)}) collective-permute-start(bf16[8,256,128]{2,1,0:T(8,128)(2,1)S(1)} %get-tuple-element.39), channel_id=1, source_target_pairs={{0,8},{1,9},{2,10},{3,11},{4,12},{5,13},{6,14},{7,15},{8,0},{9,1},... | collective-permute-start | bytes 1572872 | tf_op jit(solution)/shard_map/ppermute | solution.py:421
  48.3 0.3 collective-permute-start.8
  48.6 0.3 collective-permute-start.5
  48.9 0.7 project.6
  49.7 1.7 %collective-permute-start.18 = (f16[2,128,512]{2,1,0:T(8,128)(2,1)S(1)}, f16[2,128,512]{2,1,0:T(8,128)(2,1)S(1)}, u32[]{:S(2)}, u32[]{:S(2)}) collective-permute-start(f16[2,128,512]{2,1,0:T(8,128)(2,1)S(1)} %multiply_convert_fusion.1), channel_id=1, source_target_pairs={{0,8},{1,9},{2,10},{3,11},{4,12},{5,13},{6,14},{7,15},{8,0},{9,1},... | collective-permute-start | bytes 786440 | tf_op jit(solution)/shard_map/ppermute | solution.py:421
  51.3 0.7 project.7
  52.1 0.6 collective-permute-start.20
  52.7 8.8 %collective-permute-done.7.refs_6_ = bf16[8,256,128]{2,1,0:T(8,128)(2,1)S(1)} collective-permute-done((bf16[8,256,128]{2,1,0:T(8,128)(2,1)S(1)}, bf16[8,256,128]{2,1,0:T(8,128)(2,1)S(1)}, u32[]{:S(2)}, u32[]{:S(2)}) %collective-permute-start.7) | collective-permute-done | bytes 524320 | tf_op jit(solution)/shard_map/ppermute | solution.py:421
  61.5 10.3 %collective-permute-done.8.refs_7_ = bf16[8,256,128]{2,1,0:T(8,128)(2,1)S(1)} collective-permute-done((bf16[8,256,128]{2,1,0:T(8,128)(2,1)S(1)}, bf16[8,256,128]{2,1,0:T(8,128)(2,1)S(1)}, u32[]{:S(2)}, u32[]{:S(2)}) %collective-permute-start.8) | collective-permute-done | bytes 524320 | tf_op jit(solution)/shard_map/ppermute | solution.py:421
  71.8 0.7 project.4
  72.6 1.6 %collective-permute-start.9 = (f16[2,128,512]{2,1,0:T(8,128)(2,1)S(1)}, f16[2,128,512]{2,1,0:T(8,128)(2,1)S(1)}, u32[]{:S(2)}, u32[]{:S(2)}) collective-permute-start(f16[2,128,512]{2,1,0:T(8,128)(2,1)S(1)} %multiply_convert_fusion.3), channel_id=1, source_target_pairs={{0,4},{1,5},{2,6},{3,7},{4,0},{5,1},{6,2},{7,3},{8,12},{9,13},{10,... | collective-permute-start | bytes 786440 | tf_op jit(solution)/shard_map/ppermute | solution.py:421
  74.2 0.7 project.5
  75.0 0.6 collective-permute-start.11
  75.6 2.3 %collective-permute-done.18 = f16[2,128,512]{2,1,0:T(8,128)(2,1)S(1)} collective-permute-done((f16[2,128,512]{2,1,0:T(8,128)(2,1)S(1)}, f16[2,128,512]{2,1,0:T(8,128)(2,1)S(1)}, u32[]{:S(2)}, u32[]{:S(2)}) %collective-permute-start.18) | collective-permute-done | bytes 262176 | tf_op jit(solution)/shard_map/ppermute | solution.py:421
  77.9 0.4 collective-permute-start.19
  78.4 1.8 %collective-permute-start.21 = (f16[128,512]{1,0:T(8,128)(2,1)S(1)}, f16[128,512]{1,0:T(8,128)(2,1)S(1)}, u32[]{:S(2)}, u32[]{:S(2)}) collective-permute-start(f16[128,512]{1,0:T(8,128)(2,1)S(1)} %fusion.13), channel_id=1, source_target_pairs={{0,8},{1,9},{2,10},{3,11},{4,12},{5,13},{6,14},{7,15},{8,0},{9,1},... | collective-permute-start | bytes 393224 | tf_op jit(solution)/shard_map/ppermute | solution.py:421
  80.2 1.6 %collective-permute-done.9 = f16[2,128,512]{2,1,0:T(8,128)(2,1)S(1)} collective-permute-done((f16[2,128,512]{2,1,0:T(8,128)(2,1)S(1)}, f16[2,128,512]{2,1,0:T(8,128)(2,1)S(1)}, u32[]{:S(2)}, u32[]{:S(2)}) %collective-permute-start.9) | collective-permute-done | bytes 262176 | tf_op jit(solution)/shard_map/ppermute | solution.py:421
  81.9 0.6 collective-permute-start.10
  82.5 4.7 %collective-permute-done.11 = f16[2,128,512]{2,1,0:T(8,128)(2,1)S(1)} collective-permute-done((f16[2,128,512]{2,1,0:T(8,128)(2,1)S(1)}, f16[2,128,512]{2,1,0:T(8,128)(2,1)S(1)}, u32[]{:S(2)}, u32[]{:S(2)}) %collective-permute-start.11) | collective-permute-done | bytes 262176 | tf_op jit(solution)/shard_map/ppermute | solution.py:421
  87.3 0.4 collective-permute-start.12
  87.8 2.9 %collective-permute-start.22 = (f16[128,512]{1,0:T(8,128)(2,1)S(1)}, f16[128,512]{1,0:T(8,128)(2,1)S(1)}, u32[]{:S(2)}, u32[]{:S(2)}) collective-permute-start(f16[128,512]{1,0:T(8,128)(2,1)S(1)} %fusion.1), channel_id=1, source_target_pairs={{0,16},{1,17},{2,18},{3,19},{4,20},{5,21},{6,22},{7,23},{8,24},{9,... | collective-permute-start | bytes 393224 | tf_op jit(solution)/shard_map/ppermute | solution.py:421
  90.6 2.0 %collective-permute-done.12 = f16[128,512]{1,0:T(8,128)(2,1)S(1)} collective-permute-done((f16[128,512]{1,0:T(8,128)(2,1)S(1)}, f16[128,512]{1,0:T(8,128)(2,1)S(1)}, u32[]{:S(2)}, u32[]{:S(2)}) %collective-permute-start.12) | collective-permute-done | bytes 131104 | tf_op jit(solution)/shard_map/ppermute | solution.py:421
  92.7 2.7 %collective-permute-start.13 = (f16[128,512]{1,0:T(8,128)(2,1)S(1)}, f16[128,512]{1,0:T(8,128)(2,1)S(1)}, u32[]{:S(2)}, u32[]{:S(2)}) collective-permute-start(f16[128,512]{1,0:T(8,128)(2,1)S(1)} %fusion.6), channel_id=1, source_target_pairs={{0,16},{1,17},{2,18},{3,19},{4,20},{5,21},{6,22},{7,23},{8,24},{9,... | collective-permute-start | bytes 393224 | tf_op jit(solution)/shard_map/ppermute | solution.py:421
  95.4 5.3 %collective-permute-done.22 = f16[128,512]{1,0:T(8,128)(2,1)S(1)} collective-permute-done((f16[128,512]{1,0:T(8,128)(2,1)S(1)}, f16[128,512]{1,0:T(8,128)(2,1)S(1)}, u32[]{:S(2)}, u32[]{:S(2)}) %collective-permute-start.22) | collective-permute-done | bytes 131104 | tf_op jit(solution)/shard_map/ppermute | solution.py:421
  100.9 1.6 %collective-permute-start.25 = (f16[128,512]{1,0:T(8,128)(2,1)S(1)}, f16[128,512]{1,0:T(8,128)(2,1)S(1)}, u32[]{:S(2)}, u32[]{:S(2)}) collective-permute-start(f16[128,512]{1,0:T(8,128)(2,1)S(1)} %get-tuple-element.63), channel_id=1, source_target_pairs={{0,2},{1,3},{2,0},{3,1},{4,6},{5,7},{6,4},{7,5},{8,10},{9,11},{10,... | collective-permute-start | bytes 393224 | tf_op jit(solution)/shard_map/ppermute | solution.py:421
  102.6 0.2 collective-permute-start.27
  102.8 1.3 %collective-permute-start.23 = (f16[128,512]{1,0:T(8,128)(2,1)S(1)}, f16[128,512]{1,0:T(8,128)(2,1)S(1)}, u32[]{:S(2)}, u32[]{:S(2)}) collective-permute-start(f16[128,512]{1,0:T(8,128)(2,1)S(1)} %get-tuple-element.61), channel_id=1, source_target_pairs={{0,2},{1,3},{2,0},{3,1},{4,6},{5,7},{6,4},{7,5},{8,10},{9,11},{10,... | collective-permute-start | bytes 393224 | tf_op jit(solution)/shard_map/ppermute | solution.py:421
  104.1 3.5 %prefetch.2.refs_3_ = f32[1024,2048]{1,0:T(8,128)S(1)} custom-call(f32[1024,2048]{1,0:T(8,128)} %refs_0_.4), custom_call_target="tpu_custom_call" | custom-call | bytes 8388608 | tf_op jit(solution)/shard_map/prefetch/pallas_call | solution.py:308
  107.6 3.5 %prefetch.3.refs_4_ = f32[1024,2048]{1,0:T(8,128)S(1)} custom-call(f32[1024,2048]{1,0:T(8,128)} %refs_0_.5), custom_call_target="tpu_custom_call" | custom-call | bytes 8388608 | tf_op jit(solution)/shard_map/prefetch/pallas_call | solution.py:308
  111.4 2.9 %update.4 = (f32[1024,2048]{1,0:T(8,128)}, f32[1024,2048]{1,0:T(8,128)}, f32[256,512]{1,0:T(8,128)}) custom-call(f32[128,512]{1,0:T(8,128)S(1)} %get-tuple-element.64.refs_0_, f32[128,512]{1,0:T(8,128)S(1)} %convert_element_type.127.refs_1_, bf16[2048,512]{1,0:T(8,128)(2,1)S(1)} %get-tuple-element.32.refs_1_.refs_2_, f32[1024,2048]{1,0:T(8,128)S(1)} %prefetch.2.refs_3_, ...), custom_call_target="tpu_custom_call" | custom-call | flops 1073741824 | bytes 4194304 | tf_op jit(solution)/shard_map/update/pallas_call | solution.py:390
  114.4 0.4 collective-permute-start.24
  114.8 2.9 %update.5 = (f32[1024,2048]{1,0:T(8,128)}, f32[1024,2048]{1,0:T(8,128)}, f32[256,512]{1,0:T(8,128)}) custom-call(f32[128,512]{1,0:T(8,128)S(1)} %get-tuple-element.62.refs_0_, f32[128,512]{1,0:T(8,128)S(1)} %convert_element_type.126.refs_1_, ...), custom_call_target="tpu_custom_call", output_to_operand_aliasing={{0}: (5, {}), {1}: (6, {}), {2}: (7, {})} | custom-call | flops 1073741824 | bytes 4194304 | tf_op jit(solution)/shard_map/update/pallas_call | solution.py:390
  117.8 2.8 %update.6 = (f32[1024,2048]{1,0:T(8,128)}, f32[1024,2048]{1,0:T(8,128)}, f32[256,512]{1,0:T(8,128)}) custom-call(f32[128,512]{1,0:T(8,128)S(1)} %convert_element_type.124.refs_0_, f32[128,512]{1,0:T(8,128)S(1)} %convert_element_type.125.refs_1_, ...), custom_call_target="tpu_custom_call", output_to_operand_aliasing={{0}: (5, {}), {1}: (6, {}), {2}: (7, {})} | custom-call | flops 1073741824 | bytes 4194304 | tf_op jit(solution)/shard_map/update/pallas_call | solution.py:390
  120.7 2.8 %update.7 = (f32[1024,2048]{1,0:T(8,128)}, f32[1024,2048]{1,0:T(8,128)}, f32[256,512]{1,0:T(8,128)}) custom-call(f32[128,512]{1,0:T(8,128)S(1)} %convert_element_type.122.refs_0_, f32[128,512]{1,0:T(8,128)S(1)} %convert_element_type.123.refs_1_, ...), custom_call_target="tpu_custom_call", output_to_operand_aliasing={{0}: (5, {}), {1}: (6, {}), {2}: (7, {})} | custom-call | flops 1073741824 | bytes 4194304 | tf_op jit(solution)/shard_map/update/pallas_call | solution.py:390
  (47 shorter events, 1.7 us)
Async XLA Ops:
  5.6 3.2 %collective-permute-start.1 = (f32[256,512]{1,0:T(8,128)S(1)}, f32[256,512]{1,0:T(8,128)S(1)}, u32[]{:S(2)}, u32[]{:S(2)}) collective-permute-start(f32[256,512]{1,0:T(8,128)S(1)} %get-tuple-element.36), channel_id=1, source_target_pairs={{0,1},{1,0},{2,3},{3,2},{4,5},{5,4},{6,7},{7,6},{8,9},{9,8},{10,11... | collective-permute-start | bytes 1572872 | tf_op jit(solution)/shard_map/ppermute | solution.py:421
  8.7 10.2 %collective-permute-start = (f32[256,512]{1,0:T(8,128)S(1)}, f32[256,512]{1,0:T(8,128)S(1)}, u32[]{:S(2)}, u32[]{:S(2)}) collective-permute-start(f32[256,512]{1,0:T(8,128)S(1)} %get-tuple-element.34), channel_id=1, source_target_pairs={{0,1},{1,0},{2,3},{3,2},{4,5},{5,4},{6,7},{7,6},{8,9},{9,8},{10,11... | collective-permute-start | bytes 1572872 | tf_op jit(solution)/shard_map/ppermute | solution.py:421
  8.9 15.1 %collective-permute-start.2 = (f32[256,512]{1,0:T(8,128)S(1)}, f32[256,512]{1,0:T(8,128)S(1)}, u32[]{:S(2)}, u32[]{:S(2)}) collective-permute-start(f32[256,512]{1,0:T(8,128)S(1)} %add.74), channel_id=1, source_target_pairs={{0,2},{1,3},{2,0},{3,1},{4,6},{5,7},{6,4},{7,5},{8,10},{9,11},{10,... | collective-permute-start | bytes 1572872 | tf_op jit(solution)/shard_map/ppermute | solution.py:421
  13.9 34.4 %collective-permute-start.6 = (bf16[16,256,128]{2,1,0:T(8,128)(2,1)S(1)}, bf16[16,256,128]{2,1,0:T(8,128)(2,1)S(1)}, u32[]{:S(2)}, u32[]{:S(2)}) collective-permute-start(bf16[16,256,128]{2,1,0:T(8,128)(2,1)S(1)} %get-tuple-element.38), channel_id=1, source_target_pairs={{0,1},{1,0},{2,3},{3,2},{4,5},{5,4},{6,7},{7,6},{8,9},{9,8},{10,11... | collective-permute-start | bytes 3145736 | tf_op jit(solution)/shard_map/ppermute | solution.py:421
  15.5 14.9 %collective-permute-start.16 = (bf16[8,256,128]{2,1,0:T(8,128)(2,1)S(1)}, bf16[8,256,128]{2,1,0:T(8,128)(2,1)S(1)}, u32[]{:S(2)}, u32[]{:S(2)}) collective-permute-start(bf16[8,256,128]{2,1,0:T(8,128)(2,1)S(1)} %get-tuple-element.45), channel_id=1, source_target_pairs={{0,4},{1,5},{2,6},{3,7},{4,0},{5,1},{6,2},{7,3},{8,12},{9,13},{10,... | collective-permute-start | bytes 1572872 | tf_op jit(solution)/shard_map/ppermute | solution.py:421
  18.5 28.2 %collective-permute-start.17 = (bf16[8,256,128]{2,1,0:T(8,128)(2,1)S(1)}, bf16[8,256,128]{2,1,0:T(8,128)(2,1)S(1)}, u32[]{:S(2)}, u32[]{:S(2)}) collective-permute-start(bf16[8,256,128]{2,1,0:T(8,128)(2,1)S(1)} %get-tuple-element.46), channel_id=1, source_target_pairs={{0,5},{1,4},{2,7},{3,6},{4,1},{5,0},{6,3},{7,2},{8,13},{9,12},{10,... | collective-permute-start | bytes 1572872 | tf_op jit(solution)/shard_map/ppermute | solution.py:421
  24.2 22.5 %collective-permute-start.14 = (bf16[256,512]{1,0:T(8,128)(2,1)S(1)}, bf16[256,512]{1,0:T(8,128)(2,1)S(1)}, u32[]{:S(2)}, u32[]{:S(2)}) collective-permute-start(bf16[256,512]{1,0:T(8,128)(2,1)S(1)} %multiply_convert_fusion.4.refs_0_), channel_id=1, source_target_pairs={{0,4},{1,5},{2,6},{3,7},{4,0},{5,1},{6,2},{7,3},{8,12},{9,13},{10,... | collective-permute-start | bytes 786440 | tf_op jit(solution)/shard_map/ppermute | solution.py:421
  26.1 22.5 %collective-permute-start.4 = (bf16[256,512]{1,0:T(8,128)(2,1)S(1)}, bf16[256,512]{1,0:T(8,128)(2,1)S(1)}, u32[]{:S(2)}, u32[]{:S(2)}) collective-permute-start(bf16[256,512]{1,0:T(8,128)(2,1)S(1)} %multiply_convert_fusion.4.refs_0_), channel_id=1, source_target_pairs={{0,8},{1,9},{2,10},{3,11},{4,12},{5,13},{6,14},{7,15},{8,0},{9,1},... | collective-permute-start | bytes 786440 | tf_op jit(solution)/shard_map/ppermute | solution.py:421
  30.3 18.5 %collective-permute-start.3 = (bf16[256,512]{1,0:T(8,128)(2,1)S(1)}, bf16[256,512]{1,0:T(8,128)(2,1)S(1)}, u32[]{:S(2)}, u32[]{:S(2)}) collective-permute-start(bf16[256,512]{1,0:T(8,128)(2,1)S(1)} %multiply_convert_fusion.4.refs_0_), channel_id=1, source_target_pairs={{0,1},{1,0},{2,3},{3,2},{4,5},{5,4},{6,7},{7,6},{8,9},{9,8},{10,11... | collective-permute-start | bytes 786440 | tf_op jit(solution)/shard_map/ppermute | solution.py:421
  46.7 2.2 %collective-permute-start.15 = (bf16[256,512]{1,0:T(8,128)(2,1)S(1)}, bf16[256,512]{1,0:T(8,128)(2,1)S(1)}, u32[]{:S(2)}, u32[]{:S(2)}) collective-permute-start(bf16[256,512]{1,0:T(8,128)(2,1)S(1)} %collective-permute-done.14.refs_2_), channel_id=1, source_target_pairs={{0,1},{1,0},{2,3},{3,2},{4,5},{5,4},{6,7},{7,6},{8,9},{9,8},{10,11... | collective-permute-start | bytes 786440 | tf_op jit(solution)/shard_map/ppermute | solution.py:421
  46.7 14.8 %collective-permute-start.7 = (bf16[8,256,128]{2,1,0:T(8,128)(2,1)S(1)}, bf16[8,256,128]{2,1,0:T(8,128)(2,1)S(1)}, u32[]{:S(2)}, u32[]{:S(2)}) collective-permute-start(bf16[8,256,128]{2,1,0:T(8,128)(2,1)S(1)} %get-tuple-element.39), channel_id=1, source_target_pairs={{0,8},{1,9},{2,10},{3,11},{4,12},{5,13},{6,14},{7,15},{8,0},{9,1},... | collective-permute-start | bytes 1572872 | tf_op jit(solution)/shard_map/ppermute | solution.py:421
  48.3 23.5 %collective-permute-start.8 = (bf16[8,256,128]{2,1,0:T(8,128)(2,1)S(1)}, bf16[8,256,128]{2,1,0:T(8,128)(2,1)S(1)}, u32[]{:S(2)}, u32[]{:S(2)}) collective-permute-start(bf16[8,256,128]{2,1,0:T(8,128)(2,1)S(1)} %get-tuple-element.40), channel_id=1, source_target_pairs={{0,9},{1,8},{2,11},{3,10},{4,13},{5,12},{6,15},{7,14},{8,1},{9,0},... | collective-permute-start | bytes 1572872 | tf_op jit(solution)/shard_map/ppermute | solution.py:421
  48.6 23.3 %collective-permute-start.5 = (bf16[256,512]{1,0:T(8,128)(2,1)S(1)}, bf16[256,512]{1,0:T(8,128)(2,1)S(1)}, u32[]{:S(2)}, u32[]{:S(2)}) collective-permute-start(bf16[256,512]{1,0:T(8,128)(2,1)S(1)} %collective-permute-done.4.refs_2_), channel_id=1, source_target_pairs={{0,1},{1,0},{2,3},{3,2},{4,5},{5,4},{6,7},{7,6},{8,9},{9,8},{10,11... | collective-permute-start | bytes 786440 | tf_op jit(solution)/shard_map/ppermute | solution.py:421
  49.6 51.0 %copy-start = (f32[256,512]{1,0:T(8,128)S(1)}, f32[256,512]{1,0:T(8,128)}, u32[]{:S(2)}) copy-start(f32[256,512]{1,0:T(8,128)} %param.11) | copy-start | bytes 1572868
  49.7 28.2 %collective-permute-start.18 = (f16[2,128,512]{2,1,0:T(8,128)(2,1)S(1)}, f16[2,128,512]{2,1,0:T(8,128)(2,1)S(1)}, u32[]{:S(2)}, u32[]{:S(2)}) collective-permute-start(f16[2,128,512]{2,1,0:T(8,128)(2,1)S(1)} %multiply_convert_fusion.1), channel_id=1, source_target_pairs={{0,8},{1,9},{2,10},{3,11},{4,12},{5,13},{6,14},{7,15},{8,0},{9,1},... | collective-permute-start | bytes 786440 | tf_op jit(solution)/shard_map/ppermute | solution.py:421
  52.1 26.3 %collective-permute-start.20 = (f16[2,128,512]{2,1,0:T(8,128)(2,1)S(1)}, f16[2,128,512]{2,1,0:T(8,128)(2,1)S(1)}, u32[]{:S(2)}, u32[]{:S(2)}) collective-permute-start(f16[2,128,512]{2,1,0:T(8,128)(2,1)S(1)} %multiply_convert_fusion), channel_id=1, source_target_pairs={{0,2},{1,3},{2,0},{3,1},{4,6},{5,7},{6,4},{7,5},{8,10},{9,11},{10,... | collective-permute-start | bytes 786440 | tf_op jit(solution)/shard_map/ppermute | solution.py:421
  72.6 9.2 %collective-permute-start.9 = (f16[2,128,512]{2,1,0:T(8,128)(2,1)S(1)}, f16[2,128,512]{2,1,0:T(8,128)(2,1)S(1)}, u32[]{:S(2)}, u32[]{:S(2)}) collective-permute-start(f16[2,128,512]{2,1,0:T(8,128)(2,1)S(1)} %multiply_convert_fusion.3), channel_id=1, source_target_pairs={{0,4},{1,5},{2,6},{3,7},{4,0},{5,1},{6,2},{7,3},{8,12},{9,13},{10,... | collective-permute-start | bytes 786440 | tf_op jit(solution)/shard_map/ppermute | solution.py:421
  75.0 12.3 %collective-permute-start.11 = (f16[2,128,512]{2,1,0:T(8,128)(2,1)S(1)}, f16[2,128,512]{2,1,0:T(8,128)(2,1)S(1)}, u32[]{:S(2)}, u32[]{:S(2)}) collective-permute-start(f16[2,128,512]{2,1,0:T(8,128)(2,1)S(1)} %multiply_convert_fusion.2), channel_id=1, source_target_pairs={{0,4},{1,5},{2,6},{3,7},{4,0},{5,1},{6,2},{7,3},{8,12},{9,13},{10,... | collective-permute-start | bytes 786440 | tf_op jit(solution)/shard_map/ppermute | solution.py:421
  77.9 17.4 %collective-permute-start.19 = (f16[128,512]{1,0:T(8,128)(2,1)S(1)}, f16[128,512]{1,0:T(8,128)(2,1)S(1)}, u32[]{:S(2)}, u32[]{:S(2)}) collective-permute-start(f16[128,512]{1,0:T(8,128)(2,1)S(1)} %fusion.12), channel_id=1, source_target_pairs={{0,2},{1,3},{2,0},{3,1},{4,6},{5,7},{6,4},{7,5},{8,10},{9,11},{10,... | collective-permute-start | bytes 393224 | tf_op jit(solution)/shard_map/ppermute | solution.py:421
  78.4 9.3 %collective-permute-start.21 = (f16[128,512]{1,0:T(8,128)(2,1)S(1)}, f16[128,512]{1,0:T(8,128)(2,1)S(1)}, u32[]{:S(2)}, u32[]{:S(2)}) collective-permute-start(f16[128,512]{1,0:T(8,128)(2,1)S(1)} %fusion.13), channel_id=1, source_target_pairs={{0,8},{1,9},{2,10},{3,11},{4,12},{5,13},{6,14},{7,15},{8,0},{9,1},... | collective-permute-start | bytes 393224 | tf_op jit(solution)/shard_map/ppermute | solution.py:421
  81.9 20.6 %collective-permute-start.10 = (f16[128,512]{1,0:T(8,128)(2,1)S(1)}, f16[128,512]{1,0:T(8,128)(2,1)S(1)}, u32[]{:S(2)}, u32[]{:S(2)}) collective-permute-start(f16[128,512]{1,0:T(8,128)(2,1)S(1)} %fusion.10), channel_id=1, source_target_pairs={{0,2},{1,3},{2,0},{3,1},{4,6},{5,7},{6,4},{7,5},{8,10},{9,11},{10,... | collective-permute-start | bytes 393224 | tf_op jit(solution)/shard_map/ppermute | solution.py:421
  87.3 5.3 %collective-permute-start.12 = (f16[128,512]{1,0:T(8,128)(2,1)S(1)}, f16[128,512]{1,0:T(8,128)(2,1)S(1)}, u32[]{:S(2)}, u32[]{:S(2)}) collective-permute-start(f16[128,512]{1,0:T(8,128)(2,1)S(1)} %fusion.11), channel_id=1, source_target_pairs={{0,2},{1,3},{2,0},{3,1},{4,6},{5,7},{6,4},{7,5},{8,10},{9,11},{10,... | collective-permute-start | bytes 393224 | tf_op jit(solution)/shard_map/ppermute | solution.py:421
  87.8 12.9 %collective-permute-start.22 = (f16[128,512]{1,0:T(8,128)(2,1)S(1)}, f16[128,512]{1,0:T(8,128)(2,1)S(1)}, u32[]{:S(2)}, u32[]{:S(2)}) collective-permute-start(f16[128,512]{1,0:T(8,128)(2,1)S(1)} %fusion.1), channel_id=1, source_target_pairs={{0,16},{1,17},{2,18},{3,19},{4,20},{5,21},{6,22},{7,23},{8,24},{9,... | collective-permute-start | bytes 393224 | tf_op jit(solution)/shard_map/ppermute | solution.py:421
  92.7 9.8 %collective-permute-start.13 = (f16[128,512]{1,0:T(8,128)(2,1)S(1)}, f16[128,512]{1,0:T(8,128)(2,1)S(1)}, u32[]{:S(2)}, u32[]{:S(2)}) collective-permute-start(f16[128,512]{1,0:T(8,128)(2,1)S(1)} %fusion.6), channel_id=1, source_target_pairs={{0,16},{1,17},{2,18},{3,19},{4,20},{5,21},{6,22},{7,23},{8,24},{9,... | collective-permute-start | bytes 393224 | tf_op jit(solution)/shard_map/ppermute | solution.py:421
  100.8 10.3 %collective-permute-start.28 = (f16[128,512]{1,0:T(8,128)(2,1)S(1)}, f16[128,512]{1,0:T(8,128)(2,1)S(1)}, u32[]{:S(2)}, u32[]{:S(2)}) collective-permute-start(f16[128,512]{1,0:T(8,128)(2,1)S(1)} %get-tuple-element.63), channel_id=1, source_target_pairs={{0,1},{1,0},{2,3},{3,2},{4,5},{5,4},{6,7},{7,6},{8,9},{9,8},{10,11... | collective-permute-start | bytes 393224 | tf_op jit(solution)/shard_map/ppermute | solution.py:421
  100.9 10.3 %collective-permute-start.25 = (f16[128,512]{1,0:T(8,128)(2,1)S(1)}, f16[128,512]{1,0:T(8,128)(2,1)S(1)}, u32[]{:S(2)}, u32[]{:S(2)}) collective-permute-start(f16[128,512]{1,0:T(8,128)(2,1)S(1)} %get-tuple-element.63), channel_id=1, source_target_pairs={{0,2},{1,3},{2,0},{3,1},{4,6},{5,7},{6,4},{7,5},{8,10},{9,11},{10,... | collective-permute-start | bytes 393224 | tf_op jit(solution)/shard_map/ppermute | solution.py:421
  102.6 11.7 %collective-permute-start.27 = (f16[128,512]{1,0:T(8,128)(2,1)S(1)}, f16[128,512]{1,0:T(8,128)(2,1)S(1)}, u32[]{:S(2)}, u32[]{:S(2)}) collective-permute-start(f16[128,512]{1,0:T(8,128)(2,1)S(1)} %get-tuple-element.61), channel_id=1, source_target_pairs={{0,1},{1,0},{2,3},{3,2},{4,5},{5,4},{6,7},{7,6},{8,9},{9,8},{10,11... | collective-permute-start | bytes 393224 | tf_op jit(solution)/shard_map/ppermute | solution.py:421
  102.8 11.5 %collective-permute-start.23 = (f16[128,512]{1,0:T(8,128)(2,1)S(1)}, f16[128,512]{1,0:T(8,128)(2,1)S(1)}, u32[]{:S(2)}, u32[]{:S(2)}) collective-permute-start(f16[128,512]{1,0:T(8,128)(2,1)S(1)} %get-tuple-element.61), channel_id=1, source_target_pairs={{0,2},{1,3},{2,0},{3,1},{4,6},{5,7},{6,4},{7,5},{8,10},{9,11},{10,... | collective-permute-start | bytes 393224 | tf_op jit(solution)/shard_map/ppermute | solution.py:421
  111.2 6.6 %collective-permute-start.26 = (f16[128,512]{1,0:T(8,128)(2,1)S(1)}, f16[128,512]{1,0:T(8,128)(2,1)S(1)}, u32[]{:S(2)}, u32[]{:S(2)}) collective-permute-start(f16[128,512]{1,0:T(8,128)(2,1)S(1)} %collective-permute-done.25), channel_id=1, source_target_pairs={{0,1},{1,0},{2,3},{3,2},{4,5},{5,4},{6,7},{7,6},{8,9},{9,8},{10,11... | collective-permute-start | bytes 393224 | tf_op jit(solution)/shard_map/ppermute | solution.py:421
  114.4 6.3 %collective-permute-start.24 = (f16[128,512]{1,0:T(8,128)(2,1)S(1)}, f16[128,512]{1,0:T(8,128)(2,1)S(1)}, u32[]{:S(2)}, u32[]{:S(2)}) collective-permute-start(f16[128,512]{1,0:T(8,128)(2,1)S(1)} %collective-permute-done.23), channel_id=1, source_target_pairs={{0,1},{1,0},{2,3},{3,2},{4,5},{5,4},{6,7},{7,6},{8,9},{9,8},{10,11... | collective-permute-start | bytes 393224 | tf_op jit(solution)/shard_map/ppermute | solution.py:421
